TPU v7x, 128 devices: a whole 4x4x4 slice. The times are simulated.
128 devices in a mesh: tower: 8 (over y, x_lo), member: 16 (over z, x_hi, core).
Axes of the slice: x: 4 (x_hi: 2, x_lo: 2; x = x_hi * 2 + x_lo), y: 4, z: 4, core: 2. Of those that a mesh axis runs over, the one named last changes fastest.
Arguments:
- bag_ids: int32 [16, 16, 4, 2048], P('tower', 'member'), may hold values from 0 to 511
- touch_ids: int32 [16, 16, 128], P('tower', 'member'), may hold values from 0 to 511, as said below
- elapsed: int32 [16, 16, 128], P('tower', 'member'), may hold values from 0 to 39
- tables: float32 [16, 16, 512, 64], P('tower', 'member'), may hold values from -3 to 3
- accumulator: float32 [16, 16, 512], P('tower', 'member'), may hold values from 0.001 to 0.1
- first_weight: float32 [1024, 16, 1024], P(None, 'tower'), may hold values from -0.1875 to 0.1875
- second_weight: float32 [1024, 16, 256], P(None, 'tower'), may hold values from -0.1875 to 0.1875
- lift_weight: float32 [4096, 128], replicated, may hold values from -0.5 to 0.5
- press_weight: float32 [4096, 128], replicated, may hold values from -0.09375 to 0.09375
- head_weight: float32 [4096], replicated, may hold values from -0.09375 to 0.09375
- labels: int32 [16, 128], P('member'), may hold values 0 or 1
Outputs:
- new_tables: float32 [16, 16, 512, 64], P('tower', 'member')
- new_accumulator: float32 [16, 16, 512], P('tower', 'member')
- grad_first: float32 [1024, 16, 1024], P('member', 'tower')
- grad_second: float32 [1024, 16, 256], P('member', 'tower')
- grad_lift: float32 [4096, 128], P(('tower', 'member'))
- grad_press: float32 [4096, 128], P(('tower', 'member'))
- logits: float32 [16, 128], P('member', 'tower')
Inputs may be any that keep to these rules, and one draw needn't show every extreme that they name: `touch_ids`: distinct within each table.
All inputs are finite; a program needn't handle non-finite values. No bound on the sum of `labels` on one device may be relied on, other than what follows from the above.
Results may differ from a plain program's by a relative error of at most 0.0003.
Values sent between devices are 32-bit elements; how exact they have to be, the bound alone decides.
No kernel may reach another device: no remote copies, remote signals or barrier semaphores. Data moves between devices by JAX's collectives and lax.ppermute only.
A program may use at most 128 MiB of HBM per device.

v0:
```python
import math

import jax
import jax.numpy as jnp
from jax import lax
from jax.sharding import PartitionSpec as P

PRECISE = lax.Precision.HIGHEST
DECAY_RATE = 0.98
LEARN_RATE = 1.0
EPSILON = 1e-08


def decay_factors(touch_ids, elapsed, table_rows):
    rates = jnp.exp(elapsed.astype(jnp.float32) * math.log(DECAY_RATE))
    matches = touch_ids[..., None] == jnp.arange(table_rows, dtype=jnp.int32)
    hits = jnp.sum(matches.astype(jnp.float32), axis=-2)
    chosen = jnp.sum(jnp.where(matches, rates[..., None], jnp.float32(0.0)), axis=-2)
    return jnp.where(hits > 0.0, chosen, jnp.float32(1.0))


def bag_counts(bag_block, table_rows):
    matches = bag_block[..., None] == jnp.arange(table_rows, dtype=jnp.int32)
    return jnp.sum(matches.astype(jnp.float32), axis=1)


def per_device(
    bag_ids,
    touch_ids,
    elapsed,
    tables,
    accumulator,
    first_weight,
    second_weight,
    lift_weight,
    press_weight,
    head_weight,
    labels,
):
    table_rows = tables.shape[2]
    factors = decay_factors(touch_ids[:, 0], elapsed[:, 0], table_rows)
    decayed = tables[:, 0] * factors[..., None]
    local_bags = bag_ids[:, 0]
    towers_here = local_bags.shape[0]
    bag_size = local_bags.shape[1]
    all_samples = local_bags.shape[2]
    block_size = min(1024, all_samples)
    block_count = all_samples // block_size
    bag_blocks = jnp.transpose(
        local_bags.reshape(towers_here, bag_size, block_count, block_size), (2, 0, 1, 3)
    )

    def pool_block(bag_block):
        return jnp.einsum(
            "tbr,trw->btw", bag_counts(bag_block, table_rows), decayed, precision=PRECISE
        )

    pooled = lax.map(pool_block, bag_blocks).reshape(all_samples, towers_here, -1)
    features = lax.all_to_all(pooled, "member", split_axis=0, concat_axis=2, tiled=True)
    hidden = jnp.einsum("sti,ith->sth", features, first_weight, precision=PRECISE)
    activated = jax.nn.silu(hidden)
    tower_out = jnp.einsum("sth,hto->sto", activated, second_weight, precision=PRECISE)
    samples = tower_out.shape[0]
    flat_out = tower_out.reshape(samples, -1)
    tower_pos = lax.axis_index("tower")
    rank = lift_weight.shape[1]
    owned_rows = lax.all_to_all(flat_out, "tower", split_axis=0, concat_axis=1, tiled=True)
    owned = owned_rows.shape[0]
    targets = lax.dynamic_slice_in_dim(labels[0], tower_pos * owned, owned, 0).astype(jnp.float32)
    projected = jnp.dot(owned_rows, press_weight, precision=PRECISE)
    scaling = jnp.dot(projected, lift_weight.T, precision=PRECISE)
    crossed = owned_rows * scaling + owned_rows
    logit_values = jnp.dot(crossed, head_weight, precision=PRECISE)
    errors = jax.nn.sigmoid(logit_values) - targets
    grad_crossed = errors[:, None] * head_weight[None, :]
    grad_scaling = grad_crossed * owned_rows
    grad_projected = jnp.dot(grad_scaling, lift_weight, precision=PRECISE)
    grad_owned = grad_crossed * (scaling + 1.0) + jnp.dot(
        grad_projected, press_weight.T, precision=PRECISE
    )
    grad_pair = lax.psum_scatter(
        jnp.concatenate(
            [
                jnp.dot(grad_scaling.T, projected, precision=PRECISE),
                jnp.dot(owned_rows.T, grad_projected, precision=PRECISE),
            ],
            axis=1,
        ),
        ("tower", "member"),
        scatter_dimension=0,
        tiled=True,
    )
    grad_flat = lax.all_to_all(grad_owned, "tower", split_axis=1, concat_axis=0, tiled=True)
    logits_out = logit_values[None, :]
    grad_lift = grad_pair[:, :rank]
    grad_press = grad_pair[:, rank:]
    grad_out = grad_flat.reshape(samples, towers_here, -1)
    grad_act = jnp.einsum("sto,hto->sth", grad_out, second_weight, precision=PRECISE)
    sigmoid_hidden = jax.nn.sigmoid(hidden)
    grad_hidden = grad_act * (sigmoid_hidden * (1.0 + hidden * (1.0 - sigmoid_hidden)))
    piece = features
    grad_first = lax.psum_scatter(
        jnp.einsum("sti,sth->ith", piece, grad_hidden, precision=PRECISE),
        "member",
        scatter_dimension=0,
        tiled=True,
    )
    piece = activated
    grad_second = lax.psum_scatter(
        jnp.einsum("sth,sto->hto", piece, grad_out, precision=PRECISE),
        "member",
        scatter_dimension=0,
        tiled=True,
    )
    grad_features = jnp.einsum("sth,ith->sti", grad_hidden, first_weight, precision=PRECISE)
    grad_pooled = lax.all_to_all(grad_features, "member", split_axis=2, concat_axis=0, tiled=True)
    grad_blocks = grad_pooled.reshape(block_count, block_size, towers_here, -1)

    def add_block(total, inputs):
        bag_block, grad_block = inputs
        counts = bag_counts(bag_block, table_rows)
        return (total + jnp.einsum("tbr,btw->trw", counts, grad_block, precision=PRECISE), None)

    grad_tables, unused = lax.scan(add_block, jnp.zeros_like(decayed), (bag_blocks, grad_blocks))
    mean_square = jnp.mean(grad_tables * grad_tables, axis=-1)
    new_accumulator = accumulator[:, 0] + mean_square
    new_tables = decayed - LEARN_RATE * grad_tables / (
        jnp.sqrt(new_accumulator)[..., None] + EPSILON
    )
    return (
        new_tables[:, None],
        new_accumulator[:, None],
        grad_first,
        grad_second,
        grad_lift,
        grad_press,
        logits_out,
    )


def solution(mesh):
    placed = (
        P("tower", "member", None, None),
        P("tower", "member", None),
        P("tower", "member", None),
        P("tower", "member", None, None),
        P("tower", "member", None),
        P(None, "tower", None),
        P(None, "tower", None),
        P(),
        P(),
        P(),
        P("member", None),
    )
    return jax.shard_map(
        per_device,
        mesh=mesh,
        in_specs=placed,
        out_specs=(
            P("tower", "member", None, None),
            P("tower", "member", None),
            P("member", "tower", None),
            P("member", "tower", None),
            P(("tower", "member"), None),
            P(("tower", "member"), None),
            P("member", "tower"),
        ),
        check_vma=False,
    )
```

profile of v0, /device:TPU:0, one launch (start us, length us, event | category | flops | bytes accessed | tf_op | source)
XLA Modules:
  0.0 968.3 jit_solution(2096970943306372320)
XLA Ops:
  10.7 1.0 bitcast_multiply_fusion
  11.7 13.3 %while.21 = (s32[]{:T(128)}, f32[2,1024,2,64]{1,3,2,0:T(8,128)S(1)}, s32[2,2,4,1024]{3,2,1,0:T(4,128)S(1)}, f32[2,512,64]{1,2,0:T(8,128)S(1)}, s32[]{:T(128)}) while((s32[]{:T(128)}, f32[2,1024,2,64]{1,3,2,0:T(8,128)S(1)}, s32[2,2,4,1024]{3,2,1,0:T(4,128)S(1)}, f32[2,512,64]{1,2,0:T(8,128)S(1)}, s32[]{:T(128)}) %tuple.53), condition=%wide.region_4.5_spmd, body=%wide.region_2.4_spmd.sunk | while | flops 816840704 | bytes 9273421 | solution.py:58
  11.7 2.4 convert_reduce_fusion.5
  14.1 4.2 fusion.70
  18.3 2.4 convert_reduce_fusion.5
  20.7 4.2 fusion.70
  24.9 2.3 copy.106
  27.2 3.4 reshape.88
  30.7 26.3 %all_to_all.68 = f32[16,1,16384]{2,1,0:T(1,128)} all-to-all(f32[16,1,16384]{2,1,0:T(1,128)S(1)} %reshape.88), channel_id=1, replica_groups=mesh['tower'=8,'member'=16] {'member'}, dimensions={0} | all-to-all | bytes 2097152 | tf_op jit(solution)/shard_map/all_to_all | solution.py:59
  57.5 4.4 reduce
  61.9 2.9 reshape.89
  64.8 2.7 copy.108
  67.5 9.8 %fusion.12 = f32[128,2,1024]{2,0,1:T(8,128)S(1)} fusion(f32[128,2,1024]{0,2,1:T(8,128)S(1)} %bitcast.110, f32[1024,2,1024]{2,1,0:T(2,128)} %param.20), kind=kOutput, calls=%fused_computation.24 | convolution fusion | flops 3221225472 | bytes 10485760 | tf_op jit(solution)/shard_map/sti,ith->sth/dot_general | solution.py:60
  77.3 1.0 copy-done.5
  78.3 1.5 fusion.21
  81.0 4.5 all-to-all-start.1
  85.7 7.1 all-to-all-done.1
  92.8 2.9 fusion.41
  95.7 1.8 fusion.42
  97.5 0.9 divide_subtract_fusion
  98.5 1.2 fusion.27
  99.6 1.9 fusion.26
  101.5 1.8 fusion.43
  103.3 2.4 pad_maximum_fusion
  105.8 5.6 copy.109
  111.4 3.4 convolution_add_fusion.1
  114.9 10.6 %all_to_all.69 = f32[16,8,512]{2,0,1:T(8,128)} all-to-all(f32[16,8,512]{2,0,1:T(8,128)S(1)} %bitcast.122), channel_id=1, replica_groups=mesh['tower'=8,'member'=16] {'tower'}, dimensions={1} | all-to-all | bytes 524288 | tf_op jit(solution)/shard_map/all_to_all | solution.py:93
  125.5 1.1 reshape.80
  127.4 4.6 convolution_bitcast_fusion.2
  132.0 4.1 copy.100
  136.2 3.7 fusion.18
  139.9 1.0 copy-done.3
  140.9 9.0 convolution_bitcast_fusion.1
  150.0 13.4 %copy.98 = f32[1024,2,1024]{2,1,0:T(2,128)} copy(f32[1024,2,1024]{0,2,1:T(8,128)} %convolution_bitcast_fusion.1) | data formatting | bytes 16777216 | tf_op jit(solution)/shard_map/sti,sth->ith/transpose | solution.py:103
  163.4 1.2 copy-done.4
  164.6 14.2 %fusion.15 = f32[128,2,1024]{2,0,1:T(8,128)S(1)} fusion(f32[128,2,1024]{2,0,1:T(8,128)S(1)} %copy-done.4, f32[1024,2,1024]{2,1,0:T(2,128)} %param.20), kind=kOutput, calls=%fused_computation.25 | convolution fusion | flops 3221225472 | bytes 10485760 | tf_op jit(solution)/shard_map/sth,ith->sti/dot_general | solution.py:115
  178.8 1.3 copy.91
  180.1 3.7 all-to-all-start.3
  185.1 28.4 %all-to-all-done.3 = f32[128,2,1024]{0,1,2:T(2,128)S(1)} async-done(((f32[128,2,1024]{0,1,2:T(2,128)}), f32[128,2,1024]{0,1,2:T(2,128)S(1)}, u32[]{:S(2)}, u32[]{:S(2)}) %all-to-all-start.3) | async-done | bytes 1048608 | tf_op jit(solution)/shard_map/all_to_all | solution.py:116
  214.7 11.9 %while.22 = (s32[]{:T(128)}, f32[2,512,64]{1,2,0:T(8,128)S(1)}, s32[2,2,4,1024]{3,2,1,0:T(4,128)S(1)}, f32[2,1024,2,64]{1,0,3,2:T(2,128)S(1)}, s32[]{:T(128)}, /*index=5*/s32[]{:T(128)}) while((s32[]{:T(128)}, f32[2,512,64]{1,2,0:T(8,128)S(1)}, s32[2,2,4,1024]{3,2,1,0:T(4,128)S(1)}, f32[2,1024,2,64]{1,0,3,2:T(2,128)S(1)}, ...), condition=%wide.region_7.8_spmd.clone, body=%wide.region_5.7_spmd.clone.sunk | while | flops 816971776 | bytes 10584159 | solution.py:124
  215.3 2.4 convert_reduce_fusion.6
  217.7 2.9 convolution_add_fusion.3
  221.2 2.4 convert_reduce_fusion.6
  223.6 2.9 convolution_add_fusion.3
  228.0 727.8 %reduce-scatter.4.cloned.1.call-done = f32[32,256]{1,0:T(8,128)} async-done(((f32[4096,256]{1,0:T(8,128)}), f32[32,256]{1,0:T(8,128)}) %reduce-scatter.4.cloned.1.call-update) | async-done | bytes 32784
  955.8 1.3 fusion.40
  957.1 1.9 constant_dynamic-slice_fusion.2
  959.0 1.6 constant_dynamic-slice_fusion.1
  (53 shorter events, 9.8 us)
Async XLA Ops:
  8.0 70.3 %copy-start = (f32[1024,2,256]{2,1,0:T(2,128)S(1)}, f32[1024,2,256]{2,1,0:T(2,128)}, u32[]{:S(2)}) copy-start(f32[1024,2,256]{2,1,0:T(2,128)} %param.21) | copy-start | bytes 6291460
  77.3 1.0 copy-start.5
  79.9 17.7 %copy-start.7 = (f32[4096]{0:T(1024)S(1)}, f32[4096]{0:T(1024)}, u32[]{:S(2)}) copy-start(f32[4096]{0:T(1024)} %param.24) | copy-start | bytes 49156
  79.9 17.7 %copy-start.10 = (s32[1,128]{1,0:T(1,128)S(1)}, s32[1,128]{1,0:T(1,128)}, u32[]{:S(2)}) copy-start(s32[1,128]{1,0:T(1,128)} %param.25) | copy-start | bytes 1540
  81.0 11.8 %all-to-all-start.1 = ((f32[8,16,512]{2,1,0:T(8,128)}), f32[8,16,512]{2,1,0:T(8,128)S(1)}, u32[]{:S(2)}, u32[]{:S(2)}) async-start(f32[8,16,512]{2,1,0:T(8,128)} %all_to_all.54), calls=%async_computation.1 | async-start | bytes 524288 | tf_op jit(solution)/shard_map/all_to_all | solution.py:67
  85.5 870.3 %reduce-scatter.4.cloned.1.call-start = ((), (), s32[]{:S(2)}) async-start(), calls=%async_computation.5 | async-start | bytes 4227072
  92.8 2.9 copy-start.2
  111.4 845.8 %all-reduce.5.cloned.1.call-start = ((), (), s32[]{:S(2)}) async-start(), calls=%async_computation.6 | async-start | bytes 20971520
  127.4 8.7 copy-start.8
  139.9 1.1 copy-start.3
  163.4 1.2 copy-start.4
  178.8 5.0 copy-start.11
  180.1 33.3 %all-to-all-start.3 = ((f32[128,2,1024]{0,1,2:T(2,128)}), f32[128,2,1024]{0,1,2:T(2,128)S(1)}, u32[]{:S(2)}, u32[]{:S(2)}) async-start(f32[128,2,1024]{0,1,2:T(2,128)} %copy.91), calls=%async_computation.3 | async-start | bytes 2097152 | tf_op jit(solution)/shard_map/all_to_all | solution.py:116
  214.7 12.0 %copy-start.9 = (f32[2,1,512]{2,1,0:T(1,128)S(1)}, f32[2,1,512]{2,1,0:T(1,128)}, u32[]{:S(2)}) copy-start(f32[2,1,512]{2,1,0:T(1,128)} %param.19) | copy-start | bytes 12292
  214.7 12.6 %copy-start.6 = (f32[2,1,512,64]{2,3,1,0:T(8,128)S(1)}, f32[2,1,512,64]{2,3,1,0:T(8,128)}, u32[]{:S(2)}) copy-start(f32[2,1,512,64]{2,3,1,0:T(8,128)} %param.18) | copy-start | bytes 786436
  226.6 734.0 %copy-start.1 = (f32[1024,2,256]{2,1,0:T(2,128)S(1)}, f32[1024,2,256]{2,1,0:T(2,128)}, u32[]{:S(2)}) copy-start(f32[1024,2,256]{2,1,0:T(2,128)} %param.21) | copy-start | bytes 6291460
Sparse Core Ops, SparseCore 0:
  111.5 844.2 reduce-scatter.3
Sparse Core Ops, SparseCore 1:
  163.5 247.9 all-reduce.4
where the time goes:
time: 975 us; the launch traced here: 968 us
  waiting for transfers between devices  763 us (78%)
  matrix products  71 us (7%)
  local copies, waits for them, and re-layouts  51.3 us (5%)
  blocking collectives  36.9 us (4%)
  other arithmetic  20.5 us (2%)
  between operations  16.7 us (2%)
    unnamed x4, waiting for transfers between devices  728 us
    all_to_all x1, waiting for transfers between devices, per_device(): lax.all_to_all(grad_features, 'member', split_axis=2, concat_axis=0, tile...  28.4 us
    all_to_all x1, blocking collectives, per_device(): lax.all_to_all(pooled, 'member', split_axis=0, concat_axis=2, tiled=True)  26.3 us
  transfers between devices with their start and end apart: 4, of which 3 were waited for; matrix products, arithmetic and copies ran while one was open for 7% of the time, Pallas kernels for 0%

commit v1 on v0

v1 whole, which is shorter than its diff:
```python
import math

import jax
import jax.numpy as jnp
from jax import lax
from jax.experimental import pallas as pl
from jax.experimental.pallas import tpu as pltpu
from jax.sharding import Mesh, PartitionSpec as P

DECAY_RATE = 0.98
LEARN_RATE = 1.0
EPSILON = 1e-08
F32 = jnp.float32
BF16 = jnp.bfloat16
NN = (((1,), (0,)), ((), ()))
NT = (((1,), (1,)), ((), ()))
TOWER = ("y", "xl")
QUAD = ("xh", "core")
VMEM_LIMIT = 50 << 20


def halves(a):
    high = a.astype(BF16)
    return high, (a - high.astype(F32)).astype(BF16)


def dot1(a, b, dims):
    return lax.dot_general(a, b, dims, preferred_element_type=F32)


def dot3(a, b, dims=NN):
    return dot1(a[0], b[0], dims) + (dot1(a[0], b[1], dims) + dot1(a[1], b[0], dims))


def dot32(a, b, dims=NN):
    return dot3(halves(a), halves(b), dims)


def vmem(count):
    return [pl.BlockSpec(memory_space=pltpu.VMEM)] * count


def call(kernel, outs, spec_in, scratch=(), name=None):
    return pl.pallas_call(
        kernel,
        out_shape=outs,
        in_specs=spec_in,
        out_specs=vmem(len(outs)),
        scratch_shapes=list(scratch),
        compiler_params=pltpu.CompilerParams(vmem_limit_bytes=VMEM_LIMIT),
        name=name,
    )


SMEM_SPEC = pl.BlockSpec(memory_space=pltpu.SMEM)


def pool_kernel(bag, touch, elapsed, tables, pooled, decayed, counts):
    towers, width, rows = tables.shape
    touches = touch.shape[1]
    samples = bag.shape[2]
    chunk = samples // pooled.shape[0]
    for t in range(towers):
        ids = jnp.broadcast_to(touch[t : t + 1, :].astype(F32), (touches, touches)).T
        rates = jnp.exp(elapsed[t : t + 1, :].astype(F32) * math.log(DECAY_RATE))
        rates = jnp.broadcast_to(rates, (touches, touches)).T
        factor = []
        for block in range(rows // touches):
            row = lax.broadcasted_iota(jnp.int32, (touches, touches), 1).astype(F32) + float(block * touches)
            match = ids == row
            hits = jnp.sum(jnp.where(match, 1.0, 0.0), axis=0, keepdims=True)
            chosen = jnp.sum(jnp.where(match, rates, 0.0), axis=0, keepdims=True)
            factor.append(jnp.where(hits > 0.0, chosen, 1.0))
        table = tables[t] * jnp.concatenate(factor, axis=1)
        decayed[t] = table
        high, low = halves(table)
        both = jnp.concatenate([high, low], axis=0)
        step = 256

        def block_of(k, carry, t=t, both=both):
            at = pl.multiple_of(k * step, step)
            ids = bag[t, :, pl.ds(at, step)]
            row = lax.broadcasted_iota(jnp.int32, (rows, step), 0)
            count = jnp.zeros((rows, step), F32)
            for b in range(ids.shape[0]):
                count = count + jnp.where(row == ids[b : b + 1, :], 1.0, 0.0)
            count = count.astype(BF16)
            counts[t, :, pl.ds(at, step)] = count
            total = dot1(both, count, NN)
            total = total[:width] + total[width:]
            pooled[k // (chunk // step), t * width : (t + 1) * width, pl.ds(pl.multiple_of((k % (chunk // step)) * step, step), step)] = total
            return carry

        lax.fori_loop(0, samples // step, block_of, 0)


def forward_kernel(pay_rows, idx, x1, x2, y1, y2, w1h, w1l, w2h, w2l, press, lift, head, hidden, start, *rest):
    pay = rest[0] if pay_rows else None
    fh, fl = rest[-2:]
    sets = (x1, x2, y1, y2)
    zs, pair, samples = x1.shape
    width = pair // 2
    xh, core = idx[1], idx[2]
    hid = w1h.shape[-1]
    place = ((xh, core), (1 - xh, core), (xh, 1 - core), (1 - xh, 1 - core))
    depth = zs * width
    for t in range(2):
        for k, ref in enumerate(sets):
            block = jnp.concatenate([ref[z, t * width : (t + 1) * width, :] for z in range(zs)], axis=0)
            h, l = halves(block.T)
            fh[:, k * depth : (k + 1) * depth] = h
            fl[:, k * depth : (k + 1) * depth] = l

        def column(n, out, t=t):
            at = pl.multiple_of(n * 256, 256)
            wh, wl = [], []
            for k in range(4):
                for z in range(zs):
                    table = (z * 2 + place[k][0]) * 2 + place[k][1]
                    wh.append(w1h[t, table, :, pl.ds(at, 256)])
                    wl.append(w1l[t, table, :, pl.ds(at, 256)])
            wh = jnp.concatenate(wh, axis=0)
            wl = jnp.concatenate(wl, axis=0)
            value = dot3((fh[...], fl[...]), (wh, wl))
            hidden[t, :, pl.ds(at, 256)] = value
            act = halves(value * jax.nn.sigmoid(value))
            return out + dot3(act, (w2h[t, pl.ds(at, 256), :], w2l[t, pl.ds(at, 256), :]))

        width_out = w2h.shape[-1]
        out = lax.fori_loop(0, hid // 256, column, jnp.zeros((samples, width_out), F32))
        start[:, t * width_out : (t + 1) * width_out] = out
    if pay_rows:
        own = samples // 2
        x0 = start[pl.ds(pl.multiple_of(core * own, own), own), :]
        rank = press.shape[1]
        weighted = x0 * head[...]
        pay[0:rank, :] = dot32(x0, press[...]).T
        pay[rank : 2 * rank, :] = dot32(weighted, lift[...]).T
        direct = jnp.sum(weighted, axis=1, keepdims=True)
        pay[2 * rank : 2 * rank + 8, :] = jnp.broadcast_to(direct, (own, 128)).T[0:8, :]


def logit_kernel(mine, other, labels, pay, logits):
    total = mine[...] + other[...]
    rank = (total.shape[0] - 8) // 2
    value = jnp.sum(total[0:rank] * total[rank : 2 * rank], axis=0, keepdims=True) + total[2 * rank : 2 * rank + 1]
    logits[...] = value
    error = jax.nn.sigmoid(value) - labels[...].astype(F32)
    pay[0 : 2 * rank, :] = total[0 : 2 * rank]
    pay[2 * rank : 2 * rank + 8, :] = jnp.broadcast_to(error, (8, error.shape[1]))


def grads_kernel(idx, own, c1, xa, xb, hid_a, hid_b, w1h, w1l, w2h, w2l, press, lift, head, ghh, ghl, gout, pq, g0, g1, g2, g3, ps, qs, es):
    z, xh, core = idx[0], idx[1], idx[2]
    rank = press.shape[1]
    n = own.shape[1]
    half = 2 * n
    for base, ref, here in ((0, own, core), (0, c1, 1 - core), (half, xa, core), (half, xb, 1 - core)):
        at = pl.multiple_of(base + here * n, n)
        error = jnp.broadcast_to(ref[2 * rank : 2 * rank + 1, :], (n, n)).T
        p, q = ref[0:rank, :].T, ref[rank : 2 * rank, :].T
        ps[pl.ds(at, n), :] = p
        qs[pl.ds(at, n), :] = q
        es[pl.ds(at, n), :] = error
        pq[pl.ds(at, n), 0:rank] = error * p
        pq[pl.ds(at, n), rank : 2 * rank] = error * q
    width_out = w2h.shape[-1]
    hid = w1h.shape[-1]
    outs = (g0, g1, g2, g3)
    for g, hidden in enumerate((hid_a, hid_b)):
        rows = slice(g * half, (g + 1) * half)
        scaling = dot32(ps[rows, :], lift[...], NT)
        back = dot32(qs[rows, :], press[...], NT)
        go = es[rows, 0:1] * (head[...] * (scaling + 1.0) + back)
        gout[rows, :] = go
        for t in range(2):
            got = halves(go[:, t * width_out : (t + 1) * width_out])

            def column(k, carry, t=t, got=got, hidden=hidden, rows=rows):
                at = pl.multiple_of(k * 256, 256)
                ga = dot3(got, (w2h[t, pl.ds(at, 256), :], w2l[t, pl.ds(at, 256), :]), NT)
                value = hidden[t, :, pl.ds(at, 256)]
                s = jax.nn.sigmoid(value)
                h, l = halves(ga * (s * (1.0 + value * (1.0 - s))))
                ghh[t, rows, pl.ds(at, 256)] = h
                ghl[t, rows, pl.ds(at, 256)] = l
                return carry

            lax.fori_loop(0, hid // 256, column, 0)
    for t in range(2):
        wh, wl = [], []
        for k in range(4):
            table = (lax.rem(z + k, 4) * 2 + xh) * 2 + core
            wh.append(w1h[t, table])
            wl.append(w1l[t, table])
        w = (jnp.concatenate(wh, axis=0), jnp.concatenate(wl, axis=0))
        width = w1h.shape[2]
        for g in range(2):
            rows = slice(g * half, (g + 1) * half)
            grad = dot3(w, (ghh[t, rows, :], ghl[t, rows, :]), NT)
            lane = pl.multiple_of((xh if g == 0 else 1 - xh) * half, half)
            for k in range(4):
                outs[k][t * width : (t + 1) * width, pl.ds(lane, half)] = grad[k * width : (k + 1) * width]


def weights_kernel(idx, fq, ghh, ghl, gout, pq, hid_a, hid_b, x0a, x0b, head, w0, w1, w2, w3, act_t, cross):
    z, xh, core = idx[0], idx[1], idx[2]
    outs = (w0, w1, w2, w3)
    width = fq.shape[1] // 2
    half = hid_a.shape[1]
    quad = 2 * xh + core
    mine = pl.multiple_of(xh * half, half)
    theirs = pl.multiple_of((1 - xh) * half, half)
    width_out = gout.shape[1] // 2
    for t in range(2):
        f = []
        for k in range(4):
            at = lax.rem(z + k, 4)
            f.append(
                jnp.concatenate(
                    [
                        fq[at, t * width : (t + 1) * width, pl.ds(mine, half)],
                        fq[at, t * width : (t + 1) * width, pl.ds(theirs, half)],
                    ],
                    axis=1,
                )
            )
        f = halves(jnp.concatenate(f, axis=0))

        def column(n, carry, t=t, f=f):
            at = pl.multiple_of(n * 256, 256)
            grad = dot3(f, (ghh[t, :, pl.ds(at, 256)], ghl[t, :, pl.ds(at, 256)]))
            for k in range(4):
                outs[k][t * width : (t + 1) * width, pl.ds(at, 256)] = grad[k * width : (k + 1) * width]
            return carry

        lax.fori_loop(0, ghh.shape[-1] // 256, column, 0)
        picked = []
        for k in range(4):
            at = pl.multiple_of(lax.rem(z + k, 4) * 256, 256)
            for g, hidden in enumerate((hid_a, hid_b)):
                value = hidden[t, :, pl.ds(at, 256)]
                act_t[:, g * half : (g + 1) * half] = (value * jax.nn.sigmoid(value)).T
            picked.append(act_t[pl.ds(pl.multiple_of(quad * width, width), width), :])
        act = jnp.concatenate(picked, axis=0)
        grad = dot32(act, gout[:, t * width_out : (t + 1) * width_out])
        base = 2 * width + 16 * t
        for k in range(4):
            for b in range(4):
                outs[k][base : base + 16, b * 256 : (b + 1) * 256] = grad[k * width + 16 * b : k * width + 16 * b + 16]
    rank = pq.shape[1] // 2
    for t in range(2):
        lanes = slice(t * width_out, (t + 1) * width_out)
        x0 = jnp.concatenate([x0a[:, lanes], x0b[:, lanes]], axis=0)
        cross[lanes, 0:rank] = dot32((x0 * head[:, lanes]).T, pq[:, 0:rank])
        cross[lanes, rank : 2 * rank] = dot32(x0.T, pq[:, rank : 2 * rank])
    base = 2 * width + 32
    for k in range(4):
        block = cross[pl.ds(pl.multiple_of((lax.rem(z + k, 4) * 4 + quad) * 32, 32), 32), :]
        for b in range(4):
            outs[k][base : base + 8, b * 256 : (b + 1) * 256] = block[8 * b : 8 * b + 8]


def update_kernel(idx, p0, p1, p2, p3, counts, decayed, accumulator, new_tables, new_accumulator):
    z = idx[0]
    towers, width, rows = decayed.shape
    chunk = p0.shape[1]
    for t in range(towers):
        total = jnp.zeros((2 * width, rows), F32)
        for k, ref in enumerate((p0, p1, p2, p3)):
            at = pl.multiple_of(lax.rem(z + 4 - k, 4) * chunk, chunk)
            high, low = halves(ref[t * width : (t + 1) * width, :])
            total = total + dot1(jnp.concatenate([high, low], axis=0), counts[t, :, pl.ds(at, chunk)], NT)
        grad = total[:width] + total[width:]
        square = jnp.sum(grad * grad, axis=0, keepdims=True) * (1.0 / width)
        fresh = accumulator[t : t + 1, :] + square
        new_accumulator[t : t + 1, :] = fresh
        new_tables[t] = decayed[t] - LEARN_RATE * grad / (jnp.sqrt(fresh) + EPSILON)


def shift(x, axis, size, by):
    return lax.ppermute(x, axis, [(i, (i + by) % size) for i in range(size)])


def flip(x, axis, size, bit):
    return lax.ppermute(x, axis, [(i, i ^ bit) for i in range(size)])


def split_weight(w):
    high = lax.reduce_precision(w, 8, 7)
    return high.astype(BF16), (w - high).astype(BF16)


def per_device(bag_ids, touch_ids, elapsed, tables, accumulator, first_weight, second_weight, lift_weight, press_weight, head_weight, labels):
    f32 = lambda *shape: jax.ShapeDtypeStruct(shape, F32)
    bf16 = lambda *shape: jax.ShapeDtypeStruct(shape, BF16)
    z, xh, core = lax.axis_index("z"), lax.axis_index("xh"), lax.axis_index("core")
    idx = jnp.stack([z, xh, core]).astype(jnp.int32)
    tower = lax.axis_index(TOWER)
    rank = lift_weight.shape[1]
    local = lift_weight.shape[0] // 8
    lift = lax.dynamic_slice_in_dim(lift_weight, tower * local, local, 0)
    press = lax.dynamic_slice_in_dim(press_weight, tower * local, local, 0)
    head = lax.dynamic_slice_in_dim(head_weight, tower * local, local, 0)[None, :]

    tables_t = jnp.transpose(tables[:, 0], (0, 2, 1))
    pooled, decayed, counts = call(
        pool_kernel, [f32(4, 128, 512), f32(2, 64, 512), bf16(2, 512, 2048)], vmem(4), name="pool"
    )(bag_ids[:, 0], touch_ids[:, 0], elapsed[:, 0], tables_t)

    fq = lax.all_to_all(pooled, "z", 0, 0, tiled=True)
    x1 = lax.dynamic_slice_in_dim(fq, xh * 256, 256, 2)
    x1b = lax.dynamic_slice_in_dim(fq, (1 - xh) * 256, 256, 2)
    x2 = shift(x1b, "xh", 2, 1)
    y1 = shift(x1, "core", 2, 1)
    y1b = shift(x1b, "core", 2, 1)
    w1h, w1l = split_weight(jnp.transpose(first_weight, (1, 0, 2)).reshape(2, 16, 64, 1024))
    w2h, w2l = split_weight(jnp.transpose(second_weight, (1, 0, 2)))
    y2 = shift(x2, "core", 2, 1)
    x1_late, x2 = lax.optimization_barrier((x1, x2))
    x2b = shift(x1_late, "xh", 2, 1)
    y2b = shift(x2b, "core", 2, 1)

    scratch = [pltpu.VMEM((256, 1024), BF16)] * 2
    weights = (w1h, w1l, w2h, w2l, press, lift, head)
    hid_a, x0a, pay = call(
        lambda *refs: forward_kernel(True, *refs),
        [f32(2, 256, 1024), f32(256, 512), f32(2 * rank + 8, 128)],
        [SMEM_SPEC] + vmem(11),
        scratch,
        name="forward_a",
    )(idx, x1, x2, y1, y2, *weights)
    hid_b, x0b = call(
        lambda *refs: forward_kernel(False, *refs),
        [f32(2, 256, 1024), f32(256, 512)],
        [SMEM_SPEC] + vmem(11),
        scratch,
        name="forward_b",
    )(idx, x1b, x2b, y1b, y2b, *weights)

    pay = pay + flip(pay, TOWER, 8, 1)
    pay = pay + flip(pay, TOWER, 8, 2)
    pay, logits = call(logit_kernel, [f32(2 * rank + 8, 128), f32(1, 128)], vmem(3), name="logit")(
        pay, flip(pay, TOWER, 8, 4), labels
    )
    logits = lax.dynamic_slice_in_dim(logits, tower * 16, 16, 1)
    pays = [pay] + [flip(pay, QUAD, 4, k) for k in (1, 2, 3)]

    ghh, ghl, gout, pq, *g = call(
        grads_kernel,
        [bf16(2, 512, 1024), bf16(2, 512, 1024), f32(512, 512), f32(512, 2 * rank)] + [f32(128, 512)] * 4,
        [SMEM_SPEC] + vmem(13),
        [pltpu.VMEM((512, rank), F32)] * 3,
        name="grads",
    )(idx, *pays, hid_a, hid_b, *weights)
    got = [g[0]] + [shift(g[k], "z", 4, k) for k in (1, 2, 3)]
    w = call(
        weights_kernel,
        [f32(168, 1024)] * 4,
        [SMEM_SPEC] + vmem(10),
        [pltpu.VMEM((256, 512), F32), pltpu.VMEM((512, 2 * rank), F32)],
        name="weights",
    )(idx, fq, ghh, ghl, gout, pq, hid_a, hid_b, x0a, x0b, head)
    sent = [shift(w[k], "z", 4, k) for k in (1, 2, 3)]
    new_tables, new_accumulator = call(
        update_kernel, [f32(2, 64, 512), f32(2, 512)], [SMEM_SPEC] + vmem(7), name="update"
    )(idx, *got, counts, decayed, accumulator[:, 0])
    total = (w[0] + sent[0]) + (sent[1] + sent[2])
    grad_first = jnp.transpose(total[:128].reshape(2, 64, 1024), (1, 0, 2))
    grad_second = jnp.transpose(total[128:160].reshape(2, 16, 4, 256), (2, 1, 0, 3)).reshape(64, 2, 256)
    cross = jnp.transpose(total[160:168].reshape(8, 4, 256), (1, 0, 2)).reshape(32, 256)
    return (
        jnp.transpose(new_tables, (0, 2, 1))[:, None],
        new_accumulator[:, None],
        grad_first,
        grad_second,
        cross[:, :rank],
        cross[:, rank:],
        logits,
    )


def solution(mesh):
    split = Mesh(mesh.devices.reshape(4, 2, 4, 2, 2), ("y", "xl", "z", "xh", "core"))
    member = ("z", "xh", "core")
    placed = (
        P(TOWER, member, None, None),
        P(TOWER, member, None),
        P(TOWER, member, None),
        P(TOWER, member, None, None),
        P(TOWER, member, None),
        P(None, TOWER, None),
        P(None, TOWER, None),
        P(),
        P(),
        P(),
        P(member, None),
    )
    return jax.shard_map(
        per_device,
        mesh=split,
        in_specs=placed,
        out_specs=(
            P(TOWER, member, None, None),
            P(TOWER, member, None),
            P(member, TOWER, None),
            P(member, TOWER, None),
            P(TOWER + member, None),
            P(TOWER + member, None),
            P(member, TOWER),
        ),
        check_vma=False,
    )
```

time: 975 us -> 196 us (0.20)
  waiting for transfers between devices: 763 us -> 69.6 us
  matrix products: 71 us -> 0 us
  Pallas kernels: 0 us -> 66.9 us
  blocking collectives: 36.9 us -> 0 us
  local copies, waits for them, and re-layouts: 51.3 us -> 19.4 us
  starting transfers between devices: 8.41 us -> 27.2 us
  between operations: 16.7 us -> 0.76 us
    unnamed x4 -> x0, waiting for transfers between devices: 728 us -> none
    dot_general x17 -> x0, matrix products: 71 us -> none  [the longest x1 14.2 us: per_device(): jnp.einsum('sth,ith->sti', grad_hidden, first_weight, precision=PRECISE)]
    pallas_call x0 -> x7, Pallas kernels: none -> 66.9 us  [the longest x1 15.2 us: per_device(): call(grads_kernel, [bf16(2, 512, 1024), bf16(2, 512, 1024), f32(512, 512)...]
    ppermute x0 -> x18, waiting for transfers between devices: none -> 64.7 us  [the longest x12 52.9 us: shift(): return lax.ppermute(x, axis, [(i, (i + by) % size) for i in range(size)])]
    all_to_all x2 -> x0, blocking collectives: 36.9 us -> none  [the longest x1 26.3 us: per_device(): lax.all_to_all(pooled, 'member', split_axis=0, concat_axis=2, tiled=True)]
    all_to_all x2 -> x1, waiting for transfers between devices: 35.4 us -> 4.83 us  [per_device(): fq = lax.all_to_all(pooled, 'z', 0, 0, tiled=True)]
    ppermute x0 -> x18, starting transfers between devices: none -> 21.8 us  [the longest x12 12.8 us: shift(): return lax.ppermute(x, axis, [(i, (i + by) % size) for i in range(size)])]
    unnamed x31 -> x20, local copies, waits for them, and re-layouts: 19.2 us -> 4.72 us
  transfers between devices with their start and end apart: 4 -> 19, of which waited for: 3 -> 7; matrix products, arithmetic and copies ran while one was open for 7% -> 12% of each run, Pallas kernels for 0% -> 16%
where the time goes in v1:
time: 196 us
  waiting for transfers between devices  69.6 us (36%)
  Pallas kernels  66.9 us (34%)
  starting transfers between devices  27.2 us (14%)
  local copies, waits for them, and re-layouts  19.4 us (10%)
  other arithmetic  12 us (6%)
    ppermute x12, waiting for transfers between devices, shift(): return lax.ppermute(x, axis, [(i, (i + by) % size) for i in range(size)])  52.9 us
    pallas_call x1, Pallas kernels, per_device(): call(grads_kernel, [bf16(2, 512, 1024), bf16(2, 512, 1024), f32(512, 512)...  15.2 us
    pallas_call x1, Pallas kernels, per_device(): call(lambda *refs: forward_kernel(True, *refs), [f32(2, 256, 1024), f32(2...  13.6 us
    pallas_call x1, Pallas kernels, per_device(): call(lambda *refs: forward_kernel(False, *refs), [f32(2, 256, 1024), f32(...  13.6 us
    ppermute x12, starting transfers between devices, shift(): return lax.ppermute(x, axis, [(i, (i + by) % size) for i in range(size)])  12.8 us
    ppermute x6, waiting for transfers between devices, flip(): return lax.ppermute(x, axis, [(i, i ^ bit) for i in range(size)])  11.8 us
    pallas_call x1, Pallas kernels, per_device(): call(weights_kernel, [f32(168, 1024)] * 4, [SMEM_SPEC] + vmem(10), [pltpu...  10.9 us
    convert_element_type x2, other arithmetic, split_weight(): return (high.astype(BF16), (w - high).astype(BF16))  10.1 us
  transfers between devices with their start and end apart: 19, of which 7 were waited for; matrix products, arithmetic and copies ran while one was open for 12% of the time, Pallas kernels for 16%

profile of v1, /device:TPU:0, one launch (start us, length us, event | category | flops | bytes accessed | tf_op | source)
XLA Modules:
  0.0 195.9 jit_solution(2849420558324425778)
XLA Ops:
  0.6 0.9 copy-done.1
  1.6 0.8 copy-done.2
  2.4 0.7 copy-done.3
  3.1 0.7 copy-done.4
  3.8 9.1 %pool.1 = (f32[4,128,512]{2,1,0:T(8,128)}, f32[2,64,512]{2,1,0:T(8,128)S(1)}, bf16[2,512,2048]{2,1,0:T(8,128)(2,1)}) custom-call(s32[2,4,2048]{2,1,0:T(4,128)S(1)} %bitcast.36, s32[2,128]{1,0:T(2,128)S(1)} %bitcast.43, s32[2,128]{1,0:T(2,128)S(1)} %bitcast.44, f32[2,64,512]{2,1,0:T(8,128)S(1)} %bitcast.35), custom_call_target="tpu_custom_call" | custom-call | tf_op jit(solution)/shard_map/pool/pallas_call | solution.py:307
  12.9 5.4 %all-to-all-start = ((f32[4,128,512]{2,1,0:T(8,128)}), f32[4,128,512]{2,1,0:T(8,128)S(1)}, u32[]{:S(2)}, u32[]{:S(2)}) async-start(f32[4,128,512]{2,1,0:T(8,128)} %get-tuple-element.33), calls=%async_computation | async-start | bytes 2097152 | tf_op jit(solution)/shard_map/all_to_all | solution.py:311
  18.3 9.4 %copy.18 = f32[2,1024,1024]{2,1,0:T(8,128)} copy(f32[2,1024,1024]{2,0,1:T(2,128)} %bitcast.46) | data formatting | bytes 16777216 | tf_op jit(solution)/shard_map/transpose | solution.py:317
  27.6 0.9 dynamic_slice.22
  28.5 4.8 %all-to-all-done.fq = f32[4,128,512]{2,1,0:T(8,128)S(1)} async-done(((f32[4,128,512]{2,1,0:T(8,128)}), f32[4,128,512]{2,1,0:T(8,128)S(1)}, u32[]{:S(2)}, u32[]{:S(2)}) %all-to-all-start) | async-done | bytes 1048608 | tf_op jit(solution)/shard_map/all_to_all | solution.py:311
  33.4 0.1 constant_dynamic-slice_fusion.3
  33.5 3.1 %collective-permute-start = (f32[4,128,256]{2,1,0:T(8,128)S(1)}, f32[4,128,256]{2,1,0:T(8,128)S(1)}, u32[]{:S(2)}, u32[]{:S(2)}) collective-permute-start(f32[4,128,256]{2,1,0:T(8,128)S(1)} %get-tuple-element.70.refs_1_), channel_id=1, source_target_pairs={{0,2},{2,0},{1,3},{3,1},{4,6},{6,4},{5,7},{7,5},{8,10},{10,8},{9,1... | collective-permute-start | bytes 1572872 | tf_op jit(solution)/shard_map/ppermute | solution.py:282
  36.6 0.1 pad_add_fusion.refs_0_.idx
  36.7 1.1 constant_dynamic-slice_fusion.1
  37.7 1.6 fusion.1
  39.4 8.2 %collective-permute-done.refs_2_ = f32[4,128,256]{2,1,0:T(8,128)S(1)} collective-permute-done((f32[4,128,256]{2,1,0:T(8,128)S(1)}, f32[4,128,256]{2,1,0:T(8,128)S(1)}, u32[]{:S(2)}, u32[]{:S(2)}) %collective-permute-start) | collective-permute-done | bytes 524320 | tf_op jit(solution)/shard_map/ppermute | solution.py:282
  47.5 3.0 %collective-permute-start.9 = (f32[4,128,256]{2,1,0:T(8,128)S(1)}, f32[4,128,256]{2,1,0:T(8,128)S(1)}, u32[]{:S(2)}, u32[]{:S(2)}) collective-permute-start(f32[4,128,256]{2,1,0:T(8,128)S(1)} %get-tuple-element.38.refs_1_), channel_id=1, source_target_pairs={{0,2},{2,0},{1,3},{3,1},{4,6},{6,4},{5,7},{7,5},{8,10},{10,8},{9,1... | collective-permute-start | bytes 1572872 | tf_op jit(solution)/shard_map/ppermute | solution.py:282
  50.6 8.5 %fusion = (bf16[2,16,64,1024]{3,2,1,0:T(8,128)(2,1)}, bf16[2,16,64,1024]{3,2,1,0:T(8,128)(2,1)}) fusion(f32[2,16,64,1024]{3,2,1,0:T(8,128)} %bitcast.45), kind=kLoop, calls=%fused_computation.2 | loop fusion | flops 8388608 | bytes 16777216 | tf_op jit(solution)/shard_map/convert_element_type | solution.py:291
  59.1 13.6 %forward_a.1 = (f32[2,256,1024]{2,1,0:T(8,128)}, f32[256,512]{1,0:T(8,128)S(1)}, f32[264,128]{1,0:T(8,128)S(1)}) custom-call(s32[3]{0:T(128)S(1)} %pad_add_fusion.refs_0_.idx, f32[4,128,256]{2,1,0:T(8,128)S(1)} %get-tuple-element.38.refs_1_, f32[4,128,256]{2,1,0:T(8,128)S(1)} %collective-permute-done.refs_2_, ...), custom_call_target="tpu_custom_call" | custom-call | tf_op jit(solution)/shard_map/forward_a/pallas_call | solution.py:326
  72.7 0.6 collective-permute-start.3
  73.3 0.2 collective-permute-start.10
  73.5 0.3 collective-permute-start.11
  73.8 4.9 %collective-permute-done.3 = f32[264,128]{1,0:T(8,128)S(1)} collective-permute-done((f32[264,128]{1,0:T(8,128)S(1)}, f32[264,128]{1,0:T(8,128)S(1)}, u32[]{:S(2)}, u32[]{:S(2)}) %collective-permute-start.3) | collective-permute-done | bytes 135200 | tf_op jit(solution)/shard_map/ppermute | solution.py:286
  78.7 1.7 collective-permute-start.4
  80.4 3.6 %collective-permute-done.4 = f32[264,128]{1,0:T(8,128)S(1)} collective-permute-done((f32[264,128]{1,0:T(8,128)S(1)}, f32[264,128]{1,0:T(8,128)S(1)}, u32[]{:S(2)}, u32[]{:S(2)}) %collective-permute-start.4) | collective-permute-done | bytes 135200 | tf_op jit(solution)/shard_map/ppermute | solution.py:286
  84.0 3.3 %collective-permute-start.5 = (f32[264,128]{1,0:T(8,128)S(1)}, f32[264,128]{1,0:T(8,128)S(1)}, u32[]{:S(2)}, u32[]{:S(2)}) collective-permute-start(f32[264,128]{1,0:T(8,128)S(1)} %add.37.mine), channel_id=1, source_target_pairs={{0,64},{16,80},{32,96},{48,112},{64,0},{80,16},{96,32},{112,48},{1... | collective-permute-start | bytes 405512 | tf_op jit(solution)/shard_map/ppermute | solution.py:286
  87.3 3.3 %collective-permute-done.5.other = f32[264,128]{1,0:T(8,128)S(1)} collective-permute-done((f32[264,128]{1,0:T(8,128)S(1)}, f32[264,128]{1,0:T(8,128)S(1)}, u32[]{:S(2)}, u32[]{:S(2)}) %collective-permute-start.5) | collective-permute-done | bytes 135200 | tf_op jit(solution)/shard_map/ppermute | solution.py:286
  90.7 0.1 collective-permute-start.6
  90.8 1.1 collective-permute-start.7
  91.9 2.2 %collective-permute-start.8 = (f32[264,128]{1,0:T(8,128)S(1)}, f32[264,128]{1,0:T(8,128)S(1)}, u32[]{:S(2)}, u32[]{:S(2)}) collective-permute-start(f32[264,128]{1,0:T(8,128)S(1)} %get-tuple-element.36.own), channel_id=1, source_target_pairs={{0,3},{1,2},{2,1},{3,0},{4,7},{5,6},{6,5},{7,4},{8,11},{9,10},{10,... | collective-permute-start | bytes 405512 | tf_op jit(solution)/shard_map/ppermute | solution.py:286
  94.1 13.6 %forward_b.1 = (f32[2,256,1024]{2,1,0:T(8,128)}, f32[256,512]{1,0:T(8,128)S(1)}) custom-call(s32[3]{0:T(128)S(1)} %pad_add_fusion.refs_0_.idx, f32[4,128,256]{2,1,0:T(8,128)S(1)} %get-tuple-element.70.refs_1_, f32[4,128,256]{2,1,0:T(8,128)S(1)} %collective-permute-done.9.refs_2_, f32[4,128,256]{2,1,0:T(8,128)S(1)} %collective-permute-done.10.refs_3_, ...), custom_call_target="tpu_custom_call" | custom-call | tf_op jit(solution)/shard_map/forward_b/pallas_call | solution.py:333
  107.8 15.2 %grads.1 = (bf16[2,512,1024]{2,1,0:T(8,128)(2,1)}, bf16[2,512,1024]{2,1,0:T(8,128)(2,1)}, f32[512,512]{1,0:T(8,128)S(1)}, f32[512,256]{1,0:T(8,128)S(1)}, f32[12...) custom-call(s32[3]{0:T(128)S(1)} %pad_add_fusion.refs_0_.idx, ...), custom_call_target="tpu_custom_call" | custom-call | tf_op jit(solution)/shard_map/grads/pallas_call | solution.py:349
  122.9 1.0 copy-done
  123.9 10.9 %weights.1 = (f32[168,1024]{1,0:T(8,128)S(1)}, f32[168,1024]{1,0:T(8,128)S(1)}, f32[168,1024]{1,0:T(8,128)S(1)}, f32[168,1024]{1,0:T(8,128)}) custom-call(s32[3]{0:T(128)S(1)} %pad_add_fusion.refs_0_.idx, f32[4,128,512]{2,1,0:T(8,128)} %copy-done.6, bf16[2,512,1024]{2,1,0:T(8,128)(2,1)} %get-tuple-element.48.ghh, ...), custom_call_target="tpu_custom_call" | custom-call | tf_op jit(solution)/shard_map/weights/pallas_call | solution.py:357
  134.8 0.6 collective-permute-start.15
  135.4 2.1 %collective-permute-start.16 = (f32[168,1024]{1,0:T(8,128)S(1)}, f32[168,1024]{1,0:T(8,128)}, u32[]{:S(2)}, u32[]{:S(2)}) collective-permute-start(f32[168,1024]{1,0:T(8,128)S(1)} %get-tuple-element.56), channel_id=1, source_target_pairs={{0,8},{4,12},{8,0},{12,4},{1,9},{5,13},{9,1},{13,5},{2,10},{6,14},... | collective-permute-start | bytes 2064392 | tf_op jit(solution)/shard_map/ppermute | solution.py:282
  137.5 0.6 collective-permute-start.17
  138.1 1.4 collective-permute-start.12
  139.5 1.5 collective-permute-start.13
  141.0 38.7 %collective-permute-done.12.p1 = f32[128,512]{1,0:T(8,128)S(1)} collective-permute-done((f32[128,512]{1,0:T(8,128)S(1)}, f32[128,512]{1,0:T(8,128)S(1)}, u32[]{:S(2)}, u32[]{:S(2)}) %collective-permute-start.12) | collective-permute-done | bytes 262176 | tf_op jit(solution)/shard_map/ppermute | solution.py:282
  179.7 0.6 constant_dynamic-slice_fusion
  180.3 6.0 %collective-permute-done.14.p3 = f32[128,512]{1,0:T(8,128)S(1)} collective-permute-done((f32[128,512]{1,0:T(8,128)}, f32[128,512]{1,0:T(8,128)S(1)}, u32[]{:S(2)}, u32[]{:S(2)}) %collective-permute-start.14) | collective-permute-done | bytes 262176 | tf_op jit(solution)/shard_map/ppermute | solution.py:282
  186.3 4.5 %update.1 = (f32[2,64,512]{2,1,0:T(8,128)}, f32[2,512]{1,0:T(2,128)S(1)}) custom-call(s32[3]{0:T(128)S(1)} %pad_add_fusion.refs_0_.idx, f32[128,512]{1,0:T(8,128)S(1)} %get-tuple-element.40.p0, f32[128,512]{1,0:T(8,128)S(1)} %collective-permute-done.12.p1, f32[128,512]{1,0:T(8,128)S(1)} %collective-permute-done.13.p2, ...), custom_call_target="tpu_custom_call" | custom-call | tf_op jit(solution)/shard_map/update/pallas_call | solution.py:365
  190.8 0.6 copy.23
  191.4 1.8 add_add_fusion
  193.2 1.2 copy.29
  194.4 0.1 reshape.34
  194.5 0.8 copy.21
  195.3 0.6 fusion.2
  (35 shorter events, 0.2 us)
Async XLA Ops:
  0.6 1.0 copy-start.1
  1.6 0.8 copy-start.2
  2.4 0.7 copy-start.3
  3.1 0.7 copy-start.4
  12.9 20.5 %all-to-all-start = ((f32[4,128,512]{2,1,0:T(8,128)}), f32[4,128,512]{2,1,0:T(8,128)S(1)}, u32[]{:S(2)}, u32[]{:S(2)}) async-start(f32[4,128,512]{2,1,0:T(8,128)} %get-tuple-element.33), calls=%async_computation | async-start | bytes 2097152 | tf_op jit(solution)/shard_map/all_to_all | solution.py:311
  27.6 10.1 %copy-start.7 = (f32[1024,2,256]{2,1,0:T(2,128)S(1)}, f32[1024,2,256]{2,1,0:T(2,128)}, u32[]{:S(2)}) copy-start(f32[1024,2,256]{2,1,0:T(2,128)} %param.17) | copy-start | bytes 6291460
  33.4 6.0 %copy-start.6 = (f32[4,128,512]{2,1,0:T(8,128)}, f32[4,128,512]{2,1,0:T(8,128)S(1)}, u32[]{:S(2)}) copy-start(f32[4,128,512]{2,1,0:T(8,128)S(1)} %all-to-all-done.fq) | copy-start | bytes 3145732
  33.5 14.1 %collective-permute-start = (f32[4,128,256]{2,1,0:T(8,128)S(1)}, f32[4,128,256]{2,1,0:T(8,128)S(1)}, u32[]{:S(2)}, u32[]{:S(2)}) collective-permute-start(f32[4,128,256]{2,1,0:T(8,128)S(1)} %get-tuple-element.70.refs_1_), channel_id=1, source_target_pairs={{0,2},{2,0},{1,3},{3,1},{4,6},{6,4},{5,7},{7,5},{8,10},{10,8},{9,1... | collective-permute-start | bytes 1572872 | tf_op jit(solution)/shard_map/ppermute | solution.py:282
  39.4 19.7 %collective-permute-start.1 = (f32[4,128,256]{2,1,0:T(8,128)S(1)}, f32[4,128,256]{2,1,0:T(8,128)S(1)}, u32[]{:S(2)}, u32[]{:S(2)}) collective-permute-start(f32[4,128,256]{2,1,0:T(8,128)S(1)} %get-tuple-element.38.refs_1_), channel_id=1, source_target_pairs={{0,1},{1,0},{2,3},{3,2},{4,5},{5,4},{6,7},{7,6},{8,9},{9,8},{10,11... | collective-permute-start | bytes 1572872 | tf_op jit(solution)/shard_map/ppermute | solution.py:282
  47.5 26.0 %collective-permute-start.9 = (f32[4,128,256]{2,1,0:T(8,128)S(1)}, f32[4,128,256]{2,1,0:T(8,128)S(1)}, u32[]{:S(2)}, u32[]{:S(2)}) collective-permute-start(f32[4,128,256]{2,1,0:T(8,128)S(1)} %get-tuple-element.38.refs_1_), channel_id=1, source_target_pairs={{0,2},{2,0},{1,3},{3,1},{4,6},{6,4},{5,7},{7,5},{8,10},{10,8},{9,1... | collective-permute-start | bytes 1572872 | tf_op jit(solution)/shard_map/ppermute | solution.py:282
  50.6 8.5 %collective-permute-start.2 = (f32[4,128,256]{2,1,0:T(8,128)S(1)}, f32[4,128,256]{2,1,0:T(8,128)S(1)}, u32[]{:S(2)}, u32[]{:S(2)}) collective-permute-start(f32[4,128,256]{2,1,0:T(8,128)S(1)} %collective-permute-done.refs_2_), channel_id=1, source_target_pairs={{0,1},{1,0},{2,3},{3,2},{4,5},{5,4},{6,7},{7,6},{8,9},{9,8},{10,11... | collective-permute-start | bytes 1572872 | tf_op jit(solution)/shard_map/ppermute | solution.py:282
  59.1 31.6 %copy-start.5 = (s32[1,128]{1,0:T(1,128)S(1)}, s32[1,128]{1,0:T(1,128)}, u32[]{:S(2)}) copy-start(s32[1,128]{1,0:T(1,128)} %labels.1) | copy-start | bytes 1540
  72.7 6.0 %collective-permute-start.3 = (f32[264,128]{1,0:T(8,128)S(1)}, f32[264,128]{1,0:T(8,128)S(1)}, u32[]{:S(2)}, u32[]{:S(2)}) collective-permute-start(f32[264,128]{1,0:T(8,128)S(1)} %get-tuple-element.35), channel_id=1, source_target_pairs={{0,16},{16,0},{32,48},{48,32},{64,80},{80,64},{96,112},{112,96},{1... | collective-permute-start | bytes 405512 | tf_op jit(solution)/shard_map/ppermute | solution.py:286
  73.3 20.8 %collective-permute-start.10 = (f32[4,128,256]{2,1,0:T(8,128)S(1)}, f32[4,128,256]{2,1,0:T(8,128)S(1)}, u32[]{:S(2)}, u32[]{:S(2)}) collective-permute-start(f32[4,128,256]{2,1,0:T(8,128)S(1)} %get-tuple-element.70.refs_1_), channel_id=1, source_target_pairs={{0,1},{1,0},{2,3},{3,2},{4,5},{5,4},{6,7},{7,6},{8,9},{9,8},{10,11... | collective-permute-start | bytes 1572872 | tf_op jit(solution)/shard_map/ppermute | solution.py:282
  73.5 20.6 %collective-permute-start.11 = (f32[4,128,256]{2,1,0:T(8,128)S(1)}, f32[4,128,256]{2,1,0:T(8,128)S(1)}, u32[]{:S(2)}, u32[]{:S(2)}) collective-permute-start(f32[4,128,256]{2,1,0:T(8,128)S(1)} %collective-permute-done.9.refs_2_), channel_id=1, source_target_pairs={{0,1},{1,0},{2,3},{3,2},{4,5},{5,4},{6,7},{7,6},{8,9},{9,8},{10,11... | collective-permute-start | bytes 1572872 | tf_op jit(solution)/shard_map/ppermute | solution.py:282
  78.7 5.3 %collective-permute-start.4 = (f32[264,128]{1,0:T(8,128)S(1)}, f32[264,128]{1,0:T(8,128)S(1)}, u32[]{:S(2)}, u32[]{:S(2)}) collective-permute-start(f32[264,128]{1,0:T(8,128)S(1)} %add.36), channel_id=1, source_target_pairs={{0,32},{16,48},{32,0},{48,16},{64,96},{80,112},{96,64},{112,80},{1... | collective-permute-start | bytes 405512 | tf_op jit(solution)/shard_map/ppermute | solution.py:286
  84.0 6.6 %collective-permute-start.5 = (f32[264,128]{1,0:T(8,128)S(1)}, f32[264,128]{1,0:T(8,128)S(1)}, u32[]{:S(2)}, u32[]{:S(2)}) collective-permute-start(f32[264,128]{1,0:T(8,128)S(1)} %add.37.mine), channel_id=1, source_target_pairs={{0,64},{16,80},{32,96},{48,112},{64,0},{80,16},{96,32},{112,48},{1... | collective-permute-start | bytes 405512 | tf_op jit(solution)/shard_map/ppermute | solution.py:286
  90.7 17.1 %collective-permute-start.6 = (f32[264,128]{1,0:T(8,128)S(1)}, f32[264,128]{1,0:T(8,128)S(1)}, u32[]{:S(2)}, u32[]{:S(2)}) collective-permute-start(f32[264,128]{1,0:T(8,128)S(1)} %get-tuple-element.36.own), channel_id=1, source_target_pairs={{0,1},{1,0},{2,3},{3,2},{4,5},{5,4},{6,7},{7,6},{8,9},{9,8},{10,11... | collective-permute-start | bytes 405512 | tf_op jit(solution)/shard_map/ppermute | solution.py:286
  90.8 17.0 %collective-permute-start.7 = (f32[264,128]{1,0:T(8,128)S(1)}, f32[264,128]{1,0:T(8,128)S(1)}, u32[]{:S(2)}, u32[]{:S(2)}) collective-permute-start(f32[264,128]{1,0:T(8,128)S(1)} %get-tuple-element.36.own), channel_id=1, source_target_pairs={{0,2},{1,3},{2,0},{3,1},{4,6},{5,7},{6,4},{7,5},{8,10},{9,11},{10,... | collective-permute-start | bytes 405512 | tf_op jit(solution)/shard_map/ppermute | solution.py:286
  91.9 15.8 %collective-permute-start.8 = (f32[264,128]{1,0:T(8,128)S(1)}, f32[264,128]{1,0:T(8,128)S(1)}, u32[]{:S(2)}, u32[]{:S(2)}) collective-permute-start(f32[264,128]{1,0:T(8,128)S(1)} %get-tuple-element.36.own), channel_id=1, source_target_pairs={{0,3},{1,2},{2,1},{3,0},{4,7},{5,6},{6,5},{7,4},{8,11},{9,10},{10,... | collective-permute-start | bytes 405512 | tf_op jit(solution)/shard_map/ppermute | solution.py:286
  122.9 1.0 copy-start
  123.9 55.8 %copy-start.8 = (f32[2,1,512]{2,1,0:T(1,128)S(1)}, f32[2,1,512]{2,1,0:T(1,128)}, u32[]{:S(2)}) copy-start(f32[2,1,512]{2,1,0:T(1,128)} %param.15) | copy-start | bytes 12292
  134.8 56.5 %collective-permute-start.15 = (f32[168,1024]{1,0:T(8,128)S(1)}, f32[168,1024]{1,0:T(8,128)}, u32[]{:S(2)}, u32[]{:S(2)}) collective-permute-start(f32[168,1024]{1,0:T(8,128)S(1)} %get-tuple-element.55), channel_id=1, source_target_pairs={{0,4},{4,8},{8,12},{12,0},{1,5},{5,9},{9,13},{13,1},{2,6},{6,10},{... | collective-permute-start | bytes 2064392 | tf_op jit(solution)/shard_map/ppermute | solution.py:282
  135.4 56.0 %collective-permute-start.16 = (f32[168,1024]{1,0:T(8,128)S(1)}, f32[168,1024]{1,0:T(8,128)}, u32[]{:S(2)}, u32[]{:S(2)}) collective-permute-start(f32[168,1024]{1,0:T(8,128)S(1)} %get-tuple-element.56), channel_id=1, source_target_pairs={{0,8},{4,12},{8,0},{12,4},{1,9},{5,13},{9,1},{13,5},{2,10},{6,14},... | collective-permute-start | bytes 2064392 | tf_op jit(solution)/shard_map/ppermute | solution.py:282
  137.5 53.9 %collective-permute-start.17 = (f32[168,1024]{1,0:T(8,128)}, f32[168,1024]{1,0:T(8,128)}, u32[]{:S(2)}, u32[]{:S(2)}) collective-permute-start(f32[168,1024]{1,0:T(8,128)} %get-tuple-element.57), channel_id=1, source_target_pairs={{0,12},{4,0},{8,4},{12,8},{1,13},{5,1},{9,5},{13,9},{2,14},{6,2},{... | collective-permute-start | bytes 2064392 | tf_op jit(solution)/shard_map/ppermute | solution.py:282
  138.1 41.6 %collective-permute-start.12 = (f32[128,512]{1,0:T(8,128)S(1)}, f32[128,512]{1,0:T(8,128)S(1)}, u32[]{:S(2)}, u32[]{:S(2)}) collective-permute-start(f32[128,512]{1,0:T(8,128)S(1)} %get-tuple-element.41), channel_id=1, source_target_pairs={{0,4},{4,8},{8,12},{12,0},{1,5},{5,9},{9,13},{13,1},{2,6},{6,10},{... | collective-permute-start | bytes 786440 | tf_op jit(solution)/shard_map/ppermute | solution.py:282
  139.5 40.8 %collective-permute-start.13 = (f32[128,512]{1,0:T(8,128)}, f32[128,512]{1,0:T(8,128)S(1)}, u32[]{:S(2)}, u32[]{:S(2)}) collective-permute-start(f32[128,512]{1,0:T(8,128)} %get-tuple-element.42), channel_id=1, source_target_pairs={{0,8},{4,12},{8,0},{12,4},{1,9},{5,13},{9,1},{13,5},{2,10},{6,14},... | collective-permute-start | bytes 786440 | tf_op jit(solution)/shard_map/ppermute | solution.py:282
  179.7 6.6 %collective-permute-start.14 = (f32[128,512]{1,0:T(8,128)}, f32[128,512]{1,0:T(8,128)S(1)}, u32[]{:S(2)}, u32[]{:S(2)}) collective-permute-start(f32[128,512]{1,0:T(8,128)} %get-tuple-element.43), channel_id=1, source_target_pairs={{0,12},{4,0},{8,4},{12,8},{1,13},{5,1},{9,5},{13,9},{2,14},{6,2},{... | collective-permute-start | bytes 786440 | tf_op jit(solution)/shard_map/ppermute | solution.py:282

commit v2 on v1

v2 whole, which is shorter than its diff:
```python
import math

import jax
import jax.numpy as jnp
from jax import lax
from jax.experimental import pallas as pl
from jax.experimental.pallas import tpu as pltpu
from jax.sharding import Mesh, PartitionSpec as P

DECAY_RATE = 0.98
LEARN_RATE = 1.0
EPSILON = 1e-08
F32 = jnp.float32
BF16 = jnp.bfloat16
NN = (((1,), (0,)), ((), ()))
NT = (((1,), (1,)), ((), ()))
TOWER = ("y", "xl")
QUAD = ("xh", "core")
VMEM_LIMIT = 16 << 20


def halves(a):
    high = a.astype(BF16)
    return high, (a - high.astype(F32)).astype(BF16)


def dot1(a, b, dims):
    return lax.dot_general(a, b, dims, preferred_element_type=F32)


def dot3(a, b, dims=NN):
    return dot1(a[0], b[0], dims) + (dot1(a[0], b[1], dims) + dot1(a[1], b[0], dims))


def dot32(a, b, dims=NN):
    return dot3(halves(a), halves(b), dims)


def vmem(count):
    return [pl.BlockSpec(memory_space=pltpu.VMEM)] * count


def call(kernel, outs, spec_in, scratch=(), name=None, flops=0):
    return pl.pallas_call(
        kernel,
        cost_estimate=pl.CostEstimate(flops=int(flops), transcendentals=0, bytes_accessed=1 << 20),
        out_shape=outs,
        in_specs=spec_in,
        out_specs=vmem(len(outs)),
        scratch_shapes=list(scratch),
        compiler_params=pltpu.CompilerParams(vmem_limit_bytes=VMEM_LIMIT),
        name=name,
    )


SMEM_SPEC = pl.BlockSpec(memory_space=pltpu.SMEM)


def decay(touch, elapsed, tables, decayed):
    towers, width, rows = tables.shape
    touches = touch.shape[1]
    for t in range(towers):
        ids = jnp.broadcast_to(touch[t : t + 1, :].astype(F32), (touches, touches)).T
        rates = jnp.exp(elapsed[t : t + 1, :].astype(F32) * math.log(DECAY_RATE))
        rates = jnp.broadcast_to(rates, (touches, touches)).T
        factor = []
        for block in range(rows // touches):
            row = lax.broadcasted_iota(jnp.int32, (touches, touches), 1).astype(F32) + float(block * touches)
            match = ids == row
            hits = jnp.sum(jnp.where(match, 1.0, 0.0), axis=0, keepdims=True)
            chosen = jnp.sum(jnp.where(match, rates, 0.0), axis=0, keepdims=True)
            factor.append(jnp.where(hits > 0.0, chosen, 1.0))
        decayed[t] = tables[t] * jnp.concatenate(factor, axis=1)


def pool_half(side, bag, decayed, pooled, counts):
    towers, width, rows = decayed.shape
    chunks, _, part = pooled.shape
    for t in range(towers):
        both = jnp.concatenate(halves(decayed[t]), axis=0)

        def block_of(k, carry, t=t, both=both):
            at = pl.multiple_of(k * 2 * part + side * part, part)
            ids = bag[t, :, pl.ds(at, part)]
            row = lax.broadcasted_iota(jnp.int32, (rows, part), 0)
            count = jnp.zeros((rows, part), F32)
            for b in range(ids.shape[0]):
                count = count + jnp.where(row == ids[b : b + 1, :], 1.0, 0.0)
            count = count.astype(BF16)
            counts[t, k] = count
            total = dot1(both, count, NN)
            pooled[k, t * width : (t + 1) * width, :] = total[:width] + total[width:]
            return carry

        lax.fori_loop(0, chunks, block_of, 0)


def pool_far_kernel(idx, bag_hbm, touch_hbm, elapsed_hbm, tables_hbm, pooled, counts, decayed, bag, touch, elapsed, tables, sems):
    pairs = ((bag_hbm, bag), (touch_hbm, touch), (elapsed_hbm, elapsed), (tables_hbm, tables))
    copies = [pltpu.make_async_copy(a, b, sems.at[n]) for n, (a, b) in enumerate(pairs)]
    for copy in copies:
        copy.start()
    for copy in copies:
        copy.wait()
    decay(touch, elapsed, tables, decayed)
    pool_half(1 - idx[1], bag, decayed, pooled, counts)


def pool_near_kernel(idx, bag, decayed, pooled, counts):
    pool_half(idx[1], bag, decayed, pooled, counts)


def turn_kernel(w, high, low):
    rows = w.shape[0]
    flat = w.reshape(rows * 16, 128)
    for t in range(2):
        for b in range(8):
            h, l = halves(flat[pl.ds(b * 2 + t, rows, stride=16), :].T)
            high[t, b * 128 : (b + 1) * 128, :] = h
            low[t, b * 128 : (b + 1) * 128, :] = l


def pick_kernel(idx, w, high, low):
    rows = w.shape[2]
    flat = w.reshape(rows * 16, 128)
    for t in range(2):
        for b in range(8):
            h, l = halves(flat[pl.ds(b * 2 + t, rows, stride=16), :])
            high[t, :, b * 128 : (b + 1) * 128] = h
            low[t, :, b * 128 : (b + 1) * 128] = l


def second_kernel(w, high, low, high_t, low_t):
    rows = w.shape[0]
    flat = w.reshape(rows * 4, 128)
    for t in range(2):
        for b in range(2):
            lanes = slice(b * 128, (b + 1) * 128)
            value = flat[pl.ds(b * 2 + t, rows, stride=4), :]
            h, l = halves(value)
            high[t, :, lanes] = h
            low[t, :, lanes] = l
            h, l = halves(value.T)
            high_t[t, lanes, :] = h
            low_t[t, lanes, :] = l


def forward_kernel(with_pay, idx, x1, x2, y1, y2, w1h, w1l, w2h, w2l, press, lift, head, hidden, start, *rest):
    fh, fl = rest[-2:]
    sets = (x1, x2, y1, y2)
    zs, pair, samples = x1.shape
    width = pair // 2
    xh, core = idx[1], idx[2]
    place = ((xh, core), (1 - xh, core), (xh, 1 - core), (1 - xh, 1 - core))
    width_out = w2h.shape[1]

    def one_tower(t, carry):
        for (a, b), ref in zip(place, sets):
            for z in range(zs):
                h, l = halves(ref[z, pl.ds(pl.multiple_of(t * width, width), width), :])
                at = pl.multiple_of(((z * 2 + a) * 2 + b) * width, width)
                fh[pl.ds(at, width), :] = h
                fl[pl.ds(at, width), :] = l
        value = dot3((w1h[t], w1l[t]), (fh[...], fl[...]))
        hidden[t] = value
        act = halves(value * jax.nn.sigmoid(value))
        start[pl.ds(pl.multiple_of(t * width_out, width_out), width_out), :] = dot3((w2h[t], w2l[t]), act)
        return carry

    lax.fori_loop(0, 2, one_tower, 0)
    if with_pay:
        pay = rest[0]
        own = samples // 2
        rank = press.shape[1]
        x0 = halves(start[:, pl.ds(pl.multiple_of(core * own, own), own)])
        p = dot3(halves(press[...].T), x0)
        q = dot3(halves(lift[...].T * head[...]), x0)
        d = dot3(halves(jnp.broadcast_to(head[...], (8, head.shape[1]))), x0)
        for j in range(pay.shape[0]):
            pay[j, 0:rank, :] = p
            pay[j, rank : 2 * rank, :] = q
            pay[j, 2 * rank : 2 * rank + 8, :] = d


def logit_kernel(parts, labels, pay, logits):
    total = parts[0]
    for j in range(1, parts.shape[0]):
        total = total + parts[j]
    rank = (total.shape[0] - 8) // 2
    value = jnp.sum(total[0:rank] * total[rank : 2 * rank], axis=0, keepdims=True) + total[2 * rank : 2 * rank + 1]
    logits[...] = value
    error = jax.nn.sigmoid(value) - labels[...].astype(F32)
    pay[0 : 2 * rank, :] = total[0 : 2 * rank]
    pay[2 * rank : 2 * rank + 8, :] = jnp.broadcast_to(error, (8, error.shape[1]))


def grads_kernel(idx, own, c1, xa, xb, hid_a, hid_b, w1h, w1l, w2h, w2l, press, lift, head, ghh, ghl, gout, pq, g0, g1, g2, g3):
    core = idx[2]
    rank = press.shape[1]
    n = own.shape[1]
    half = 2 * n
    outs = (g0, g1, g2, g3)
    width = w1h.shape[1] // 4
    width_out = w2h.shape[2]
    column = jnp.broadcast_to(head[...], (128, head.shape[1])).T[:, 0:1]
    first_core = core == 0
    for g, (mine, other, hidden) in enumerate(((own, c1, hid_a), (xa, xb, hid_b))):
        left = jnp.where(first_core, mine[...], other[...])
        right = jnp.where(first_core, other[...], mine[...])
        both = jnp.concatenate([left, right], axis=1)
        p, q, error = both[0:rank], both[rank : 2 * rank], both[2 * rank : 2 * rank + 1]
        lanes = slice(g * half, (g + 1) * half)
        pq[0:rank, lanes] = error * p
        pq[rank : 2 * rank, lanes] = error * q
        scaling = dot32(lift[...], p)
        back = dot32(press[...], q)
        gout[:, lanes] = error * (column * (scaling + 1.0) + back)

        def one_tower(t, carry, lanes=lanes, hidden=hidden):
            go = halves(gout[pl.ds(pl.multiple_of(t * width_out, width_out), width_out), lanes])
            ga = dot3((w2h[t], w2l[t]), go)
            value = hidden[t]
            s = jax.nn.sigmoid(value)
            gh = halves(ga * (s * (1.0 + value * (1.0 - s))))
            ghh[t, :, lanes] = gh[0]
            ghl[t, :, lanes] = gh[1]
            grad = dot3((w1h[t], w1l[t]), gh)
            for k in range(4):
                outs[k][pl.ds(pl.multiple_of(t * width, width), width), lanes] = grad[k * width : (k + 1) * width]
            return carry

        lax.fori_loop(0, 2, one_tower, 0)


def weights_kernel(idx, near, far, ghh, ghl, gout, hid_a, hid_b, x0a, x0b, pq, *blocks):
    z, quad = idx[0], 2 * idx[1] + idx[2]
    width = near.shape[1] // 2
    width_out = gout.shape[0] // 2
    for t in range(2):
        outs = blocks[4 * t : 4 * t + 4]
        rows = slice(t * width, (t + 1) * width)
        f, act = [], []
        for k in range(4):
            at = lax.rem(z + k, 4)
            f.append(jnp.concatenate([near[at, rows, :], far[at, rows, :]], axis=1))
            pick = pl.ds(pl.multiple_of((at * 4 + quad) * width, width), width)
            value = jnp.concatenate([hid_a[t, pick, :], hid_b[t, pick, :]], axis=1)
            act.append(value * jax.nn.sigmoid(value))
        grad = dot3(halves(jnp.concatenate(f, axis=0)), (ghh[t], ghl[t]), NT)
        for k in range(4):
            outs[k][0:width, :] = grad[k * width : (k + 1) * width]
        grad = dot32(jnp.concatenate(act, axis=0), gout[t * width_out : (t + 1) * width_out, :], NT)
        for k in range(4):
            for b in range(4):
                outs[k][width : width + 16, b * 256 : (b + 1) * 256] = grad[k * width + 16 * b : k * width + 16 * b + 16]
    rank = pq.shape[0] // 2
    x0 = []
    for k in range(4):
        pick = pl.ds(pl.multiple_of((lax.rem(z + k, 4) * 4 + quad) * 32, 32), 32)
        x0.append(jnp.concatenate([x0a[pick, :], x0b[pick, :]], axis=1))
    x0 = jnp.concatenate(x0, axis=0)
    both = dot32(x0, pq[...], NT)
    for k in range(4):
        for b in range(4):
            outs[k][width + 16 : width + 24, b * 256 : (b + 1) * 256] = both[32 * k + 8 * b : 32 * k + 8 * b + 8]


def update_kernel(idx, p0, p1, p2, p3, near, far, decayed, accumulator, new_tables, new_accumulator):
    z = idx[0]
    towers, width, rows = decayed.shape
    half = p0.shape[1] // 2
    for t in range(towers):
        total = jnp.zeros((2 * width, rows), F32)
        for k, ref in enumerate((p0, p1, p2, p3)):
            at = lax.rem(z + 4 - k, 4)
            both = jnp.concatenate(halves(ref[t * width : (t + 1) * width, :]), axis=0)
            total = total + dot1(both[:, :half], near[t, at], NT)
            total = total + dot1(both[:, half:], far[t, at], NT)
        grad = total[:width] + total[width:]
        square = jnp.sum(grad * grad, axis=0, keepdims=True) * (1.0 / width)
        fresh = accumulator[t : t + 1, :] + square
        new_accumulator[t : t + 1, :] = fresh
        new_tables[t] = decayed[t] - LEARN_RATE * grad / (jnp.sqrt(fresh) + EPSILON)


def sum_kernel(head, *refs):
    parts, (first, second, lift, press) = refs[:6], refs[6:]
    for t in range(2):
        a, b, c = parts[3 * t : 3 * t + 3]
        total = a[...] + (b[...] + c[...])
        for k in range(8):
            first[pl.ds(2 * k + t, 64, stride=16), :] = total[0:64, k * 128 : (k + 1) * 128]
        for b in range(4):
            for o in range(2):
                lanes = slice(b * 256 + o * 128, b * 256 + (o + 1) * 128)
                second[pl.ds(b * 64 + 2 * o + t, 16, stride=4), :] = total[64:80, lanes]
        if t == 1:
            column = jnp.broadcast_to(head[...], (128, 32)).T
            for b in range(4):
                at = slice(8 * b, 8 * b + 8)
                lift[at, :] = column[at] * total[80:88, b * 256 : b * 256 + 128]
                press[at, :] = total[80:88, b * 256 + 128 : (b + 1) * 256]


def shift(x, axis, size, by):
    return lax.ppermute(x, axis, [(i, (i + by) % size) for i in range(size)])


def flip(x, axis, size, bit):
    return lax.ppermute(x, axis, [(i, i ^ bit) for i in range(size)])


def per_device(bag_ids, touch_ids, elapsed, tables, accumulator, first_weight, second_weight, lift_weight, press_weight, head_weight, labels):
    f32 = lambda *shape: jax.ShapeDtypeStruct(shape, F32)
    bf16 = lambda *shape: jax.ShapeDtypeStruct(shape, BF16)
    z, xh, core = lax.axis_index("z"), lax.axis_index("xh"), lax.axis_index("core")
    idx = jnp.stack([z, xh, core]).astype(jnp.int32)
    tower = lax.axis_index(TOWER)
    rank = lift_weight.shape[1]
    local = lift_weight.shape[0] // 8
    any_spec = pl.BlockSpec(memory_space=pl.ANY)

    tables_t = jnp.transpose(tables[:, 0], (0, 2, 1))
    bag = bag_ids[:, 0]
    hbm = lambda x: pltpu.with_memory_space_constraint(x, pltpu.HBM)
    pooled_far, counts_far, decayed = call(
        pool_far_kernel,
        [f32(4, 128, 256), bf16(2, 4, 512, 256), f32(2, 64, 512)],
        [SMEM_SPEC] + [any_spec] * 4,
        [
            pltpu.VMEM((2, 4, 2048), jnp.int32),
            pltpu.VMEM((2, 128), jnp.int32),
            pltpu.VMEM((2, 128), jnp.int32),
            pltpu.VMEM((2, 64, 512), F32),
            pltpu.SemaphoreType.DMA((4,)),
        ],
        name="pool_far",
        flops=1e6,
    )(idx, hbm(bag), hbm(touch_ids[:, 0]), hbm(elapsed[:, 0]), hbm(tables_t))
    fq_far = lax.all_to_all(pooled_far, "z", 0, 0, tiled=True)
    pooled_near, counts_near = call(
        pool_near_kernel, [f32(4, 128, 256), bf16(2, 4, 512, 256)], [SMEM_SPEC] + vmem(2), name="pool_near", flops=1e6
    )(idx, bag, decayed)
    fq_near = lax.all_to_all(pooled_near, "z", 0, 0, tiled=True)

    _, first_weight, second_weight, lift_weight, press_weight, head_weight = lax.optimization_barrier(
        (decayed, first_weight, second_weight, lift_weight, press_weight, head_weight)
    )
    lift = lax.dynamic_slice_in_dim(lift_weight, tower * local, local, 0)
    press = lax.dynamic_slice_in_dim(press_weight, tower * local, local, 0)
    head = lax.dynamic_slice_in_dim(head_weight, tower * local, local, 0)[None, :]
    mine = lax.dynamic_slice_in_dim(head[0], ((z * 2 + xh) * 2 + core) * 32, 32, 0)[None, :]
    view = first_weight.reshape(1024, 2, 8, 128).transpose(0, 2, 1, 3).reshape(1024, 16, 128)
    w1th, w1tl = pl.pallas_call(
        turn_kernel,
        grid=(8,),
        in_specs=[pl.BlockSpec((128, 16, 128), lambda i: (i, 0, 0))],
        out_specs=[pl.BlockSpec((2, 1024, 128), lambda i: (0, 0, i))] * 2,
        out_shape=[bf16(2, 1024, 1024)] * 2,
        compiler_params=pltpu.CompilerParams(vmem_limit_bytes=VMEM_LIMIT),
        cost_estimate=pl.CostEstimate(flops=int(1e6), transcendentals=0, bytes_accessed=1 << 20),
        name="turn",
    )(hbm(view))
    w1qh, w1ql = pl.pallas_call(
        pick_kernel,
        grid_spec=pltpu.PrefetchScalarGridSpec(
            num_scalar_prefetch=1,
            grid=(4,),
            in_specs=[pl.BlockSpec((1, 1, 64, 16, 128), lambda k, i: (lax.rem(i[0] + k, 4), 2 * i[1] + i[2], 0, 0, 0))],
            out_specs=[pl.BlockSpec((2, 64, 1024), lambda k, i: (0, k, 0))] * 2,
        ),
        out_shape=[bf16(2, 256, 1024)] * 2,
        compiler_params=pltpu.CompilerParams(vmem_limit_bytes=VMEM_LIMIT),
        cost_estimate=pl.CostEstimate(flops=int(1e6), transcendentals=0, bytes_accessed=1 << 20),
        name="pick",
    )(idx, hbm(view.reshape(4, 4, 64, 16, 128)))
    w2h, w2l, w2th, w2tl = call(
        second_kernel, [bf16(2, 1024, 256)] * 2 + [bf16(2, 256, 1024)] * 2, vmem(1), name="second", flops=1e6
    )(second_weight.reshape(1024, 2, 2, 128).transpose(0, 2, 1, 3).reshape(1024, 4, 128))

    ready, _ = lax.optimization_barrier((fq_far, pooled_near))
    x2 = flip(ready, "xh", 2, 1)
    y1 = flip(fq_near, "core", 2, 1)
    y2 = flip(x2, "core", 2, 1)
    x2b = flip(fq_near, "xh", 2, 1)
    y1b = flip(fq_far, "core", 2, 1)
    y2b = flip(x2b, "core", 2, 1)

    scratch = [pltpu.VMEM((1024, 256), BF16)] * 2
    weights = (w1th, w1tl, w2th, w2tl, press, lift, head)
    hid_a, x0a, pay = call(
        lambda *refs: forward_kernel(True, *refs),
        [f32(2, 1024, 256), f32(512, 256), f32(8, 2 * rank + 8, 128)],
        [SMEM_SPEC] + vmem(11),
        scratch,
        name="forward_a",
        flops=1e6,
    )(idx, fq_near, x2, y1, y2, *weights)
    parts = lax.all_to_all(pay, TOWER, 0, 0, tiled=True)
    hid_b, x0b = call(
        lambda *refs: forward_kernel(False, *refs),
        [f32(2, 1024, 256), f32(512, 256)],
        [SMEM_SPEC] + vmem(11),
        scratch,
        name="forward_b",
        flops=1e6,
    )(idx, fq_far, x2b, y1b, y2b, *weights)
    pay, logits = call(logit_kernel, [f32(2 * rank + 8, 128), f32(1, 128)], vmem(2), name="logit", flops=1e6)(parts, labels)
    logits = lax.dynamic_slice_in_dim(logits, tower * 16, 16, 1)
    pays = [pay] + [flip(pay, QUAD, 4, k) for k in (1, 2, 3)]

    ghh, ghl, gout, pq, *g = call(
        grads_kernel,
        [bf16(2, 1024, 512), bf16(2, 1024, 512), f32(512, 512), f32(2 * rank, 512)] + [f32(128, 512)] * 4,
        [SMEM_SPEC] + vmem(13),
        name="grads",
        flops=9e9,
    )(idx, *pays, hid_a, hid_b, w1qh, w1ql, w2h, w2l, press, lift, head)
    got = [g[0]] + [shift(g[k], "z", 4, k) for k in (1, 2, 3)]
    w = call(
        weights_kernel,
        [f32(80, 1024)] * 4 + [f32(88, 1024)] * 4,
        [SMEM_SPEC] + vmem(10),
        name="weights",
        flops=5e9,
    )(idx, fq_near, fq_far, ghh, ghl, gout, hid_a, hid_b, x0a, x0b, pq)
    w, v = w[:4], w[4:]
    up = shift(w[2], "z", 4, 1)
    down = shift(v[2], "z", 4, 3)
    v1 = shift(v[1], "z", 4, 1)
    w3 = shift(w[3], "z", 4, 3)
    w1 = shift(w[1] + up, "z", 4, 1)
    v3 = shift(v[3] + down, "z", 4, 3)
    new_tables, new_accumulator = call(
        update_kernel, [f32(2, 64, 512), f32(2, 512)], [SMEM_SPEC] + vmem(8), name="update", flops=5e9
    )(idx, *got, counts_near, counts_far, decayed, accumulator[:, 0])
    first, second, lift_out, press_out = call(
        sum_kernel, [f32(1024, 128), f32(256, 128), f32(32, rank), f32(32, rank)], vmem(7), name="sum", flops=1e6
    )(mine, w[0], w1, w3, v[0], v1, v3)
    return (
        jnp.transpose(new_tables, (0, 2, 1))[:, None],
        new_accumulator[:, None],
        first.reshape(64, 8, 2, 128).transpose(0, 2, 1, 3).reshape(64, 2, 1024),
        second.reshape(64, 2, 2, 128).transpose(0, 2, 1, 3).reshape(64, 2, 256),
        lift_out,
        press_out,
        logits,
    )


def solution(mesh):
    split = Mesh(mesh.devices.reshape(4, 2, 4, 2, 2), ("y", "xl", "z", "xh", "core"))
    member = ("z", "xh", "core")
    placed = (
        P(TOWER, member, None, None),
        P(TOWER, member, None),
        P(TOWER, member, None),
        P(TOWER, member, None, None),
        P(TOWER, member, None),
        P(None, TOWER, None),
        P(None, TOWER, None),
        P(),
        P(),
        P(),
        P(member, None),
    )
    return jax.shard_map(
        per_device,
        mesh=split,
        in_specs=placed,
        out_specs=(
            P(TOWER, member, None, None),
            P(TOWER, member, None),
            P(member, TOWER, None),
            P(member, TOWER, None),
            P(TOWER + member, None),
            P(TOWER + member, None),
            P(member, TOWER),
        ),
        check_vma=False,
    )
```

time: 196 us -> 164 us (0.84)
  waiting for transfers between devices: 69.6 us -> 42.7 us
  Pallas kernels: 66.9 us -> 56.4 us
  blocking collectives: 0 us -> 10.5 us
  other arithmetic: 12 us -> 2.11 us
  starting transfers between devices: 27.2 us -> 32.6 us
    ppermute x12 -> x9, waiting for transfers between devices: 52.9 us -> 14.8 us  [shift(): return lax.ppermute(x, axis, [(i, (i + by) % size) for i in range(size)])]
    ppermute x6 -> x9, waiting for transfers between devices: 11.8 us -> 24.6 us  [flip(): return lax.ppermute(x, axis, [(i, i ^ bit) for i in range(size)])]
    pallas_call x7 -> x12, Pallas kernels: 66.9 us -> 56.4 us  [the longest x1 9.62 us: per_device(): call(grads_kernel, [bf16(2, 1024, 512), bf16(2, 1024, 512), f32(512, 512)...]
    all_to_all x0 -> x1, blocking collectives: none -> 10.5 us  [per_device(): fq_near = lax.all_to_all(pooled_near, 'z', 0, 0, tiled=True)]
    convert_element_type x2 -> x0, other arithmetic: 10.1 us -> none  [split_weight(): return (high.astype(BF16), (w - high).astype(BF16))]
    transpose x2 -> x0, local copies, waits for them, and re-layouts: 10.1 us -> none  [the longest x1 9.36 us: per_device(): jnp.transpose(first_weight, (1, 0, 2)).reshape(2, 16, 64, 1024)]
    unnamed x20 -> x64, local copies, waits for them, and re-layouts: 4.72 us -> 14.5 us
    all_to_all x1 -> x2, starting transfers between devices: 5.39 us -> 10.6 us  [the longest x1 5.39 us: per_device(): fq_far = lax.all_to_all(pooled_far, 'z', 0, 0, tiled=True)]
  transfers between devices with their start and end apart: 19 -> 20, of which waited for: 7 -> 6; matrix products, arithmetic and copies ran while one was open for 12% -> 4% of each run, Pallas kernels for 16% -> 17%
where the time goes in v2:
time: 164 us; the launch traced here: 163 us
  Pallas kernels  56.4 us (34%)
  waiting for transfers between devices  42.7 us (26%)
  starting transfers between devices  32.6 us (20%)
  local copies, waits for them, and re-layouts  17.7 us (11%)
  blocking collectives  10.5 us (6%)
  other arithmetic  2.11 us (1%)
    ppermute x9, waiting for transfers between devices, flip(): return lax.ppermute(x, axis, [(i, i ^ bit) for i in range(size)])  24.6 us
    ppermute x9, waiting for transfers between devices, shift(): return lax.ppermute(x, axis, [(i, (i + by) % size) for i in range(size)])  14.8 us
    unnamed x64, local copies, waits for them, and re-layouts  14.5 us
    ppermute x9, starting transfers between devices, shift(): return lax.ppermute(x, axis, [(i, (i + by) % size) for i in range(size)])  12.4 us
    all_to_all x1, blocking collectives, per_device(): fq_near = lax.all_to_all(pooled_near, 'z', 0, 0, tiled=True)  10.5 us
    pallas_call x1, Pallas kernels, per_device(): call(grads_kernel, [bf16(2, 1024, 512), bf16(2, 1024, 512), f32(512, 512)...  9.62 us
    ppermute x9, starting transfers between devices, flip(): return lax.ppermute(x, axis, [(i, i ^ bit) for i in range(size)])  9.58 us
    pallas_call x1, Pallas kernels, per_device(): pl.pallas_call(turn_kernel, grid=(8,), in_specs=[pl.BlockSpec((128, 16, 1...  8.59 us
  transfers between devices with their start and end apart: 20, of which 6 were waited for; matrix products, arithmetic and copies ran while one was open for 4% of the time, Pallas kernels for 17%

profile of v2, /device:TPU:0, one launch (start us, length us, event | category | flops | bytes accessed | tf_op | source)
XLA Modules:
  0.0 162.9 jit_solution(1496013631001288185)
XLA Ops:
  0.7 5.8 %pool_far.1 = (f32[4,128,256]{2,1,0:T(8,128)}, bf16[2,4,512,256]{3,2,1,0:T(8,128)(2,1)S(1)}, f32[2,64,512]{2,1,0:T(8,128)S(1)}) custom-call(s32[3]{0:T(128)S(1)} %pad_add_fusion.idx.refs_0_, s32[2,4,2048]{2,1,0:T(4,128)} %bitcast.44, s32[2,128]{1,0:T(2,128)} %bitcast.54, s32[2,128]{1,0:T(2,128)} %bitcast.55, f32[2,64,512]{2,1,0:T(8,128)} %bitcast.53), custom_call_target="tpu_custom_call" | custom-call | flops 1000000 | bytes 1048576 | tf_op jit(solution)/shard_map/pool_far/pallas_call | solution.py:326
  6.6 1.3 copy-done.16
  7.9 5.4 %all-to-all-start.1 = ((f32[4,128,256]{2,1,0:T(8,128)}), f32[4,128,256]{2,1,0:T(8,128)S(1)}, u32[]{:S(2)}, u32[]{:S(2)}) async-start(f32[4,128,256]{2,1,0:T(8,128)} %get-tuple-element.57), calls=%async_computation.1 | async-start | bytes 1048576 | tf_op jit(solution)/shard_map/all_to_all | solution.py:340
  13.3 0.8 copy-done.12
  14.1 3.9 %pool_near.1 = (f32[4,128,256]{2,1,0:T(8,128)S(1)}, bf16[2,4,512,256]{3,2,1,0:T(8,128)(2,1)S(1)}) custom-call(s32[3]{0:T(128)S(1)} %pad_add_fusion.idx.refs_0_, s32[2,4,2048]{2,1,0:T(4,128)S(1)} %bitcast.45, f32[2,64,512]{2,1,0:T(8,128)S(1)} %get-tuple-element.55.decayed), custom_call_target="tpu_custom_call" | custom-call | flops 1000000 | bytes 1048576 | tf_op jit(solution)/shard_map/pool_near/pallas_call | solution.py:341
  18.0 1.4 copy-done.18
  19.4 3.4 %all-to-all-done.1.refs_1_.far = f32[4,128,256]{2,1,0:T(8,128)S(1)} async-done(((f32[4,128,256]{2,1,0:T(8,128)}), f32[4,128,256]{2,1,0:T(8,128)S(1)}, u32[]{:S(2)}, u32[]{:S(2)}) %all-to-all-start.1) | async-done | bytes 524320 | tf_op jit(solution)/shard_map/all_to_all | solution.py:340
  22.8 3.0 %collective-permute-start = (f32[4,128,256]{2,1,0:T(8,128)S(1)}, f32[4,128,256]{2,1,0:T(8,128)S(1)}, u32[]{:S(2)}, u32[]{:S(2)}) collective-permute-start(f32[4,128,256]{2,1,0:T(8,128)S(1)} %all-to-all-done.1.refs_1_.far), channel_id=1, source_target_pairs={{0,2},{2,0},{1,3},{3,1},{4,6},{6,4},{5,7},{7,5},{8,10},{10,8},{9,1... | collective-permute-start | bytes 1572872 | tf_op jit(solution)/shard_map/ppermute | solution.py:310
  25.8 10.5 %all_to_all.15.refs_1_.near = f32[4,128,256]{2,1,0:T(8,128)S(1)} all-to-all(f32[4,128,256]{2,1,0:T(8,128)S(1)} %get-tuple-element.56), channel_id=1, replica_groups=mesh['y'=4,'xl'=2,'z'=4,'xh'=2,'core'=2] {'z'}, dimensions={0} | all-to-all | bytes 1048576 | tf_op jit(solution)/shard_map/all_to_all | solution.py:344
  36.8 0.8 dynamic_slice.19
  37.5 8.6 %turn.1 = (bf16[2,1024,1024]{2,1,0:T(8,128)(2,1)S(1)}, bf16[2,1024,1024]{2,1,0:T(8,128)(2,1)S(1)}) custom-call(f32[1024,16,128]{2,1,0:T(8,128)} %bitcast.51), custom_call_target="tpu_custom_call" | custom-call | flops 1000000 | bytes 1048576 | tf_op jit(solution)/shard_map/turn/pallas_call | solution.py:354
  46.2 0.7 second.1
  46.9 1.4 copy-done.22
  48.3 1.6 copy-done.24
  49.9 1.1 constant_dynamic-slice_fusion.1
  51.0 7.9 %forward_a.1 = (f32[2,1024,256]{2,1,0:T(8,128)S(1)}, f32[512,256]{1,0:T(8,128)S(1)}, f32[8,264,128]{2,1,0:T(8,128)S(1)}) custom-call(s32[3]{0:T(128)S(1)} %pad_add_fusion.idx.refs_0_, f32[4,128,256]{2,1,0:T(8,128)S(1)} %all_to_all.15.refs_1_.near, f32[4,128,256]{2,1,0:T(8,128)S(1)} %collective-permute-done.refs_2_, ...), custom_call_target="tpu_custom_call" | custom-call | flops 1000000 | bytes 1048576 | tf_op jit(solution)/shard_map/forward_a/pallas_call | solution.py:391
  58.9 1.0 copy-done.11
  59.9 1.3 copy-done.20
  61.2 0.8 copy-done.26
  62.0 5.2 %all-to-all-start.2 = ((f32[8,264,128]{2,1,0:T(8,128)}), f32[8,264,128]{2,1,0:T(8,128)S(1)}, u32[]{:S(2)}, u32[]{:S(2)}) async-start(f32[8,264,128]{2,1,0:T(8,128)} %copy-done.11), calls=%async_computation.2 | async-start | bytes 2162688 | tf_op jit(solution)/shard_map/all_to_all | solution.py:399
  67.2 2.7 %collective-permute-start.6 = (f32[4,128,256]{2,1,0:T(8,128)}, f32[4,128,256]{2,1,0:T(8,128)}, u32[]{:S(2)}, u32[]{:S(2)}) collective-permute-start(f32[4,128,256]{2,1,0:T(8,128)} %copy-done.8), channel_id=1, source_target_pairs={{0,2},{2,0},{1,3},{3,1},{4,6},{6,4},{5,7},{7,5},{8,10},{10,8},{9,1... | collective-permute-start | bytes 1572872 | tf_op jit(solution)/shard_map/ppermute | solution.py:310
  69.9 24.4 %collective-permute-done.6.refs_2_ = f32[4,128,256]{2,1,0:T(8,128)} collective-permute-done((f32[4,128,256]{2,1,0:T(8,128)}, f32[4,128,256]{2,1,0:T(8,128)}, u32[]{:S(2)}, u32[]{:S(2)}) %collective-permute-start.6) | collective-permute-done | bytes 524320 | tf_op jit(solution)/shard_map/ppermute | solution.py:310
  94.4 0.6 collective-permute-start.3
  95.0 0.8 collective-permute-start.4
  95.8 2.1 %collective-permute-start.5 = (f32[264,128]{1,0:T(8,128)S(1)}, f32[264,128]{1,0:T(8,128)S(1)}, u32[]{:S(2)}, u32[]{:S(2)}) collective-permute-start(f32[264,128]{1,0:T(8,128)S(1)} %get-tuple-element.69.own), channel_id=1, source_target_pairs={{0,3},{1,2},{2,1},{3,0},{4,7},{5,6},{6,5},{7,4},{8,11},{9,10},{10,... | collective-permute-start | bytes 405512 | tf_op jit(solution)/shard_map/ppermute | solution.py:310
  97.9 4.3 %pick.1 = (bf16[2,256,1024]{2,1,0:T(8,128)(2,1)S(1)}, bf16[2,256,1024]{2,1,0:T(8,128)(2,1)S(1)}) custom-call(s32[3]{0:T(128)S(1)} %pad_add_fusion.idx.refs_0_, f32[4,4,64,16,128]{4,3,2,1,0:T(8,128)} %bitcast.52), custom_call_target="tpu_custom_call" | custom-call | flops 1000000 | bytes 1048576 | tf_op jit(solution)/shard_map/pick/pallas_call | solution.py:364
  102.4 7.6 %forward_b.1 = (f32[2,1024,256]{2,1,0:T(8,128)S(1)}, f32[512,256]{1,0:T(8,128)S(1)}) custom-call(s32[3]{0:T(128)S(1)} %pad_add_fusion.idx.refs_0_, f32[4,128,256]{2,1,0:T(8,128)S(1)} %copy-done.7, f32[4,128,256]{2,1,0:T(8,128)} %collective-permute-done.6.refs_2_, f32[4,128,256]{2,1,0:T(8,128)} %collective-permute-done.7.refs_3_, ...), custom_call_target="tpu_custom_call" | custom-call | flops 1000000 | bytes 1048576 | tf_op jit(solution)/shard_map/forward_b/pallas_call | solution.py:400
  110.1 9.6 %grads.1 = (bf16[2,1024,512]{2,1,0:T(8,128)(2,1)S(1)}, bf16[2,1024,512]{2,1,0:T(8,128)(2,1)S(1)}, f32[512,512]{1,0:T(8,128)S(1)}, f32[256,512]{1,0:T(8,128)S(1)}...) custom-call(s32[3]{0:T(128)S(1)} %pad_add_fusion.idx.refs_0_, ...), custom_call_target="tpu_custom_call" | custom-call | flops 8999999488 | bytes 1048576 | tf_op jit(solution)/shard_map/grads/pallas_call | solution.py:412
  119.7 3.5 %weights.1 = (f32[80,1024]{1,0:T(8,128)S(1)}, f32[80,1024]{1,0:T(8,128)S(1)}, f32[80,1024]{1,0:T(8,128)}, f32[80,1024]{1,0:T(8,128)S(1)}, f32[88,1024]{1,0:T(8,1...) custom-call(s32[3]{0:T(128)S(1)} %pad_add_fusion.idx.refs_0_, ...), custom_call_target="tpu_custom_call" | custom-call | flops 5000000000 | bytes 1048576 | tf_op jit(solution)/shard_map/weights/pallas_call | solution.py:420
  123.3 1.2 collective-permute-start.16
  124.5 0.9 collective-permute-start.12
  125.3 0.6 collective-permute-start.9
  125.9 3.3 %collective-permute-start.10 = (f32[128,512]{1,0:T(8,128)}, f32[128,512]{1,0:T(8,128)}, u32[]{:S(2)}, u32[]{:S(2)}) collective-permute-start(f32[128,512]{1,0:T(8,128)} %get-tuple-element.78), channel_id=1, source_target_pairs={{0,8},{4,12},{8,0},{12,4},{1,9},{5,13},{9,1},{13,5},{2,10},{6,14},... | collective-permute-start | bytes 786440 | tf_op jit(solution)/shard_map/ppermute | solution.py:306
  129.2 0.8 dynamic-slice_bitcast_fusion.head
  130.0 0.6 constant_dynamic-slice_fusion
  130.5 6.0 %collective-permute-done.12 = f32[80,1024]{1,0:T(8,128)} collective-permute-done((f32[80,1024]{1,0:T(8,128)}, f32[80,1024]{1,0:T(8,128)}, u32[]{:S(2)}, u32[]{:S(2)}) %collective-permute-start.12) | collective-permute-done | bytes 327712 | tf_op jit(solution)/shard_map/ppermute | solution.py:306
  136.5 1.0 add.32
  137.5 3.3 %collective-permute-start.15 = (f32[88,1024]{1,0:T(8,128)S(1)}, f32[88,1024]{1,0:T(8,128)S(1)}, u32[]{:S(2)}, u32[]{:S(2)}) collective-permute-start(f32[88,1024]{1,0:T(8,128)S(1)} %get-tuple-element.95), channel_id=1, source_target_pairs={{0,4},{4,8},{8,12},{12,0},{1,5},{5,9},{9,13},{13,1},{2,6},{6,10},{... | collective-permute-start | bytes 1081352 | tf_op jit(solution)/shard_map/ppermute | solution.py:306
  140.8 1.0 add.33
  141.9 5.8 %collective-permute-done.9.p1 = f32[128,512]{1,0:T(8,128)S(1)} collective-permute-done((f32[128,512]{1,0:T(8,128)}, f32[128,512]{1,0:T(8,128)S(1)}, u32[]{:S(2)}, u32[]{:S(2)}) %collective-permute-start.9) | collective-permute-done | bytes 262176 | tf_op jit(solution)/shard_map/ppermute | solution.py:306
  147.6 3.2 %collective-permute-start.17 = (f32[88,1024]{1,0:T(8,128)S(1)}, f32[88,1024]{1,0:T(8,128)S(1)}, u32[]{:S(2)}, u32[]{:S(2)}) collective-permute-start(f32[88,1024]{1,0:T(8,128)S(1)} %add.33), channel_id=1, source_target_pairs={{0,12},{4,0},{8,4},{12,8},{1,13},{5,1},{9,5},{13,9},{2,14},{6,2},{... | collective-permute-start | bytes 1081352 | tf_op jit(solution)/shard_map/ppermute | solution.py:306
  150.9 1.6 copy-done.17
  152.5 1.6 copy-done.19
  154.1 0.9 copy-done.29
  155.0 3.3 %update.1 = (f32[2,64,512]{2,1,0:T(8,128)}, f32[2,512]{1,0:T(2,128)S(1)}) custom-call(s32[3]{0:T(128)S(1)} %pad_add_fusion.idx.refs_0_, f32[128,512]{1,0:T(8,128)S(1)} %copy-done.29, f32[128,512]{1,0:T(8,128)S(1)} %collective-permute-done.9.p1, f32[128,512]{1,0:T(8,128)} %collective-permute-done.10.p2, f32[128,512]{1,0:T(8,128)} %collective-permute-done.11.p3, ...), custom_call_target="tpu_custom_call" | custom-call | flops 5000000000 | bytes 1048576 | tf_op jit(solution)/shard_map/update/pallas_call | solution.py:434
  158.3 0.6 copy.23
  158.9 3.0 %collective-permute-done.13.refs_1_ = f32[80,1024]{1,0:T(8,128)S(1)} collective-permute-done((f32[80,1024]{1,0:T(8,128)S(1)}, f32[80,1024]{1,0:T(8,128)S(1)}, u32[]{:S(2)}, u32[]{:S(2)}) %collective-permute-start.13) | collective-permute-done | bytes 327712 | tf_op jit(solution)/shard_map/ppermute | solution.py:306
  161.9 1.0 sum.1
  (76 shorter events, 0.8 us)
Async XLA Ops:
  6.6 1.3 copy-start.16
  7.9 38.2 %copy-start.13 = (f32[2,64,512]{2,1,0:T(8,128)}, f32[2,64,512]{2,1,0:T(8,128)S(1)}, u32[]{:S(2)}) copy-start(f32[2,64,512]{2,1,0:T(8,128)S(1)} %get-tuple-element.55.decayed) | copy-start | bytes 786436
  7.9 14.9 %all-to-all-start.1 = ((f32[4,128,256]{2,1,0:T(8,128)}), f32[4,128,256]{2,1,0:T(8,128)S(1)}, u32[]{:S(2)}, u32[]{:S(2)}) async-start(f32[4,128,256]{2,1,0:T(8,128)} %get-tuple-element.57), calls=%async_computation.1 | async-start | bytes 1048576 | tf_op jit(solution)/shard_map/all_to_all | solution.py:340
  18.0 1.4 copy-start.18
  22.8 23.4 %copy-start.6 = (f32[4,128,256]{2,1,0:T(8,128)}, f32[4,128,256]{2,1,0:T(8,128)S(1)}, u32[]{:S(2)}) copy-start(f32[4,128,256]{2,1,0:T(8,128)S(1)} %all-to-all-done.1.refs_1_.far) | copy-start | bytes 1572868
  22.8 13.7 %collective-permute-start = (f32[4,128,256]{2,1,0:T(8,128)S(1)}, f32[4,128,256]{2,1,0:T(8,128)S(1)}, u32[]{:S(2)}, u32[]{:S(2)}) collective-permute-start(f32[4,128,256]{2,1,0:T(8,128)S(1)} %all-to-all-done.1.refs_1_.far), channel_id=1, source_target_pairs={{0,2},{2,0},{1,3},{3,1},{4,6},{6,4},{5,7},{7,5},{8,10},{10,8},{9,1... | collective-permute-start | bytes 1572872 | tf_op jit(solution)/shard_map/ppermute | solution.py:310
  36.2 14.7 %copy-start.8 = (f32[4,128,256]{2,1,0:T(8,128)}, f32[4,128,256]{2,1,0:T(8,128)S(1)}, u32[]{:S(2)}) copy-start(f32[4,128,256]{2,1,0:T(8,128)S(1)} %all_to_all.15.refs_1_.near) | copy-start | bytes 1572868
  36.3 14.7 %collective-permute-start.1 = (f32[4,128,256]{2,1,0:T(8,128)S(1)}, f32[4,128,256]{2,1,0:T(8,128)}, u32[]{:S(2)}, u32[]{:S(2)}) collective-permute-start(f32[4,128,256]{2,1,0:T(8,128)S(1)} %all_to_all.15.refs_1_.near), channel_id=1, source_target_pairs={{0,1},{1,0},{2,3},{3,2},{4,5},{5,4},{6,7},{7,6},{8,9},{9,8},{10,11... | collective-permute-start | bytes 1572872 | tf_op jit(solution)/shard_map/ppermute | solution.py:310
  36.4 14.5 %collective-permute-start.2 = (f32[4,128,256]{2,1,0:T(8,128)S(1)}, f32[4,128,256]{2,1,0:T(8,128)}, u32[]{:S(2)}, u32[]{:S(2)}) collective-permute-start(f32[4,128,256]{2,1,0:T(8,128)S(1)} %collective-permute-done.refs_2_), channel_id=1, source_target_pairs={{0,1},{1,0},{2,3},{3,2},{4,5},{5,4},{6,7},{7,6},{8,9},{9,8},{10,11... | collective-permute-start | bytes 1572872 | tf_op jit(solution)/shard_map/ppermute | solution.py:310
  37.5 8.6 %copy-start.10 = (f32[1024,2,256]{2,1,0:T(2,128)S(1)}, f32[1024,2,256]{2,1,0:T(2,128)}, u32[]{:S(2)}) copy-start(f32[1024,2,256]{2,1,0:T(2,128)} %param.17) | copy-start | bytes 6291460
  46.1 12.7 %copy-start = (bf16[2,1024,1024]{2,1,0:T(8,128)(2,1)}, bf16[2,1024,1024]{2,1,0:T(8,128)(2,1)S(1)}, u32[]{:S(2)}) copy-start(bf16[2,1024,1024]{2,1,0:T(8,128)(2,1)S(1)} %get-tuple-element.60.refs_5_) | copy-start | bytes 12582916
  46.2 12.7 %copy-start.2 = (bf16[2,1024,1024]{2,1,0:T(8,128)(2,1)}, bf16[2,1024,1024]{2,1,0:T(8,128)(2,1)S(1)}, u32[]{:S(2)}) copy-start(bf16[2,1024,1024]{2,1,0:T(8,128)(2,1)S(1)} %get-tuple-element.61.refs_6_) | copy-start | bytes 12582916
  46.8 1.4 copy-start.22
  48.3 1.6 copy-start.24
  50.9 7.9 %copy-start.4 = (f32[512,128]{1,0:T(8,128)}, f32[512,128]{1,0:T(8,128)S(1)}, u32[]{:S(2)}) copy-start(f32[512,128]{1,0:T(8,128)S(1)} %get-tuple-element.111.refs_9_.press) | copy-start | bytes 786436
  58.9 1.0 copy-start.11
  59.8 1.3 copy-start.20
  62.0 32.3 %copy-start.15 = (s32[1,128]{1,0:T(1,128)S(1)}, s32[1,128]{1,0:T(1,128)}, u32[]{:S(2)}) copy-start(s32[1,128]{1,0:T(1,128)} %labels.1) | copy-start | bytes 1540
  62.0 32.3 %all-to-all-start.2 = ((f32[8,264,128]{2,1,0:T(8,128)}), f32[8,264,128]{2,1,0:T(8,128)S(1)}, u32[]{:S(2)}, u32[]{:S(2)}) async-start(f32[8,264,128]{2,1,0:T(8,128)} %copy-done.11), calls=%async_computation.2 | async-start | bytes 2162688 | tf_op jit(solution)/shard_map/all_to_all | solution.py:399
  67.2 27.1 %collective-permute-start.6 = (f32[4,128,256]{2,1,0:T(8,128)}, f32[4,128,256]{2,1,0:T(8,128)}, u32[]{:S(2)}, u32[]{:S(2)}) collective-permute-start(f32[4,128,256]{2,1,0:T(8,128)} %copy-done.8), channel_id=1, source_target_pairs={{0,2},{2,0},{1,3},{3,1},{4,6},{6,4},{5,7},{7,5},{8,10},{10,8},{9,1... | collective-permute-start | bytes 1572872 | tf_op jit(solution)/shard_map/ppermute | solution.py:310
  69.9 32.4 %collective-permute-start.7 = (f32[4,128,256]{2,1,0:T(8,128)}, f32[4,128,256]{2,1,0:T(8,128)}, u32[]{:S(2)}, u32[]{:S(2)}) collective-permute-start(f32[4,128,256]{2,1,0:T(8,128)} %copy-done.6), channel_id=1, source_target_pairs={{0,1},{1,0},{2,3},{3,2},{4,5},{5,4},{6,7},{7,6},{8,9},{9,8},{10,11... | collective-permute-start | bytes 1572872 | tf_op jit(solution)/shard_map/ppermute | solution.py:310
  94.3 8.0 %collective-permute-start.8 = (f32[4,128,256]{2,1,0:T(8,128)}, f32[4,128,256]{2,1,0:T(8,128)}, u32[]{:S(2)}, u32[]{:S(2)}) collective-permute-start(f32[4,128,256]{2,1,0:T(8,128)} %collective-permute-done.6.refs_2_), channel_id=1, source_target_pairs={{0,1},{1,0},{2,3},{3,2},{4,5},{5,4},{6,7},{7,6},{8,9},{9,8},{10,11... | collective-permute-start | bytes 1572872 | tf_op jit(solution)/shard_map/ppermute | solution.py:310
  94.3 8.0 %copy-start.5 = (f32[512,128]{1,0:T(8,128)S(1)}, f32[512,128]{1,0:T(8,128)}, u32[]{:S(2)}) copy-start(f32[512,128]{1,0:T(8,128)} %copy-done.4) | copy-start | bytes 786436
  94.3 8.0 %copy-start.7 = (f32[4,128,256]{2,1,0:T(8,128)S(1)}, f32[4,128,256]{2,1,0:T(8,128)}, u32[]{:S(2)}) copy-start(f32[4,128,256]{2,1,0:T(8,128)} %copy-done.6) | copy-start | bytes 1572868
  94.4 15.6 %collective-permute-start.3 = (f32[264,128]{1,0:T(8,128)S(1)}, f32[264,128]{1,0:T(8,128)S(1)}, u32[]{:S(2)}, u32[]{:S(2)}) collective-permute-start(f32[264,128]{1,0:T(8,128)S(1)} %get-tuple-element.69.own), channel_id=1, source_target_pairs={{0,1},{1,0},{2,3},{3,2},{4,5},{5,4},{6,7},{7,6},{8,9},{9,8},{10,11... | collective-permute-start | bytes 405512 | tf_op jit(solution)/shard_map/ppermute | solution.py:310
  95.0 15.1 %collective-permute-start.4 = (f32[264,128]{1,0:T(8,128)S(1)}, f32[264,128]{1,0:T(8,128)S(1)}, u32[]{:S(2)}, u32[]{:S(2)}) collective-permute-start(f32[264,128]{1,0:T(8,128)S(1)} %get-tuple-element.69.own), channel_id=1, source_target_pairs={{0,2},{1,3},{2,0},{3,1},{4,6},{5,7},{6,4},{7,5},{8,10},{9,11},{10,... | collective-permute-start | bytes 405512 | tf_op jit(solution)/shard_map/ppermute | solution.py:310
  95.8 14.2 %collective-permute-start.5 = (f32[264,128]{1,0:T(8,128)S(1)}, f32[264,128]{1,0:T(8,128)S(1)}, u32[]{:S(2)}, u32[]{:S(2)}) collective-permute-start(f32[264,128]{1,0:T(8,128)S(1)} %get-tuple-element.69.own), channel_id=1, source_target_pairs={{0,3},{1,2},{2,1},{3,0},{4,7},{5,6},{6,5},{7,4},{8,11},{9,10},{10,... | collective-permute-start | bytes 405512 | tf_op jit(solution)/shard_map/ppermute | solution.py:310
  97.9 4.4 %copy-start.1 = (bf16[2,1024,1024]{2,1,0:T(8,128)(2,1)S(1)}, bf16[2,1024,1024]{2,1,0:T(8,128)(2,1)}, u32[]{:S(2)}) copy-start(bf16[2,1024,1024]{2,1,0:T(8,128)(2,1)} %copy-done) | copy-start | bytes 12582916
  97.9 4.4 %copy-start.3 = (bf16[2,1024,1024]{2,1,0:T(8,128)(2,1)S(1)}, bf16[2,1024,1024]{2,1,0:T(8,128)(2,1)}, u32[]{:S(2)}) copy-start(bf16[2,1024,1024]{2,1,0:T(8,128)(2,1)} %copy-done.2) | copy-start | bytes 12582916
  102.3 7.8 %copy-start.21 = (f32[2,1024,256]{2,1,0:T(8,128)S(1)}, f32[2,1024,256]{2,1,0:T(8,128)}, u32[]{:S(2)}) copy-start(f32[2,1024,256]{2,1,0:T(8,128)} %copy-done.20) | copy-start | bytes 6291460
  102.3 7.8 %copy-start.23 = (bf16[2,1024,256]{2,1,0:T(8,128)(2,1)S(1)}, bf16[2,1024,256]{2,1,0:T(8,128)(2,1)}, u32[]{:S(2)}) copy-start(bf16[2,1024,256]{2,1,0:T(8,128)(2,1)} %copy-done.22) | copy-start | bytes 3145732
  102.3 7.8 %copy-start.25 = (bf16[2,1024,256]{2,1,0:T(8,128)(2,1)S(1)}, bf16[2,1024,256]{2,1,0:T(8,128)(2,1)}, u32[]{:S(2)}) copy-start(bf16[2,1024,256]{2,1,0:T(8,128)(2,1)} %copy-done.24) | copy-start | bytes 3145732
  110.1 9.6 %copy-start.9 = (f32[4,128,256]{2,1,0:T(8,128)S(1)}, f32[4,128,256]{2,1,0:T(8,128)}, u32[]{:S(2)}) copy-start(f32[4,128,256]{2,1,0:T(8,128)} %copy-done.8) | copy-start | bytes 1572868
  110.1 9.6 %copy-start.27 = (f32[512,256]{1,0:T(8,128)S(1)}, f32[512,256]{1,0:T(8,128)}, u32[]{:S(2)}) copy-start(f32[512,256]{1,0:T(8,128)} %copy-done.26) | copy-start | bytes 1572868
  119.7 3.6 %copy-start.28 = (f32[128,512]{1,0:T(8,128)}, f32[128,512]{1,0:T(8,128)S(1)}, u32[]{:S(2)}) copy-start(f32[128,512]{1,0:T(8,128)S(1)} %get-tuple-element.76.p0) | copy-start | bytes 786436
  119.7 9.4 %copy-start.30 = (f32[2,1,512]{2,1,0:T(1,128)S(1)}, f32[2,1,512]{2,1,0:T(1,128)}, u32[]{:S(2)}) copy-start(f32[2,1,512]{2,1,0:T(1,128)} %param.15) | copy-start | bytes 12292
  123.3 27.6 %copy-start.14 = (f32[2,64,512]{2,1,0:T(8,128)S(1)}, f32[2,64,512]{2,1,0:T(8,128)}, u32[]{:S(2)}) copy-start(f32[2,64,512]{2,1,0:T(8,128)} %copy-done.13) | copy-start | bytes 786436
  123.3 14.2 %collective-permute-start.16 = (f32[88,1024]{1,0:T(8,128)S(1)}, f32[88,1024]{1,0:T(8,128)}, u32[]{:S(2)}, u32[]{:S(2)}) collective-permute-start(f32[88,1024]{1,0:T(8,128)S(1)} %get-tuple-element.97), channel_id=1, source_target_pairs={{0,12},{4,0},{8,4},{12,8},{1,13},{5,1},{9,5},{13,9},{2,14},{6,2},{... | collective-permute-start | bytes 1081352 | tf_op jit(solution)/shard_map/ppermute | solution.py:306
  124.5 12.0 %collective-permute-start.12 = (f32[80,1024]{1,0:T(8,128)}, f32[80,1024]{1,0:T(8,128)}, u32[]{:S(2)}, u32[]{:S(2)}) collective-permute-start(f32[80,1024]{1,0:T(8,128)} %get-tuple-element.92), channel_id=1, source_target_pairs={{0,4},{4,8},{8,12},{12,0},{1,5},{5,9},{9,13},{13,1},{2,6},{6,10},{... | collective-permute-start | bytes 983048 | tf_op jit(solution)/shard_map/ppermute | solution.py:306
  125.3 22.3 %collective-permute-start.9 = (f32[128,512]{1,0:T(8,128)}, f32[128,512]{1,0:T(8,128)S(1)}, u32[]{:S(2)}, u32[]{:S(2)}) collective-permute-start(f32[128,512]{1,0:T(8,128)} %get-tuple-element.77), channel_id=1, source_target_pairs={{0,4},{4,8},{8,12},{12,0},{1,5},{5,9},{9,13},{13,1},{2,6},{6,10},{... | collective-permute-start | bytes 786440 | tf_op jit(solution)/shard_map/ppermute | solution.py:306
  125.9 21.8 %collective-permute-start.10 = (f32[128,512]{1,0:T(8,128)}, f32[128,512]{1,0:T(8,128)}, u32[]{:S(2)}, u32[]{:S(2)}) collective-permute-start(f32[128,512]{1,0:T(8,128)} %get-tuple-element.78), channel_id=1, source_target_pairs={{0,8},{4,12},{8,0},{12,4},{1,9},{5,13},{9,1},{13,5},{2,10},{6,14},... | collective-permute-start | bytes 786440 | tf_op jit(solution)/shard_map/ppermute | solution.py:306
  129.2 21.7 %collective-permute-start.11 = (f32[128,512]{1,0:T(8,128)}, f32[128,512]{1,0:T(8,128)}, u32[]{:S(2)}, u32[]{:S(2)}) collective-permute-start(f32[128,512]{1,0:T(8,128)} %get-tuple-element.79), channel_id=1, source_target_pairs={{0,12},{4,0},{8,4},{12,8},{1,13},{5,1},{9,5},{13,9},{2,14},{6,2},{... | collective-permute-start | bytes 786440 | tf_op jit(solution)/shard_map/ppermute | solution.py:306
  136.5 22.4 %collective-permute-start.14 = (f32[80,1024]{1,0:T(8,128)S(1)}, f32[80,1024]{1,0:T(8,128)S(1)}, u32[]{:S(2)}, u32[]{:S(2)}) collective-permute-start(f32[80,1024]{1,0:T(8,128)S(1)} %get-tuple-element.93), channel_id=1, source_target_pairs={{0,12},{4,0},{8,4},{12,8},{1,13},{5,1},{9,5},{13,9},{2,14},{6,2},{... | collective-permute-start | bytes 983048 | tf_op jit(solution)/shard_map/ppermute | solution.py:306
  137.5 21.4 %collective-permute-start.15 = (f32[88,1024]{1,0:T(8,128)S(1)}, f32[88,1024]{1,0:T(8,128)S(1)}, u32[]{:S(2)}, u32[]{:S(2)}) collective-permute-start(f32[88,1024]{1,0:T(8,128)S(1)} %get-tuple-element.95), channel_id=1, source_target_pairs={{0,4},{4,8},{8,12},{12,0},{1,5},{5,9},{9,13},{13,1},{2,6},{6,10},{... | collective-permute-start | bytes 1081352 | tf_op jit(solution)/shard_map/ppermute | solution.py:306
  147.6 14.3 %collective-permute-start.13 = (f32[80,1024]{1,0:T(8,128)S(1)}, f32[80,1024]{1,0:T(8,128)S(1)}, u32[]{:S(2)}, u32[]{:S(2)}) collective-permute-start(f32[80,1024]{1,0:T(8,128)S(1)} %add.32), channel_id=1, source_target_pairs={{0,4},{4,8},{8,12},{12,0},{1,5},{5,9},{9,13},{13,1},{2,6},{6,10},{... | collective-permute-start | bytes 983048 | tf_op jit(solution)/shard_map/ppermute | solution.py:306
  147.6 14.3 %collective-permute-start.17 = (f32[88,1024]{1,0:T(8,128)S(1)}, f32[88,1024]{1,0:T(8,128)S(1)}, u32[]{:S(2)}, u32[]{:S(2)}) collective-permute-start(f32[88,1024]{1,0:T(8,128)S(1)} %add.33), channel_id=1, source_target_pairs={{0,12},{4,0},{8,4},{12,8},{1,13},{5,1},{9,5},{13,9},{2,14},{6,2},{... | collective-permute-start | bytes 1081352 | tf_op jit(solution)/shard_map/ppermute | solution.py:306
  150.9 1.6 copy-start.17
  152.5 1.6 copy-start.19
  (3 other events, 2.6 us)

commit v3 on v2

v3 whole, which is shorter than its diff:
```python
import math

import jax
import jax.numpy as jnp
from jax import lax
from jax.experimental import pallas as pl
from jax.experimental.pallas import tpu as pltpu
from jax.sharding import Mesh, PartitionSpec as P

DECAY_RATE = 0.98
LEARN_RATE = 1.0
EPSILON = 1e-08
F32 = jnp.float32
BF16 = jnp.bfloat16
NN = (((1,), (0,)), ((), ()))
NT = (((1,), (1,)), ((), ()))
TOWER = ("y", "xl")
QUAD = ("xh", "core")
VMEM_LIMIT = 16 << 20


def halves(a):
    high = a.astype(BF16)
    return high, (a - high.astype(F32)).astype(BF16)


def dot1(a, b, dims):
    return lax.dot_general(a, b, dims, preferred_element_type=F32)


def dot3(a, b, dims=NN):
    return dot1(a[0], b[0], dims) + (dot1(a[0], b[1], dims) + dot1(a[1], b[0], dims))


def dot32(a, b, dims=NN):
    return dot3(halves(a), halves(b), dims)


def vmem(count):
    return [pl.BlockSpec(memory_space=pltpu.VMEM)] * count


def call(kernel, outs, spec_in, scratch=(), name=None, flops=0):
    return pl.pallas_call(
        kernel,
        cost_estimate=pl.CostEstimate(flops=int(flops), transcendentals=0, bytes_accessed=1 << 20),
        out_shape=outs,
        in_specs=spec_in,
        out_specs=vmem(len(outs)),
        scratch_shapes=list(scratch),
        compiler_params=pltpu.CompilerParams(vmem_limit_bytes=VMEM_LIMIT),
        name=name,
    )


SMEM_SPEC = pl.BlockSpec(memory_space=pltpu.SMEM)


def decay(touch, elapsed, tables, decayed):
    towers, width, rows = tables.shape
    touches = touch.shape[1]
    for t in range(towers):
        ids = jnp.broadcast_to(touch[t : t + 1, :].astype(F32), (touches, touches)).T
        rates = jnp.exp(elapsed[t : t + 1, :].astype(F32) * math.log(DECAY_RATE))
        rates = jnp.broadcast_to(rates, (touches, touches)).T
        factor = []
        for block in range(rows // touches):
            row = lax.broadcasted_iota(jnp.int32, (touches, touches), 1).astype(F32) + float(block * touches)
            match = ids == row
            hits = jnp.sum(jnp.where(match, 1.0, 0.0), axis=0, keepdims=True)
            chosen = jnp.sum(jnp.where(match, rates, 0.0), axis=0, keepdims=True)
            factor.append(jnp.where(hits > 0.0, chosen, 1.0))
        decayed[t] = tables[t] * jnp.concatenate(factor, axis=1)


def pool_half(idx, side, bag, decayed, pooled, counts):
    towers, width, rows = decayed.shape
    part = pooled[0].shape[1]
    for t in range(towers):
        both = jnp.concatenate(halves(decayed[t]), axis=0)
        for k, out in enumerate(pooled):
            chunk = lax.rem(idx[0] + k, 4)
            at = pl.multiple_of(chunk * 2 * part + side * part, part)
            ids = bag[t, :, pl.ds(at, part)]
            row = lax.broadcasted_iota(jnp.int32, (rows, part), 0)
            count = jnp.zeros((rows, part), F32)
            for b in range(ids.shape[0]):
                count = count + jnp.where(row == ids[b : b + 1, :], 1.0, 0.0)
            count = count.astype(BF16)
            counts[t, chunk] = count
            total = dot1(both, count, NN)
            out[t * width : (t + 1) * width, :] = total[:width] + total[width:]


def pool_far_kernel(idx, bag_hbm, touch_hbm, elapsed_hbm, tables_hbm, p0, p1, p2, p3, counts, decayed, bag, touch, elapsed, tables, sems):
    pairs = ((bag_hbm, bag), (touch_hbm, touch), (elapsed_hbm, elapsed), (tables_hbm, tables))
    copies = [pltpu.make_async_copy(a, b, sems.at[n]) for n, (a, b) in enumerate(pairs)]
    for copy in copies:
        copy.start()
    for copy in copies:
        copy.wait()
    decay(touch, elapsed, tables, decayed)
    pool_half(idx, 1 - idx[1], bag, decayed, (p0, p1, p2, p3), counts)


def pool_near_kernel(idx, bag, decayed, p0, p1, p2, p3, counts):
    pool_half(idx, idx[1], bag, decayed, (p0, p1, p2, p3), counts)


def pack_kernel(idx, p0, p1, p2, p3, out):
    for k, ref in enumerate((p0, p1, p2, p3)):
        out[lax.rem(idx[0] + 4 - k, 4)] = ref[...]


def turn_kernel(w, high, low):
    rows = w.shape[0]
    flat = w.reshape(rows * 16, 128)
    for t in range(2):
        for b in range(8):
            h, l = halves(flat[pl.ds(b * 2 + t, rows, stride=16), :].T)
            high[t, b * 128 : (b + 1) * 128, :] = h
            low[t, b * 128 : (b + 1) * 128, :] = l


def pick_kernel(idx, w, high, low):
    rows = w.shape[2]
    flat = w.reshape(rows * 16, 128)
    for t in range(2):
        for b in range(8):
            h, l = halves(flat[pl.ds(b * 2 + t, rows, stride=16), :])
            high[t, :, b * 128 : (b + 1) * 128] = h
            low[t, :, b * 128 : (b + 1) * 128] = l


def prepare_kernel(idx, second_hbm, lift_hbm, press_hbm, heads, high_t, low_t, lift, press, head, second, sems):
    tower = idx[3]
    rows = pl.ds(pl.multiple_of(tower * lift.shape[0], lift.shape[0]), lift.shape[0])
    pairs = ((second_hbm, second), (lift_hbm.at[rows, :], lift), (press_hbm.at[rows, :], press))
    copies = [pltpu.make_async_copy(a, b, sems.at[n]) for n, (a, b) in enumerate(pairs)]
    for copy in copies:
        copy.start()
    head[...] = jnp.concatenate([heads[pl.ds(tower * 4 + b, 1), :] for b in range(4)], axis=1)
    for copy in copies:
        copy.wait()
    count = second.shape[0]
    flat = second.reshape(count * 4, 128)
    for t in range(2):
        for b in range(2):
            lanes = slice(b * 128, (b + 1) * 128)
            h, l = halves(flat[pl.ds(b * 2 + t, count, stride=4), :].T)
            high_t[t, lanes, :] = h
            low_t[t, lanes, :] = l


def natural_kernel(w, high, low):
    rows = w.shape[0]
    flat = w.reshape(rows * 4, 128)
    for t in range(2):
        for b in range(2):
            lanes = slice(b * 128, (b + 1) * 128)
            h, l = halves(flat[pl.ds(b * 2 + t, rows, stride=4), :])
            high[t, :, lanes] = h
            low[t, :, lanes] = l


def forward_kernel(towers, with_pay, idx, x1, x2, y1, y2, w1h, w1l, w2h, w2l, press, lift, head, hidden, start, *rest):
    fh, fl = rest[-2:]
    sets = (x1, x2, y1, y2)
    zs, pair, samples = x1.shape
    width = pair // 2
    xh, core = idx[1], idx[2]
    place = ((xh, core), (1 - xh, core), (xh, 1 - core), (1 - xh, 1 - core))
    width_out = w2h.shape[1]

    def one_tower(t, slot):
        for (a, b), ref in zip(place, sets):
            for z in range(zs):
                h, l = halves(ref[z, pl.ds(pl.multiple_of(t * width, width), width), :])
                at = pl.multiple_of(((z * 2 + a) * 2 + b) * width, width)
                fh[pl.ds(at, width), :] = h
                fl[pl.ds(at, width), :] = l
        value = dot3((w1h[t], w1l[t]), (fh[...], fl[...]))
        hidden[slot] = value
        act = halves(value * jax.nn.sigmoid(value))
        start[pl.ds(pl.multiple_of(slot * width_out, width_out), width_out), :] = dot3((w2h[t], w2l[t]), act)

    if len(towers) == 2:

        def step(t, carry):
            one_tower(t, t)
            return carry

        lax.fori_loop(0, 2, step, 0)
    else:
        one_tower(towers[0], 0)
    if with_pay:
        pay = rest[0]
        own = samples // 2
        rank = press.shape[1]
        x0 = halves(start[:, pl.ds(pl.multiple_of(core * own, own), own)])
        p = dot3(halves(press[...].T), x0)
        q = dot3(halves(lift[...].T * head[...]), x0)
        d = dot3(halves(jnp.broadcast_to(head[...], (8, head.shape[1]))), x0)
        pay[0:rank, :] = p
        pay[rank : 2 * rank, :] = q
        pay[2 * rank : 2 * rank + 8, :] = d


def logit_kernel(idx, mine, other, labels, pay, logits):
    total = mine[...] + other[...]
    rank = (total.shape[0] - 8) // 2
    value = jnp.sum(total[0:rank] * total[rank : 2 * rank], axis=0, keepdims=True) + total[2 * rank : 2 * rank + 1]
    turned = pltpu.roll(jnp.broadcast_to(value, (8, 128)), lax.rem(128 - 16 * idx[3], 128), 1)
    logits[...] = turned[0:1, 0:16]
    error = jax.nn.sigmoid(value) - labels[...].astype(F32)
    pay[0 : 2 * rank, :] = total[0 : 2 * rank]
    pay[2 * rank : 2 * rank + 8, :] = jnp.broadcast_to(error, (8, error.shape[1]))


def grads_kernel(idx, own, c1, xa, xb, hid_a, hid_b0, hid_b1, w1h, w1l, w2h, w2l, press, lift, head, ghh, ghl, gout, pq, g0, g1, g2, g3):
    core = idx[2]
    rank = press.shape[1]
    n = own.shape[1]
    half = 2 * n
    outs = (g0, g1, g2, g3)
    width = w1h.shape[1] // 4
    width_out = w2h.shape[2]
    column = jnp.broadcast_to(head[...], (128, head.shape[1])).T[:, 0:1]
    first_core = core == 0
    for g, (mine, other, hidden) in enumerate(((own, c1, (hid_a.at[0], hid_a.at[1])), (xa, xb, (hid_b0.at[0], hid_b1.at[0])))):
        left = jnp.where(first_core, mine[...], other[...])
        right = jnp.where(first_core, other[...], mine[...])
        both = jnp.concatenate([left, right], axis=1)
        p, q, error = both[0:rank], both[rank : 2 * rank], both[2 * rank : 2 * rank + 1]
        lanes = slice(g * half, (g + 1) * half)
        pq[0:rank, lanes] = error * p
        pq[rank : 2 * rank, lanes] = error * q
        scaling = dot32(lift[...], p)
        back = dot32(press[...], q)
        gout[:, lanes] = error * (column * (scaling + 1.0) + back)

        for t in range(2):
            go = halves(gout[t * width_out : (t + 1) * width_out, lanes])
            ga = dot3((w2h[t], w2l[t]), go)
            value = hidden[t][...]
            s = jax.nn.sigmoid(value)
            gh = halves(ga * (s * (1.0 + value * (1.0 - s))))
            ghh[t, :, lanes] = gh[0]
            ghl[t, :, lanes] = gh[1]
            grad = dot3((w1h[t], w1l[t]), gh)
            for k in range(4):
                outs[k][t * width : (t + 1) * width, lanes] = grad[k * width : (k + 1) * width]


def weights_kernel(idx, near, far, ghh, ghl, gout, hid_a, hid_b0, hid_b1, x0a, x0b0, x0b1, pq, g1, g3, *blocks):
    hid_b, x0b = (hid_b0, hid_b1), (x0b0, x0b1)
    z, quad = idx[0], 2 * idx[1] + idx[2]
    width = near.shape[1] // 2
    width_out = gout.shape[0] // 2
    for t in range(2):
        outs = blocks[4 * t : 4 * t + 4]
        rows = slice(t * width, (t + 1) * width)
        f, act = [], []
        for k in range(4):
            at = lax.rem(z + k, 4)
            f.append(jnp.concatenate([near[at, rows, :], far[at, rows, :]], axis=1))
            pick = pl.ds(pl.multiple_of((at * 4 + quad) * width, width), width)
            value = jnp.concatenate([hid_a[t, pick, :], hid_b[t][0, pick, :]], axis=1)
            act.append(value * jax.nn.sigmoid(value))
        grad = dot3(halves(jnp.concatenate(f, axis=0)), (ghh[t], ghl[t]), NT)
        for k in range(4):
            outs[k][0:width, :] = grad[k * width : (k + 1) * width]
        grad = dot32(jnp.concatenate(act, axis=0), gout[t * width_out : (t + 1) * width_out, :], NT)
        for k in range(4):
            for b in range(4):
                outs[k][width : width + 16, b * 256 : (b + 1) * 256] = grad[k * width + 16 * b : k * width + 16 * b + 16]
    for out, ref in ((blocks[5], g1), (blocks[3], g3)):
        base = out.shape[0] - width
        for t in range(2):
            out[base:, t * 512 : (t + 1) * 512] = ref[t * width : (t + 1) * width, :]
    rank = pq.shape[0] // 2
    x0 = []
    for k in range(4):
        block = lax.rem(z + k, 4) * 4 + quad
        pick = pl.ds(pl.multiple_of(block * 32, 32), 32)
        near_half = pl.ds(pl.multiple_of(lax.rem(block, 8) * 32, 32), 32)
        later = jnp.where(block < 8, x0b[0][near_half, :], x0b[1][near_half, :])
        x0.append(jnp.concatenate([x0a[pick, :], later], axis=1))
    x0 = jnp.concatenate(x0, axis=0)
    both = dot32(x0, pq[...], NT)
    for k in range(4):
        for b in range(4):
            outs[k][width + 16 : width + 24, b * 256 : (b + 1) * 256] = both[32 * k + 8 * b : 32 * k + 8 * b + 8]


def update_kernel(idx, p0, p1, p2, p3, near, far, decayed, accumulator, new_tables, new_accumulator):
    z = idx[0]
    towers, width, rows = decayed.shape
    half = p0.shape[1] // 2
    for t in range(towers):
        total = jnp.zeros((2 * width, rows), F32)
        for k, ref in enumerate((p0, p1, p2, p3)):
            at = lax.rem(z + 4 - k, 4)
            if ref.shape[0] == towers * width:
                value = ref[t * width : (t + 1) * width, :]
            else:
                value = ref[ref.shape[0] - width :, t * 2 * half : (t + 1) * 2 * half]
            both = jnp.concatenate(halves(value), axis=0)
            total = total + dot1(both[:, :half], near[t, at], NT)
            total = total + dot1(both[:, half:], far[t, at], NT)
        grad = total[:width] + total[width:]
        square = jnp.sum(grad * grad, axis=0, keepdims=True) * (1.0 / width)
        fresh = accumulator[t : t + 1, :] + square
        new_accumulator[t : t + 1, :] = fresh
        new_tables[t] = decayed[t] - LEARN_RATE * grad / (jnp.sqrt(fresh) + EPSILON)


def sum_kernel(idx, head, *refs):
    parts, (first, second, lift, press, wide) = refs[:6], refs[6:]
    for t in range(2):
        a, b, c = parts[3 * t : 3 * t + 3]
        total = a[...] + (b[0 : a.shape[0]] + c[0 : a.shape[0]])
        for k in range(8):
            first[pl.ds(2 * k + t, 64, stride=16), :] = total[0:64, k * 128 : (k + 1) * 128]
        for b in range(4):
            for o in range(2):
                lanes = slice(b * 256 + o * 128, b * 256 + (o + 1) * 128)
                second[pl.ds(b * 64 + 2 * o + t, 16, stride=4), :] = total[64:80, lanes]
        if t == 1:
            wide[...] = jnp.broadcast_to(head[...], (128, head.shape[1])).T
            device = (idx[0] * 2 + idx[1]) * 2 + idx[2]
            column = wide[pl.ds(pl.multiple_of(device * 32, 32), 32), :]
            for b in range(4):
                at = slice(8 * b, 8 * b + 8)
                lift[at, :] = column[at] * total[80:88, b * 256 : b * 256 + 128]
                press[at, :] = total[80:88, b * 256 + 128 : (b + 1) * 256]


def shift(x, axis, size, by):
    return lax.ppermute(x, axis, [(i, (i + by) % size) for i in range(size)])


def flip(x, axis, size, bit):
    return lax.ppermute(x, axis, [(i, i ^ bit) for i in range(size)])


def per_device(bag_ids, touch_ids, elapsed, tables, accumulator, first_weight, second_weight, lift_weight, press_weight, head_weight, labels):
    f32 = lambda *shape: jax.ShapeDtypeStruct(shape, F32)
    bf16 = lambda *shape: jax.ShapeDtypeStruct(shape, BF16)
    axes = [lax.axis_index(name) for name in ("z", "xh", "core", TOWER)]
    idx = jnp.stack(axes).astype(jnp.int32)
    rank = lift_weight.shape[1]
    local = lift_weight.shape[0] // 8
    any_spec = pl.BlockSpec(memory_space=pl.ANY)

    tables_t = jnp.transpose(tables[:, 0], (0, 2, 1))
    bag = bag_ids[:, 0]
    hbm = lambda x: pltpu.with_memory_space_constraint(x, pltpu.HBM)
    *far, counts_far, decayed = call(
        pool_far_kernel,
        [f32(128, 256)] * 4 + [bf16(2, 4, 512, 256), f32(2, 64, 512)],
        [SMEM_SPEC] + [any_spec] * 4,
        [
            pltpu.VMEM((2, 4, 2048), jnp.int32),
            pltpu.VMEM((2, 128), jnp.int32),
            pltpu.VMEM((2, 128), jnp.int32),
            pltpu.VMEM((2, 64, 512), F32),
            pltpu.SemaphoreType.DMA((4,)),
        ],
        name="pool_far",
        flops=1e6,
    )(idx, hbm(bag), hbm(touch_ids[:, 0]), hbm(elapsed[:, 0]), hbm(tables_t))
    pack = call(pack_kernel, [f32(4, 128, 256)], [SMEM_SPEC] + vmem(4), name="pack", flops=1e6)
    far = [far[0]] + [shift(far[k], "z", 4, k) for k in (1, 2, 3)]
    *near, counts_near = call(
        pool_near_kernel, [f32(128, 256)] * 4 + [bf16(2, 4, 512, 256)], [SMEM_SPEC] + vmem(2), name="pool_near", flops=1e6
    )(idx, bag, decayed)
    *far, _ = lax.optimization_barrier((*far, near[0]))
    (fq_far,) = pack(idx, *far)
    x2 = flip(fq_far, "xh", 2, 1)
    near = [near[0]] + [shift(near[k], "z", 4, k) for k in (1, 2, 3)]

    _, first_weight = lax.optimization_barrier((fq_far, first_weight))
    view = first_weight.reshape(1024, 2, 8, 128).transpose(0, 2, 1, 3).reshape(1024, 16, 128)
    w1th, w1tl = pl.pallas_call(
        turn_kernel,
        grid=(8,),
        in_specs=[pl.BlockSpec((128, 16, 128), lambda i: (i, 0, 0))],
        out_specs=[pl.BlockSpec((2, 1024, 128), lambda i: (0, 0, i))] * 2,
        out_shape=[bf16(2, 1024, 1024)] * 2,
        compiler_params=pltpu.CompilerParams(vmem_limit_bytes=VMEM_LIMIT),
        cost_estimate=pl.CostEstimate(flops=int(1e6), transcendentals=0, bytes_accessed=1 << 20),
        name="turn",
    )(hbm(view))
    *near, _ = lax.optimization_barrier((*near, w1th))
    (fq_near,) = pack(idx, *near)
    y1 = flip(fq_near, "core", 2, 1)
    y2 = flip(x2, "core", 2, 1)
    x2b = flip(fq_near, "xh", 2, 1)
    y1b = flip(fq_far, "core", 2, 1)
    y2b = flip(x2b, "core", 2, 1)

    _, second_weight, lift_weight, press_weight, head_weight = lax.optimization_barrier(
        (w1th, second_weight, lift_weight, press_weight, head_weight)
    )
    second_view = second_weight.reshape(1024, 2, 2, 128).transpose(0, 2, 1, 3).reshape(1024, 4, 128)
    w2th, w2tl, lift, press, head = call(
        prepare_kernel,
        [bf16(2, 256, 1024)] * 2 + [f32(local, rank), f32(local, rank), f32(1, local)],
        [SMEM_SPEC] + [any_spec] * 3 + vmem(1),
        [pltpu.VMEM((1024, 4, 128), F32), pltpu.SemaphoreType.DMA((3,))],
        name="prepare",
        flops=1e6,
    )(idx, hbm(second_view), hbm(lift_weight), hbm(press_weight), head_weight.reshape(32, 128))

    scratch = [pltpu.VMEM((1024, 256), BF16)] * 2
    weights = (w1th, w1tl, w2th, w2tl, press, lift, head)
    hid_a, x0a, pay = call(
        lambda *refs: forward_kernel((0, 1), True, *refs),
        [f32(2, 1024, 256), f32(512, 256), f32(2 * rank + 8, 128)],
        [SMEM_SPEC] + vmem(11),
        scratch,
        name="forward_a",
        flops=1e6,
    )(idx, fq_near, x2, y1, y2, *weights)
    pay, x2b = lax.optimization_barrier((pay, x2b))
    y2b = flip(x2b, "core", 2, 1)

    def later_half(at, t):
        return call(
            lambda *refs: forward_kernel((t,), False, *refs),
            [f32(1, 1024, 256), f32(256, 256)],
            [SMEM_SPEC] + vmem(11),
            scratch,
            name="forward_b%d" % t,
            flops=4e9,
        )(at, fq_far, x2b, y1b, y2b, *weights)

    view, second_view, pay = lax.optimization_barrier((view, second_view, pay))
    other = flip(pay, TOWER, 8, 1)
    w1qh, w1ql = pl.pallas_call(
        pick_kernel,
        grid_spec=pltpu.PrefetchScalarGridSpec(
            num_scalar_prefetch=1,
            grid=(4,),
            in_specs=[pl.BlockSpec((1, 1, 64, 16, 128), lambda k, i: (lax.rem(i[0] + k, 4), 2 * i[1] + i[2], 0, 0, 0))],
            out_specs=[pl.BlockSpec((2, 64, 1024), lambda k, i: (0, k, 0))] * 2,
        ),
        out_shape=[bf16(2, 256, 1024)] * 2,
        compiler_params=pltpu.CompilerParams(vmem_limit_bytes=VMEM_LIMIT),
        cost_estimate=pl.CostEstimate(flops=int(4e9), transcendentals=0, bytes_accessed=1 << 20),
        name="pick",
    )(idx, hbm(view.reshape(4, 4, 64, 16, 128)))
    w2h, w2l = call(natural_kernel, [bf16(2, 1024, 256)] * 2, vmem(1), name="natural", flops=1e9)(second_view)
    other, w1qh, w2h = lax.optimization_barrier((other, w1qh, w2h))
    pay = pay + other
    after, pay = lax.optimization_barrier((idx, pay))
    other = flip(pay, TOWER, 8, 2)
    hid_b0, x0b0 = later_half(after, 0)
    other, x0b0 = lax.optimization_barrier((other, x0b0))
    pay = pay + other
    after, pay = lax.optimization_barrier((idx, pay))
    other = flip(pay, TOWER, 8, 4)
    hid_b1, x0b1 = later_half(after, 1)
    other, x0b1 = lax.optimization_barrier((other, x0b1))
    pay, logits = call(logit_kernel, [f32(2 * rank + 8, 128), f32(1, 16)], [SMEM_SPEC] + vmem(3), name="logit", flops=1e6)(
        idx, pay, other, labels
    )
    pays = [pay] + [flip(pay, QUAD, 4, k) for k in (1, 2, 3)]

    ghh, ghl, gout, pq, *g = call(
        grads_kernel,
        [bf16(2, 1024, 512), bf16(2, 1024, 512), f32(512, 512), f32(2 * rank, 512)] + [f32(128, 512)] * 4,
        [SMEM_SPEC] + vmem(14),
        name="grads",
        flops=9e9,
    )(idx, *pays, hid_a, hid_b0, hid_b1, w1qh, w1ql, w2h, w2l, press, lift, head)
    w = call(
        weights_kernel,
        [f32(rows, 1024) for rows in (80, 80, 80, 144, 88, 152, 88, 88)],
        [SMEM_SPEC] + vmem(14),
        name="weights",
        flops=5e9,
    )(idx, fq_near, fq_far, ghh, ghl, gout, hid_a, hid_b0, hid_b1, x0a, x0b0, x0b1, pq, g[1], g[3])
    w, v = w[:4], w[4:]
    up = shift(w[2], "z", 4, 1)
    down = shift(v[2], "z", 4, 3)
    v1 = shift(v[1], "z", 4, 1)
    w3 = shift(w[3], "z", 4, 3)
    g2 = shift(g[2], "z", 4, 2)
    w1 = shift(w[1] + up, "z", 4, 1)
    v3 = shift(v[3] + down, "z", 4, 3)
    new_tables, new_accumulator = call(
        update_kernel, [f32(2, 64, 512), f32(2, 512)], [SMEM_SPEC] + vmem(8), name="update", flops=5e9
    )(idx, g[0], v1, g2, w3, counts_near, counts_far, decayed, accumulator[:, 0])
    first, second, lift_out, press_out = call(
        sum_kernel,
        [f32(1024, 128), f32(256, 128), f32(32, rank), f32(32, rank)],
        [SMEM_SPEC] + vmem(7),
        [pltpu.VMEM((local, 128), F32)],
        name="sum",
        flops=1e6,
    )(idx, head, w[0], w1, w3, v[0], v1, v3)
    return (
        jnp.transpose(new_tables, (0, 2, 1))[:, None],
        new_accumulator[:, None],
        first.reshape(64, 8, 2, 128).transpose(0, 2, 1, 3).reshape(64, 2, 1024),
        second.reshape(64, 2, 2, 128).transpose(0, 2, 1, 3).reshape(64, 2, 256),
        lift_out,
        press_out,
        logits,
    )


def solution(mesh):
    split = Mesh(mesh.devices.reshape(4, 2, 4, 2, 2), ("y", "xl", "z", "xh", "core"))
    member = ("z", "xh", "core")
    placed = (
        P(TOWER, member, None, None),
        P(TOWER, member, None),
        P(TOWER, member, None),
        P(TOWER, member, None, None),
        P(TOWER, member, None),
        P(None, TOWER, None),
        P(None, TOWER, None),
        P(),
        P(),
        P(),
        P(member, None),
    )
    return jax.shard_map(
        per_device,
        mesh=split,
        in_specs=placed,
        out_specs=(
            P(TOWER, member, None, None),
            P(TOWER, member, None),
            P(member, TOWER, None),
            P(member, TOWER, None),
            P(TOWER + member, None),
            P(TOWER + member, None),
            P(member, TOWER),
        ),
        check_vma=False,
    )
```

time: 164 us -> 132 us (0.80)
  local copies, waits for them, and re-layouts: 17.7 us -> 1.46 us
  blocking collectives: 10.5 us -> 0 us
  Pallas kernels: 56.4 us -> 53.1 us
  other arithmetic: 2.11 us -> 0.2 us
    ppermute x9 -> x13, waiting for transfers between devices: 14.8 us -> 29.5 us  [shift(): return lax.ppermute(x, axis, [(i, (i + by) % size) for i in range(size)])]
    unnamed x64 -> x12, local copies, waits for them, and re-layouts: 14.5 us -> 1.46 us
    ppermute x9 -> x12, waiting for transfers between devices: 24.6 us -> 12.9 us  [flip(): return lax.ppermute(x, axis, [(i, i ^ bit) for i in range(size)])]
    all_to_all x2 -> x0, starting transfers between devices: 10.6 us -> none  [the longest x1 5.39 us: per_device(): fq_far = lax.all_to_all(pooled_far, 'z', 0, 0, tiled=True)]
    all_to_all x1 -> x0, blocking collectives: 10.5 us -> none  [per_device(): fq_near = lax.all_to_all(pooled_near, 'z', 0, 0, tiled=True)]
    ppermute x9 -> x13, starting transfers between devices: 12.4 us -> 20.3 us  [shift(): return lax.ppermute(x, axis, [(i, (i + by) % size) for i in range(size)])]
    ppermute x9 -> x12, starting transfers between devices: 9.58 us -> 13.1 us  [flip(): return lax.ppermute(x, axis, [(i, i ^ bit) for i in range(size)])]
    all_to_all x2 -> x0, waiting for transfers between devices: 3.35 us -> none  [the longest x1 3.35 us: per_device(): fq_far = lax.all_to_all(pooled_far, 'z', 0, 0, tiled=True)]
  transfers between devices with their start and end apart: 20 -> 25, of which waited for: 6 -> 8; matrix products, arithmetic and copies ran while one was open for 4% -> 1% of each run, Pallas kernels for 17% -> 27%
where the time goes in v3:
time: 132 us; the launch traced here: 131 us
  Pallas kernels  53.1 us (40%)
  waiting for transfers between devices  42.4 us (32%)
  starting transfers between devices  33.4 us (25%)
  local copies, waits for them, and re-layouts  1.46 us (1%)
    ppermute x13, waiting for transfers between devices, shift(): return lax.ppermute(x, axis, [(i, (i + by) % size) for i in range(size)])  29.5 us
    ppermute x13, starting transfers between devices, shift(): return lax.ppermute(x, axis, [(i, (i + by) % size) for i in range(size)])  20.3 us
    ppermute x12, starting transfers between devices, flip(): return lax.ppermute(x, axis, [(i, i ^ bit) for i in range(size)])  13.1 us
    ppermute x12, waiting for transfers between devices, flip(): return lax.ppermute(x, axis, [(i, i ^ bit) for i in range(size)])  12.9 us
    pallas_call x1, Pallas kernels, per_device(): pl.pallas_call(turn_kernel, grid=(8,), in_specs=[pl.BlockSpec((128, 16, 1...  8.46 us
    pallas_call x2, Pallas kernels, later_half(): call(lambda *refs: forward_kernel((t,), False, *refs), [f32(1, 1024, 256)...  7.21 us
    pallas_call x1, Pallas kernels, per_device(): call(lambda *refs: forward_kernel((0, 1), True, *refs), [f32(2, 1024, 256...  7.19 us
    pallas_call x1, Pallas kernels, per_device(): call(grads_kernel, [bf16(2, 1024, 512), bf16(2, 1024, 512), f32(512, 512)...  6.71 us
  transfers between devices with their start and end apart: 25, of which 8 were waited for; matrix products, arithmetic and copies ran while one was open for 1% of the time, Pallas kernels for 27%

profile of v3, /device:TPU:0, one launch (start us, length us, event | category | flops | bytes accessed | tf_op | source)
XLA Modules:
  0.0 131.5 jit_solution(13409568463393046390)
XLA Ops:
  0.6 0.1 pad_add_fusion.idx.refs_0_
  0.7 4.0 %pool_far.1 = (f32[128,256]{1,0:T(8,128)S(1)}, f32[128,256]{1,0:T(8,128)S(1)}, f32[128,256]{1,0:T(8,128)S(1)}, f32[128,256]{1,0:T(8,128)S(1)}, bf16[2,4,512,256]...) custom-call(s32[4]{0:T(128)S(1)} %pad_add_fusion.idx.refs_0_, s32[2,4,2048]{2,1,0:T(4,128)} %bitcast.43, ...), custom_call_target="tpu_custom_call" | custom-call | flops 1000000 | bytes 1048576 | tf_op jit(solution)/shard_map/pool_far/pallas_call | solution.py:359
  4.7 2.1 %collective-permute-start = (f32[128,256]{1,0:T(8,128)S(1)}, f32[128,256]{1,0:T(8,128)S(1)}, u32[]{:S(2)}, u32[]{:S(2)}) collective-permute-start(f32[128,256]{1,0:T(8,128)S(1)} %get-tuple-element.90), channel_id=1, source_target_pairs={{0,4},{4,8},{8,12},{12,0},{1,5},{5,9},{9,13},{13,1},{2,6},{6,10},{... | collective-permute-start | bytes 393224 | tf_op jit(solution)/shard_map/ppermute | solution.py:340
  6.8 3.6 %collective-permute-start.1 = (f32[128,256]{1,0:T(8,128)S(1)}, f32[128,256]{1,0:T(8,128)S(1)}, u32[]{:S(2)}, u32[]{:S(2)}) collective-permute-start(f32[128,256]{1,0:T(8,128)S(1)} %get-tuple-element.91), channel_id=1, source_target_pairs={{0,8},{4,12},{8,0},{12,4},{1,9},{5,13},{9,1},{13,5},{2,10},{6,14},... | collective-permute-start | bytes 393224 | tf_op jit(solution)/shard_map/ppermute | solution.py:340
  10.4 1.0 collective-permute-start.2
  11.4 0.8 copy-done.1
  12.2 2.8 %pool_near.1 = (f32[128,256]{1,0:T(8,128)S(1)}, f32[128,256]{1,0:T(8,128)S(1)}, f32[128,256]{1,0:T(8,128)S(1)}, f32[128,256]{1,0:T(8,128)S(1)}, bf16[2,4,512,256]{3,2,1,0:T(8,128)(2,1)S(1)}) custom-call(s32[4]{0:T(128)S(1)} %pad_add_fusion.idx.refs_0_, s32[2,4,2048]{2,1,0:T(4,128)S(1)} %bitcast.44, f32[2,64,512]{2,1,0:T(8,128)S(1)} %get-tuple-element.93.decayed), custom_call_target="tpu_custom_call" | custom-call | flops 1000000 | bytes 1048576 | tf_op jit(solution)/shard_map/pool_near/pallas_call | solution.py:375
  15.1 1.3 %collective-permute-done.1.p2 = f32[128,256]{1,0:T(8,128)S(1)} collective-permute-done((f32[128,256]{1,0:T(8,128)S(1)}, f32[128,256]{1,0:T(8,128)S(1)}, u32[]{:S(2)}, u32[]{:S(2)}) %collective-permute-start.1) | collective-permute-done | bytes 131104 | tf_op jit(solution)/shard_map/ppermute | solution.py:340
  16.4 0.6 pack.2.refs_1_.far
  17.0 3.1 %collective-permute-start.6 = (f32[4,128,256]{2,1,0:T(8,128)S(1)}, f32[4,128,256]{2,1,0:T(8,128)S(1)}, u32[]{:S(2)}, u32[]{:S(2)}) collective-permute-start(f32[4,128,256]{2,1,0:T(8,128)S(1)} %pack.2.refs_1_.far), channel_id=1, source_target_pairs={{0,2},{2,0},{1,3},{3,1},{4,6},{6,4},{5,7},{7,5},{8,10},{10,8},{9,1... | collective-permute-start | bytes 1572872 | tf_op jit(solution)/shard_map/ppermute | solution.py:344
  20.1 1.2 collective-permute-start.3
  21.3 2.4 %collective-permute-start.4 = (f32[128,256]{1,0:T(8,128)S(1)}, f32[128,256]{1,0:T(8,128)S(1)}, u32[]{:S(2)}, u32[]{:S(2)}) collective-permute-start(f32[128,256]{1,0:T(8,128)S(1)} %get-tuple-element.103), channel_id=1, source_target_pairs={{0,8},{4,12},{8,0},{12,4},{1,9},{5,13},{9,1},{13,5},{2,10},{6,14},... | collective-permute-start | bytes 393224 | tf_op jit(solution)/shard_map/ppermute | solution.py:340
  23.7 1.2 collective-permute-start.5
  25.0 8.5 %turn.1 = (bf16[2,1024,1024]{2,1,0:T(8,128)(2,1)S(1)}, bf16[2,1024,1024]{2,1,0:T(8,128)(2,1)S(1)}) custom-call(f32[1024,16,128]{2,1,0:T(8,128)} %bitcast.48), custom_call_target="tpu_custom_call" | custom-call | flops 1000000 | bytes 1048576 | tf_op jit(solution)/shard_map/turn/pallas_call | solution.py:385
  33.5 0.6 pack.3.refs_1_.near
  34.1 0.1 collective-permute-start.7
  34.2 0.5 collective-permute-start.8
  34.7 0.5 collective-permute-start.9
  35.2 2.8 %prepare.1 = (bf16[2,256,1024]{2,1,0:T(8,128)(2,1)S(1)}, bf16[2,256,1024]{2,1,0:T(8,128)(2,1)S(1)}, f32[512,128]{1,0:T(8,128)S(1)}, f32[512,128]{1,0:T(8,128)S(1)}, f32[1,512]{1,0:T(1,128)S(1)}) custom-call(s32[4]{0:T(128)S(1)} %pad_add_fusion.idx.refs_0_, f32[1024,4,128]{2,1,0:T(4,128)} %bitcast.41, f32[4096,128]{1,0:T(8,128)} %lift_hbm, ...), custom_call_target="tpu_custom_call" | custom-call | flops 1000000 | bytes 1048576 | tf_op jit(solution)/shard_map/prepare/pallas_call | solution.py:407
  38.0 7.2 %forward_a.1 = (f32[2,1024,256]{2,1,0:T(8,128)S(1)}, f32[512,256]{1,0:T(8,128)S(1)}, f32[264,128]{1,0:T(8,128)S(1)}) custom-call(s32[4]{0:T(128)S(1)} %pad_add_fusion.idx.refs_0_, f32[4,128,256]{2,1,0:T(8,128)S(1)} %pack.3.refs_1_.near, f32[4,128,256]{2,1,0:T(8,128)S(1)} %collective-permute-done.6.refs_2_, ...), custom_call_target="tpu_custom_call" | custom-call | flops 1000000 | bytes 1048576 | tf_op jit(solution)/shard_map/forward_a/pallas_call | solution.py:418
  45.2 4.9 %collective-permute-done.9.refs_2_ = f32[4,128,256]{2,1,0:T(8,128)S(1)} collective-permute-done((f32[4,128,256]{2,1,0:T(8,128)S(1)}, f32[4,128,256]{2,1,0:T(8,128)S(1)}, u32[]{:S(2)}, u32[]{:S(2)}) %collective-permute-start.9) | collective-permute-done | bytes 524320 | tf_op jit(solution)/shard_map/ppermute | solution.py:344
  50.1 0.6 collective-permute-start.10
  50.7 3.5 %pick.1 = (bf16[2,256,1024]{2,1,0:T(8,128)(2,1)S(1)}, bf16[2,256,1024]{2,1,0:T(8,128)(2,1)S(1)}) custom-call(s32[4]{0:T(128)S(1)} %pad_add_fusion.idx.refs_0_, f32[4,4,64,16,128]{4,3,2,1,0:T(8,128)} %bitcast.49), custom_call_target="tpu_custom_call" | custom-call | flops 4000000000 | bytes 1048576 | tf_op jit(solution)/shard_map/pick/pallas_call | solution.py:441
  54.2 0.5 natural.1
  54.8 1.3 %collective-permute-done.10 = f32[264,128]{1,0:T(8,128)S(1)} collective-permute-done((f32[264,128]{1,0:T(8,128)S(1)}, f32[264,128]{1,0:T(8,128)S(1)}, u32[]{:S(2)}, u32[]{:S(2)}) %collective-permute-start.10) | collective-permute-done | bytes 135200 | tf_op jit(solution)/shard_map/ppermute | solution.py:344
  56.1 1.7 %collective-permute-start.11 = (f32[264,128]{1,0:T(8,128)S(1)}, f32[264,128]{1,0:T(8,128)S(1)}, u32[]{:S(2)}, u32[]{:S(2)}) collective-permute-start(f32[264,128]{1,0:T(8,128)S(1)} %add.16), channel_id=1, source_target_pairs={{0,32},{16,48},{32,0},{48,16},{64,96},{80,112},{96,64},{112,80},{1... | collective-permute-start | bytes 405512 | tf_op jit(solution)/shard_map/ppermute | solution.py:344
  57.8 3.6 %forward_b0.1 = (f32[1,1024,256]{2,1,0:T(8,128)S(1)}, f32[256,256]{1,0:T(8,128)S(1)}) custom-call(s32[4]{0:T(128)S(1)} %pad_add_fusion.idx.refs_0_, f32[4,128,256]{2,1,0:T(8,128)S(1)} %pack.2.refs_1_.far, f32[4,128,256]{2,1,0:T(8,128)S(1)} %collective-permute-done.9.refs_2_, f32[4,128,256]{2,1,0:T(8,128)S(1)} %collective-permute-done.12.refs_3_, ...), custom_call_target="tpu_custom_call" | custom-call | flops 4000000000 | bytes 1048576 | tf_op jit(solution)/shard_map/forward_b0/pallas_call | solution.py:430
  61.4 3.3 %collective-permute-start.14 = (f32[264,128]{1,0:T(8,128)S(1)}, f32[264,128]{1,0:T(8,128)S(1)}, u32[]{:S(2)}, u32[]{:S(2)}) collective-permute-start(f32[264,128]{1,0:T(8,128)S(1)} %add.17.mine), channel_id=1, source_target_pairs={{0,64},{16,80},{32,96},{48,112},{64,0},{80,16},{96,32},{112,48},{1... | collective-permute-start | bytes 405512 | tf_op jit(solution)/shard_map/ppermute | solution.py:344
  64.7 3.6 %forward_b1.1 = (f32[1,1024,256]{2,1,0:T(8,128)S(1)}, f32[256,256]{1,0:T(8,128)S(1)}) custom-call(s32[4]{0:T(128)S(1)} %pad_add_fusion.idx.refs_0_, f32[4,128,256]{2,1,0:T(8,128)S(1)} %pack.2.refs_1_.far, f32[4,128,256]{2,1,0:T(8,128)S(1)} %collective-permute-done.9.refs_2_, f32[4,128,256]{2,1,0:T(8,128)S(1)} %collective-permute-done.12.refs_3_, ...), custom_call_target="tpu_custom_call" | custom-call | flops 4000000000 | bytes 1048576 | tf_op jit(solution)/shard_map/forward_b1/pallas_call | solution.py:430
  68.3 1.2 logit.1
  69.5 1.2 collective-permute-start.16
  70.7 2.2 %collective-permute-start.17 = (f32[264,128]{1,0:T(8,128)S(1)}, f32[264,128]{1,0:T(8,128)S(1)}, u32[]{:S(2)}, u32[]{:S(2)}) collective-permute-start(f32[264,128]{1,0:T(8,128)S(1)} %get-tuple-element.135.own), channel_id=1, source_target_pairs={{0,3},{1,2},{2,1},{3,0},{4,7},{5,6},{6,5},{7,4},{8,11},{9,10},{10,... | collective-permute-start | bytes 405512 | tf_op jit(solution)/shard_map/ppermute | solution.py:344
  72.9 4.5 %collective-permute-done.16.xa = f32[264,128]{1,0:T(8,128)S(1)} collective-permute-done((f32[264,128]{1,0:T(8,128)S(1)}, f32[264,128]{1,0:T(8,128)S(1)}, u32[]{:S(2)}, u32[]{:S(2)}) %collective-permute-start.16) | collective-permute-done | bytes 135200 | tf_op jit(solution)/shard_map/ppermute | solution.py:344
  77.4 2.1 %collective-permute-done.17.xb = f32[264,128]{1,0:T(8,128)S(1)} collective-permute-done((f32[264,128]{1,0:T(8,128)S(1)}, f32[264,128]{1,0:T(8,128)S(1)}, u32[]{:S(2)}, u32[]{:S(2)}) %collective-permute-start.17) | collective-permute-done | bytes 135200 | tf_op jit(solution)/shard_map/ppermute | solution.py:344
  79.5 6.7 %grads.1 = (bf16[2,1024,512]{2,1,0:T(8,128)(2,1)S(1)}, bf16[2,1024,512]{2,1,0:T(8,128)(2,1)S(1)}, f32[512,512]{1,0:T(8,128)S(1)}, f32[256,512]{1,0:T(8,128)S(1)}...) custom-call(s32[4]{0:T(128)S(1)} %pad_add_fusion.idx.refs_0_, ...), custom_call_target="tpu_custom_call" | custom-call | flops 8999999488 | bytes 1048576 | tf_op jit(solution)/shard_map/grads/pallas_call | solution.py:471
  86.2 3.1 %weights.1 = (f32[80,1024]{1,0:T(8,128)S(1)}, f32[80,1024]{1,0:T(8,128)S(1)}, f32[80,1024]{1,0:T(8,128)S(1)}, f32[144,1024]{1,0:T(8,128)S(1)}, f32[88,1024]{1,0:...) custom-call(s32[4]{0:T(128)S(1)} %pad_add_fusion.idx.refs_0_, ...), custom_call_target="tpu_custom_call" | custom-call | flops 5000000000 | bytes 1048576 | tf_op jit(solution)/shard_map/weights/pallas_call | solution.py:478
  89.3 0.9 collective-permute-start.18
  90.2 2.5 %collective-permute-start.20 = (f32[144,1024]{1,0:T(8,128)S(1)}, f32[144,1024]{1,0:T(8,128)S(1)}, u32[]{:S(2)}, u32[]{:S(2)}) collective-permute-start(f32[144,1024]{1,0:T(8,128)S(1)} %get-tuple-element.155), channel_id=1, source_target_pairs={{0,12},{4,0},{8,4},{12,8},{1,13},{5,1},{9,5},{13,9},{2,14},{6,2},{... | collective-permute-start | bytes 1769480 | tf_op jit(solution)/shard_map/ppermute | solution.py:340
  92.7 2.0 %collective-permute-start.21 = (f32[80,1024]{1,0:T(8,128)S(1)}, f32[80,1024]{1,0:T(8,128)S(1)}, u32[]{:S(2)}, u32[]{:S(2)}) collective-permute-start(f32[80,1024]{1,0:T(8,128)S(1)} %get-tuple-element.162), channel_id=1, source_target_pairs={{0,4},{4,8},{8,12},{12,0},{1,5},{5,9},{9,13},{13,1},{2,6},{6,10},{... | collective-permute-start | bytes 983048 | tf_op jit(solution)/shard_map/ppermute | solution.py:340
  94.7 0.1 collective-permute-start.19
  94.8 24.6 %collective-permute-done.21 = f32[80,1024]{1,0:T(8,128)S(1)} collective-permute-done((f32[80,1024]{1,0:T(8,128)S(1)}, f32[80,1024]{1,0:T(8,128)S(1)}, u32[]{:S(2)}, u32[]{:S(2)}) %collective-permute-start.21) | collective-permute-done | bytes 327712 | tf_op jit(solution)/shard_map/ppermute | solution.py:340
  119.4 0.1 collective-permute-start.22
  119.6 3.3 %collective-permute-start.24 = (f32[88,1024]{1,0:T(8,128)S(1)}, f32[88,1024]{1,0:T(8,128)S(1)}, u32[]{:S(2)}, u32[]{:S(2)}) collective-permute-start(f32[88,1024]{1,0:T(8,128)S(1)} %add.19), channel_id=1, source_target_pairs={{0,12},{4,0},{8,4},{12,8},{1,13},{5,1},{9,5},{13,9},{2,14},{6,2},{... | collective-permute-start | bytes 1081352 | tf_op jit(solution)/shard_map/ppermute | solution.py:340
  122.9 2.8 %update.1 = (f32[2,64,512]{2,1,0:T(8,128)}, f32[2,512]{1,0:T(2,128)S(1)}) custom-call(s32[4]{0:T(128)S(1)} %pad_add_fusion.idx.refs_0_, f32[128,512]{1,0:T(8,128)S(1)} %get-tuple-element.143.p0, f32[152,1024]{1,0:T(8,128)S(1)} %collective-permute-done.18.p1.refs_4_, f32[128,512]{1,0:T(8,128)S(1)} %collective-permute-done.19.p2, ...), custom_call_target="tpu_custom_call" | custom-call | flops 5000000000 | bytes 1048576 | tf_op jit(solution)/shard_map/update/pallas_call | solution.py:493
  125.7 0.6 copy.23
  126.3 3.5 %collective-permute-done.22.refs_1_ = f32[80,1024]{1,0:T(8,128)S(1)} collective-permute-done((f32[80,1024]{1,0:T(8,128)S(1)}, f32[80,1024]{1,0:T(8,128)S(1)}, u32[]{:S(2)}, u32[]{:S(2)}) %collective-permute-start.22) | collective-permute-done | bytes 327712 | tf_op jit(solution)/shard_map/ppermute | solution.py:340
  129.7 0.1 collective-permute-done.24.refs_5_
  129.8 1.6 %sum.1 = (f32[1024,128]{1,0:T(8,128)}, f32[256,128]{1,0:T(8,128)}, f32[32,128]{1,0:T(8,128)}, f32[32,128]{1,0:T(8,128)}) custom-call(s32[4]{0:T(128)S(1)} %pad_add_fusion.idx.refs_0_, f32[1,512]{1,0:T(1,128)S(1)} %get-tuple-element.117.refs_11_.head, f32[80,1024]{1,0:T(8,128)S(1)} %get-tuple-element.160.refs_0_, ...), custom_call_target="tpu_custom_call" | custom-call | flops 1000000 | bytes 1048576 | tf_op jit(solution)/shard_map/sum/pallas_call | solution.py:496
  (35 shorter events, 0.2 us)
Async XLA Ops:
  4.7 10.3 %collective-permute-start = (f32[128,256]{1,0:T(8,128)S(1)}, f32[128,256]{1,0:T(8,128)S(1)}, u32[]{:S(2)}, u32[]{:S(2)}) collective-permute-start(f32[128,256]{1,0:T(8,128)S(1)} %get-tuple-element.90), channel_id=1, source_target_pairs={{0,4},{4,8},{8,12},{12,0},{1,5},{5,9},{9,13},{13,1},{2,6},{6,10},{... | collective-permute-start | bytes 393224 | tf_op jit(solution)/shard_map/ppermute | solution.py:340
  6.8 9.6 %collective-permute-start.1 = (f32[128,256]{1,0:T(8,128)S(1)}, f32[128,256]{1,0:T(8,128)S(1)}, u32[]{:S(2)}, u32[]{:S(2)}) collective-permute-start(f32[128,256]{1,0:T(8,128)S(1)} %get-tuple-element.91), channel_id=1, source_target_pairs={{0,8},{4,12},{8,0},{12,4},{1,9},{5,13},{9,1},{13,5},{2,10},{6,14},... | collective-permute-start | bytes 393224 | tf_op jit(solution)/shard_map/ppermute | solution.py:340
  10.4 6.0 %collective-permute-start.2 = (f32[128,256]{1,0:T(8,128)S(1)}, f32[128,256]{1,0:T(8,128)S(1)}, u32[]{:S(2)}, u32[]{:S(2)}) collective-permute-start(f32[128,256]{1,0:T(8,128)S(1)} %get-tuple-element.92), channel_id=1, source_target_pairs={{0,12},{4,0},{8,4},{12,8},{1,13},{5,1},{9,5},{13,9},{2,14},{6,2},{... | collective-permute-start | bytes 393224 | tf_op jit(solution)/shard_map/ppermute | solution.py:340
  11.4 0.8 copy-start.1
  17.0 17.2 %collective-permute-start.6 = (f32[4,128,256]{2,1,0:T(8,128)S(1)}, f32[4,128,256]{2,1,0:T(8,128)S(1)}, u32[]{:S(2)}, u32[]{:S(2)}) collective-permute-start(f32[4,128,256]{2,1,0:T(8,128)S(1)} %pack.2.refs_1_.far), channel_id=1, source_target_pairs={{0,2},{2,0},{1,3},{3,1},{4,6},{6,4},{5,7},{7,5},{8,10},{10,8},{9,1... | collective-permute-start | bytes 1572872 | tf_op jit(solution)/shard_map/ppermute | solution.py:344
  20.1 13.3 %collective-permute-start.3 = (f32[128,256]{1,0:T(8,128)S(1)}, f32[128,256]{1,0:T(8,128)S(1)}, u32[]{:S(2)}, u32[]{:S(2)}) collective-permute-start(f32[128,256]{1,0:T(8,128)S(1)} %get-tuple-element.102), channel_id=1, source_target_pairs={{0,4},{4,8},{8,12},{12,0},{1,5},{5,9},{9,13},{13,1},{2,6},{6,10},{... | collective-permute-start | bytes 393224 | tf_op jit(solution)/shard_map/ppermute | solution.py:340
  21.3 12.1 %collective-permute-start.4 = (f32[128,256]{1,0:T(8,128)S(1)}, f32[128,256]{1,0:T(8,128)S(1)}, u32[]{:S(2)}, u32[]{:S(2)}) collective-permute-start(f32[128,256]{1,0:T(8,128)S(1)} %get-tuple-element.103), channel_id=1, source_target_pairs={{0,8},{4,12},{8,0},{12,4},{1,9},{5,13},{9,1},{13,5},{2,10},{6,14},... | collective-permute-start | bytes 393224 | tf_op jit(solution)/shard_map/ppermute | solution.py:340
  23.7 9.7 %collective-permute-start.5 = (f32[128,256]{1,0:T(8,128)S(1)}, f32[128,256]{1,0:T(8,128)S(1)}, u32[]{:S(2)}, u32[]{:S(2)}) collective-permute-start(f32[128,256]{1,0:T(8,128)S(1)} %get-tuple-element.104), channel_id=1, source_target_pairs={{0,12},{4,0},{8,4},{12,8},{1,13},{5,1},{9,5},{13,9},{2,14},{6,2},{... | collective-permute-start | bytes 393224 | tf_op jit(solution)/shard_map/ppermute | solution.py:340
  25.0 10.2 %copy-start.2 = (f32[4096]{0:T(1024)S(1)}, f32[4096]{0:T(1024)}, u32[]{:S(2)}) copy-start(f32[4096]{0:T(1024)} %param.20) | copy-start | bytes 49156
  34.1 4.0 %collective-permute-start.7 = (f32[4,128,256]{2,1,0:T(8,128)S(1)}, f32[4,128,256]{2,1,0:T(8,128)S(1)}, u32[]{:S(2)}, u32[]{:S(2)}) collective-permute-start(f32[4,128,256]{2,1,0:T(8,128)S(1)} %pack.3.refs_1_.near), channel_id=1, source_target_pairs={{0,1},{1,0},{2,3},{3,2},{4,5},{5,4},{6,7},{7,6},{8,9},{9,8},{10,11... | collective-permute-start | bytes 1572872 | tf_op jit(solution)/shard_map/ppermute | solution.py:344
  34.2 3.9 %collective-permute-start.8 = (f32[4,128,256]{2,1,0:T(8,128)S(1)}, f32[4,128,256]{2,1,0:T(8,128)S(1)}, u32[]{:S(2)}, u32[]{:S(2)}) collective-permute-start(f32[4,128,256]{2,1,0:T(8,128)S(1)} %collective-permute-done.6.refs_2_), channel_id=1, source_target_pairs={{0,1},{1,0},{2,3},{3,2},{4,5},{5,4},{6,7},{7,6},{8,9},{9,8},{10,11... | collective-permute-start | bytes 1572872 | tf_op jit(solution)/shard_map/ppermute | solution.py:344
  34.7 15.4 %collective-permute-start.9 = (f32[4,128,256]{2,1,0:T(8,128)S(1)}, f32[4,128,256]{2,1,0:T(8,128)S(1)}, u32[]{:S(2)}, u32[]{:S(2)}) collective-permute-start(f32[4,128,256]{2,1,0:T(8,128)S(1)} %pack.3.refs_1_.near), channel_id=1, source_target_pairs={{0,2},{2,0},{1,3},{3,1},{4,6},{6,4},{5,7},{7,5},{8,10},{10,8},{9,1... | collective-permute-start | bytes 1572872 | tf_op jit(solution)/shard_map/ppermute | solution.py:344
  35.2 22.6 %collective-permute-start.12 = (f32[4,128,256]{2,1,0:T(8,128)S(1)}, f32[4,128,256]{2,1,0:T(8,128)S(1)}, u32[]{:S(2)}, u32[]{:S(2)}) collective-permute-start(f32[4,128,256]{2,1,0:T(8,128)S(1)} %pack.2.refs_1_.far), channel_id=1, source_target_pairs={{0,1},{1,0},{2,3},{3,2},{4,5},{5,4},{6,7},{7,6},{8,9},{9,8},{10,11... | collective-permute-start | bytes 1572872 | tf_op jit(solution)/shard_map/ppermute | solution.py:344
  50.1 7.7 %collective-permute-start.13 = (f32[4,128,256]{2,1,0:T(8,128)S(1)}, f32[4,128,256]{2,1,0:T(8,128)S(1)}, u32[]{:S(2)}, u32[]{:S(2)}) collective-permute-start(f32[4,128,256]{2,1,0:T(8,128)S(1)} %collective-permute-done.9.refs_2_), channel_id=1, source_target_pairs={{0,1},{1,0},{2,3},{3,2},{4,5},{5,4},{6,7},{7,6},{8,9},{9,8},{10,11... | collective-permute-start | bytes 1572872 | tf_op jit(solution)/shard_map/ppermute | solution.py:344
  50.1 6.0 %collective-permute-start.10 = (f32[264,128]{1,0:T(8,128)S(1)}, f32[264,128]{1,0:T(8,128)S(1)}, u32[]{:S(2)}, u32[]{:S(2)}) collective-permute-start(f32[264,128]{1,0:T(8,128)S(1)} %get-tuple-element.120), channel_id=1, source_target_pairs={{0,16},{16,0},{32,48},{48,32},{64,80},{80,64},{96,112},{112,96},{1... | collective-permute-start | bytes 405512 | tf_op jit(solution)/shard_map/ppermute | solution.py:344
  50.7 3.5 %copy-start = (f32[1024,2,256]{2,1,0:T(2,128)S(1)}, f32[1024,2,256]{2,1,0:T(2,128)}, u32[]{:S(2)}) copy-start(f32[1024,2,256]{2,1,0:T(2,128)} %param.17) | copy-start | bytes 6291460
  56.1 5.3 %collective-permute-start.11 = (f32[264,128]{1,0:T(8,128)S(1)}, f32[264,128]{1,0:T(8,128)S(1)}, u32[]{:S(2)}, u32[]{:S(2)}) collective-permute-start(f32[264,128]{1,0:T(8,128)S(1)} %add.16), channel_id=1, source_target_pairs={{0,32},{16,48},{32,0},{48,16},{64,96},{80,112},{96,64},{112,80},{1... | collective-permute-start | bytes 405512 | tf_op jit(solution)/shard_map/ppermute | solution.py:344
  61.4 6.9 %copy-start.3 = (s32[1,128]{1,0:T(1,128)S(1)}, s32[1,128]{1,0:T(1,128)}, u32[]{:S(2)}) copy-start(s32[1,128]{1,0:T(1,128)} %labels.1) | copy-start | bytes 1540
  61.4 6.9 %collective-permute-start.14 = (f32[264,128]{1,0:T(8,128)S(1)}, f32[264,128]{1,0:T(8,128)S(1)}, u32[]{:S(2)}, u32[]{:S(2)}) collective-permute-start(f32[264,128]{1,0:T(8,128)S(1)} %add.17.mine), channel_id=1, source_target_pairs={{0,64},{16,80},{32,96},{48,112},{64,0},{80,16},{96,32},{112,48},{1... | collective-permute-start | bytes 405512 | tf_op jit(solution)/shard_map/ppermute | solution.py:344
  69.5 3.4 %collective-permute-start.15 = (f32[264,128]{1,0:T(8,128)S(1)}, f32[264,128]{1,0:T(8,128)S(1)}, u32[]{:S(2)}, u32[]{:S(2)}) collective-permute-start(f32[264,128]{1,0:T(8,128)S(1)} %get-tuple-element.135.own), channel_id=1, source_target_pairs={{0,1},{1,0},{2,3},{3,2},{4,5},{5,4},{6,7},{7,6},{8,9},{9,8},{10,11... | collective-permute-start | bytes 405512 | tf_op jit(solution)/shard_map/ppermute | solution.py:344
  69.5 7.9 %collective-permute-start.16 = (f32[264,128]{1,0:T(8,128)S(1)}, f32[264,128]{1,0:T(8,128)S(1)}, u32[]{:S(2)}, u32[]{:S(2)}) collective-permute-start(f32[264,128]{1,0:T(8,128)S(1)} %get-tuple-element.135.own), channel_id=1, source_target_pairs={{0,2},{1,3},{2,0},{3,1},{4,6},{5,7},{6,4},{7,5},{8,10},{9,11},{10,... | collective-permute-start | bytes 405512 | tf_op jit(solution)/shard_map/ppermute | solution.py:344
  70.7 8.8 %collective-permute-start.17 = (f32[264,128]{1,0:T(8,128)S(1)}, f32[264,128]{1,0:T(8,128)S(1)}, u32[]{:S(2)}, u32[]{:S(2)}) collective-permute-start(f32[264,128]{1,0:T(8,128)S(1)} %get-tuple-element.135.own), channel_id=1, source_target_pairs={{0,3},{1,2},{2,1},{3,0},{4,7},{5,6},{6,5},{7,4},{8,11},{9,10},{10,... | collective-permute-start | bytes 405512 | tf_op jit(solution)/shard_map/ppermute | solution.py:344
  86.2 8.5 %copy-start.4 = (f32[2,1,512]{2,1,0:T(1,128)S(1)}, f32[2,1,512]{2,1,0:T(1,128)}, u32[]{:S(2)}) copy-start(f32[2,1,512]{2,1,0:T(1,128)} %param.15) | copy-start | bytes 12292
  89.3 33.5 %collective-permute-start.18 = (f32[152,1024]{1,0:T(8,128)S(1)}, f32[152,1024]{1,0:T(8,128)S(1)}, u32[]{:S(2)}, u32[]{:S(2)}) collective-permute-start(f32[152,1024]{1,0:T(8,128)S(1)} %get-tuple-element.153), channel_id=1, source_target_pairs={{0,4},{4,8},{8,12},{12,0},{1,5},{5,9},{9,13},{13,1},{2,6},{6,10},{... | collective-permute-start | bytes 1867784 | tf_op jit(solution)/shard_map/ppermute | solution.py:340
  90.2 32.7 %collective-permute-start.20 = (f32[144,1024]{1,0:T(8,128)S(1)}, f32[144,1024]{1,0:T(8,128)S(1)}, u32[]{:S(2)}, u32[]{:S(2)}) collective-permute-start(f32[144,1024]{1,0:T(8,128)S(1)} %get-tuple-element.155), channel_id=1, source_target_pairs={{0,12},{4,0},{8,4},{12,8},{1,13},{5,1},{9,5},{13,9},{2,14},{6,2},{... | collective-permute-start | bytes 1769480 | tf_op jit(solution)/shard_map/ppermute | solution.py:340
  92.6 26.9 %collective-permute-start.23 = (f32[88,1024]{1,0:T(8,128)S(1)}, f32[88,1024]{1,0:T(8,128)S(1)}, u32[]{:S(2)}, u32[]{:S(2)}) collective-permute-start(f32[88,1024]{1,0:T(8,128)S(1)} %get-tuple-element.165), channel_id=1, source_target_pairs={{0,12},{4,0},{8,4},{12,8},{1,13},{5,1},{9,5},{13,9},{2,14},{6,2},{... | collective-permute-start | bytes 1081352 | tf_op jit(solution)/shard_map/ppermute | solution.py:340
  92.7 26.7 %collective-permute-start.21 = (f32[80,1024]{1,0:T(8,128)S(1)}, f32[80,1024]{1,0:T(8,128)S(1)}, u32[]{:S(2)}, u32[]{:S(2)}) collective-permute-start(f32[80,1024]{1,0:T(8,128)S(1)} %get-tuple-element.162), channel_id=1, source_target_pairs={{0,4},{4,8},{8,12},{12,0},{1,5},{5,9},{9,13},{13,1},{2,6},{6,10},{... | collective-permute-start | bytes 983048 | tf_op jit(solution)/shard_map/ppermute | solution.py:340
  94.7 28.2 %collective-permute-start.19 = (f32[128,512]{1,0:T(8,128)S(1)}, f32[128,512]{1,0:T(8,128)S(1)}, u32[]{:S(2)}, u32[]{:S(2)}) collective-permute-start(f32[128,512]{1,0:T(8,128)S(1)} %get-tuple-element.154), channel_id=1, source_target_pairs={{0,8},{4,12},{8,0},{12,4},{1,9},{5,13},{9,1},{13,5},{2,10},{6,14},... | collective-permute-start | bytes 786440 | tf_op jit(solution)/shard_map/ppermute | solution.py:340
  119.4 10.3 %collective-permute-start.22 = (f32[80,1024]{1,0:T(8,128)S(1)}, f32[80,1024]{1,0:T(8,128)S(1)}, u32[]{:S(2)}, u32[]{:S(2)}) collective-permute-start(f32[80,1024]{1,0:T(8,128)S(1)} %add.18), channel_id=1, source_target_pairs={{0,4},{4,8},{8,12},{12,0},{1,5},{5,9},{9,13},{13,1},{2,6},{6,10},{... | collective-permute-start | bytes 983048 | tf_op jit(solution)/shard_map/ppermute | solution.py:340
  119.6 10.2 %collective-permute-start.24 = (f32[88,1024]{1,0:T(8,128)S(1)}, f32[88,1024]{1,0:T(8,128)S(1)}, u32[]{:S(2)}, u32[]{:S(2)}) collective-permute-start(f32[88,1024]{1,0:T(8,128)S(1)} %add.19), channel_id=1, source_target_pairs={{0,12},{4,0},{8,4},{12,8},{1,13},{5,1},{9,5},{13,9},{2,14},{6,2},{... | collective-permute-start | bytes 1081352 | tf_op jit(solution)/shard_map/ppermute | solution.py:340

commit v4 on v3

--- a/solution.py
+++ b/solution.py
@@ -112,24 +112,38 @@
         out[lax.rem(idx[0] + 4 - k, 4)] = ref[...]
 
 
-def turn_kernel(w, high, low):
-    rows = w.shape[0]
-    flat = w.reshape(rows * 16, 128)
-    for t in range(2):
-        for b in range(8):
-            h, l = halves(flat[pl.ds(b * 2 + t, rows, stride=16), :].T)
-            high[t, b * 128 : (b + 1) * 128, :] = h
-            low[t, b * 128 : (b + 1) * 128, :] = l
-
-
-def pick_kernel(idx, w, high, low):
-    rows = w.shape[2]
-    flat = w.reshape(rows * 16, 128)
-    for t in range(2):
-        for b in range(8):
-            h, l = halves(flat[pl.ds(b * 2 + t, rows, stride=16), :])
-            high[t, :, b * 128 : (b + 1) * 128] = h
-            low[t, :, b * 128 : (b + 1) * 128] = l
+def turn_kernel(at, w_hbm, high, low, w, sems):
+    pieces, rows = w.shape[:2]
+    copies = [pltpu.make_async_copy(w_hbm.at[pl.ds((at * pieces + n) * rows, rows)], w.at[n], sems.at[n]) for n in range(pieces)]
+    for copy in copies:
+        copy.start()
+    for n, copy in enumerate(copies):
+        copy.wait()
+        flat = w.at[n].reshape(rows * 16, 128)
+        for t in range(2):
+            for b in range(8):
+                h, l = halves(flat[pl.ds(b * 2 + t, rows, stride=16), :].T)
+                high[t, b * 128 : (b + 1) * 128, n * rows : (n + 1) * rows] = h
+                low[t, b * 128 : (b + 1) * 128, n * rows : (n + 1) * rows] = l
+
+
+def pick_kernel(idx, w_hbm, high, low, w, sems):
+    rows = w.shape[1]
+    quad = 2 * idx[1] + idx[2]
+    copies = []
+    for k in range(4):
+        table = lax.rem(idx[0] + k, 4) * 4 + quad
+        copies.append(pltpu.make_async_copy(w_hbm.at[pl.ds(pl.multiple_of(table * rows, rows), rows)], w.at[k], sems.at[k]))
+    for copy in copies:
+        copy.start()
+    for k, copy in enumerate(copies):
+        copy.wait()
+        flat = w.at[k].reshape(rows * 16, 128)
+        for t in range(2):
+            for b in range(8):
+                h, l = halves(flat[pl.ds(b * 2 + t, rows, stride=16), :])
+                high[t, k * rows : (k + 1) * rows, b * 128 : (b + 1) * 128] = h
+                low[t, k * rows : (k + 1) * rows, b * 128 : (b + 1) * 128] = l
 
 
 def prepare_kernel(idx, second_hbm, lift_hbm, press_hbm, heads, high_t, low_t, lift, press, head, second, sems):
@@ -163,7 +177,7 @@
             low[t, :, lanes] = l
 
 
-def forward_kernel(towers, with_pay, idx, x1, x2, y1, y2, w1h, w1l, w2h, w2l, press, lift, head, hidden, start, *rest):
+def forward_kernel(towers, with_pay, idx, x1, x2, y1, y2, w1ha, w1la, w1hb, w1lb, w2h, w2l, press, lift, head, hidden, start, *rest):
     fh, fl = rest[-2:]
     sets = (x1, x2, y1, y2)
     zs, pair, samples = x1.shape
@@ -179,7 +193,9 @@
                 at = pl.multiple_of(((z * 2 + a) * 2 + b) * width, width)
                 fh[pl.ds(at, width), :] = h
                 fl[pl.ds(at, width), :] = l
-        value = dot3((w1h[t], w1l[t]), (fh[...], fl[...]))
+        deep = w1ha.shape[2]
+        value = dot3((w1ha[t], w1la[t]), (fh[0:deep, :], fl[0:deep, :]))
+        value = value + dot3((w1hb[t], w1lb[t]), (fh[deep:, :], fl[deep:, :]))
         hidden[slot] = value
         act = halves(value * jax.nn.sigmoid(value))
         start[pl.ds(pl.multiple_of(slot * width_out, width_out), width_out), :] = dot3((w2h[t], w2l[t]), act)
@@ -217,97 +233,114 @@
     pay[2 * rank : 2 * rank + 8, :] = jnp.broadcast_to(error, (8, error.shape[1]))
 
 
-def grads_kernel(idx, own, c1, xa, xb, hid_a, hid_b0, hid_b1, w1h, w1l, w2h, w2l, press, lift, head, ghh, ghl, gout, pq, g0, g1, g2, g3):
-    core = idx[2]
+def grads_kernel(towers, with_pq, idx, mine, other, hidden, w1h, w1l, w2h, w2l, press, lift, head, ghh, ghl, gout, g0, g1, g2, g3, *pq):
     rank = press.shape[1]
-    n = own.shape[1]
-    half = 2 * n
-    outs = (g0, g1, g2, g3)
     width = w1h.shape[1] // 4
     width_out = w2h.shape[2]
+    first_core = idx[2] == 0
+    left = jnp.where(first_core, mine[...], other[...])
+    right = jnp.where(first_core, other[...], mine[...])
+    both = jnp.concatenate([left, right], axis=1)
+    error = both[2 * rank : 2 * rank + 1]
+    if with_pq:
+        pq[0][...] = error * both[0 : 2 * rank]
+    p, q = halves(both[0:rank]), halves(both[rank : 2 * rank])
     column = jnp.broadcast_to(head[...], (128, head.shape[1])).T[:, 0:1]
-    first_core = core == 0
-    for g, (mine, other, hidden) in enumerate(((own, c1, (hid_a.at[0], hid_a.at[1])), (xa, xb, (hid_b0.at[0], hid_b1.at[0])))):
-        left = jnp.where(first_core, mine[...], other[...])
-        right = jnp.where(first_core, other[...], mine[...])
-        both = jnp.concatenate([left, right], axis=1)
-        p, q, error = both[0:rank], both[rank : 2 * rank], both[2 * rank : 2 * rank + 1]
-        lanes = slice(g * half, (g + 1) * half)
-        pq[0:rank, lanes] = error * p
-        pq[rank : 2 * rank, lanes] = error * q
-        scaling = dot32(lift[...], p)
-        back = dot32(press[...], q)
-        gout[:, lanes] = error * (column * (scaling + 1.0) + back)
-
-        for t in range(2):
-            go = halves(gout[t * width_out : (t + 1) * width_out, lanes])
-            ga = dot3((w2h[t], w2l[t]), go)
-            value = hidden[t][...]
-            s = jax.nn.sigmoid(value)
-            gh = halves(ga * (s * (1.0 + value * (1.0 - s))))
-            ghh[t, :, lanes] = gh[0]
-            ghl[t, :, lanes] = gh[1]
-            grad = dot3((w1h[t], w1l[t]), gh)
-            for k in range(4):
-                outs[k][t * width : (t + 1) * width, lanes] = grad[k * width : (k + 1) * width]
-
-
-def weights_kernel(idx, near, far, ghh, ghl, gout, hid_a, hid_b0, hid_b1, x0a, x0b0, x0b1, pq, g1, g3, *blocks):
-    hid_b, x0b = (hid_b0, hid_b1), (x0b0, x0b1)
+    for slot, t in enumerate(towers):
+        rows = slice(t * width_out, (t + 1) * width_out)
+        scaling = dot3(halves(lift[rows, :]), p)
+        back = dot3(halves(press[rows, :]), q)
+        go = error * (column[rows] * (scaling + 1.0) + back)
+        gout[slot] = go
+        ga = dot3((w2h[t], w2l[t]), halves(go))
+        value = hidden[slot]
+        s = jax.nn.sigmoid(value)
+        gh = halves(ga * (s * (1.0 + value * (1.0 - s))))
+        ghh[slot] = gh[0]
+        ghl[slot] = gh[1]
+        grad = dot3((w1h[t], w1l[t]), gh)
+        for k, out in enumerate((g0, g1, g2, g3)):
+            out[slot] = grad[k * width : (k + 1) * width]
+
+
+def weights_kernel(t, riders, idx, near, far, ghha, ghla, ghhb, ghlb, gouta, goutb, hid_a, hid_b, *rest):
+    if t == 1:
+        rest, far_block = rest[:-1], rest[-1]
+    blocks, rest = rest[-4:], rest[:-4]
     z, quad = idx[0], 2 * idx[1] + idx[2]
     width = near.shape[1] // 2
-    width_out = gout.shape[0] // 2
-    for t in range(2):
-        outs = blocks[4 * t : 4 * t + 4]
-        rows = slice(t * width, (t + 1) * width)
-        f, act = [], []
+    rows = slice(t * width, (t + 1) * width)
+    fa, fb, acta, actb = [], [], [], []
+    for k in range(4):
+        at = lax.rem(z + k, 4)
+        fa.append(near[at, rows, :])
+        fb.append(far[at, rows, :])
+        pick = pl.ds(pl.multiple_of((at * 4 + quad) * width, width), width)
+        value = hid_a[t, pick, :]
+        acta.append(value * jax.nn.sigmoid(value))
+        value = hid_b[0, pick, :]
+        actb.append(value * jax.nn.sigmoid(value))
+    join = lambda parts: halves(jnp.concatenate(parts, axis=0))
+    grad = dot3(join(fa), (ghha[t], ghla[t]), NT) + dot3(join(fb), (ghhb[0], ghlb[0]), NT)
+    for k in range(4):
+        blocks[k][0:width, :] = grad[k * width : (k + 1) * width]
+    grad = dot3(join(acta), halves(gouta[t]), NT) + dot3(join(actb), halves(goutb[0]), NT)
+    for k in range(4):
+        for b in range(4):
+            blocks[k][width : width + 16, b * 256 : (b + 1) * 256] = grad[k * width + 16 * b : k * width + 16 * b + 16]
+    low = width // 2
+    for n, k in enumerate(riders):
+        ga, gb = rest[2 * n], rest[2 * n + 1]
+        base = blocks[k].shape[0] - low
+        blocks[k][base:, 0:256] = ga[t, 0:low, :]
+        blocks[k][base:, 256:512] = gb[0, 0:low, :]
+        blocks[k][base:, 512:768] = ga[t, low:, :]
+        blocks[k][base:, 768:1024] = gb[0, low:, :]
+    if t == 1:
+        x0a, x0b0, x0b1, pqa, pqb, ga, gb0, gb1 = rest[4:]
+        for n, gb in enumerate((gb0, gb1)):
+            for b in range(2):
+                part = slice(b * low, (b + 1) * low)
+                far_block[n * low : (n + 1) * low, b * 512 : b * 512 + 256] = ga[n, part, :]
+                far_block[n * low : (n + 1) * low, b * 512 + 256 : (b + 1) * 512] = gb[0, part, :]
+        parts_a, parts_b = [], []
         for k in range(4):
-            at = lax.rem(z + k, 4)
-            f.append(jnp.concatenate([near[at, rows, :], far[at, rows, :]], axis=1))
-            pick = pl.ds(pl.multiple_of((at * 4 + quad) * width, width), width)
-            value = jnp.concatenate([hid_a[t, pick, :], hid_b[t][0, pick, :]], axis=1)
-            act.append(value * jax.nn.sigmoid(value))
-        grad = dot3(halves(jnp.concatenate(f, axis=0)), (ghh[t], ghl[t]), NT)
-        for k in range(4):
-            outs[k][0:width, :] = grad[k * width : (k + 1) * width]
-        grad = dot32(jnp.concatenate(act, axis=0), gout[t * width_out : (t + 1) * width_out, :], NT)
+            block = lax.rem(z + k, 4) * 4 + quad
+            parts_a.append(x0a[pl.ds(pl.multiple_of(block * 32, 32), 32), :])
+            inner = pl.ds(pl.multiple_of(lax.rem(block, 8) * 32, 32), 32)
+            parts_b.append(jnp.where(block < 8, x0b0[inner, :], x0b1[inner, :]))
+        both = dot3(join(parts_a), halves(pqa[...]), NT) + dot3(join(parts_b), halves(pqb[...]), NT)
         for k in range(4):
             for b in range(4):
-                outs[k][width : width + 16, b * 256 : (b + 1) * 256] = grad[k * width + 16 * b : k * width + 16 * b + 16]
-    for out, ref in ((blocks[5], g1), (blocks[3], g3)):
-        base = out.shape[0] - width
-        for t in range(2):
-            out[base:, t * 512 : (t + 1) * 512] = ref[t * width : (t + 1) * width, :]
-    rank = pq.shape[0] // 2
-    x0 = []
-    for k in range(4):
-        block = lax.rem(z + k, 4) * 4 + quad
-        pick = pl.ds(pl.multiple_of(block * 32, 32), 32)
-        near_half = pl.ds(pl.multiple_of(lax.rem(block, 8) * 32, 32), 32)
-        later = jnp.where(block < 8, x0b[0][near_half, :], x0b[1][near_half, :])
-        x0.append(jnp.concatenate([x0a[pick, :], later], axis=1))
-    x0 = jnp.concatenate(x0, axis=0)
-    both = dot32(x0, pq[...], NT)
-    for k in range(4):
-        for b in range(4):
-            outs[k][width + 16 : width + 24, b * 256 : (b + 1) * 256] = both[32 * k + 8 * b : 32 * k + 8 * b + 8]
-
-
-def update_kernel(idx, p0, p1, p2, p3, near, far, decayed, accumulator, new_tables, new_accumulator):
+                blocks[k][width + 16 : width + 24, b * 256 : (b + 1) * 256] = both[32 * k + 8 * b : 32 * k + 8 * b + 8]
+
+
+def update_kernel(idx, ga, gb0, gb1, w_up, w_down, v_up, v_down, opposite, near, far, decayed, accumulator, new_tables, new_accumulator):
     z = idx[0]
     towers, width, rows = decayed.shape
-    half = p0.shape[1] // 2
+    low = width // 2
+
+    def rider(ref, start=None):
+        start = ref.shape[0] - low if start is None else start
+        block = ref[start : start + low, :]
+        return (
+            jnp.concatenate([block[:, 0:256], block[:, 512:768]], axis=0),
+            jnp.concatenate([block[:, 256:512], block[:, 768:1024]], axis=0),
+        )
+
     for t in range(towers):
+        gb = (gb0, gb1)[t]
+        pieces = (
+            (ga[t], gb[0]),
+            rider((w_up, v_up)[t]),
+            rider(opposite, low * t),
+            rider((w_down, v_down)[t]),
+        )
         total = jnp.zeros((2 * width, rows), F32)
-        for k, ref in enumerate((p0, p1, p2, p3)):
+        for k, (a, b) in enumerate(pieces):
             at = lax.rem(z + 4 - k, 4)
-            if ref.shape[0] == towers * width:
-                value = ref[t * width : (t + 1) * width, :]
-            else:
-                value = ref[ref.shape[0] - width :, t * 2 * half : (t + 1) * 2 * half]
-            both = jnp.concatenate(halves(value), axis=0)
-            total = total + dot1(both[:, :half], near[t, at], NT)
-            total = total + dot1(both[:, half:], far[t, at], NT)
+            total = total + dot1(jnp.concatenate(halves(a), axis=0), near[t, at], NT)
+            total = total + dot1(jnp.concatenate(halves(b), axis=0), far[t, at], NT)
         grad = total[:width] + total[width:]
         square = jnp.sum(grad * grad, axis=0, keepdims=True) * (1.0 / width)
         fresh = accumulator[t : t + 1, :] + square
@@ -375,24 +408,29 @@
     *near, counts_near = call(
         pool_near_kernel, [f32(128, 256)] * 4 + [bf16(2, 4, 512, 256)], [SMEM_SPEC] + vmem(2), name="pool_near", flops=1e6
     )(idx, bag, decayed)
-    *far, _ = lax.optimization_barrier((*far, near[0]))
+    view = first_weight.reshape(1024, 2, 8, 128).transpose(0, 2, 1, 3).reshape(1024, 16, 128)
+
+    def turn(view, at):
+        return pl.pallas_call(
+            lambda *refs: turn_kernel(at, *refs),
+            in_specs=[any_spec],
+            out_specs=vmem(2),
+            out_shape=[bf16(2, 1024, 512)] * 2,
+            scratch_shapes=[pltpu.VMEM((4, 128, 16, 128), F32), pltpu.SemaphoreType.DMA((4,))],
+            compiler_params=pltpu.CompilerParams(vmem_limit_bytes=VMEM_LIMIT),
+            cost_estimate=pl.CostEstimate(flops=int(1e6), transcendentals=0, bytes_accessed=1 << 20),
+            name="turn_%d" % at,
+        )(hbm(view))
+
+    view, _ = lax.optimization_barrier((view, decayed))
+    w1ha, w1la = turn(view, 0)
+    *far, _, _ = lax.optimization_barrier((*far, near[0], w1ha))
     (fq_far,) = pack(idx, *far)
     x2 = flip(fq_far, "xh", 2, 1)
     near = [near[0]] + [shift(near[k], "z", 4, k) for k in (1, 2, 3)]
-
-    _, first_weight = lax.optimization_barrier((fq_far, first_weight))
-    view = first_weight.reshape(1024, 2, 8, 128).transpose(0, 2, 1, 3).reshape(1024, 16, 128)
-    w1th, w1tl = pl.pallas_call(
-        turn_kernel,
-        grid=(8,),
-        in_specs=[pl.BlockSpec((128, 16, 128), lambda i: (i, 0, 0))],
-        out_specs=[pl.BlockSpec((2, 1024, 128), lambda i: (0, 0, i))] * 2,
-        out_shape=[bf16(2, 1024, 1024)] * 2,
-        compiler_params=pltpu.CompilerParams(vmem_limit_bytes=VMEM_LIMIT),
-        cost_estimate=pl.CostEstimate(flops=int(1e6), transcendentals=0, bytes_accessed=1 << 20),
-        name="turn",
-    )(hbm(view))
-    *near, _ = lax.optimization_barrier((*near, w1th))
+    view, _ = lax.optimization_barrier((view, fq_far))
+    w1hb, w1lb = turn(view, 1)
+    *near, _ = lax.optimization_barrier((*near, w1hb))
     (fq_near,) = pack(idx, *near)
     y1 = flip(fq_near, "core", 2, 1)
     y2 = flip(x2, "core", 2, 1)
@@ -401,7 +439,7 @@
     y2b = flip(x2b, "core", 2, 1)
 
     _, second_weight, lift_weight, press_weight, head_weight = lax.optimization_barrier(
-        (w1th, second_weight, lift_weight, press_weight, head_weight)
+        (w1hb, second_weight, lift_weight, press_weight, head_weight)
     )
     second_view = second_weight.reshape(1024, 2, 2, 128).transpose(0, 2, 1, 3).reshape(1024, 4, 128)
     w2th, w2tl, lift, press, head = call(
@@ -414,23 +452,21 @@
     )(idx, hbm(second_view), hbm(lift_weight), hbm(press_weight), head_weight.reshape(32, 128))
 
     scratch = [pltpu.VMEM((1024, 256), BF16)] * 2
-    weights = (w1th, w1tl, w2th, w2tl, press, lift, head)
+    weights = (w1ha, w1la, w1hb, w1lb, w2th, w2tl, press, lift, head)
     hid_a, x0a, pay = call(
         lambda *refs: forward_kernel((0, 1), True, *refs),
         [f32(2, 1024, 256), f32(512, 256), f32(2 * rank + 8, 128)],
-        [SMEM_SPEC] + vmem(11),
+        [SMEM_SPEC] + vmem(13),
         scratch,
         name="forward_a",
         flops=1e6,
     )(idx, fq_near, x2, y1, y2, *weights)
-    pay, x2b = lax.optimization_barrier((pay, x2b))
-    y2b = flip(x2b, "core", 2, 1)
-
-    def later_half(at, t):
+
+    def later_half(at, t, y2b):
         return call(
             lambda *refs: forward_kernel((t,), False, *refs),
             [f32(1, 1024, 256), f32(256, 256)],
-            [SMEM_SPEC] + vmem(11),
+            [SMEM_SPEC] + vmem(13),
             scratch,
             name="forward_b%d" % t,
             flops=4e9,
@@ -438,61 +474,82 @@
 
     view, second_view, pay = lax.optimization_barrier((view, second_view, pay))
     other = flip(pay, TOWER, 8, 1)
-    w1qh, w1ql = pl.pallas_call(
+    w1qh, w1ql = call(
         pick_kernel,
-        grid_spec=pltpu.PrefetchScalarGridSpec(
-            num_scalar_prefetch=1,
-            grid=(4,),
-            in_specs=[pl.BlockSpec((1, 1, 64, 16, 128), lambda k, i: (lax.rem(i[0] + k, 4), 2 * i[1] + i[2], 0, 0, 0))],
-            out_specs=[pl.BlockSpec((2, 64, 1024), lambda k, i: (0, k, 0))] * 2,
-        ),
-        out_shape=[bf16(2, 256, 1024)] * 2,
-        compiler_params=pltpu.CompilerParams(vmem_limit_bytes=VMEM_LIMIT),
-        cost_estimate=pl.CostEstimate(flops=int(4e9), transcendentals=0, bytes_accessed=1 << 20),
+        [bf16(2, 256, 1024)] * 2,
+        [SMEM_SPEC, any_spec],
+        [pltpu.VMEM((4, 64, 16, 128), F32), pltpu.SemaphoreType.DMA((4,))],
         name="pick",
-    )(idx, hbm(view.reshape(4, 4, 64, 16, 128)))
-    w2h, w2l = call(natural_kernel, [bf16(2, 1024, 256)] * 2, vmem(1), name="natural", flops=1e9)(second_view)
-    other, w1qh, w2h = lax.optimization_barrier((other, w1qh, w2h))
+        flops=1e6,
+    )(idx, hbm(view))
+    w2h, w2l = call(natural_kernel, [bf16(2, 1024, 256)] * 2, vmem(1), name="natural", flops=1e6)(second_view)
+    other, w1qh, w2h, x2b = lax.optimization_barrier((other, w1qh, w2h, x2b))
     pay = pay + other
     after, pay = lax.optimization_barrier((idx, pay))
     other = flip(pay, TOWER, 8, 2)
-    hid_b0, x0b0 = later_half(after, 0)
+    y2b = flip(x2b, "core", 2, 1)
+    hid_b0, x0b0 = later_half(after, 0, y2b)
     other, x0b0 = lax.optimization_barrier((other, x0b0))
     pay = pay + other
     after, pay = lax.optimization_barrier((idx, pay))
     other = flip(pay, TOWER, 8, 4)
-    hid_b1, x0b1 = later_half(after, 1)
+    hid_b1, x0b1 = later_half(after, 1, y2b)
     other, x0b1 = lax.optimization_barrier((other, x0b1))
     pay, logits = call(logit_kernel, [f32(2 * rank + 8, 128), f32(1, 16)], [SMEM_SPEC] + vmem(3), name="logit", flops=1e6)(
         idx, pay, other, labels
     )
-    pays = [pay] + [flip(pay, QUAD, 4, k) for k in (1, 2, 3)]
-
-    ghh, ghl, gout, pq, *g = call(
-        grads_kernel,
-        [bf16(2, 1024, 512), bf16(2, 1024, 512), f32(512, 512), f32(2 * rank, 512)] + [f32(128, 512)] * 4,
-        [SMEM_SPEC] + vmem(14),
-        name="grads",
-        flops=9e9,
-    )(idx, *pays, hid_a, hid_b0, hid_b1, w1qh, w1ql, w2h, w2l, press, lift, head)
-    w = call(
-        weights_kernel,
-        [f32(rows, 1024) for rows in (80, 80, 80, 144, 88, 152, 88, 88)],
-        [SMEM_SPEC] + vmem(14),
-        name="weights",
-        flops=5e9,
-    )(idx, fq_near, fq_far, ghh, ghl, gout, hid_a, hid_b0, hid_b1, x0a, x0b0, x0b1, pq, g[1], g[3])
-    w, v = w[:4], w[4:]
+    c1 = flip(pay, "core", 2, 1)
+    xa = flip(pay, "xh", 2, 1)
+
+    def grads(towers, with_pq, mine, other, hidden, name):
+        n = len(towers)
+        return call(
+            lambda *refs: grads_kernel(towers, with_pq, *refs),
+            [bf16(n, 1024, 256)] * 2 + [f32(n, 256, 256)] + [f32(n, 64, 256)] * 4 + [f32(2 * rank, 256)] * with_pq,
+            [SMEM_SPEC] + vmem(10),
+            name=name,
+            flops=4e9,
+        )(idx, mine, other, hidden, w1qh, w1ql, w2h, w2l, press, lift, head)
+
+    ghha, ghla, gouta, *ga, pqa = grads((0, 1), True, pay, c1, hid_a, "grads_a")
+
+    xa, pqa = lax.optimization_barrier((xa, pqa))
+    xb = flip(xa, "core", 2, 1)
+
+    def weights_of(t, riders, rows, ghhb, ghlb, goutb, hid_b, extra):
+        return call(
+            lambda *refs: weights_kernel(t, riders, *refs),
+            [f32(n, 1024) for n in rows],
+            [SMEM_SPEC] + vmem(10 + len(extra)),
+            name="weights_%d" % t,
+            flops=3e9,
+        )(idx, fq_near, fq_far, ghha, ghla, ghhb, ghlb, gouta, goutb, hid_a, hid_b, *extra)
+
+    ghh0, ghl0, gout0, *gb0, pqb = grads((0,), True, xa, xb, hid_b0, "grads_b0")
+    w = weights_of(0, (2, 3), (80, 80, 112, 112), ghh0, ghl0, gout0, hid_b0, (ga[1], gb0[1], ga[3], gb0[3]))
     up = shift(w[2], "z", 4, 1)
+    w3 = shift(w[3], "z", 4, 3)
+    ghh1, ghl1, gout1, *gb1 = grads((1,), False, xa, xb, hid_b1, "grads_b1")
+    v = weights_of(
+        1,
+        (1, 2),
+        (88, 120, 120, 88, 64),
+        ghh1,
+        ghl1,
+        gout1,
+        hid_b1,
+        (ga[1], gb1[1], ga[3], gb1[3], x0a, x0b0, x0b1, pqa, pqb, ga[2], gb0[2], gb1[2]),
+    )
     down = shift(v[2], "z", 4, 3)
     v1 = shift(v[1], "z", 4, 1)
-    w3 = shift(w[3], "z", 4, 3)
-    g2 = shift(g[2], "z", 4, 2)
-    w1 = shift(w[1] + up, "z", 4, 1)
-    v3 = shift(v[3] + down, "z", 4, 3)
+    g2 = shift(v[4], "z", 4, 2)
+    up, w3 = lax.optimization_barrier((up, w3))
+    down, v1 = lax.optimization_barrier((down, v1))
+    w1 = shift(w[1] + up[0:80], "z", 4, 1)
+    v3 = shift(v[3] + down[0:88], "z", 4, 3)
     new_tables, new_accumulator = call(
-        update_kernel, [f32(2, 64, 512), f32(2, 512)], [SMEM_SPEC] + vmem(8), name="update", flops=5e9
-    )(idx, g[0], v1, g2, w3, counts_near, counts_far, decayed, accumulator[:, 0])
+        update_kernel, [f32(2, 64, 512), f32(2, 512)], [SMEM_SPEC] + vmem(12), name="update", flops=5e9
+    )(idx, ga[0], gb0[0], gb1[0], up, w3, v1, down, g2, counts_near, counts_far, decayed, accumulator[:, 0])
     first, second, lift_out, press_out = call(
         sum_kernel,
         [f32(1024, 128), f32(256, 128), f32(32, rank), f32(32, rank)],

time: 132 us -> 120 us (0.909)
  waiting for transfers between devices: 42.4 us -> 31.9 us
  starting transfers between devices: 33.4 us -> 32 us
    ppermute x12, waiting for transfers between devices: 12.9 us -> 7.07 us  [flip(): return lax.ppermute(x, axis, [(i, i ^ bit) for i in range(size)])]
    ppermute x13, waiting for transfers between devices: 29.5 us -> 24.9 us  [shift(): return lax.ppermute(x, axis, [(i, (i + by) % size) for i in range(size)])]
    ppermute x13, starting transfers between devices: 20.3 us -> 18.2 us  [shift(): return lax.ppermute(x, axis, [(i, (i + by) % size) for i in range(size)])]
    pallas_call x5 -> x9, Pallas kernels: 24.6 us -> 25.1 us  [the longest x3 9.89 us: grads(): call(lambda *refs: grads_kernel(towers, with_pq, *refs), [bf16(n, 1024, 2...]
  transfers between devices with their start and end apart: 25 -> 25, of which waited for: 8 -> 13; matrix products, arithmetic and copies ran while one was open for 1% -> 1% of each run, Pallas kernels for 27% -> 35%
where the time goes in v4:
time: 120 us
  Pallas kernels  53.6 us (45%)
  starting transfers between devices  32 us (27%)
  waiting for transfers between devices  31.9 us (27%)
  local copies, waits for them, and re-layouts  1.46 us (1%)
    ppermute x13, waiting for transfers between devices, shift(): return lax.ppermute(x, axis, [(i, (i + by) % size) for i in range(size)])  24.9 us
    ppermute x13, starting transfers between devices, shift(): return lax.ppermute(x, axis, [(i, (i + by) % size) for i in range(size)])  18.2 us
    ppermute x12, starting transfers between devices, flip(): return lax.ppermute(x, axis, [(i, i ^ bit) for i in range(size)])  13.8 us
    pallas_call x3, Pallas kernels, grads(): call(lambda *refs: grads_kernel(towers, with_pq, *refs), [bf16(n, 1024, 2...  9.89 us
    pallas_call x2, Pallas kernels, later_half(): call(lambda *refs: forward_kernel((t,), False, *refs), [f32(1, 1024, 256)...  7.22 us
    pallas_call x1, Pallas kernels, per_device(): call(lambda *refs: forward_kernel((0, 1), True, *refs), [f32(2, 1024, 256...  7.19 us
    ppermute x12, waiting for transfers between devices, flip(): return lax.ppermute(x, axis, [(i, i ^ bit) for i in range(size)])  7.07 us
    pallas_call x2, Pallas kernels, turn(): pl.pallas_call(lambda *refs: turn_kernel(at, *refs), in_specs=[any_spec],...  6.07 us
  transfers between devices with their start and end apart: 25, of which 13 were waited for; matrix products, arithmetic and copies ran while one was open for 1% of the time, Pallas kernels for 35%

profile of v4, /device:TPU:0, one launch (start us, length us, event | category | flops | bytes accessed | tf_op | source)
XLA Modules:
  0.0 120.1 jit_solution(2357374395761120168)
XLA Ops:
  0.7 4.0 %pool_far.1 = (f32[128,256]{1,0:T(8,128)S(1)}, f32[128,256]{1,0:T(8,128)S(1)}, f32[128,256]{1,0:T(8,128)S(1)}, f32[128,256]{1,0:T(8,128)S(1)}, bf16[2,4,512,256]...) custom-call(s32[4]{0:T(128)S(1)} %pad_add_fusion.idx.refs_0_, s32[2,4,2048]{2,1,0:T(4,128)} %bitcast.42, ...), custom_call_target="tpu_custom_call" | custom-call | flops 1000000 | bytes 1048576 | tf_op jit(solution)/shard_map/pool_far/pallas_call | solution.py:392
  4.7 2.1 %collective-permute-start = (f32[128,256]{1,0:T(8,128)S(1)}, f32[128,256]{1,0:T(8,128)S(1)}, u32[]{:S(2)}, u32[]{:S(2)}) collective-permute-start(f32[128,256]{1,0:T(8,128)S(1)} %get-tuple-element.116), channel_id=1, source_target_pairs={{0,4},{4,8},{8,12},{12,0},{1,5},{5,9},{9,13},{13,1},{2,6},{6,10},{... | collective-permute-start | bytes 393224 | tf_op jit(solution)/shard_map/ppermute | solution.py:373
  6.8 3.6 %collective-permute-start.1 = (f32[128,256]{1,0:T(8,128)S(1)}, f32[128,256]{1,0:T(8,128)S(1)}, u32[]{:S(2)}, u32[]{:S(2)}) collective-permute-start(f32[128,256]{1,0:T(8,128)S(1)} %get-tuple-element.117), channel_id=1, source_target_pairs={{0,8},{4,12},{8,0},{12,4},{1,9},{5,13},{9,1},{13,5},{2,10},{6,14},... | collective-permute-start | bytes 393224 | tf_op jit(solution)/shard_map/ppermute | solution.py:373
  10.4 1.0 collective-permute-start.2
  11.4 0.8 copy-done.1
  12.2 2.8 %pool_near.1 = (f32[128,256]{1,0:T(8,128)S(1)}, f32[128,256]{1,0:T(8,128)S(1)}, f32[128,256]{1,0:T(8,128)S(1)}, f32[128,256]{1,0:T(8,128)S(1)}, bf16[2,4,512,256]{3,2,1,0:T(8,128)(2,1)S(1)}) custom-call(s32[4]{0:T(128)S(1)} %pad_add_fusion.idx.refs_0_, s32[2,4,2048]{2,1,0:T(4,128)S(1)} %bitcast.43, f32[2,64,512]{2,1,0:T(8,128)S(1)} %get-tuple-element.113.decayed), custom_call_target="tpu_custom_call" | custom-call | flops 1000000 | bytes 1048576 | tf_op jit(solution)/shard_map/pool_near/pallas_call | solution.py:408
  15.0 3.0 %turn_0.1 = (bf16[2,1024,512]{2,1,0:T(8,128)(2,1)S(1)}, bf16[2,1024,512]{2,1,0:T(8,128)(2,1)S(1)}) custom-call(f32[1024,16,128]{2,1,0:T(8,128)} %bitcast.47), custom_call_target="tpu_custom_call" | custom-call | flops 1000000 | bytes 1048576 | tf_op jit(solution)/shard_map/turn_0/pallas_call | solution.py:414
  18.1 0.6 pack.2.refs_1_.refs_2_
  18.7 3.1 %collective-permute-start.6 = (f32[4,128,256]{2,1,0:T(8,128)S(1)}, f32[4,128,256]{2,1,0:T(8,128)S(1)}, u32[]{:S(2)}, u32[]{:S(2)}) collective-permute-start(f32[4,128,256]{2,1,0:T(8,128)S(1)} %pack.2.refs_1_.refs_2_), channel_id=1, source_target_pairs={{0,2},{2,0},{1,3},{3,1},{4,6},{6,4},{5,7},{7,5},{8,10},{10,8},{9,1... | collective-permute-start | bytes 1572872 | tf_op jit(solution)/shard_map/ppermute | solution.py:377
  21.8 1.0 collective-permute-start.3
  22.8 0.9 collective-permute-start.4
  23.7 1.8 %collective-permute-start.5 = (f32[128,256]{1,0:T(8,128)S(1)}, f32[128,256]{1,0:T(8,128)S(1)}, u32[]{:S(2)}, u32[]{:S(2)}) collective-permute-start(f32[128,256]{1,0:T(8,128)S(1)} %get-tuple-element.130), channel_id=1, source_target_pairs={{0,12},{4,0},{8,4},{12,8},{1,13},{5,1},{9,5},{13,9},{2,14},{6,2},{... | collective-permute-start | bytes 393224 | tf_op jit(solution)/shard_map/ppermute | solution.py:373
  25.5 3.0 %turn_1.1 = (bf16[2,1024,512]{2,1,0:T(8,128)(2,1)S(1)}, bf16[2,1024,512]{2,1,0:T(8,128)(2,1)S(1)}) custom-call(f32[1024,16,128]{2,1,0:T(8,128)} %bitcast.48), custom_call_target="tpu_custom_call" | custom-call | flops 1000000 | bytes 1048576 | tf_op jit(solution)/shard_map/turn_1/pallas_call | solution.py:414
  28.6 1.6 %collective-permute-done.3.p1 = f32[128,256]{1,0:T(8,128)S(1)} collective-permute-done((f32[128,256]{1,0:T(8,128)S(1)}, f32[128,256]{1,0:T(8,128)S(1)}, u32[]{:S(2)}, u32[]{:S(2)}) %collective-permute-start.3) | collective-permute-done | bytes 131104 | tf_op jit(solution)/shard_map/ppermute | solution.py:373
  30.6 0.6 pack.3.refs_1_
  31.3 1.9 %collective-permute-done.6.refs_2_ = f32[4,128,256]{2,1,0:T(8,128)S(1)} collective-permute-done((f32[4,128,256]{2,1,0:T(8,128)S(1)}, f32[4,128,256]{2,1,0:T(8,128)S(1)}, u32[]{:S(2)}, u32[]{:S(2)}) %collective-permute-start.6) | collective-permute-done | bytes 524320 | tf_op jit(solution)/shard_map/ppermute | solution.py:377
  33.1 3.0 %collective-permute-start.10 = (f32[4,128,256]{2,1,0:T(8,128)S(1)}, f32[4,128,256]{2,1,0:T(8,128)S(1)}, u32[]{:S(2)}, u32[]{:S(2)}) collective-permute-start(f32[4,128,256]{2,1,0:T(8,128)S(1)} %pack.3.refs_1_), channel_id=1, source_target_pairs={{0,2},{2,0},{1,3},{3,1},{4,6},{6,4},{5,7},{7,5},{8,10},{10,8},{9,1... | collective-permute-start | bytes 1572872 | tf_op jit(solution)/shard_map/ppermute | solution.py:377
  36.2 2.8 %prepare.1 = (bf16[2,256,1024]{2,1,0:T(8,128)(2,1)S(1)}, bf16[2,256,1024]{2,1,0:T(8,128)(2,1)S(1)}, f32[512,128]{1,0:T(8,128)S(1)}, f32[512,128]{1,0:T(8,128)S(1)}, f32[1,512]{1,0:T(1,128)S(1)}) custom-call(s32[4]{0:T(128)S(1)} %pad_add_fusion.idx.refs_0_, f32[1024,4,128]{2,1,0:T(4,128)} %bitcast.40, f32[4096,128]{1,0:T(8,128)} %lift_hbm, ...), custom_call_target="tpu_custom_call" | custom-call | flops 1000000 | bytes 1048576 | tf_op jit(solution)/shard_map/prepare/pallas_call | solution.py:445
  39.0 7.2 %forward_a.1 = (f32[2,1024,256]{2,1,0:T(8,128)S(1)}, f32[512,256]{1,0:T(8,128)S(1)}, f32[264,128]{1,0:T(8,128)S(1)}) custom-call(s32[4]{0:T(128)S(1)} %pad_add_fusion.idx.refs_0_, f32[4,128,256]{2,1,0:T(8,128)S(1)} %pack.3.refs_1_, f32[4,128,256]{2,1,0:T(8,128)S(1)} %collective-permute-done.6.refs_2_, f32[4,128,256]{2,1,0:T(8,128)S(1)} %collective-permute-done.7.refs_3_, ...), custom_call_target="tpu_custom_call" | custom-call | flops 1000000 | bytes 1048576 | tf_op jit(solution)/shard_map/forward_a/pallas_call | solution.py:456
  46.2 0.7 collective-permute-start.9
  46.9 2.5 %pick.1 = (bf16[2,256,1024]{2,1,0:T(8,128)(2,1)S(1)}, bf16[2,256,1024]{2,1,0:T(8,128)(2,1)S(1)}) custom-call(s32[4]{0:T(128)S(1)} %pad_add_fusion.idx.refs_0_, f32[1024,16,128]{2,1,0:T(8,128)} %bitcast.49), custom_call_target="tpu_custom_call" | custom-call | flops 1000000 | bytes 1048576 | tf_op jit(solution)/shard_map/pick/pallas_call | solution.py:477
  49.4 0.5 natural.1
  49.9 2.1 %collective-permute-done.9 = f32[264,128]{1,0:T(8,128)S(1)} collective-permute-done((f32[264,128]{1,0:T(8,128)S(1)}, f32[264,128]{1,0:T(8,128)S(1)}, u32[]{:S(2)}, u32[]{:S(2)}) %collective-permute-start.9) | collective-permute-done | bytes 135200 | tf_op jit(solution)/shard_map/ppermute | solution.py:377
  52.0 1.7 %collective-permute-start.11 = (f32[264,128]{1,0:T(8,128)S(1)}, f32[264,128]{1,0:T(8,128)S(1)}, u32[]{:S(2)}, u32[]{:S(2)}) collective-permute-start(f32[264,128]{1,0:T(8,128)S(1)} %add.16), channel_id=1, source_target_pairs={{0,32},{16,48},{32,0},{48,16},{64,96},{80,112},{96,64},{112,80},{1... | collective-permute-start | bytes 405512 | tf_op jit(solution)/shard_map/ppermute | solution.py:377
  53.9 3.6 %forward_b0.1 = (f32[1,1024,256]{2,1,0:T(8,128)S(1)}, f32[256,256]{1,0:T(8,128)S(1)}) custom-call(s32[4]{0:T(128)S(1)} %pad_add_fusion.idx.refs_0_, f32[4,128,256]{2,1,0:T(8,128)S(1)} %pack.2.refs_1_.refs_2_, f32[4,128,256]{2,1,0:T(8,128)S(1)} %collective-permute-done.10.refs_2_, f32[4,128,256]{2,1,0:T(8,128)S(1)} %collective-permute-done.12.refs_3_, ...), custom_call_target="tpu_custom_call" | custom-call | flops 4000000000 | bytes 1048576 | tf_op jit(solution)/shard_map/forward_b0/pallas_call | solution.py:466
  57.5 0.6 collective-permute-done.11
  58.1 3.3 %collective-permute-start.14 = (f32[264,128]{1,0:T(8,128)S(1)}, f32[264,128]{1,0:T(8,128)S(1)}, u32[]{:S(2)}, u32[]{:S(2)}) collective-permute-start(f32[264,128]{1,0:T(8,128)S(1)} %add.17.mine), channel_id=1, source_target_pairs={{0,64},{16,80},{32,96},{48,112},{64,0},{80,16},{96,32},{112,48},{1... | collective-permute-start | bytes 405512 | tf_op jit(solution)/shard_map/ppermute | solution.py:377
  61.4 3.6 %forward_b1.1 = (f32[1,1024,256]{2,1,0:T(8,128)S(1)}, f32[256,256]{1,0:T(8,128)S(1)}) custom-call(s32[4]{0:T(128)S(1)} %pad_add_fusion.idx.refs_0_, f32[4,128,256]{2,1,0:T(8,128)S(1)} %pack.2.refs_1_.refs_2_, f32[4,128,256]{2,1,0:T(8,128)S(1)} %collective-permute-done.10.refs_2_, f32[4,128,256]{2,1,0:T(8,128)S(1)} %collective-permute-done.12.refs_3_, ...), custom_call_target="tpu_custom_call" | custom-call | flops 4000000000 | bytes 1048576 | tf_op jit(solution)/shard_map/forward_b1/pallas_call | solution.py:466
  65.1 1.2 logit.1
  66.2 1.9 %collective-permute-start.16 = (f32[264,128]{1,0:T(8,128)S(1)}, f32[264,128]{1,0:T(8,128)S(1)}, u32[]{:S(2)}, u32[]{:S(2)}) collective-permute-start(f32[264,128]{1,0:T(8,128)S(1)} %get-tuple-element.161.refs_1_), channel_id=1, source_target_pairs={{0,2},{2,0},{1,3},{3,1},{4,6},{6,4},{5,7},{7,5},{8,10},{10,8},{9,1... | collective-permute-start | bytes 405512 | tf_op jit(solution)/shard_map/ppermute | solution.py:377
  68.2 4.6 %grads_a.1 = (bf16[2,1024,256]{2,1,0:T(8,128)(2,1)S(1)}, bf16[2,1024,256]{2,1,0:T(8,128)(2,1)S(1)}, f32[2,256,256]{2,1,0:T(8,128)S(1)}, f32[2,64,256]{2,1,0:T(8,...) custom-call(s32[4]{0:T(128)S(1)} %pad_add_fusion.idx.refs_0_, ...), custom_call_target="tpu_custom_call" | custom-call | flops 4000000000 | bytes 1048576 | tf_op jit(solution)/shard_map/grads_a/pallas_call | solution.py:506
  72.8 0.9 collective-permute-done.16.refs_1_
  73.7 1.4 %collective-permute-done.17.refs_2_ = f32[264,128]{1,0:T(8,128)S(1)} collective-permute-done((f32[264,128]{1,0:T(8,128)S(1)}, f32[264,128]{1,0:T(8,128)S(1)}, u32[]{:S(2)}, u32[]{:S(2)}) %collective-permute-start.17) | collective-permute-done | bytes 135200 | tf_op jit(solution)/shard_map/ppermute | solution.py:377
  75.1 2.6 %grads_b0.1 = (bf16[1,1024,256]{2,1,0:T(8,128)(2,1)S(1)}, bf16[1,1024,256]{2,1,0:T(8,128)(2,1)S(1)}, f32[1,256,256]{2,1,0:T(8,128)S(1)}, f32[1,64,256]{2,1,0:T(8...) custom-call(s32[4]{0:T(128)S(1)} %pad_add_fusion.idx.refs_0_, ...), custom_call_target="tpu_custom_call" | custom-call | flops 4000000000 | bytes 1048576 | tf_op jit(solution)/shard_map/grads_b0/pallas_call | solution.py:506
  77.7 1.8 %weights_0.1 = (f32[80,1024]{1,0:T(8,128)S(1)}, f32[80,1024]{1,0:T(8,128)S(1)}, f32[112,1024]{1,0:T(8,128)S(1)}, f32[112,1024]{1,0:T(8,128)S(1)}) custom-call(s32[4]{0:T(128)S(1)} %pad_add_fusion.idx.refs_0_, f32[4,128,256]{2,1,0:T(8,128)S(1)} %pack.3.refs_1_, f32[4,128,256]{2,1,0:T(8,128)S(1)} %pack.2.refs_1_.refs_2_, ...), custom_call_target="tpu_custom_call" | custom-call | flops 3000000000 | bytes 1048576 | tf_op jit(solution)/shard_map/weights_0/pallas_call | solution.py:520
  79.6 1.1 collective-permute-start.18
  80.6 2.2 %collective-permute-start.19 = (f32[112,1024]{1,0:T(8,128)S(1)}, f32[112,1024]{1,0:T(8,128)S(1)}, u32[]{:S(2)}, u32[]{:S(2)}) collective-permute-start(f32[112,1024]{1,0:T(8,128)S(1)} %get-tuple-element.185), channel_id=1, source_target_pairs={{0,12},{4,0},{8,4},{12,8},{1,13},{5,1},{9,5},{13,9},{2,14},{6,2},{... | collective-permute-start | bytes 1376264 | tf_op jit(solution)/shard_map/ppermute | solution.py:373
  82.9 2.6 %grads_b1.1 = (bf16[1,1024,256]{2,1,0:T(8,128)(2,1)S(1)}, bf16[1,1024,256]{2,1,0:T(8,128)(2,1)S(1)}, f32[1,256,256]{2,1,0:T(8,128)S(1)}, f32[1,64,256]{2,1,0:T(8...) custom-call(s32[4]{0:T(128)S(1)} %pad_add_fusion.idx.refs_0_, ...), custom_call_target="tpu_custom_call" | custom-call | flops 4000000000 | bytes 1048576 | tf_op jit(solution)/shard_map/grads_b1/pallas_call | solution.py:506
  85.5 2.1 %weights_1.1 = (f32[88,1024]{1,0:T(8,128)S(1)}, f32[120,1024]{1,0:T(8,128)S(1)}, f32[120,1024]{1,0:T(8,128)S(1)}, f32[88,1024]{1,0:T(8,128)S(1)}, f32[64,1024]{1,0:T(8,128)S(1)}) custom-call(s32[4]{0:T(128)S(1)} %pad_add_fusion.idx.refs_0_, f32[4,128,256]{2,1,0:T(8,128)S(1)} %pack.3.refs_1_, f32[4,128,256]{2,1,0:T(8,128)S(1)} %pack.2.refs_1_.refs_2_, ...), custom_call_target="tpu_custom_call" | custom-call | flops 3000000000 | bytes 1048576 | tf_op jit(solution)/shard_map/weights_1/pallas_call | solution.py:520
  87.7 2.0 %collective-permute-start.21 = (f32[120,1024]{1,0:T(8,128)S(1)}, f32[120,1024]{1,0:T(8,128)S(1)}, u32[]{:S(2)}, u32[]{:S(2)}) collective-permute-start(f32[120,1024]{1,0:T(8,128)S(1)} %get-tuple-element.202), channel_id=1, source_target_pairs={{0,4},{4,8},{8,12},{12,0},{1,5},{5,9},{9,13},{13,1},{2,6},{6,10},{... | collective-permute-start | bytes 1474568 | tf_op jit(solution)/shard_map/ppermute | solution.py:373
  89.7 4.5 %collective-permute-done.18.w_up = f32[112,1024]{1,0:T(8,128)S(1)} collective-permute-done((f32[112,1024]{1,0:T(8,128)S(1)}, f32[112,1024]{1,0:T(8,128)S(1)}, u32[]{:S(2)}, u32[]{:S(2)}) %collective-permute-start.18) | collective-permute-done | bytes 458784 | tf_op jit(solution)/shard_map/ppermute | solution.py:373
  94.3 14.5 %collective-permute-done.20.v_down = f32[120,1024]{1,0:T(8,128)S(1)} collective-permute-done((f32[120,1024]{1,0:T(8,128)S(1)}, f32[120,1024]{1,0:T(8,128)S(1)}, u32[]{:S(2)}, u32[]{:S(2)}) %collective-permute-start.20) | collective-permute-done | bytes 491552 | tf_op jit(solution)/shard_map/ppermute | solution.py:373
  108.9 1.5 %collective-permute-done.21.v_up.refs_4_ = f32[120,1024]{1,0:T(8,128)S(1)} collective-permute-done((f32[120,1024]{1,0:T(8,128)S(1)}, f32[120,1024]{1,0:T(8,128)S(1)}, u32[]{:S(2)}, u32[]{:S(2)}) %collective-permute-start.21) | collective-permute-done | bytes 491552 | tf_op jit(solution)/shard_map/ppermute | solution.py:373
  110.4 2.4 %collective-permute-start.24 = (f32[88,1024]{1,0:T(8,128)S(1)}, f32[88,1024]{1,0:T(8,128)S(1)}, u32[]{:S(2)}, u32[]{:S(2)}) collective-permute-start(f32[88,1024]{1,0:T(8,128)S(1)} %slice_add_fusion), channel_id=1, source_target_pairs={{0,12},{4,0},{8,4},{12,8},{1,13},{5,1},{9,5},{13,9},{2,14},{6,2},{... | collective-permute-start | bytes 1081352 | tf_op jit(solution)/shard_map/ppermute | solution.py:373
  112.8 2.8 %update.1 = (f32[2,64,512]{2,1,0:T(8,128)}, f32[2,512]{1,0:T(2,128)S(1)}) custom-call(s32[4]{0:T(128)S(1)} %pad_add_fusion.idx.refs_0_, f32[2,64,256]{2,1,0:T(8,128)S(1)} %get-tuple-element.167.ga, f32[1,64,256]{2,1,0:T(8,128)S(1)} %get-tuple-element.171.gb0, f32[1,64,256]{2,1,0:T(8,128)S(1)} %get-tuple-element.173.gb1, ...), custom_call_target="tpu_custom_call" | custom-call | flops 5000000000 | bytes 1048576 | tf_op jit(solution)/shard_map/update/pallas_call | solution.py:550
  115.6 0.6 copy.23
  116.6 1.9 %collective-permute-done.24.refs_5_ = f32[88,1024]{1,0:T(8,128)S(1)} collective-permute-done((f32[88,1024]{1,0:T(8,128)S(1)}, f32[88,1024]{1,0:T(8,128)S(1)}, u32[]{:S(2)}, u32[]{:S(2)}) %collective-permute-start.24) | collective-permute-done | bytes 360480 | tf_op jit(solution)/shard_map/ppermute | solution.py:373
  118.5 1.6 %sum.1 = (f32[1024,128]{1,0:T(8,128)}, f32[256,128]{1,0:T(8,128)}, f32[32,128]{1,0:T(8,128)}, f32[32,128]{1,0:T(8,128)}) custom-call(s32[4]{0:T(128)S(1)} %pad_add_fusion.idx.refs_0_, f32[1,512]{1,0:T(1,128)S(1)} %get-tuple-element.144.refs_13_.refs_10_.head, f32[80,1024]{1,0:T(8,128)S(1)} %get-tuple-element.210.refs_0_, ...), custom_call_target="tpu_custom_call" | custom-call | flops 1000000 | bytes 1048576 | tf_op jit(solution)/shard_map/sum/pallas_call | solution.py:553
  (39 shorter events, 1.5 us)
Async XLA Ops:
  4.7 13.4 %collective-permute-start = (f32[128,256]{1,0:T(8,128)S(1)}, f32[128,256]{1,0:T(8,128)S(1)}, u32[]{:S(2)}, u32[]{:S(2)}) collective-permute-start(f32[128,256]{1,0:T(8,128)S(1)} %get-tuple-element.116), channel_id=1, source_target_pairs={{0,4},{4,8},{8,12},{12,0},{1,5},{5,9},{9,13},{13,1},{2,6},{6,10},{... | collective-permute-start | bytes 393224 | tf_op jit(solution)/shard_map/ppermute | solution.py:373
  6.8 11.3 %collective-permute-start.1 = (f32[128,256]{1,0:T(8,128)S(1)}, f32[128,256]{1,0:T(8,128)S(1)}, u32[]{:S(2)}, u32[]{:S(2)}) collective-permute-start(f32[128,256]{1,0:T(8,128)S(1)} %get-tuple-element.117), channel_id=1, source_target_pairs={{0,8},{4,12},{8,0},{12,4},{1,9},{5,13},{9,1},{13,5},{2,10},{6,14},... | collective-permute-start | bytes 393224 | tf_op jit(solution)/shard_map/ppermute | solution.py:373
  10.4 7.7 %collective-permute-start.2 = (f32[128,256]{1,0:T(8,128)S(1)}, f32[128,256]{1,0:T(8,128)S(1)}, u32[]{:S(2)}, u32[]{:S(2)}) collective-permute-start(f32[128,256]{1,0:T(8,128)S(1)} %get-tuple-element.118), channel_id=1, source_target_pairs={{0,12},{4,0},{8,4},{12,8},{1,13},{5,1},{9,5},{13,9},{2,14},{6,2},{... | collective-permute-start | bytes 393224 | tf_op jit(solution)/shard_map/ppermute | solution.py:373
  11.4 0.8 copy-start.1
  18.7 14.4 %collective-permute-start.6 = (f32[4,128,256]{2,1,0:T(8,128)S(1)}, f32[4,128,256]{2,1,0:T(8,128)S(1)}, u32[]{:S(2)}, u32[]{:S(2)}) collective-permute-start(f32[4,128,256]{2,1,0:T(8,128)S(1)} %pack.2.refs_1_.refs_2_), channel_id=1, source_target_pairs={{0,2},{2,0},{1,3},{3,1},{4,6},{6,4},{5,7},{7,5},{8,10},{10,8},{9,1... | collective-permute-start | bytes 1572872 | tf_op jit(solution)/shard_map/ppermute | solution.py:377
  21.8 8.4 %collective-permute-start.3 = (f32[128,256]{1,0:T(8,128)S(1)}, f32[128,256]{1,0:T(8,128)S(1)}, u32[]{:S(2)}, u32[]{:S(2)}) collective-permute-start(f32[128,256]{1,0:T(8,128)S(1)} %get-tuple-element.128), channel_id=1, source_target_pairs={{0,4},{4,8},{8,12},{12,0},{1,5},{5,9},{9,13},{13,1},{2,6},{6,10},{... | collective-permute-start | bytes 393224 | tf_op jit(solution)/shard_map/ppermute | solution.py:373
  22.8 7.4 %collective-permute-start.4 = (f32[128,256]{1,0:T(8,128)S(1)}, f32[128,256]{1,0:T(8,128)S(1)}, u32[]{:S(2)}, u32[]{:S(2)}) collective-permute-start(f32[128,256]{1,0:T(8,128)S(1)} %get-tuple-element.129), channel_id=1, source_target_pairs={{0,8},{4,12},{8,0},{12,4},{1,9},{5,13},{9,1},{13,5},{2,10},{6,14},... | collective-permute-start | bytes 393224 | tf_op jit(solution)/shard_map/ppermute | solution.py:373
  23.7 12.4 %copy-start.2 = (f32[4096]{0:T(1024)S(1)}, f32[4096]{0:T(1024)}, u32[]{:S(2)}) copy-start(f32[4096]{0:T(1024)} %param.20) | copy-start | bytes 49156
  23.7 6.9 %collective-permute-start.5 = (f32[128,256]{1,0:T(8,128)S(1)}, f32[128,256]{1,0:T(8,128)S(1)}, u32[]{:S(2)}, u32[]{:S(2)}) collective-permute-start(f32[128,256]{1,0:T(8,128)S(1)} %get-tuple-element.130), channel_id=1, source_target_pairs={{0,12},{4,0},{8,4},{12,8},{1,13},{5,1},{9,5},{13,9},{2,14},{6,2},{... | collective-permute-start | bytes 393224 | tf_op jit(solution)/shard_map/ppermute | solution.py:373
  31.2 7.8 %collective-permute-start.7 = (f32[4,128,256]{2,1,0:T(8,128)S(1)}, f32[4,128,256]{2,1,0:T(8,128)S(1)}, u32[]{:S(2)}, u32[]{:S(2)}) collective-permute-start(f32[4,128,256]{2,1,0:T(8,128)S(1)} %pack.3.refs_1_), channel_id=1, source_target_pairs={{0,1},{1,0},{2,3},{3,2},{4,5},{5,4},{6,7},{7,6},{8,9},{9,8},{10,11... | collective-permute-start | bytes 1572872 | tf_op jit(solution)/shard_map/ppermute | solution.py:377
  33.1 5.9 %collective-permute-start.8 = (f32[4,128,256]{2,1,0:T(8,128)S(1)}, f32[4,128,256]{2,1,0:T(8,128)S(1)}, u32[]{:S(2)}, u32[]{:S(2)}) collective-permute-start(f32[4,128,256]{2,1,0:T(8,128)S(1)} %collective-permute-done.6.refs_2_), channel_id=1, source_target_pairs={{0,1},{1,0},{2,3},{3,2},{4,5},{5,4},{6,7},{7,6},{8,9},{9,8},{10,11... | collective-permute-start | bytes 1572872 | tf_op jit(solution)/shard_map/ppermute | solution.py:377
  33.1 16.8 %collective-permute-start.10 = (f32[4,128,256]{2,1,0:T(8,128)S(1)}, f32[4,128,256]{2,1,0:T(8,128)S(1)}, u32[]{:S(2)}, u32[]{:S(2)}) collective-permute-start(f32[4,128,256]{2,1,0:T(8,128)S(1)} %pack.3.refs_1_), channel_id=1, source_target_pairs={{0,2},{2,0},{1,3},{3,1},{4,6},{6,4},{5,7},{7,5},{8,10},{10,8},{9,1... | collective-permute-start | bytes 1572872 | tf_op jit(solution)/shard_map/ppermute | solution.py:377
  46.2 3.2 %copy-start = (f32[1024,2,256]{2,1,0:T(2,128)S(1)}, f32[1024,2,256]{2,1,0:T(2,128)}, u32[]{:S(2)}) copy-start(f32[1024,2,256]{2,1,0:T(2,128)} %param.17) | copy-start | bytes 6291460
  46.2 5.8 %collective-permute-start.9 = (f32[264,128]{1,0:T(8,128)S(1)}, f32[264,128]{1,0:T(8,128)S(1)}, u32[]{:S(2)}, u32[]{:S(2)}) collective-permute-start(f32[264,128]{1,0:T(8,128)S(1)} %get-tuple-element.146), channel_id=1, source_target_pairs={{0,16},{16,0},{32,48},{48,32},{64,80},{80,64},{96,112},{112,96},{1... | collective-permute-start | bytes 405512 | tf_op jit(solution)/shard_map/ppermute | solution.py:377
  46.9 6.8 %collective-permute-start.12 = (f32[4,128,256]{2,1,0:T(8,128)S(1)}, f32[4,128,256]{2,1,0:T(8,128)S(1)}, u32[]{:S(2)}, u32[]{:S(2)}) collective-permute-start(f32[4,128,256]{2,1,0:T(8,128)S(1)} %pack.2.refs_1_.refs_2_), channel_id=1, source_target_pairs={{0,1},{1,0},{2,3},{3,2},{4,5},{5,4},{6,7},{7,6},{8,9},{9,8},{10,11... | collective-permute-start | bytes 1572872 | tf_op jit(solution)/shard_map/ppermute | solution.py:377
  52.0 1.9 %collective-permute-start.13 = (f32[4,128,256]{2,1,0:T(8,128)S(1)}, f32[4,128,256]{2,1,0:T(8,128)S(1)}, u32[]{:S(2)}, u32[]{:S(2)}) collective-permute-start(f32[4,128,256]{2,1,0:T(8,128)S(1)} %collective-permute-done.10.refs_2_), channel_id=1, source_target_pairs={{0,1},{1,0},{2,3},{3,2},{4,5},{5,4},{6,7},{7,6},{8,9},{9,8},{10,11... | collective-permute-start | bytes 1572872 | tf_op jit(solution)/shard_map/ppermute | solution.py:377
  52.0 6.1 %collective-permute-start.11 = (f32[264,128]{1,0:T(8,128)S(1)}, f32[264,128]{1,0:T(8,128)S(1)}, u32[]{:S(2)}, u32[]{:S(2)}) collective-permute-start(f32[264,128]{1,0:T(8,128)S(1)} %add.16), channel_id=1, source_target_pairs={{0,32},{16,48},{32,0},{48,16},{64,96},{80,112},{96,64},{112,80},{1... | collective-permute-start | bytes 405512 | tf_op jit(solution)/shard_map/ppermute | solution.py:377
  58.1 6.9 %copy-start.3 = (s32[1,128]{1,0:T(1,128)S(1)}, s32[1,128]{1,0:T(1,128)}, u32[]{:S(2)}) copy-start(s32[1,128]{1,0:T(1,128)} %labels.1) | copy-start | bytes 1540
  58.1 6.9 %collective-permute-start.14 = (f32[264,128]{1,0:T(8,128)S(1)}, f32[264,128]{1,0:T(8,128)S(1)}, u32[]{:S(2)}, u32[]{:S(2)}) collective-permute-start(f32[264,128]{1,0:T(8,128)S(1)} %add.17.mine), channel_id=1, source_target_pairs={{0,64},{16,80},{32,96},{48,112},{64,0},{80,16},{96,32},{112,48},{1... | collective-permute-start | bytes 405512 | tf_op jit(solution)/shard_map/ppermute | solution.py:377
  66.2 2.0 %collective-permute-start.15 = (f32[264,128]{1,0:T(8,128)S(1)}, f32[264,128]{1,0:T(8,128)S(1)}, u32[]{:S(2)}, u32[]{:S(2)}) collective-permute-start(f32[264,128]{1,0:T(8,128)S(1)} %get-tuple-element.161.refs_1_), channel_id=1, source_target_pairs={{0,1},{1,0},{2,3},{3,2},{4,5},{5,4},{6,7},{7,6},{8,9},{9,8},{10,11... | collective-permute-start | bytes 405512 | tf_op jit(solution)/shard_map/ppermute | solution.py:377
  66.2 7.5 %collective-permute-start.16 = (f32[264,128]{1,0:T(8,128)S(1)}, f32[264,128]{1,0:T(8,128)S(1)}, u32[]{:S(2)}, u32[]{:S(2)}) collective-permute-start(f32[264,128]{1,0:T(8,128)S(1)} %get-tuple-element.161.refs_1_), channel_id=1, source_target_pairs={{0,2},{2,0},{1,3},{3,1},{4,6},{6,4},{5,7},{7,5},{8,10},{10,8},{9,1... | collective-permute-start | bytes 405512 | tf_op jit(solution)/shard_map/ppermute | solution.py:377
  73.7 1.4 %collective-permute-start.17 = (f32[264,128]{1,0:T(8,128)S(1)}, f32[264,128]{1,0:T(8,128)S(1)}, u32[]{:S(2)}, u32[]{:S(2)}) collective-permute-start(f32[264,128]{1,0:T(8,128)S(1)} %collective-permute-done.16.refs_1_), channel_id=1, source_target_pairs={{0,1},{1,0},{2,3},{3,2},{4,5},{5,4},{6,7},{7,6},{8,9},{9,8},{10,11... | collective-permute-start | bytes 405512 | tf_op jit(solution)/shard_map/ppermute | solution.py:377
  79.6 14.6 %collective-permute-start.18 = (f32[112,1024]{1,0:T(8,128)S(1)}, f32[112,1024]{1,0:T(8,128)S(1)}, u32[]{:S(2)}, u32[]{:S(2)}) collective-permute-start(f32[112,1024]{1,0:T(8,128)S(1)} %get-tuple-element.184), channel_id=1, source_target_pairs={{0,4},{4,8},{8,12},{12,0},{1,5},{5,9},{9,13},{13,1},{2,6},{6,10},{... | collective-permute-start | bytes 1376264 | tf_op jit(solution)/shard_map/ppermute | solution.py:373
  80.6 13.6 %collective-permute-start.19 = (f32[112,1024]{1,0:T(8,128)S(1)}, f32[112,1024]{1,0:T(8,128)S(1)}, u32[]{:S(2)}, u32[]{:S(2)}) collective-permute-start(f32[112,1024]{1,0:T(8,128)S(1)} %get-tuple-element.185), channel_id=1, source_target_pairs={{0,12},{4,0},{8,4},{12,8},{1,13},{5,1},{9,5},{13,9},{2,14},{6,2},{... | collective-permute-start | bytes 1376264 | tf_op jit(solution)/shard_map/ppermute | solution.py:373
  85.5 4.2 %copy-start.4 = (f32[2,1,512]{2,1,0:T(1,128)S(1)}, f32[2,1,512]{2,1,0:T(1,128)}, u32[]{:S(2)}) copy-start(f32[2,1,512]{2,1,0:T(1,128)} %param.15) | copy-start | bytes 12292
  87.6 21.3 %collective-permute-start.20 = (f32[120,1024]{1,0:T(8,128)S(1)}, f32[120,1024]{1,0:T(8,128)S(1)}, u32[]{:S(2)}, u32[]{:S(2)}) collective-permute-start(f32[120,1024]{1,0:T(8,128)S(1)} %get-tuple-element.201), channel_id=1, source_target_pairs={{0,12},{4,0},{8,4},{12,8},{1,13},{5,1},{9,5},{13,9},{2,14},{6,2},{... | collective-permute-start | bytes 1474568 | tf_op jit(solution)/shard_map/ppermute | solution.py:373
  87.7 22.7 %collective-permute-start.21 = (f32[120,1024]{1,0:T(8,128)S(1)}, f32[120,1024]{1,0:T(8,128)S(1)}, u32[]{:S(2)}, u32[]{:S(2)}) collective-permute-start(f32[120,1024]{1,0:T(8,128)S(1)} %get-tuple-element.202), channel_id=1, source_target_pairs={{0,4},{4,8},{8,12},{12,0},{1,5},{5,9},{9,13},{13,1},{2,6},{6,10},{... | collective-permute-start | bytes 1474568 | tf_op jit(solution)/shard_map/ppermute | solution.py:373
  89.7 23.1 %collective-permute-start.22 = (f32[64,1024]{1,0:T(8,128)S(1)}, f32[64,1024]{1,0:T(8,128)S(1)}, u32[]{:S(2)}, u32[]{:S(2)}) collective-permute-start(f32[64,1024]{1,0:T(8,128)S(1)} %get-tuple-element.205), channel_id=1, source_target_pairs={{0,8},{4,12},{8,0},{12,4},{1,9},{5,13},{9,1},{13,5},{2,10},{6,14},... | collective-permute-start | bytes 786440 | tf_op jit(solution)/shard_map/ppermute | solution.py:373
  94.2 22.3 %collective-permute-start.23 = (f32[80,1024]{1,0:T(8,128)S(1)}, f32[80,1024]{1,0:T(8,128)S(1)}, u32[]{:S(2)}, u32[]{:S(2)}) collective-permute-start(f32[80,1024]{1,0:T(8,128)S(1)} %slice_add_fusion.1), channel_id=1, source_target_pairs={{0,4},{4,8},{8,12},{12,0},{1,5},{5,9},{9,13},{13,1},{2,6},{6,10},{... | collective-permute-start | bytes 983048 | tf_op jit(solution)/shard_map/ppermute | solution.py:373
  110.4 8.1 %collective-permute-start.24 = (f32[88,1024]{1,0:T(8,128)S(1)}, f32[88,1024]{1,0:T(8,128)S(1)}, u32[]{:S(2)}, u32[]{:S(2)}) collective-permute-start(f32[88,1024]{1,0:T(8,128)S(1)} %slice_add_fusion), channel_id=1, source_target_pairs={{0,12},{4,0},{8,4},{12,8},{1,13},{5,1},{9,5},{13,9},{2,14},{6,2},{... | collective-permute-start | bytes 1081352 | tf_op jit(solution)/shard_map/ppermute | solution.py:373

commit v5 on v4

--- a/solution.py
+++ b/solution.py
@@ -146,16 +146,14 @@
                 low[t, k * rows : (k + 1) * rows, b * 128 : (b + 1) * 128] = l
 
 
-def prepare_kernel(idx, second_hbm, lift_hbm, press_hbm, heads, high_t, low_t, lift, press, head, second, sems):
+def prepare_kernel(idx, second, lift_hbm, press_hbm, heads, high_t, low_t, lift, press, head, sems):
     tower = idx[3]
     rows = pl.ds(pl.multiple_of(tower * lift.shape[0], lift.shape[0]), lift.shape[0])
-    pairs = ((second_hbm, second), (lift_hbm.at[rows, :], lift), (press_hbm.at[rows, :], press))
+    pairs = ((lift_hbm.at[rows, :], lift), (press_hbm.at[rows, :], press))
     copies = [pltpu.make_async_copy(a, b, sems.at[n]) for n, (a, b) in enumerate(pairs)]
     for copy in copies:
         copy.start()
     head[...] = jnp.concatenate([heads[pl.ds(tower * 4 + b, 1), :] for b in range(4)], axis=1)
-    for copy in copies:
-        copy.wait()
     count = second.shape[0]
     flat = second.reshape(count * 4, 128)
     for t in range(2):
@@ -164,6 +162,8 @@
             h, l = halves(flat[pl.ds(b * 2 + t, count, stride=4), :].T)
             high_t[t, lanes, :] = h
             low_t[t, lanes, :] = l
+    for copy in copies:
+        copy.wait()
 
 
 def natural_kernel(w, high, low):
@@ -389,12 +389,11 @@
     tables_t = jnp.transpose(tables[:, 0], (0, 2, 1))
     bag = bag_ids[:, 0]
     hbm = lambda x: pltpu.with_memory_space_constraint(x, pltpu.HBM)
-    *far, counts_far, decayed = call(
+    *far, counts_far, decayed, bag_here = call(
         pool_far_kernel,
-        [f32(128, 256)] * 4 + [bf16(2, 4, 512, 256), f32(2, 64, 512)],
+        [f32(128, 256)] * 4 + [bf16(2, 4, 512, 256), f32(2, 64, 512), jax.ShapeDtypeStruct((2, 4, 2048), jnp.int32)],
         [SMEM_SPEC] + [any_spec] * 4,
         [
-            pltpu.VMEM((2, 4, 2048), jnp.int32),
             pltpu.VMEM((2, 128), jnp.int32),
             pltpu.VMEM((2, 128), jnp.int32),
             pltpu.VMEM((2, 64, 512), F32),
@@ -407,7 +406,7 @@
     far = [far[0]] + [shift(far[k], "z", 4, k) for k in (1, 2, 3)]
     *near, counts_near = call(
         pool_near_kernel, [f32(128, 256)] * 4 + [bf16(2, 4, 512, 256)], [SMEM_SPEC] + vmem(2), name="pool_near", flops=1e6
-    )(idx, bag, decayed)
+    )(idx, bag_here, decayed)
     view = first_weight.reshape(1024, 2, 8, 128).transpose(0, 2, 1, 3).reshape(1024, 16, 128)
 
     def turn(view, at):
@@ -438,18 +437,16 @@
     y1b = flip(fq_far, "core", 2, 1)
     y2b = flip(x2b, "core", 2, 1)
 
-    _, second_weight, lift_weight, press_weight, head_weight = lax.optimization_barrier(
-        (w1hb, second_weight, lift_weight, press_weight, head_weight)
-    )
+    _, lift_weight, press_weight = lax.optimization_barrier((w1hb, lift_weight, press_weight))
     second_view = second_weight.reshape(1024, 2, 2, 128).transpose(0, 2, 1, 3).reshape(1024, 4, 128)
     w2th, w2tl, lift, press, head = call(
         prepare_kernel,
         [bf16(2, 256, 1024)] * 2 + [f32(local, rank), f32(local, rank), f32(1, local)],
-        [SMEM_SPEC] + [any_spec] * 3 + vmem(1),
-        [pltpu.VMEM((1024, 4, 128), F32), pltpu.SemaphoreType.DMA((3,))],
+        [SMEM_SPEC] + vmem(1) + [any_spec] * 2 + vmem(1),
+        [pltpu.SemaphoreType.DMA((2,))],
         name="prepare",
         flops=1e6,
-    )(idx, hbm(second_view), hbm(lift_weight), hbm(press_weight), head_weight.reshape(32, 128))
+    )(idx, second_view, hbm(lift_weight), hbm(press_weight), head_weight.reshape(32, 128))
 
     scratch = [pltpu.VMEM((1024, 256), BF16)] * 2
     weights = (w1ha, w1la, w1hb, w1lb, w2th, w2tl, press, lift, head)
@@ -492,7 +489,7 @@
     other, x0b0 = lax.optimization_barrier((other, x0b0))
     pay = pay + other
     after, pay = lax.optimization_barrier((idx, pay))
-    other = flip(pay, TOWER, 8, 4)
+    other = flip(pay, TOWER, 8, 6)
     hid_b1, x0b1 = later_half(after, 1, y2b)
     other, x0b1 = lax.optimization_barrier((other, x0b1))
     pay, logits = call(logit_kernel, [f32(2 * rank + 8, 128), f32(1, 16)], [SMEM_SPEC] + vmem(3), name="logit", flops=1e6)(

time: 120 us -> 119 us (level)
    ppermute x13, waiting for transfers between devices: 24.9 us -> 23.6 us  [shift(): return lax.ppermute(x, axis, [(i, (i + by) % size) for i in range(size)])]
    pallas_call x1, Pallas kernels: 2.84 us -> 1.59 us  [per_device(): call(prepare_kernel, [bf16(2, 256, 1024)] * 2 + [f32(local, rank), f32(lo...]
  transfers between devices with their start and end apart: 25 -> 25, of which waited for: 13 -> 13; matrix products, arithmetic and copies ran while one was open for 1% -> 1% of each run, Pallas kernels for 35% -> 34%
where the time goes in v5:
time: 119 us
  Pallas kernels  52.5 us (44%)
  starting transfers between devices  32.6 us (27%)
  waiting for transfers between devices  31.8 us (27%)
    ppermute x13, waiting for transfers between devices, shift(): return lax.ppermute(x, axis, [(i, (i + by) % size) for i in range(size)])  23.6 us
    ppermute x13, starting transfers between devices, shift(): return lax.ppermute(x, axis, [(i, (i + by) % size) for i in range(size)])  19 us
    ppermute x12, starting transfers between devices, flip(): return lax.ppermute(x, axis, [(i, i ^ bit) for i in range(size)])  13.6 us
    pallas_call x3, Pallas kernels, grads(): call(lambda *refs: grads_kernel(towers, with_pq, *refs), [bf16(n, 1024, 2...  9.89 us
    ppermute x12, waiting for transfers between devices, flip(): return lax.ppermute(x, axis, [(i, i ^ bit) for i in range(size)])  8.26 us
    pallas_call x2, Pallas kernels, later_half(): call(lambda *refs: forward_kernel((t,), False, *refs), [f32(1, 1024, 256)...  7.23 us
    pallas_call x1, Pallas kernels, per_device(): call(lambda *refs: forward_kernel((0, 1), True, *refs), [f32(2, 1024, 256...  7.18 us
    pallas_call x2, Pallas kernels, turn(): pl.pallas_call(lambda *refs: turn_kernel(at, *refs), in_specs=[any_spec],...  6.22 us
  transfers between devices with their start and end apart: 25, of which 13 were waited for; matrix products, arithmetic and copies ran while one was open for 1% of the time, Pallas kernels for 34%

profile of v5, /device:TPU:0, one launch (start us, length us, event | category | flops | bytes accessed | tf_op | source)
XLA Modules:
  0.0 118.7 jit_solution(18402917062704691254)
XLA Ops:
  0.7 4.0 %pool_far.1 = (f32[128,256]{1,0:T(8,128)S(1)}, f32[128,256]{1,0:T(8,128)S(1)}, f32[128,256]{1,0:T(8,128)S(1)}, f32[128,256]{1,0:T(8,128)S(1)}, bf16[2,4,512,256]...) custom-call(s32[4]{0:T(128)S(1)} %pad_add_fusion.idx.refs_0_, s32[2,4,2048]{2,1,0:T(4,128)} %bitcast.49, ...), custom_call_target="tpu_custom_call" | custom-call | flops 1000000 | bytes 1048576 | tf_op jit(solution)/shard_map/pool_far/pallas_call | solution.py:392
  4.7 2.1 %collective-permute-start = (f32[128,256]{1,0:T(8,128)S(1)}, f32[128,256]{1,0:T(8,128)S(1)}, u32[]{:S(2)}, u32[]{:S(2)}) collective-permute-start(f32[128,256]{1,0:T(8,128)S(1)} %get-tuple-element.115), channel_id=1, source_target_pairs={{0,4},{4,8},{8,12},{12,0},{1,5},{5,9},{9,13},{13,1},{2,6},{6,10},{... | collective-permute-start | bytes 393224 | tf_op jit(solution)/shard_map/ppermute | solution.py:373
  6.8 3.6 %collective-permute-start.1 = (f32[128,256]{1,0:T(8,128)S(1)}, f32[128,256]{1,0:T(8,128)S(1)}, u32[]{:S(2)}, u32[]{:S(2)}) collective-permute-start(f32[128,256]{1,0:T(8,128)S(1)} %get-tuple-element.116), channel_id=1, source_target_pairs={{0,8},{4,12},{8,0},{12,4},{1,9},{5,13},{9,1},{13,5},{2,10},{6,14},... | collective-permute-start | bytes 393224 | tf_op jit(solution)/shard_map/ppermute | solution.py:373
  10.4 1.0 collective-permute-start.2
  11.4 2.8 %pool_near.1 = (f32[128,256]{1,0:T(8,128)S(1)}, f32[128,256]{1,0:T(8,128)S(1)}, f32[128,256]{1,0:T(8,128)S(1)}, f32[128,256]{1,0:T(8,128)S(1)}, bf16[2,4,512,256]{3,2,1,0:T(8,128)(2,1)S(1)}) custom-call(s32[4]{0:T(128)S(1)} %pad_add_fusion.idx.refs_0_, s32[2,4,2048]{2,1,0:T(4,128)S(1)} %get-tuple-element.118.bag, f32[2,64,512]{2,1,0:T(8,128)S(1)} %get-tuple-element.112.decayed), custom_call_target="tpu_custom_call" | custom-call | flops 1000000 | bytes 1048576 | tf_op jit(solution)/shard_map/pool_near/pallas_call | solution.py:407
  14.2 3.0 %turn_0.1 = (bf16[2,1024,512]{2,1,0:T(8,128)(2,1)S(1)}, bf16[2,1024,512]{2,1,0:T(8,128)(2,1)S(1)}) custom-call(f32[1024,16,128]{2,1,0:T(8,128)} %bitcast.45), custom_call_target="tpu_custom_call" | custom-call | flops 1000000 | bytes 1048576 | tf_op jit(solution)/shard_map/turn_0/pallas_call | solution.py:413
  17.3 0.6 pack.2.refs_1_.refs_2_
  17.9 3.1 %collective-permute-start.6 = (f32[4,128,256]{2,1,0:T(8,128)S(1)}, f32[4,128,256]{2,1,0:T(8,128)S(1)}, u32[]{:S(2)}, u32[]{:S(2)}) collective-permute-start(f32[4,128,256]{2,1,0:T(8,128)S(1)} %pack.2.refs_1_.refs_2_), channel_id=1, source_target_pairs={{0,2},{2,0},{1,3},{3,1},{4,6},{6,4},{5,7},{7,5},{8,10},{10,8},{9,1... | collective-permute-start | bytes 1572872 | tf_op jit(solution)/shard_map/ppermute | solution.py:377
  21.0 1.0 collective-permute-start.3
  22.0 1.7 %collective-permute-start.4 = (f32[128,256]{1,0:T(8,128)S(1)}, f32[128,256]{1,0:T(8,128)S(1)}, u32[]{:S(2)}, u32[]{:S(2)}) collective-permute-start(f32[128,256]{1,0:T(8,128)S(1)} %get-tuple-element.127), channel_id=1, source_target_pairs={{0,8},{4,12},{8,0},{12,4},{1,9},{5,13},{9,1},{13,5},{2,10},{6,14},... | collective-permute-start | bytes 393224 | tf_op jit(solution)/shard_map/ppermute | solution.py:373
  23.7 1.2 %collective-permute-start.5 = (f32[128,256]{1,0:T(8,128)S(1)}, f32[128,256]{1,0:T(8,128)S(1)}, u32[]{:S(2)}, u32[]{:S(2)}) collective-permute-start(f32[128,256]{1,0:T(8,128)S(1)} %get-tuple-element.128), channel_id=1, source_target_pairs={{0,12},{4,0},{8,4},{12,8},{1,13},{5,1},{9,5},{13,9},{2,14},{6,2},{... | collective-permute-start | bytes 393224 | tf_op jit(solution)/shard_map/ppermute | solution.py:373
  25.0 3.2 %turn_1.1 = (bf16[2,1024,512]{2,1,0:T(8,128)(2,1)S(1)}, bf16[2,1024,512]{2,1,0:T(8,128)(2,1)S(1)}) custom-call(f32[1024,16,128]{2,1,0:T(8,128)} %bitcast.46), custom_call_target="tpu_custom_call" | custom-call | flops 1000000 | bytes 1048576 | tf_op jit(solution)/shard_map/turn_1/pallas_call | solution.py:413
  28.2 1.1 collective-permute-done.3.p1
  29.7 0.6 pack.3.refs_1_
  30.4 1.9 %collective-permute-done.6.refs_2_ = f32[4,128,256]{2,1,0:T(8,128)S(1)} collective-permute-done((f32[4,128,256]{2,1,0:T(8,128)S(1)}, f32[4,128,256]{2,1,0:T(8,128)S(1)}, u32[]{:S(2)}, u32[]{:S(2)}) %collective-permute-start.6) | collective-permute-done | bytes 524320 | tf_op jit(solution)/shard_map/ppermute | solution.py:377
  32.3 3.0 %collective-permute-start.10 = (f32[4,128,256]{2,1,0:T(8,128)S(1)}, f32[4,128,256]{2,1,0:T(8,128)S(1)}, u32[]{:S(2)}, u32[]{:S(2)}) collective-permute-start(f32[4,128,256]{2,1,0:T(8,128)S(1)} %pack.3.refs_1_), channel_id=1, source_target_pairs={{0,2},{2,0},{1,3},{3,1},{4,6},{6,4},{5,7},{7,5},{8,10},{10,8},{9,1... | collective-permute-start | bytes 1572872 | tf_op jit(solution)/shard_map/ppermute | solution.py:377
  35.3 1.6 %prepare.1 = (bf16[2,256,1024]{2,1,0:T(8,128)(2,1)S(1)}, bf16[2,256,1024]{2,1,0:T(8,128)(2,1)S(1)}, f32[512,128]{1,0:T(8,128)S(1)}, f32[512,128]{1,0:T(8,128)S(1)}, f32[1,512]{1,0:T(1,128)S(1)}) custom-call(s32[4]{0:T(128)S(1)} %pad_add_fusion.idx.refs_0_, f32[1024,4,128]{2,1,0:T(4,128)S(1)} %bitcast.40, f32[4096,128]{1,0:T(8,128)} %lift_hbm, ...), custom_call_target="tpu_custom_call" | custom-call | flops 1000000 | bytes 1048576 | tf_op jit(solution)/shard_map/prepare/pallas_call | solution.py:442
  36.9 7.2 %forward_a.1 = (f32[2,1024,256]{2,1,0:T(8,128)S(1)}, f32[512,256]{1,0:T(8,128)S(1)}, f32[264,128]{1,0:T(8,128)S(1)}) custom-call(s32[4]{0:T(128)S(1)} %pad_add_fusion.idx.refs_0_, f32[4,128,256]{2,1,0:T(8,128)S(1)} %pack.3.refs_1_, f32[4,128,256]{2,1,0:T(8,128)S(1)} %collective-permute-done.6.refs_2_, f32[4,128,256]{2,1,0:T(8,128)S(1)} %collective-permute-done.7.refs_3_, ...), custom_call_target="tpu_custom_call" | custom-call | flops 1000000 | bytes 1048576 | tf_op jit(solution)/shard_map/forward_a/pallas_call | solution.py:453
  44.1 0.7 collective-permute-start.9
  44.8 2.5 %pick.1 = (bf16[2,256,1024]{2,1,0:T(8,128)(2,1)S(1)}, bf16[2,256,1024]{2,1,0:T(8,128)(2,1)S(1)}) custom-call(s32[4]{0:T(128)S(1)} %pad_add_fusion.idx.refs_0_, f32[1024,16,128]{2,1,0:T(8,128)} %bitcast.47), custom_call_target="tpu_custom_call" | custom-call | flops 1000000 | bytes 1048576 | tf_op jit(solution)/shard_map/pick/pallas_call | solution.py:474
  47.8 0.7 collective-permute-done.10.refs_2_
  48.5 2.6 %collective-permute-done.9 = f32[264,128]{1,0:T(8,128)S(1)} collective-permute-done((f32[264,128]{1,0:T(8,128)S(1)}, f32[264,128]{1,0:T(8,128)S(1)}, u32[]{:S(2)}, u32[]{:S(2)}) %collective-permute-start.9) | collective-permute-done | bytes 135200 | tf_op jit(solution)/shard_map/ppermute | solution.py:377
  51.1 1.7 %collective-permute-start.11 = (f32[264,128]{1,0:T(8,128)S(1)}, f32[264,128]{1,0:T(8,128)S(1)}, u32[]{:S(2)}, u32[]{:S(2)}) collective-permute-start(f32[264,128]{1,0:T(8,128)S(1)} %add.16), channel_id=1, source_target_pairs={{0,32},{16,48},{32,0},{48,16},{64,96},{80,112},{96,64},{112,80},{1... | collective-permute-start | bytes 405512 | tf_op jit(solution)/shard_map/ppermute | solution.py:377
  53.0 3.6 %forward_b0.1 = (f32[1,1024,256]{2,1,0:T(8,128)S(1)}, f32[256,256]{1,0:T(8,128)S(1)}) custom-call(s32[4]{0:T(128)S(1)} %pad_add_fusion.idx.refs_0_, f32[4,128,256]{2,1,0:T(8,128)S(1)} %pack.2.refs_1_.refs_2_, f32[4,128,256]{2,1,0:T(8,128)S(1)} %collective-permute-done.10.refs_2_, f32[4,128,256]{2,1,0:T(8,128)S(1)} %collective-permute-done.12.refs_3_, ...), custom_call_target="tpu_custom_call" | custom-call | flops 4000000000 | bytes 1048576 | tf_op jit(solution)/shard_map/forward_b0/pallas_call | solution.py:463
  56.6 0.6 collective-permute-done.11
  57.2 3.1 %collective-permute-start.14 = (f32[264,128]{1,0:T(8,128)S(1)}, f32[264,128]{1,0:T(8,128)S(1)}, u32[]{:S(2)}, u32[]{:S(2)}) collective-permute-start(f32[264,128]{1,0:T(8,128)S(1)} %add.17.mine), channel_id=1, source_target_pairs={{0,96},{16,112},{32,64},{48,80},{64,32},{80,48},{96,0},{112,16},{1... | collective-permute-start | bytes 405512 | tf_op jit(solution)/shard_map/ppermute | solution.py:377
  60.3 3.6 %forward_b1.1 = (f32[1,1024,256]{2,1,0:T(8,128)S(1)}, f32[256,256]{1,0:T(8,128)S(1)}) custom-call(s32[4]{0:T(128)S(1)} %pad_add_fusion.idx.refs_0_, f32[4,128,256]{2,1,0:T(8,128)S(1)} %pack.2.refs_1_.refs_2_, f32[4,128,256]{2,1,0:T(8,128)S(1)} %collective-permute-done.10.refs_2_, f32[4,128,256]{2,1,0:T(8,128)S(1)} %collective-permute-done.12.refs_3_, ...), custom_call_target="tpu_custom_call" | custom-call | flops 4000000000 | bytes 1048576 | tf_op jit(solution)/shard_map/forward_b1/pallas_call | solution.py:463
  64.0 1.2 logit.1
  65.1 2.0 %collective-permute-start.16 = (f32[264,128]{1,0:T(8,128)S(1)}, f32[264,128]{1,0:T(8,128)S(1)}, u32[]{:S(2)}, u32[]{:S(2)}) collective-permute-start(f32[264,128]{1,0:T(8,128)S(1)} %get-tuple-element.159.refs_1_), channel_id=1, source_target_pairs={{0,2},{2,0},{1,3},{3,1},{4,6},{6,4},{5,7},{7,5},{8,10},{10,8},{9,1... | collective-permute-start | bytes 405512 | tf_op jit(solution)/shard_map/ppermute | solution.py:377
  67.2 4.6 %grads_a.1 = (bf16[2,1024,256]{2,1,0:T(8,128)(2,1)S(1)}, bf16[2,1024,256]{2,1,0:T(8,128)(2,1)S(1)}, f32[2,256,256]{2,1,0:T(8,128)S(1)}, f32[2,64,256]{2,1,0:T(8,...) custom-call(s32[4]{0:T(128)S(1)} %pad_add_fusion.idx.refs_0_, ...), custom_call_target="tpu_custom_call" | custom-call | flops 4000000000 | bytes 1048576 | tf_op jit(solution)/shard_map/grads_a/pallas_call | solution.py:503
  71.8 0.9 collective-permute-done.16.refs_1_
  72.6 1.4 %collective-permute-done.17.refs_2_ = f32[264,128]{1,0:T(8,128)S(1)} collective-permute-done((f32[264,128]{1,0:T(8,128)S(1)}, f32[264,128]{1,0:T(8,128)S(1)}, u32[]{:S(2)}, u32[]{:S(2)}) %collective-permute-start.17) | collective-permute-done | bytes 135200 | tf_op jit(solution)/shard_map/ppermute | solution.py:377
  74.0 2.6 %grads_b0.1 = (bf16[1,1024,256]{2,1,0:T(8,128)(2,1)S(1)}, bf16[1,1024,256]{2,1,0:T(8,128)(2,1)S(1)}, f32[1,256,256]{2,1,0:T(8,128)S(1)}, f32[1,64,256]{2,1,0:T(8...) custom-call(s32[4]{0:T(128)S(1)} %pad_add_fusion.idx.refs_0_, ...), custom_call_target="tpu_custom_call" | custom-call | flops 4000000000 | bytes 1048576 | tf_op jit(solution)/shard_map/grads_b0/pallas_call | solution.py:503
  76.6 1.8 %weights_0.1 = (f32[80,1024]{1,0:T(8,128)S(1)}, f32[80,1024]{1,0:T(8,128)S(1)}, f32[112,1024]{1,0:T(8,128)S(1)}, f32[112,1024]{1,0:T(8,128)S(1)}) custom-call(s32[4]{0:T(128)S(1)} %pad_add_fusion.idx.refs_0_, f32[4,128,256]{2,1,0:T(8,128)S(1)} %pack.3.refs_1_, f32[4,128,256]{2,1,0:T(8,128)S(1)} %pack.2.refs_1_.refs_2_, ...), custom_call_target="tpu_custom_call" | custom-call | flops 3000000000 | bytes 1048576 | tf_op jit(solution)/shard_map/weights_0/pallas_call | solution.py:517
  78.5 1.1 collective-permute-start.18
  79.5 2.2 %collective-permute-start.19 = (f32[112,1024]{1,0:T(8,128)S(1)}, f32[112,1024]{1,0:T(8,128)S(1)}, u32[]{:S(2)}, u32[]{:S(2)}) collective-permute-start(f32[112,1024]{1,0:T(8,128)S(1)} %get-tuple-element.183), channel_id=1, source_target_pairs={{0,12},{4,0},{8,4},{12,8},{1,13},{5,1},{9,5},{13,9},{2,14},{6,2},{... | collective-permute-start | bytes 1376264 | tf_op jit(solution)/shard_map/ppermute | solution.py:373
  81.8 2.6 %grads_b1.1 = (bf16[1,1024,256]{2,1,0:T(8,128)(2,1)S(1)}, bf16[1,1024,256]{2,1,0:T(8,128)(2,1)S(1)}, f32[1,256,256]{2,1,0:T(8,128)S(1)}, f32[1,64,256]{2,1,0:T(8...) custom-call(s32[4]{0:T(128)S(1)} %pad_add_fusion.idx.refs_0_, ...), custom_call_target="tpu_custom_call" | custom-call | flops 4000000000 | bytes 1048576 | tf_op jit(solution)/shard_map/grads_b1/pallas_call | solution.py:503
  84.4 2.1 %weights_1.1 = (f32[88,1024]{1,0:T(8,128)S(1)}, f32[120,1024]{1,0:T(8,128)S(1)}, f32[120,1024]{1,0:T(8,128)S(1)}, f32[88,1024]{1,0:T(8,128)S(1)}, f32[64,1024]{1,0:T(8,128)S(1)}) custom-call(s32[4]{0:T(128)S(1)} %pad_add_fusion.idx.refs_0_, f32[4,128,256]{2,1,0:T(8,128)S(1)} %pack.3.refs_1_, f32[4,128,256]{2,1,0:T(8,128)S(1)} %pack.2.refs_1_.refs_2_, ...), custom_call_target="tpu_custom_call" | custom-call | flops 3000000000 | bytes 1048576 | tf_op jit(solution)/shard_map/weights_1/pallas_call | solution.py:517
  86.5 0.6 collective-permute-start.20
  87.1 1.5 %collective-permute-start.21 = (f32[120,1024]{1,0:T(8,128)S(1)}, f32[120,1024]{1,0:T(8,128)S(1)}, u32[]{:S(2)}, u32[]{:S(2)}) collective-permute-start(f32[120,1024]{1,0:T(8,128)S(1)} %get-tuple-element.200), channel_id=1, source_target_pairs={{0,4},{4,8},{8,12},{12,0},{1,5},{5,9},{9,13},{13,1},{2,6},{6,10},{... | collective-permute-start | bytes 1474568 | tf_op jit(solution)/shard_map/ppermute | solution.py:373
  88.6 4.5 %collective-permute-done.18.w_up = f32[112,1024]{1,0:T(8,128)S(1)} collective-permute-done((f32[112,1024]{1,0:T(8,128)S(1)}, f32[112,1024]{1,0:T(8,128)S(1)}, u32[]{:S(2)}, u32[]{:S(2)}) %collective-permute-start.18) | collective-permute-done | bytes 458784 | tf_op jit(solution)/shard_map/ppermute | solution.py:373
  93.2 14.8 %collective-permute-done.20.v_down = f32[120,1024]{1,0:T(8,128)S(1)} collective-permute-done((f32[120,1024]{1,0:T(8,128)S(1)}, f32[120,1024]{1,0:T(8,128)S(1)}, u32[]{:S(2)}, u32[]{:S(2)}) %collective-permute-start.20) | collective-permute-done | bytes 491552 | tf_op jit(solution)/shard_map/ppermute | solution.py:373
  108.0 1.2 %collective-permute-done.21.v_up.refs_4_ = f32[120,1024]{1,0:T(8,128)S(1)} collective-permute-done((f32[120,1024]{1,0:T(8,128)S(1)}, f32[120,1024]{1,0:T(8,128)S(1)}, u32[]{:S(2)}, u32[]{:S(2)}) %collective-permute-start.21) | collective-permute-done | bytes 491552 | tf_op jit(solution)/shard_map/ppermute | solution.py:373
  109.3 2.8 %collective-permute-start.24 = (f32[88,1024]{1,0:T(8,128)S(1)}, f32[88,1024]{1,0:T(8,128)S(1)}, u32[]{:S(2)}, u32[]{:S(2)}) collective-permute-start(f32[88,1024]{1,0:T(8,128)S(1)} %slice_add_fusion), channel_id=1, source_target_pairs={{0,12},{4,0},{8,4},{12,8},{1,13},{5,1},{9,5},{13,9},{2,14},{6,2},{... | collective-permute-start | bytes 1081352 | tf_op jit(solution)/shard_map/ppermute | solution.py:373
  112.1 2.8 %update.1 = (f32[2,64,512]{2,1,0:T(8,128)}, f32[2,512]{1,0:T(2,128)S(1)}) custom-call(s32[4]{0:T(128)S(1)} %pad_add_fusion.idx.refs_0_, f32[2,64,256]{2,1,0:T(8,128)S(1)} %get-tuple-element.165.ga, f32[1,64,256]{2,1,0:T(8,128)S(1)} %get-tuple-element.169.gb0, f32[1,64,256]{2,1,0:T(8,128)S(1)} %get-tuple-element.171.gb1, ...), custom_call_target="tpu_custom_call" | custom-call | flops 5000000000 | bytes 1048576 | tf_op jit(solution)/shard_map/update/pallas_call | solution.py:547
  114.9 0.6 copy.23
  115.5 1.5 %collective-permute-done.24.refs_5_ = f32[88,1024]{1,0:T(8,128)S(1)} collective-permute-done((f32[88,1024]{1,0:T(8,128)S(1)}, f32[88,1024]{1,0:T(8,128)S(1)}, u32[]{:S(2)}, u32[]{:S(2)}) %collective-permute-start.24) | collective-permute-done | bytes 360480 | tf_op jit(solution)/shard_map/ppermute | solution.py:373
  117.1 1.6 %sum.1 = (f32[1024,128]{1,0:T(8,128)}, f32[256,128]{1,0:T(8,128)}, f32[32,128]{1,0:T(8,128)}, f32[32,128]{1,0:T(8,128)}) custom-call(s32[4]{0:T(128)S(1)} %pad_add_fusion.idx.refs_0_, f32[1,512]{1,0:T(1,128)S(1)} %get-tuple-element.142.refs_13_.refs_10_.head, f32[80,1024]{1,0:T(8,128)S(1)} %get-tuple-element.208.refs_0_, ...), custom_call_target="tpu_custom_call" | custom-call | flops 1000000 | bytes 1048576 | tf_op jit(solution)/shard_map/sum/pallas_call | solution.py:550
  (37 shorter events, 1.6 us)
Async XLA Ops:
  4.7 12.5 %collective-permute-start = (f32[128,256]{1,0:T(8,128)S(1)}, f32[128,256]{1,0:T(8,128)S(1)}, u32[]{:S(2)}, u32[]{:S(2)}) collective-permute-start(f32[128,256]{1,0:T(8,128)S(1)} %get-tuple-element.115), channel_id=1, source_target_pairs={{0,4},{4,8},{8,12},{12,0},{1,5},{5,9},{9,13},{13,1},{2,6},{6,10},{... | collective-permute-start | bytes 393224 | tf_op jit(solution)/shard_map/ppermute | solution.py:373
  6.8 10.5 %collective-permute-start.1 = (f32[128,256]{1,0:T(8,128)S(1)}, f32[128,256]{1,0:T(8,128)S(1)}, u32[]{:S(2)}, u32[]{:S(2)}) collective-permute-start(f32[128,256]{1,0:T(8,128)S(1)} %get-tuple-element.116), channel_id=1, source_target_pairs={{0,8},{4,12},{8,0},{12,4},{1,9},{5,13},{9,1},{13,5},{2,10},{6,14},... | collective-permute-start | bytes 393224 | tf_op jit(solution)/shard_map/ppermute | solution.py:373
  10.4 6.9 %collective-permute-start.2 = (f32[128,256]{1,0:T(8,128)S(1)}, f32[128,256]{1,0:T(8,128)S(1)}, u32[]{:S(2)}, u32[]{:S(2)}) collective-permute-start(f32[128,256]{1,0:T(8,128)S(1)} %get-tuple-element.117), channel_id=1, source_target_pairs={{0,12},{4,0},{8,4},{12,8},{1,13},{5,1},{9,5},{13,9},{2,14},{6,2},{... | collective-permute-start | bytes 393224 | tf_op jit(solution)/shard_map/ppermute | solution.py:373
  17.9 14.4 %collective-permute-start.6 = (f32[4,128,256]{2,1,0:T(8,128)S(1)}, f32[4,128,256]{2,1,0:T(8,128)S(1)}, u32[]{:S(2)}, u32[]{:S(2)}) collective-permute-start(f32[4,128,256]{2,1,0:T(8,128)S(1)} %pack.2.refs_1_.refs_2_), channel_id=1, source_target_pairs={{0,2},{2,0},{1,3},{3,1},{4,6},{6,4},{5,7},{7,5},{8,10},{10,8},{9,1... | collective-permute-start | bytes 1572872 | tf_op jit(solution)/shard_map/ppermute | solution.py:377
  21.0 8.3 %collective-permute-start.3 = (f32[128,256]{1,0:T(8,128)S(1)}, f32[128,256]{1,0:T(8,128)S(1)}, u32[]{:S(2)}, u32[]{:S(2)}) collective-permute-start(f32[128,256]{1,0:T(8,128)S(1)} %get-tuple-element.126), channel_id=1, source_target_pairs={{0,4},{4,8},{8,12},{12,0},{1,5},{5,9},{9,13},{13,1},{2,6},{6,10},{... | collective-permute-start | bytes 393224 | tf_op jit(solution)/shard_map/ppermute | solution.py:373
  22.0 7.3 %collective-permute-start.4 = (f32[128,256]{1,0:T(8,128)S(1)}, f32[128,256]{1,0:T(8,128)S(1)}, u32[]{:S(2)}, u32[]{:S(2)}) collective-permute-start(f32[128,256]{1,0:T(8,128)S(1)} %get-tuple-element.127), channel_id=1, source_target_pairs={{0,8},{4,12},{8,0},{12,4},{1,9},{5,13},{9,1},{13,5},{2,10},{6,14},... | collective-permute-start | bytes 393224 | tf_op jit(solution)/shard_map/ppermute | solution.py:373
  23.7 11.6 %copy-start.1 = (f32[4096]{0:T(1024)S(1)}, f32[4096]{0:T(1024)}, u32[]{:S(2)}) copy-start(f32[4096]{0:T(1024)} %param.20) | copy-start | bytes 49156
  23.7 6.0 %collective-permute-start.5 = (f32[128,256]{1,0:T(8,128)S(1)}, f32[128,256]{1,0:T(8,128)S(1)}, u32[]{:S(2)}, u32[]{:S(2)}) collective-permute-start(f32[128,256]{1,0:T(8,128)S(1)} %get-tuple-element.128), channel_id=1, source_target_pairs={{0,12},{4,0},{8,4},{12,8},{1,13},{5,1},{9,5},{13,9},{2,14},{6,2},{... | collective-permute-start | bytes 393224 | tf_op jit(solution)/shard_map/ppermute | solution.py:373
  25.0 10.3 %copy-start = (f32[1024,2,256]{2,1,0:T(2,128)S(1)}, f32[1024,2,256]{2,1,0:T(2,128)}, u32[]{:S(2)}) copy-start(f32[1024,2,256]{2,1,0:T(2,128)} %param.17) | copy-start | bytes 6291460
  30.3 6.6 %collective-permute-start.7 = (f32[4,128,256]{2,1,0:T(8,128)S(1)}, f32[4,128,256]{2,1,0:T(8,128)S(1)}, u32[]{:S(2)}, u32[]{:S(2)}) collective-permute-start(f32[4,128,256]{2,1,0:T(8,128)S(1)} %pack.3.refs_1_), channel_id=1, source_target_pairs={{0,1},{1,0},{2,3},{3,2},{4,5},{5,4},{6,7},{7,6},{8,9},{9,8},{10,11... | collective-permute-start | bytes 1572872 | tf_op jit(solution)/shard_map/ppermute | solution.py:377
  32.3 4.6 %collective-permute-start.8 = (f32[4,128,256]{2,1,0:T(8,128)S(1)}, f32[4,128,256]{2,1,0:T(8,128)S(1)}, u32[]{:S(2)}, u32[]{:S(2)}) collective-permute-start(f32[4,128,256]{2,1,0:T(8,128)S(1)} %collective-permute-done.6.refs_2_), channel_id=1, source_target_pairs={{0,1},{1,0},{2,3},{3,2},{4,5},{5,4},{6,7},{7,6},{8,9},{9,8},{10,11... | collective-permute-start | bytes 1572872 | tf_op jit(solution)/shard_map/ppermute | solution.py:377
  32.3 16.2 %collective-permute-start.10 = (f32[4,128,256]{2,1,0:T(8,128)S(1)}, f32[4,128,256]{2,1,0:T(8,128)S(1)}, u32[]{:S(2)}, u32[]{:S(2)}) collective-permute-start(f32[4,128,256]{2,1,0:T(8,128)S(1)} %pack.3.refs_1_), channel_id=1, source_target_pairs={{0,2},{2,0},{1,3},{3,1},{4,6},{6,4},{5,7},{7,5},{8,10},{10,8},{9,1... | collective-permute-start | bytes 1572872 | tf_op jit(solution)/shard_map/ppermute | solution.py:377
  44.1 7.0 %collective-permute-start.9 = (f32[264,128]{1,0:T(8,128)S(1)}, f32[264,128]{1,0:T(8,128)S(1)}, u32[]{:S(2)}, u32[]{:S(2)}) collective-permute-start(f32[264,128]{1,0:T(8,128)S(1)} %get-tuple-element.144), channel_id=1, source_target_pairs={{0,16},{16,0},{32,48},{48,32},{64,80},{80,64},{96,112},{112,96},{1... | collective-permute-start | bytes 405512 | tf_op jit(solution)/shard_map/ppermute | solution.py:377
  44.8 8.0 %collective-permute-start.12 = (f32[4,128,256]{2,1,0:T(8,128)S(1)}, f32[4,128,256]{2,1,0:T(8,128)S(1)}, u32[]{:S(2)}, u32[]{:S(2)}) collective-permute-start(f32[4,128,256]{2,1,0:T(8,128)S(1)} %pack.2.refs_1_.refs_2_), channel_id=1, source_target_pairs={{0,1},{1,0},{2,3},{3,2},{4,5},{5,4},{6,7},{7,6},{8,9},{9,8},{10,11... | collective-permute-start | bytes 1572872 | tf_op jit(solution)/shard_map/ppermute | solution.py:377
  51.1 1.9 %collective-permute-start.13 = (f32[4,128,256]{2,1,0:T(8,128)S(1)}, f32[4,128,256]{2,1,0:T(8,128)S(1)}, u32[]{:S(2)}, u32[]{:S(2)}) collective-permute-start(f32[4,128,256]{2,1,0:T(8,128)S(1)} %collective-permute-done.10.refs_2_), channel_id=1, source_target_pairs={{0,1},{1,0},{2,3},{3,2},{4,5},{5,4},{6,7},{7,6},{8,9},{9,8},{10,11... | collective-permute-start | bytes 1572872 | tf_op jit(solution)/shard_map/ppermute | solution.py:377
  51.1 6.1 %collective-permute-start.11 = (f32[264,128]{1,0:T(8,128)S(1)}, f32[264,128]{1,0:T(8,128)S(1)}, u32[]{:S(2)}, u32[]{:S(2)}) collective-permute-start(f32[264,128]{1,0:T(8,128)S(1)} %add.16), channel_id=1, source_target_pairs={{0,32},{16,48},{32,0},{48,16},{64,96},{80,112},{96,64},{112,80},{1... | collective-permute-start | bytes 405512 | tf_op jit(solution)/shard_map/ppermute | solution.py:377
  57.2 6.7 %copy-start.2 = (s32[1,128]{1,0:T(1,128)S(1)}, s32[1,128]{1,0:T(1,128)}, u32[]{:S(2)}) copy-start(s32[1,128]{1,0:T(1,128)} %labels.1) | copy-start | bytes 1540
  57.2 6.7 %collective-permute-start.14 = (f32[264,128]{1,0:T(8,128)S(1)}, f32[264,128]{1,0:T(8,128)S(1)}, u32[]{:S(2)}, u32[]{:S(2)}) collective-permute-start(f32[264,128]{1,0:T(8,128)S(1)} %add.17.mine), channel_id=1, source_target_pairs={{0,96},{16,112},{32,64},{48,80},{64,32},{80,48},{96,0},{112,16},{1... | collective-permute-start | bytes 405512 | tf_op jit(solution)/shard_map/ppermute | solution.py:377
  65.1 2.0 %collective-permute-start.15 = (f32[264,128]{1,0:T(8,128)S(1)}, f32[264,128]{1,0:T(8,128)S(1)}, u32[]{:S(2)}, u32[]{:S(2)}) collective-permute-start(f32[264,128]{1,0:T(8,128)S(1)} %get-tuple-element.159.refs_1_), channel_id=1, source_target_pairs={{0,1},{1,0},{2,3},{3,2},{4,5},{5,4},{6,7},{7,6},{8,9},{9,8},{10,11... | collective-permute-start | bytes 405512 | tf_op jit(solution)/shard_map/ppermute | solution.py:377
  65.1 7.5 %collective-permute-start.16 = (f32[264,128]{1,0:T(8,128)S(1)}, f32[264,128]{1,0:T(8,128)S(1)}, u32[]{:S(2)}, u32[]{:S(2)}) collective-permute-start(f32[264,128]{1,0:T(8,128)S(1)} %get-tuple-element.159.refs_1_), channel_id=1, source_target_pairs={{0,2},{2,0},{1,3},{3,1},{4,6},{6,4},{5,7},{7,5},{8,10},{10,8},{9,1... | collective-permute-start | bytes 405512 | tf_op jit(solution)/shard_map/ppermute | solution.py:377
  72.6 1.4 %collective-permute-start.17 = (f32[264,128]{1,0:T(8,128)S(1)}, f32[264,128]{1,0:T(8,128)S(1)}, u32[]{:S(2)}, u32[]{:S(2)}) collective-permute-start(f32[264,128]{1,0:T(8,128)S(1)} %collective-permute-done.16.refs_1_), channel_id=1, source_target_pairs={{0,1},{1,0},{2,3},{3,2},{4,5},{5,4},{6,7},{7,6},{8,9},{9,8},{10,11... | collective-permute-start | bytes 405512 | tf_op jit(solution)/shard_map/ppermute | solution.py:377
  78.5 14.6 %collective-permute-start.18 = (f32[112,1024]{1,0:T(8,128)S(1)}, f32[112,1024]{1,0:T(8,128)S(1)}, u32[]{:S(2)}, u32[]{:S(2)}) collective-permute-start(f32[112,1024]{1,0:T(8,128)S(1)} %get-tuple-element.182), channel_id=1, source_target_pairs={{0,4},{4,8},{8,12},{12,0},{1,5},{5,9},{9,13},{13,1},{2,6},{6,10},{... | collective-permute-start | bytes 1376264 | tf_op jit(solution)/shard_map/ppermute | solution.py:373
  79.5 13.6 %collective-permute-start.19 = (f32[112,1024]{1,0:T(8,128)S(1)}, f32[112,1024]{1,0:T(8,128)S(1)}, u32[]{:S(2)}, u32[]{:S(2)}) collective-permute-start(f32[112,1024]{1,0:T(8,128)S(1)} %get-tuple-element.183), channel_id=1, source_target_pairs={{0,12},{4,0},{8,4},{12,8},{1,13},{5,1},{9,5},{13,9},{2,14},{6,2},{... | collective-permute-start | bytes 1376264 | tf_op jit(solution)/shard_map/ppermute | solution.py:373
  84.4 4.2 %copy-start.3 = (f32[2,1,512]{2,1,0:T(1,128)S(1)}, f32[2,1,512]{2,1,0:T(1,128)}, u32[]{:S(2)}) copy-start(f32[2,1,512]{2,1,0:T(1,128)} %param.15) | copy-start | bytes 12292
  86.5 21.5 %collective-permute-start.20 = (f32[120,1024]{1,0:T(8,128)S(1)}, f32[120,1024]{1,0:T(8,128)S(1)}, u32[]{:S(2)}, u32[]{:S(2)}) collective-permute-start(f32[120,1024]{1,0:T(8,128)S(1)} %get-tuple-element.199), channel_id=1, source_target_pairs={{0,12},{4,0},{8,4},{12,8},{1,13},{5,1},{9,5},{13,9},{2,14},{6,2},{... | collective-permute-start | bytes 1474568 | tf_op jit(solution)/shard_map/ppermute | solution.py:373
  87.1 22.2 %collective-permute-start.21 = (f32[120,1024]{1,0:T(8,128)S(1)}, f32[120,1024]{1,0:T(8,128)S(1)}, u32[]{:S(2)}, u32[]{:S(2)}) collective-permute-start(f32[120,1024]{1,0:T(8,128)S(1)} %get-tuple-element.200), channel_id=1, source_target_pairs={{0,4},{4,8},{8,12},{12,0},{1,5},{5,9},{9,13},{13,1},{2,6},{6,10},{... | collective-permute-start | bytes 1474568 | tf_op jit(solution)/shard_map/ppermute | solution.py:373
  88.6 23.5 %collective-permute-start.22 = (f32[64,1024]{1,0:T(8,128)S(1)}, f32[64,1024]{1,0:T(8,128)S(1)}, u32[]{:S(2)}, u32[]{:S(2)}) collective-permute-start(f32[64,1024]{1,0:T(8,128)S(1)} %get-tuple-element.203), channel_id=1, source_target_pairs={{0,8},{4,12},{8,0},{12,4},{1,9},{5,13},{9,1},{13,5},{2,10},{6,14},... | collective-permute-start | bytes 786440 | tf_op jit(solution)/shard_map/ppermute | solution.py:373
  93.1 22.4 %collective-permute-start.23 = (f32[80,1024]{1,0:T(8,128)S(1)}, f32[80,1024]{1,0:T(8,128)S(1)}, u32[]{:S(2)}, u32[]{:S(2)}) collective-permute-start(f32[80,1024]{1,0:T(8,128)S(1)} %slice_add_fusion.1), channel_id=1, source_target_pairs={{0,4},{4,8},{8,12},{12,0},{1,5},{5,9},{9,13},{13,1},{2,6},{6,10},{... | collective-permute-start | bytes 983048 | tf_op jit(solution)/shard_map/ppermute | solution.py:373
  109.3 7.8 %collective-permute-start.24 = (f32[88,1024]{1,0:T(8,128)S(1)}, f32[88,1024]{1,0:T(8,128)S(1)}, u32[]{:S(2)}, u32[]{:S(2)}) collective-permute-start(f32[88,1024]{1,0:T(8,128)S(1)} %slice_add_fusion), channel_id=1, source_target_pairs={{0,12},{4,0},{8,4},{12,8},{1,13},{5,1},{9,5},{13,9},{2,14},{6,2},{... | collective-permute-start | bytes 1081352 | tf_op jit(solution)/shard_map/ppermute | solution.py:373

commit v6 on v5

--- a/solution.py
+++ b/solution.py
@@ -233,7 +233,8 @@
     pay[2 * rank : 2 * rank + 8, :] = jnp.broadcast_to(error, (8, error.shape[1]))
 
 
-def grads_kernel(towers, with_pq, idx, mine, other, hidden, w1h, w1l, w2h, w2l, press, lift, head, ghh, ghl, gout, g0, g1, g2, g3, *pq):
+def grads_kernel(towers, with_pq, extra, idx, mine, other, hidden, w1h, w1l, w2h, w2l, press, lift, head, *refs):
+    ghh, ghl, gout, g0, g1, g2, g3, *pq = refs[extra:]
     rank = press.shape[1]
     width = w1h.shape[1] // 4
     width_out = w2h.shape[2]
@@ -288,21 +289,16 @@
     for k in range(4):
         for b in range(4):
             blocks[k][width : width + 16, b * 256 : (b + 1) * 256] = grad[k * width + 16 * b : k * width + 16 * b + 16]
-    low = width // 2
+    low = width // 4
     for n, k in enumerate(riders):
-        ga, gb = rest[2 * n], rest[2 * n + 1]
         base = blocks[k].shape[0] - low
-        blocks[k][base:, 0:256] = ga[t, 0:low, :]
-        blocks[k][base:, 256:512] = gb[0, 0:low, :]
-        blocks[k][base:, 512:768] = ga[t, low:, :]
-        blocks[k][base:, 768:1024] = gb[0, low:, :]
+        for b in range(4):
+            blocks[k][base:, b * 256 : (b + 1) * 256] = rest[n][0, b * low : (b + 1) * low, :]
     if t == 1:
-        x0a, x0b0, x0b1, pqa, pqb, ga, gb0, gb1 = rest[4:]
+        x0a, x0b0, x0b1, pqa, pqb, gb0, gb1 = rest[2:]
         for n, gb in enumerate((gb0, gb1)):
-            for b in range(2):
-                part = slice(b * low, (b + 1) * low)
-                far_block[n * low : (n + 1) * low, b * 512 : b * 512 + 256] = ga[n, part, :]
-                far_block[n * low : (n + 1) * low, b * 512 + 256 : (b + 1) * 512] = gb[0, part, :]
+            for b in range(4):
+                far_block[n * low : (n + 1) * low, b * 256 : (b + 1) * 256] = gb[0, b * low : (b + 1) * low, :]
         parts_a, parts_b = [], []
         for k in range(4):
             block = lax.rem(z + k, 4) * 4 + quad
@@ -315,26 +311,22 @@
                 blocks[k][width + 16 : width + 24, b * 256 : (b + 1) * 256] = both[32 * k + 8 * b : 32 * k + 8 * b + 8]
 
 
-def update_kernel(idx, ga, gb0, gb1, w_up, w_down, v_up, v_down, opposite, near, far, decayed, accumulator, new_tables, new_accumulator):
+def update_kernel(idx, ga0, ga1, ga2, ga3, gb0, gb1, w_up, w_down, v_up, v_down, opposite, near, far, decayed, accumulator, new_tables, new_accumulator):
     z = idx[0]
     towers, width, rows = decayed.shape
-    low = width // 2
+    low = width // 4
 
     def rider(ref, start=None):
         start = ref.shape[0] - low if start is None else start
         block = ref[start : start + low, :]
-        return (
-            jnp.concatenate([block[:, 0:256], block[:, 512:768]], axis=0),
-            jnp.concatenate([block[:, 256:512], block[:, 768:1024]], axis=0),
-        )
+        return jnp.concatenate([block[:, b * 256 : (b + 1) * 256] for b in range(4)], axis=0)
 
     for t in range(towers):
-        gb = (gb0, gb1)[t]
         pieces = (
-            (ga[t], gb[0]),
-            rider((w_up, v_up)[t]),
-            rider(opposite, low * t),
-            rider((w_down, v_down)[t]),
+            (ga0[t], (gb0, gb1)[t][0]),
+            (ga1[t], rider((w_up, v_up)[t])),
+            (ga2[t], rider(opposite, low * t)),
+            (ga3[t], rider((w_down, v_down)[t])),
         )
         total = jnp.zeros((2 * width, rows), F32)
         for k, (a, b) in enumerate(pieces):
@@ -498,18 +490,19 @@
     c1 = flip(pay, "core", 2, 1)
     xa = flip(pay, "xh", 2, 1)
 
-    def grads(towers, with_pq, mine, other, hidden, name):
+    def grads(towers, with_pq, mine, other, hidden, name, flops, extra=()):
         n = len(towers)
         return call(
-            lambda *refs: grads_kernel(towers, with_pq, *refs),
+            lambda *refs: grads_kernel(towers, with_pq, len(extra), *refs),
             [bf16(n, 1024, 256)] * 2 + [f32(n, 256, 256)] + [f32(n, 64, 256)] * 4 + [f32(2 * rank, 256)] * with_pq,
-            [SMEM_SPEC] + vmem(10),
+            [SMEM_SPEC] + vmem(10 + len(extra)),
             name=name,
-            flops=4e9,
-        )(idx, mine, other, hidden, w1qh, w1ql, w2h, w2l, press, lift, head)
-
-    ghha, ghla, gouta, *ga, pqa = grads((0, 1), True, pay, c1, hid_a, "grads_a")
-
+            flops=flops,
+        )(idx, mine, other, hidden, w1qh, w1ql, w2h, w2l, press, lift, head, *extra)
+
+    ghha, ghla, gouta, *ga, pqa = grads((0, 1), True, pay, c1, hid_a, "grads_a", 4e9)
+
+    gone = [shift(ga[k], "z", 4, k) for k in (1, 2, 3)]
     xa, pqa = lax.optimization_barrier((xa, pqa))
     xb = flip(xa, "core", 2, 1)
 
@@ -522,20 +515,20 @@
             flops=3e9,
         )(idx, fq_near, fq_far, ghha, ghla, ghhb, ghlb, gouta, goutb, hid_a, hid_b, *extra)
 
-    ghh0, ghl0, gout0, *gb0, pqb = grads((0,), True, xa, xb, hid_b0, "grads_b0")
-    w = weights_of(0, (2, 3), (80, 80, 112, 112), ghh0, ghl0, gout0, hid_b0, (ga[1], gb0[1], ga[3], gb0[3]))
+    ghh0, ghl0, gout0, *gb0, pqb = grads((0,), True, xa, xb, hid_b0, "grads_b0", 4e9)
+    w = weights_of(0, (2, 3), (80, 80, 96, 96), ghh0, ghl0, gout0, hid_b0, (gb0[1], gb0[3]))
     up = shift(w[2], "z", 4, 1)
     w3 = shift(w[3], "z", 4, 3)
-    ghh1, ghl1, gout1, *gb1 = grads((1,), False, xa, xb, hid_b1, "grads_b1")
+    ghh1, ghl1, gout1, *gb1 = grads((1,), False, xa, xb, hid_b1, "grads_b1", 4e9, gone)
     v = weights_of(
         1,
         (1, 2),
-        (88, 120, 120, 88, 64),
+        (88, 104, 104, 88, 32),
         ghh1,
         ghl1,
         gout1,
         hid_b1,
-        (ga[1], gb1[1], ga[3], gb1[3], x0a, x0b0, x0b1, pqa, pqb, ga[2], gb0[2], gb1[2]),
+        (gb1[1], gb1[3], x0a, x0b0, x0b1, pqa, pqb, gb0[2], gb1[2]),
     )
     down = shift(v[2], "z", 4, 3)
     v1 = shift(v[1], "z", 4, 1)
@@ -545,8 +538,8 @@
     w1 = shift(w[1] + up[0:80], "z", 4, 1)
     v3 = shift(v[3] + down[0:88], "z", 4, 3)
     new_tables, new_accumulator = call(
-        update_kernel, [f32(2, 64, 512), f32(2, 512)], [SMEM_SPEC] + vmem(12), name="update", flops=5e9
-    )(idx, ga[0], gb0[0], gb1[0], up, w3, v1, down, g2, counts_near, counts_far, decayed, accumulator[:, 0])
+        update_kernel, [f32(2, 64, 512), f32(2, 512)], [SMEM_SPEC] + vmem(15), name="update", flops=5e9
+    )(idx, ga[0], *gone, gb0[0], gb1[0], up, w3, v1, down, g2, counts_near, counts_far, decayed, accumulator[:, 0])
     first, second, lift_out, press_out = call(
         sum_kernel,
         [f32(1024, 128), f32(256, 128), f32(32, rank), f32(32, rank)],

time: 119 us -> 117 us (0.983)
  waiting for transfers between devices: 31.8 us -> 26 us
  starting transfers between devices: 32.6 us -> 36.3 us
    ppermute x13 -> x16, waiting for transfers between devices: 23.6 us -> 19 us  [shift(): return lax.ppermute(x, axis, [(i, (i + by) % size) for i in range(size)])]
    ppermute x13 -> x16, starting transfers between devices: 19 us -> 22.7 us  [shift(): return lax.ppermute(x, axis, [(i, (i + by) % size) for i in range(size)])]
    ppermute x12, waiting for transfers between devices: 8.26 us -> 6.91 us  [flip(): return lax.ppermute(x, axis, [(i, i ^ bit) for i in range(size)])]
  transfers between devices with their start and end apart: 25 -> 28, of which waited for: 13 -> 14; matrix products, arithmetic and copies ran while one was open for 1% -> 1% of each run, Pallas kernels for 34% -> 39%
where the time goes in v6:
time: 117 us
  Pallas kernels  52.6 us (45%)
  starting transfers between devices  36.3 us (31%)
  waiting for transfers between devices  26 us (22%)
    ppermute x16, starting transfers between devices, shift(): return lax.ppermute(x, axis, [(i, (i + by) % size) for i in range(size)])  22.7 us
    ppermute x16, waiting for transfers between devices, shift(): return lax.ppermute(x, axis, [(i, (i + by) % size) for i in range(size)])  19 us
    ppermute x12, starting transfers between devices, flip(): return lax.ppermute(x, axis, [(i, i ^ bit) for i in range(size)])  13.6 us
    pallas_call x3, Pallas kernels, grads(): call(lambda *refs: grads_kernel(towers, with_pq, len(extra), *refs), [bf1...  9.91 us
    pallas_call x2, Pallas kernels, later_half(): call(lambda *refs: forward_kernel((t,), False, *refs), [f32(1, 1024, 256)...  7.23 us
    pallas_call x1, Pallas kernels, per_device(): call(lambda *refs: forward_kernel((0, 1), True, *refs), [f32(2, 1024, 256...  7.18 us
    ppermute x12, waiting for transfers between devices, flip(): return lax.ppermute(x, axis, [(i, i ^ bit) for i in range(size)])  6.91 us
    pallas_call x2, Pallas kernels, turn(): pl.pallas_call(lambda *refs: turn_kernel(at, *refs), in_specs=[any_spec],...  6.22 us
  transfers between devices with their start and end apart: 28, of which 14 were waited for; matrix products, arithmetic and copies ran while one was open for 1% of the time, Pallas kernels for 39%

profile of v6, /device:TPU:0, one launch (start us, length us, event | category | flops | bytes accessed | tf_op | source)
XLA Modules:
  0.0 116.5 jit_solution(10315319877687823834)
XLA Ops:
  0.7 4.0 %pool_far.1 = (f32[128,256]{1,0:T(8,128)S(1)}, f32[128,256]{1,0:T(8,128)S(1)}, f32[128,256]{1,0:T(8,128)S(1)}, f32[128,256]{1,0:T(8,128)S(1)}, bf16[2,4,512,256]...) custom-call(s32[4]{0:T(128)S(1)} %pad_add_fusion.idx.refs_0_, s32[2,4,2048]{2,1,0:T(4,128)} %bitcast.49, ...), custom_call_target="tpu_custom_call" | custom-call | flops 1000000 | bytes 1048576 | tf_op jit(solution)/shard_map/pool_far/pallas_call | solution.py:384
  4.7 2.1 %collective-permute-start = (f32[128,256]{1,0:T(8,128)S(1)}, f32[128,256]{1,0:T(8,128)S(1)}, u32[]{:S(2)}, u32[]{:S(2)}) collective-permute-start(f32[128,256]{1,0:T(8,128)S(1)} %get-tuple-element.115), channel_id=1, source_target_pairs={{0,4},{4,8},{8,12},{12,0},{1,5},{5,9},{9,13},{13,1},{2,6},{6,10},{... | collective-permute-start | bytes 393224 | tf_op jit(solution)/shard_map/ppermute | solution.py:365
  6.8 3.6 %collective-permute-start.1 = (f32[128,256]{1,0:T(8,128)S(1)}, f32[128,256]{1,0:T(8,128)S(1)}, u32[]{:S(2)}, u32[]{:S(2)}) collective-permute-start(f32[128,256]{1,0:T(8,128)S(1)} %get-tuple-element.116), channel_id=1, source_target_pairs={{0,8},{4,12},{8,0},{12,4},{1,9},{5,13},{9,1},{13,5},{2,10},{6,14},... | collective-permute-start | bytes 393224 | tf_op jit(solution)/shard_map/ppermute | solution.py:365
  10.4 1.0 collective-permute-start.2
  11.4 2.8 %pool_near.1 = (f32[128,256]{1,0:T(8,128)S(1)}, f32[128,256]{1,0:T(8,128)S(1)}, f32[128,256]{1,0:T(8,128)S(1)}, f32[128,256]{1,0:T(8,128)S(1)}, bf16[2,4,512,256]{3,2,1,0:T(8,128)(2,1)S(1)}) custom-call(s32[4]{0:T(128)S(1)} %pad_add_fusion.idx.refs_0_, s32[2,4,2048]{2,1,0:T(4,128)S(1)} %get-tuple-element.118.bag, f32[2,64,512]{2,1,0:T(8,128)S(1)} %get-tuple-element.112.decayed), custom_call_target="tpu_custom_call" | custom-call | flops 1000000 | bytes 1048576 | tf_op jit(solution)/shard_map/pool_near/pallas_call | solution.py:399
  14.2 3.0 %turn_0.1 = (bf16[2,1024,512]{2,1,0:T(8,128)(2,1)S(1)}, bf16[2,1024,512]{2,1,0:T(8,128)(2,1)S(1)}) custom-call(f32[1024,16,128]{2,1,0:T(8,128)} %bitcast.45), custom_call_target="tpu_custom_call" | custom-call | flops 1000000 | bytes 1048576 | tf_op jit(solution)/shard_map/turn_0/pallas_call | solution.py:405
  17.9 3.1 %collective-permute-start.6 = (f32[4,128,256]{2,1,0:T(8,128)S(1)}, f32[4,128,256]{2,1,0:T(8,128)S(1)}, u32[]{:S(2)}, u32[]{:S(2)}) collective-permute-start(f32[4,128,256]{2,1,0:T(8,128)S(1)} %pack.2.refs_1_.refs_2_), channel_id=1, source_target_pairs={{0,2},{2,0},{1,3},{3,1},{4,6},{6,4},{5,7},{7,5},{8,10},{10,8},{9,1... | collective-permute-start | bytes 1572872 | tf_op jit(solution)/shard_map/ppermute | solution.py:369
  21.0 1.0 collective-permute-start.3
  22.0 1.7 %collective-permute-start.4 = (f32[128,256]{1,0:T(8,128)S(1)}, f32[128,256]{1,0:T(8,128)S(1)}, u32[]{:S(2)}, u32[]{:S(2)}) collective-permute-start(f32[128,256]{1,0:T(8,128)S(1)} %get-tuple-element.127), channel_id=1, source_target_pairs={{0,8},{4,12},{8,0},{12,4},{1,9},{5,13},{9,1},{13,5},{2,10},{6,14},... | collective-permute-start | bytes 393224 | tf_op jit(solution)/shard_map/ppermute | solution.py:365
  23.7 1.2 %collective-permute-start.5 = (f32[128,256]{1,0:T(8,128)S(1)}, f32[128,256]{1,0:T(8,128)S(1)}, u32[]{:S(2)}, u32[]{:S(2)}) collective-permute-start(f32[128,256]{1,0:T(8,128)S(1)} %get-tuple-element.128), channel_id=1, source_target_pairs={{0,12},{4,0},{8,4},{12,8},{1,13},{5,1},{9,5},{13,9},{2,14},{6,2},{... | collective-permute-start | bytes 393224 | tf_op jit(solution)/shard_map/ppermute | solution.py:365
  25.0 3.2 %turn_1.1 = (bf16[2,1024,512]{2,1,0:T(8,128)(2,1)S(1)}, bf16[2,1024,512]{2,1,0:T(8,128)(2,1)S(1)}) custom-call(f32[1024,16,128]{2,1,0:T(8,128)} %bitcast.46), custom_call_target="tpu_custom_call" | custom-call | flops 1000000 | bytes 1048576 | tf_op jit(solution)/shard_map/turn_1/pallas_call | solution.py:405
  28.2 1.1 collective-permute-done.3.p1
  30.4 1.9 %collective-permute-done.6.refs_2_ = f32[4,128,256]{2,1,0:T(8,128)S(1)} collective-permute-done((f32[4,128,256]{2,1,0:T(8,128)S(1)}, f32[4,128,256]{2,1,0:T(8,128)S(1)}, u32[]{:S(2)}, u32[]{:S(2)}) %collective-permute-start.6) | collective-permute-done | bytes 524320 | tf_op jit(solution)/shard_map/ppermute | solution.py:369
  32.3 3.0 %collective-permute-start.10 = (f32[4,128,256]{2,1,0:T(8,128)S(1)}, f32[4,128,256]{2,1,0:T(8,128)S(1)}, u32[]{:S(2)}, u32[]{:S(2)}) collective-permute-start(f32[4,128,256]{2,1,0:T(8,128)S(1)} %pack.3.refs_1_), channel_id=1, source_target_pairs={{0,2},{2,0},{1,3},{3,1},{4,6},{6,4},{5,7},{7,5},{8,10},{10,8},{9,1... | collective-permute-start | bytes 1572872 | tf_op jit(solution)/shard_map/ppermute | solution.py:369
  35.3 1.6 %prepare.1 = (bf16[2,256,1024]{2,1,0:T(8,128)(2,1)S(1)}, bf16[2,256,1024]{2,1,0:T(8,128)(2,1)S(1)}, f32[512,128]{1,0:T(8,128)S(1)}, f32[512,128]{1,0:T(8,128)S(1)}, f32[1,512]{1,0:T(1,128)S(1)}) custom-call(s32[4]{0:T(128)S(1)} %pad_add_fusion.idx.refs_0_, f32[1024,4,128]{2,1,0:T(4,128)S(1)} %bitcast.40, f32[4096,128]{1,0:T(8,128)} %lift_hbm, ...), custom_call_target="tpu_custom_call" | custom-call | flops 1000000 | bytes 1048576 | tf_op jit(solution)/shard_map/prepare/pallas_call | solution.py:434
  36.9 7.2 %forward_a.1 = (f32[2,1024,256]{2,1,0:T(8,128)S(1)}, f32[512,256]{1,0:T(8,128)S(1)}, f32[264,128]{1,0:T(8,128)S(1)}) custom-call(s32[4]{0:T(128)S(1)} %pad_add_fusion.idx.refs_0_, f32[4,128,256]{2,1,0:T(8,128)S(1)} %pack.3.refs_1_, f32[4,128,256]{2,1,0:T(8,128)S(1)} %collective-permute-done.6.refs_2_, f32[4,128,256]{2,1,0:T(8,128)S(1)} %collective-permute-done.7.refs_3_, ...), custom_call_target="tpu_custom_call" | custom-call | flops 1000000 | bytes 1048576 | tf_op jit(solution)/shard_map/forward_a/pallas_call | solution.py:445
  44.1 0.7 collective-permute-start.9
  44.8 2.5 %pick.1 = (bf16[2,256,1024]{2,1,0:T(8,128)(2,1)S(1)}, bf16[2,256,1024]{2,1,0:T(8,128)(2,1)S(1)}) custom-call(s32[4]{0:T(128)S(1)} %pad_add_fusion.idx.refs_0_, f32[1024,16,128]{2,1,0:T(8,128)} %bitcast.47), custom_call_target="tpu_custom_call" | custom-call | flops 1000000 | bytes 1048576 | tf_op jit(solution)/shard_map/pick/pallas_call | solution.py:466
  47.8 0.7 collective-permute-done.10.refs_2_
  48.5 2.6 %collective-permute-done.9 = f32[264,128]{1,0:T(8,128)S(1)} collective-permute-done((f32[264,128]{1,0:T(8,128)S(1)}, f32[264,128]{1,0:T(8,128)S(1)}, u32[]{:S(2)}, u32[]{:S(2)}) %collective-permute-start.9) | collective-permute-done | bytes 135200 | tf_op jit(solution)/shard_map/ppermute | solution.py:369
  51.1 1.7 %collective-permute-start.11 = (f32[264,128]{1,0:T(8,128)S(1)}, f32[264,128]{1,0:T(8,128)S(1)}, u32[]{:S(2)}, u32[]{:S(2)}) collective-permute-start(f32[264,128]{1,0:T(8,128)S(1)} %add.16), channel_id=1, source_target_pairs={{0,32},{16,48},{32,0},{48,16},{64,96},{80,112},{96,64},{112,80},{1... | collective-permute-start | bytes 405512 | tf_op jit(solution)/shard_map/ppermute | solution.py:369
  53.0 3.6 %forward_b0.1 = (f32[1,1024,256]{2,1,0:T(8,128)S(1)}, f32[256,256]{1,0:T(8,128)S(1)}) custom-call(s32[4]{0:T(128)S(1)} %pad_add_fusion.idx.refs_0_, f32[4,128,256]{2,1,0:T(8,128)S(1)} %pack.2.refs_1_.refs_2_, f32[4,128,256]{2,1,0:T(8,128)S(1)} %collective-permute-done.10.refs_2_, f32[4,128,256]{2,1,0:T(8,128)S(1)} %collective-permute-done.12.refs_3_, ...), custom_call_target="tpu_custom_call" | custom-call | flops 4000000000 | bytes 1048576 | tf_op jit(solution)/shard_map/forward_b0/pallas_call | solution.py:455
  57.2 3.1 %collective-permute-start.14 = (f32[264,128]{1,0:T(8,128)S(1)}, f32[264,128]{1,0:T(8,128)S(1)}, u32[]{:S(2)}, u32[]{:S(2)}) collective-permute-start(f32[264,128]{1,0:T(8,128)S(1)} %add.17.mine), channel_id=1, source_target_pairs={{0,96},{16,112},{32,64},{48,80},{64,32},{80,48},{96,0},{112,16},{1... | collective-permute-start | bytes 405512 | tf_op jit(solution)/shard_map/ppermute | solution.py:369
  60.3 3.6 %forward_b1.1 = (f32[1,1024,256]{2,1,0:T(8,128)S(1)}, f32[256,256]{1,0:T(8,128)S(1)}) custom-call(s32[4]{0:T(128)S(1)} %pad_add_fusion.idx.refs_0_, f32[4,128,256]{2,1,0:T(8,128)S(1)} %pack.2.refs_1_.refs_2_, f32[4,128,256]{2,1,0:T(8,128)S(1)} %collective-permute-done.10.refs_2_, f32[4,128,256]{2,1,0:T(8,128)S(1)} %collective-permute-done.12.refs_3_, ...), custom_call_target="tpu_custom_call" | custom-call | flops 4000000000 | bytes 1048576 | tf_op jit(solution)/shard_map/forward_b1/pallas_call | solution.py:455
  64.0 1.2 logit.1
  65.1 2.0 %collective-permute-start.19 = (f32[264,128]{1,0:T(8,128)S(1)}, f32[264,128]{1,0:T(8,128)S(1)}, u32[]{:S(2)}, u32[]{:S(2)}) collective-permute-start(f32[264,128]{1,0:T(8,128)S(1)} %get-tuple-element.159.refs_1_), channel_id=1, source_target_pairs={{0,2},{2,0},{1,3},{3,1},{4,6},{6,4},{5,7},{7,5},{8,10},{10,8},{9,1... | collective-permute-start | bytes 405512 | tf_op jit(solution)/shard_map/ppermute | solution.py:369
  67.2 4.6 %grads_a.1 = (bf16[2,1024,256]{2,1,0:T(8,128)(2,1)S(1)}, bf16[2,1024,256]{2,1,0:T(8,128)(2,1)S(1)}, f32[2,256,256]{2,1,0:T(8,128)S(1)}, f32[2,64,256]{2,1,0:T(8,...) custom-call(s32[4]{0:T(128)S(1)} %pad_add_fusion.idx.refs_0_, ...), custom_call_target="tpu_custom_call" | custom-call | flops 4000000000 | bytes 1048576 | tf_op jit(solution)/shard_map/grads_a/pallas_call | solution.py:495
  71.8 0.9 collective-permute-done.19.refs_1_
  72.6 1.0 collective-permute-start.16
  73.7 2.2 %collective-permute-start.17 = (f32[2,64,256]{2,1,0:T(8,128)S(1)}, f32[2,64,256]{2,1,0:T(8,128)S(1)}, u32[]{:S(2)}, u32[]{:S(2)}) collective-permute-start(f32[2,64,256]{2,1,0:T(8,128)S(1)} %get-tuple-element.167), channel_id=1, source_target_pairs={{0,8},{4,12},{8,0},{12,4},{1,9},{5,13},{9,1},{13,5},{2,10},{6,14},... | collective-permute-start | bytes 393224 | tf_op jit(solution)/shard_map/ppermute | solution.py:365
  76.3 2.7 %grads_b0.1 = (bf16[1,1024,256]{2,1,0:T(8,128)(2,1)S(1)}, bf16[1,1024,256]{2,1,0:T(8,128)(2,1)S(1)}, f32[1,256,256]{2,1,0:T(8,128)S(1)}, f32[1,64,256]{2,1,0:T(8...) custom-call(s32[4]{0:T(128)S(1)} %pad_add_fusion.idx.refs_0_, ...), custom_call_target="tpu_custom_call" | custom-call | flops 4000000000 | bytes 1048576 | tf_op jit(solution)/shard_map/grads_b0/pallas_call | solution.py:495
  79.0 1.8 %weights_0.1 = (f32[80,1024]{1,0:T(8,128)S(1)}, f32[80,1024]{1,0:T(8,128)S(1)}, f32[96,1024]{1,0:T(8,128)S(1)}, f32[96,1024]{1,0:T(8,128)S(1)}) custom-call(s32[4]{0:T(128)S(1)} %pad_add_fusion.idx.refs_0_, f32[4,128,256]{2,1,0:T(8,128)S(1)} %pack.3.refs_1_, f32[4,128,256]{2,1,0:T(8,128)S(1)} %pack.2.refs_1_.refs_2_, ...), custom_call_target="tpu_custom_call" | custom-call | flops 3000000000 | bytes 1048576 | tf_op jit(solution)/shard_map/weights_0/pallas_call | solution.py:510
  80.8 1.6 %collective-permute-start.21 = (f32[96,1024]{1,0:T(8,128)S(1)}, f32[96,1024]{1,0:T(8,128)S(1)}, u32[]{:S(2)}, u32[]{:S(2)}) collective-permute-start(f32[96,1024]{1,0:T(8,128)S(1)} %get-tuple-element.183), channel_id=1, source_target_pairs={{0,4},{4,8},{8,12},{12,0},{1,5},{5,9},{9,13},{13,1},{2,6},{6,10},{... | collective-permute-start | bytes 1179656 | tf_op jit(solution)/shard_map/ppermute | solution.py:365
  82.4 1.7 %collective-permute-start.22 = (f32[96,1024]{1,0:T(8,128)S(1)}, f32[96,1024]{1,0:T(8,128)S(1)}, u32[]{:S(2)}, u32[]{:S(2)}) collective-permute-start(f32[96,1024]{1,0:T(8,128)S(1)} %get-tuple-element.184), channel_id=1, source_target_pairs={{0,12},{4,0},{8,4},{12,8},{1,13},{5,1},{9,5},{13,9},{2,14},{6,2},{... | collective-permute-start | bytes 1179656 | tf_op jit(solution)/shard_map/ppermute | solution.py:365
  84.1 2.6 %grads_b1.1 = (bf16[1,1024,256]{2,1,0:T(8,128)(2,1)S(1)}, bf16[1,1024,256]{2,1,0:T(8,128)(2,1)S(1)}, f32[1,256,256]{2,1,0:T(8,128)S(1)}, f32[1,64,256]{2,1,0:T(8...) custom-call(s32[4]{0:T(128)S(1)} %pad_add_fusion.idx.refs_0_, ...), custom_call_target="tpu_custom_call" | custom-call | flops 4000000000 | bytes 1048576 | tf_op jit(solution)/shard_map/grads_b1/pallas_call | solution.py:495
  86.8 2.1 %weights_1.1 = (f32[88,1024]{1,0:T(8,128)S(1)}, f32[104,1024]{1,0:T(8,128)S(1)}, f32[104,1024]{1,0:T(8,128)S(1)}, f32[88,1024]{1,0:T(8,128)S(1)}, f32[32,1024]{1,0:T(8,128)S(1)}) custom-call(s32[4]{0:T(128)S(1)} %pad_add_fusion.idx.refs_0_, f32[4,128,256]{2,1,0:T(8,128)S(1)} %pack.3.refs_1_, f32[4,128,256]{2,1,0:T(8,128)S(1)} %pack.2.refs_1_.refs_2_, ...), custom_call_target="tpu_custom_call" | custom-call | flops 3000000000 | bytes 1048576 | tf_op jit(solution)/shard_map/weights_1/pallas_call | solution.py:510
  88.9 1.7 %collective-permute-start.23 = (f32[104,1024]{1,0:T(8,128)S(1)}, f32[104,1024]{1,0:T(8,128)S(1)}, u32[]{:S(2)}, u32[]{:S(2)}) collective-permute-start(f32[104,1024]{1,0:T(8,128)S(1)} %get-tuple-element.199), channel_id=1, source_target_pairs={{0,12},{4,0},{8,4},{12,8},{1,13},{5,1},{9,5},{13,9},{2,14},{6,2},{... | collective-permute-start | bytes 1277960 | tf_op jit(solution)/shard_map/ppermute | solution.py:365
  91.0 1.3 %collective-permute-start.25 = (f32[32,1024]{1,0:T(8,128)S(1)}, f32[32,1024]{1,0:T(8,128)S(1)}, u32[]{:S(2)}, u32[]{:S(2)}) collective-permute-start(f32[32,1024]{1,0:T(8,128)S(1)} %get-tuple-element.203), channel_id=1, source_target_pairs={{0,8},{4,12},{8,0},{12,4},{1,9},{5,13},{9,1},{13,5},{2,10},{6,14},... | collective-permute-start | bytes 393224 | tf_op jit(solution)/shard_map/ppermute | solution.py:365
  92.2 0.8 collective-permute-done.21.w_up
  93.1 1.4 %collective-permute-done.22.w_down.refs_2_ = f32[96,1024]{1,0:T(8,128)S(1)} collective-permute-done((f32[96,1024]{1,0:T(8,128)S(1)}, f32[96,1024]{1,0:T(8,128)S(1)}, u32[]{:S(2)}, u32[]{:S(2)}) %collective-permute-start.22) | collective-permute-done | bytes 393248 | tf_op jit(solution)/shard_map/ppermute | solution.py:365
  94.5 1.0 collective-permute-start.26
  95.5 8.8 %collective-permute-done.23.v_down = f32[104,1024]{1,0:T(8,128)S(1)} collective-permute-done((f32[104,1024]{1,0:T(8,128)S(1)}, f32[104,1024]{1,0:T(8,128)S(1)}, u32[]{:S(2)}, u32[]{:S(2)}) %collective-permute-start.23) | collective-permute-done | bytes 426016 | tf_op jit(solution)/shard_map/ppermute | solution.py:365
  104.3 3.0 %collective-permute-done.24.v_up.refs_4_ = f32[104,1024]{1,0:T(8,128)S(1)} collective-permute-done((f32[104,1024]{1,0:T(8,128)S(1)}, f32[104,1024]{1,0:T(8,128)S(1)}, u32[]{:S(2)}, u32[]{:S(2)}) %collective-permute-start.24) | collective-permute-done | bytes 426016 | tf_op jit(solution)/shard_map/ppermute | solution.py:365
  107.4 0.7 collective-permute-start.27
  108.1 2.8 %update.1 = (f32[2,64,512]{2,1,0:T(8,128)}, f32[2,512]{1,0:T(2,128)S(1)}) custom-call(s32[4]{0:T(128)S(1)} %pad_add_fusion.idx.refs_0_, f32[2,64,256]{2,1,0:T(8,128)S(1)} %get-tuple-element.165.ga0, f32[2,64,256]{2,1,0:T(8,128)S(1)} %collective-permute-done.16.refs_11_.ga1, f32[2,64,256]{2,1,0:T(8,128)S(1)} %collective-permute-done.17.refs_12_.ga2, ...), custom_call_target="tpu_custom_call" | custom-call | flops 5000000000 | bytes 1048576 | tf_op jit(solution)/shard_map/update/pallas_call | solution.py:540
  111.5 1.7 %collective-permute-done.26.refs_1_ = f32[80,1024]{1,0:T(8,128)S(1)} collective-permute-done((f32[80,1024]{1,0:T(8,128)S(1)}, f32[80,1024]{1,0:T(8,128)S(1)}, u32[]{:S(2)}, u32[]{:S(2)}) %collective-permute-start.26) | collective-permute-done | bytes 327712 | tf_op jit(solution)/shard_map/ppermute | solution.py:365
  113.1 1.8 %collective-permute-done.27.refs_5_ = f32[88,1024]{1,0:T(8,128)S(1)} collective-permute-done((f32[88,1024]{1,0:T(8,128)S(1)}, f32[88,1024]{1,0:T(8,128)S(1)}, u32[]{:S(2)}, u32[]{:S(2)}) %collective-permute-start.27) | collective-permute-done | bytes 360480 | tf_op jit(solution)/shard_map/ppermute | solution.py:365
  114.9 1.6 %sum.1 = (f32[1024,128]{1,0:T(8,128)}, f32[256,128]{1,0:T(8,128)}, f32[32,128]{1,0:T(8,128)}, f32[32,128]{1,0:T(8,128)}) custom-call(s32[4]{0:T(128)S(1)} %pad_add_fusion.idx.refs_0_, f32[1,512]{1,0:T(1,128)S(1)} %get-tuple-element.142.refs_13_.refs_10_.head, f32[80,1024]{1,0:T(8,128)S(1)} %get-tuple-element.208.refs_0_, ...), custom_call_target="tpu_custom_call" | custom-call | flops 1000000 | bytes 1048576 | tf_op jit(solution)/shard_map/sum/pallas_call | solution.py:543
  (43 shorter events, 4.7 us)
Async XLA Ops:
  4.7 12.5 %collective-permute-start = (f32[128,256]{1,0:T(8,128)S(1)}, f32[128,256]{1,0:T(8,128)S(1)}, u32[]{:S(2)}, u32[]{:S(2)}) collective-permute-start(f32[128,256]{1,0:T(8,128)S(1)} %get-tuple-element.115), channel_id=1, source_target_pairs={{0,4},{4,8},{8,12},{12,0},{1,5},{5,9},{9,13},{13,1},{2,6},{6,10},{... | collective-permute-start | bytes 393224 | tf_op jit(solution)/shard_map/ppermute | solution.py:365
  6.8 10.5 %collective-permute-start.1 = (f32[128,256]{1,0:T(8,128)S(1)}, f32[128,256]{1,0:T(8,128)S(1)}, u32[]{:S(2)}, u32[]{:S(2)}) collective-permute-start(f32[128,256]{1,0:T(8,128)S(1)} %get-tuple-element.116), channel_id=1, source_target_pairs={{0,8},{4,12},{8,0},{12,4},{1,9},{5,13},{9,1},{13,5},{2,10},{6,14},... | collective-permute-start | bytes 393224 | tf_op jit(solution)/shard_map/ppermute | solution.py:365
  10.4 6.9 %collective-permute-start.2 = (f32[128,256]{1,0:T(8,128)S(1)}, f32[128,256]{1,0:T(8,128)S(1)}, u32[]{:S(2)}, u32[]{:S(2)}) collective-permute-start(f32[128,256]{1,0:T(8,128)S(1)} %get-tuple-element.117), channel_id=1, source_target_pairs={{0,12},{4,0},{8,4},{12,8},{1,13},{5,1},{9,5},{13,9},{2,14},{6,2},{... | collective-permute-start | bytes 393224 | tf_op jit(solution)/shard_map/ppermute | solution.py:365
  17.9 14.4 %collective-permute-start.6 = (f32[4,128,256]{2,1,0:T(8,128)S(1)}, f32[4,128,256]{2,1,0:T(8,128)S(1)}, u32[]{:S(2)}, u32[]{:S(2)}) collective-permute-start(f32[4,128,256]{2,1,0:T(8,128)S(1)} %pack.2.refs_1_.refs_2_), channel_id=1, source_target_pairs={{0,2},{2,0},{1,3},{3,1},{4,6},{6,4},{5,7},{7,5},{8,10},{10,8},{9,1... | collective-permute-start | bytes 1572872 | tf_op jit(solution)/shard_map/ppermute | solution.py:369
  21.0 8.3 %collective-permute-start.3 = (f32[128,256]{1,0:T(8,128)S(1)}, f32[128,256]{1,0:T(8,128)S(1)}, u32[]{:S(2)}, u32[]{:S(2)}) collective-permute-start(f32[128,256]{1,0:T(8,128)S(1)} %get-tuple-element.126), channel_id=1, source_target_pairs={{0,4},{4,8},{8,12},{12,0},{1,5},{5,9},{9,13},{13,1},{2,6},{6,10},{... | collective-permute-start | bytes 393224 | tf_op jit(solution)/shard_map/ppermute | solution.py:365
  22.0 7.3 %collective-permute-start.4 = (f32[128,256]{1,0:T(8,128)S(1)}, f32[128,256]{1,0:T(8,128)S(1)}, u32[]{:S(2)}, u32[]{:S(2)}) collective-permute-start(f32[128,256]{1,0:T(8,128)S(1)} %get-tuple-element.127), channel_id=1, source_target_pairs={{0,8},{4,12},{8,0},{12,4},{1,9},{5,13},{9,1},{13,5},{2,10},{6,14},... | collective-permute-start | bytes 393224 | tf_op jit(solution)/shard_map/ppermute | solution.py:365
  23.7 11.6 %copy-start.1 = (f32[4096]{0:T(1024)S(1)}, f32[4096]{0:T(1024)}, u32[]{:S(2)}) copy-start(f32[4096]{0:T(1024)} %param.20) | copy-start | bytes 49156
  23.7 6.0 %collective-permute-start.5 = (f32[128,256]{1,0:T(8,128)S(1)}, f32[128,256]{1,0:T(8,128)S(1)}, u32[]{:S(2)}, u32[]{:S(2)}) collective-permute-start(f32[128,256]{1,0:T(8,128)S(1)} %get-tuple-element.128), channel_id=1, source_target_pairs={{0,12},{4,0},{8,4},{12,8},{1,13},{5,1},{9,5},{13,9},{2,14},{6,2},{... | collective-permute-start | bytes 393224 | tf_op jit(solution)/shard_map/ppermute | solution.py:365
  25.0 10.3 %copy-start = (f32[1024,2,256]{2,1,0:T(2,128)S(1)}, f32[1024,2,256]{2,1,0:T(2,128)}, u32[]{:S(2)}) copy-start(f32[1024,2,256]{2,1,0:T(2,128)} %param.17) | copy-start | bytes 6291460
  30.3 6.6 %collective-permute-start.7 = (f32[4,128,256]{2,1,0:T(8,128)S(1)}, f32[4,128,256]{2,1,0:T(8,128)S(1)}, u32[]{:S(2)}, u32[]{:S(2)}) collective-permute-start(f32[4,128,256]{2,1,0:T(8,128)S(1)} %pack.3.refs_1_), channel_id=1, source_target_pairs={{0,1},{1,0},{2,3},{3,2},{4,5},{5,4},{6,7},{7,6},{8,9},{9,8},{10,11... | collective-permute-start | bytes 1572872 | tf_op jit(solution)/shard_map/ppermute | solution.py:369
  32.3 4.6 %collective-permute-start.8 = (f32[4,128,256]{2,1,0:T(8,128)S(1)}, f32[4,128,256]{2,1,0:T(8,128)S(1)}, u32[]{:S(2)}, u32[]{:S(2)}) collective-permute-start(f32[4,128,256]{2,1,0:T(8,128)S(1)} %collective-permute-done.6.refs_2_), channel_id=1, source_target_pairs={{0,1},{1,0},{2,3},{3,2},{4,5},{5,4},{6,7},{7,6},{8,9},{9,8},{10,11... | collective-permute-start | bytes 1572872 | tf_op jit(solution)/shard_map/ppermute | solution.py:369
  32.3 16.2 %collective-permute-start.10 = (f32[4,128,256]{2,1,0:T(8,128)S(1)}, f32[4,128,256]{2,1,0:T(8,128)S(1)}, u32[]{:S(2)}, u32[]{:S(2)}) collective-permute-start(f32[4,128,256]{2,1,0:T(8,128)S(1)} %pack.3.refs_1_), channel_id=1, source_target_pairs={{0,2},{2,0},{1,3},{3,1},{4,6},{6,4},{5,7},{7,5},{8,10},{10,8},{9,1... | collective-permute-start | bytes 1572872 | tf_op jit(solution)/shard_map/ppermute | solution.py:369
  44.1 7.0 %collective-permute-start.9 = (f32[264,128]{1,0:T(8,128)S(1)}, f32[264,128]{1,0:T(8,128)S(1)}, u32[]{:S(2)}, u32[]{:S(2)}) collective-permute-start(f32[264,128]{1,0:T(8,128)S(1)} %get-tuple-element.144), channel_id=1, source_target_pairs={{0,16},{16,0},{32,48},{48,32},{64,80},{80,64},{96,112},{112,96},{1... | collective-permute-start | bytes 405512 | tf_op jit(solution)/shard_map/ppermute | solution.py:369
  44.8 8.0 %collective-permute-start.12 = (f32[4,128,256]{2,1,0:T(8,128)S(1)}, f32[4,128,256]{2,1,0:T(8,128)S(1)}, u32[]{:S(2)}, u32[]{:S(2)}) collective-permute-start(f32[4,128,256]{2,1,0:T(8,128)S(1)} %pack.2.refs_1_.refs_2_), channel_id=1, source_target_pairs={{0,1},{1,0},{2,3},{3,2},{4,5},{5,4},{6,7},{7,6},{8,9},{9,8},{10,11... | collective-permute-start | bytes 1572872 | tf_op jit(solution)/shard_map/ppermute | solution.py:369
  51.1 1.9 %collective-permute-start.13 = (f32[4,128,256]{2,1,0:T(8,128)S(1)}, f32[4,128,256]{2,1,0:T(8,128)S(1)}, u32[]{:S(2)}, u32[]{:S(2)}) collective-permute-start(f32[4,128,256]{2,1,0:T(8,128)S(1)} %collective-permute-done.10.refs_2_), channel_id=1, source_target_pairs={{0,1},{1,0},{2,3},{3,2},{4,5},{5,4},{6,7},{7,6},{8,9},{9,8},{10,11... | collective-permute-start | bytes 1572872 | tf_op jit(solution)/shard_map/ppermute | solution.py:369
  51.1 6.1 %collective-permute-start.11 = (f32[264,128]{1,0:T(8,128)S(1)}, f32[264,128]{1,0:T(8,128)S(1)}, u32[]{:S(2)}, u32[]{:S(2)}) collective-permute-start(f32[264,128]{1,0:T(8,128)S(1)} %add.16), channel_id=1, source_target_pairs={{0,32},{16,48},{32,0},{48,16},{64,96},{80,112},{96,64},{112,80},{1... | collective-permute-start | bytes 405512 | tf_op jit(solution)/shard_map/ppermute | solution.py:369
  57.2 6.7 %copy-start.2 = (s32[1,128]{1,0:T(1,128)S(1)}, s32[1,128]{1,0:T(1,128)}, u32[]{:S(2)}) copy-start(s32[1,128]{1,0:T(1,128)} %labels.1) | copy-start | bytes 1540
  57.2 6.7 %collective-permute-start.14 = (f32[264,128]{1,0:T(8,128)S(1)}, f32[264,128]{1,0:T(8,128)S(1)}, u32[]{:S(2)}, u32[]{:S(2)}) collective-permute-start(f32[264,128]{1,0:T(8,128)S(1)} %add.17.mine), channel_id=1, source_target_pairs={{0,96},{16,112},{32,64},{48,80},{64,32},{80,48},{96,0},{112,16},{1... | collective-permute-start | bytes 405512 | tf_op jit(solution)/shard_map/ppermute | solution.py:369
  65.1 2.0 %collective-permute-start.15 = (f32[264,128]{1,0:T(8,128)S(1)}, f32[264,128]{1,0:T(8,128)S(1)}, u32[]{:S(2)}, u32[]{:S(2)}) collective-permute-start(f32[264,128]{1,0:T(8,128)S(1)} %get-tuple-element.159.refs_1_), channel_id=1, source_target_pairs={{0,1},{1,0},{2,3},{3,2},{4,5},{5,4},{6,7},{7,6},{8,9},{9,8},{10,11... | collective-permute-start | bytes 405512 | tf_op jit(solution)/shard_map/ppermute | solution.py:369
  65.1 7.5 %collective-permute-start.19 = (f32[264,128]{1,0:T(8,128)S(1)}, f32[264,128]{1,0:T(8,128)S(1)}, u32[]{:S(2)}, u32[]{:S(2)}) collective-permute-start(f32[264,128]{1,0:T(8,128)S(1)} %get-tuple-element.159.refs_1_), channel_id=1, source_target_pairs={{0,2},{2,0},{1,3},{3,1},{4,6},{6,4},{5,7},{7,5},{8,10},{10,8},{9,1... | collective-permute-start | bytes 405512 | tf_op jit(solution)/shard_map/ppermute | solution.py:369
  72.6 3.7 %collective-permute-start.20 = (f32[264,128]{1,0:T(8,128)S(1)}, f32[264,128]{1,0:T(8,128)S(1)}, u32[]{:S(2)}, u32[]{:S(2)}) collective-permute-start(f32[264,128]{1,0:T(8,128)S(1)} %collective-permute-done.19.refs_1_), channel_id=1, source_target_pairs={{0,1},{1,0},{2,3},{3,2},{4,5},{5,4},{6,7},{7,6},{8,9},{9,8},{10,11... | collective-permute-start | bytes 405512 | tf_op jit(solution)/shard_map/ppermute | solution.py:369
  72.6 11.5 %collective-permute-start.16 = (f32[2,64,256]{2,1,0:T(8,128)S(1)}, f32[2,64,256]{2,1,0:T(8,128)S(1)}, u32[]{:S(2)}, u32[]{:S(2)}) collective-permute-start(f32[2,64,256]{2,1,0:T(8,128)S(1)} %get-tuple-element.166), channel_id=1, source_target_pairs={{0,4},{4,8},{8,12},{12,0},{1,5},{5,9},{9,13},{13,1},{2,6},{6,10},{... | collective-permute-start | bytes 393224 | tf_op jit(solution)/shard_map/ppermute | solution.py:365
  73.7 10.5 %collective-permute-start.17 = (f32[2,64,256]{2,1,0:T(8,128)S(1)}, f32[2,64,256]{2,1,0:T(8,128)S(1)}, u32[]{:S(2)}, u32[]{:S(2)}) collective-permute-start(f32[2,64,256]{2,1,0:T(8,128)S(1)} %get-tuple-element.167), channel_id=1, source_target_pairs={{0,8},{4,12},{8,0},{12,4},{1,9},{5,13},{9,1},{13,5},{2,10},{6,14},... | collective-permute-start | bytes 393224 | tf_op jit(solution)/shard_map/ppermute | solution.py:365
  75.8 8.3 %collective-permute-start.18 = (f32[2,64,256]{2,1,0:T(8,128)S(1)}, f32[2,64,256]{2,1,0:T(8,128)S(1)}, u32[]{:S(2)}, u32[]{:S(2)}) collective-permute-start(f32[2,64,256]{2,1,0:T(8,128)S(1)} %get-tuple-element.168), channel_id=1, source_target_pairs={{0,12},{4,0},{8,4},{12,8},{1,13},{5,1},{9,5},{13,9},{2,14},{6,2},{... | collective-permute-start | bytes 393224 | tf_op jit(solution)/shard_map/ppermute | solution.py:365
  80.8 12.2 %collective-permute-start.21 = (f32[96,1024]{1,0:T(8,128)S(1)}, f32[96,1024]{1,0:T(8,128)S(1)}, u32[]{:S(2)}, u32[]{:S(2)}) collective-permute-start(f32[96,1024]{1,0:T(8,128)S(1)} %get-tuple-element.183), channel_id=1, source_target_pairs={{0,4},{4,8},{8,12},{12,0},{1,5},{5,9},{9,13},{13,1},{2,6},{6,10},{... | collective-permute-start | bytes 1179656 | tf_op jit(solution)/shard_map/ppermute | solution.py:365
  82.4 12.1 %collective-permute-start.22 = (f32[96,1024]{1,0:T(8,128)S(1)}, f32[96,1024]{1,0:T(8,128)S(1)}, u32[]{:S(2)}, u32[]{:S(2)}) collective-permute-start(f32[96,1024]{1,0:T(8,128)S(1)} %get-tuple-element.184), channel_id=1, source_target_pairs={{0,12},{4,0},{8,4},{12,8},{1,13},{5,1},{9,5},{13,9},{2,14},{6,2},{... | collective-permute-start | bytes 1179656 | tf_op jit(solution)/shard_map/ppermute | solution.py:365
  86.8 4.2 %copy-start.3 = (f32[2,1,512]{2,1,0:T(1,128)S(1)}, f32[2,1,512]{2,1,0:T(1,128)}, u32[]{:S(2)}) copy-start(f32[2,1,512]{2,1,0:T(1,128)} %param.15) | copy-start | bytes 12292
  88.9 15.4 %collective-permute-start.23 = (f32[104,1024]{1,0:T(8,128)S(1)}, f32[104,1024]{1,0:T(8,128)S(1)}, u32[]{:S(2)}, u32[]{:S(2)}) collective-permute-start(f32[104,1024]{1,0:T(8,128)S(1)} %get-tuple-element.199), channel_id=1, source_target_pairs={{0,12},{4,0},{8,4},{12,8},{1,13},{5,1},{9,5},{13,9},{2,14},{6,2},{... | collective-permute-start | bytes 1277960 | tf_op jit(solution)/shard_map/ppermute | solution.py:365
  90.6 16.7 %collective-permute-start.24 = (f32[104,1024]{1,0:T(8,128)S(1)}, f32[104,1024]{1,0:T(8,128)S(1)}, u32[]{:S(2)}, u32[]{:S(2)}) collective-permute-start(f32[104,1024]{1,0:T(8,128)S(1)} %get-tuple-element.200), channel_id=1, source_target_pairs={{0,4},{4,8},{8,12},{12,0},{1,5},{5,9},{9,13},{13,1},{2,6},{6,10},{... | collective-permute-start | bytes 1277960 | tf_op jit(solution)/shard_map/ppermute | solution.py:365
  91.0 17.1 %collective-permute-start.25 = (f32[32,1024]{1,0:T(8,128)S(1)}, f32[32,1024]{1,0:T(8,128)S(1)}, u32[]{:S(2)}, u32[]{:S(2)}) collective-permute-start(f32[32,1024]{1,0:T(8,128)S(1)} %get-tuple-element.203), channel_id=1, source_target_pairs={{0,8},{4,12},{8,0},{12,4},{1,9},{5,13},{9,1},{13,5},{2,10},{6,14},... | collective-permute-start | bytes 393224 | tf_op jit(solution)/shard_map/ppermute | solution.py:365
  94.5 18.6 %collective-permute-start.26 = (f32[80,1024]{1,0:T(8,128)S(1)}, f32[80,1024]{1,0:T(8,128)S(1)}, u32[]{:S(2)}, u32[]{:S(2)}) collective-permute-start(f32[80,1024]{1,0:T(8,128)S(1)} %slice_add_fusion.1), channel_id=1, source_target_pairs={{0,4},{4,8},{8,12},{12,0},{1,5},{5,9},{9,13},{13,1},{2,6},{6,10},{... | collective-permute-start | bytes 983048 | tf_op jit(solution)/shard_map/ppermute | solution.py:365
  107.4 7.5 %collective-permute-start.27 = (f32[88,1024]{1,0:T(8,128)S(1)}, f32[88,1024]{1,0:T(8,128)S(1)}, u32[]{:S(2)}, u32[]{:S(2)}) collective-permute-start(f32[88,1024]{1,0:T(8,128)S(1)} %slice_add_fusion), channel_id=1, source_target_pairs={{0,12},{4,0},{8,4},{12,8},{1,13},{5,1},{9,5},{13,9},{2,14},{6,2},{... | collective-permute-start | bytes 1081352 | tf_op jit(solution)/shard_map/ppermute | solution.py:365

commit v7 on v6

--- a/solution.py
+++ b/solution.py
@@ -17,6 +17,7 @@
 TOWER = ("y", "xl")
 QUAD = ("xh", "core")
 VMEM_LIMIT = 16 << 20
+PIECE = 256
 
 
 def halves(a):
@@ -127,7 +128,7 @@
                 low[t, b * 128 : (b + 1) * 128, n * rows : (n + 1) * rows] = l
 
 
-def pick_kernel(idx, w_hbm, high, low, w, sems):
+def pick_kernel(idx, w_hbm, head, high, low, column, w, wide, sems):
     rows = w.shape[1]
     quad = 2 * idx[1] + idx[2]
     copies = []
@@ -136,6 +137,9 @@
         copies.append(pltpu.make_async_copy(w_hbm.at[pl.ds(pl.multiple_of(table * rows, rows), rows)], w.at[k], sems.at[k]))
     for copy in copies:
         copy.start()
+    wide[...] = jnp.broadcast_to(head[...], (128, head.shape[1])).T
+    device = (idx[0] * 2 + idx[1]) * 2 + idx[2]
+    column[...] = wide[pl.ds(pl.multiple_of(device * 32, 32), 32), :]
     for k, copy in enumerate(copies):
         copy.wait()
         flat = w.at[k].reshape(rows * 16, 128)
@@ -253,13 +257,18 @@
         back = dot3(halves(press[rows, :]), q)
         go = error * (column[rows] * (scaling + 1.0) + back)
         gout[slot] = go
-        ga = dot3((w2h[t], w2l[t]), halves(go))
-        value = hidden[slot]
-        s = jax.nn.sigmoid(value)
-        gh = halves(ga * (s * (1.0 + value * (1.0 - s))))
-        ghh[slot] = gh[0]
-        ghl[slot] = gh[1]
-        grad = dot3((w1h[t], w1l[t]), gh)
+        go = halves(go)
+        grad = None
+        for n in range(w2h.shape[1] // PIECE):
+            part = slice(n * PIECE, (n + 1) * PIECE)
+            ga = dot3((w2h[t, part, :], w2l[t, part, :]), go)
+            value = hidden[slot, part, :]
+            s = jax.nn.sigmoid(value)
+            gh = halves(ga * (s * (1.0 + value * (1.0 - s))))
+            ghh[slot, part, :] = gh[0]
+            ghl[slot, part, :] = gh[1]
+            out = dot3((w1h[t, :, part], w1l[t, :, part]), gh)
+            grad = out if grad is None else grad + out
         for k, out in enumerate((g0, g1, g2, g3)):
             out[slot] = grad[k * width : (k + 1) * width]
 
@@ -340,8 +349,8 @@
         new_tables[t] = decayed[t] - LEARN_RATE * grad / (jnp.sqrt(fresh) + EPSILON)
 
 
-def sum_kernel(idx, head, *refs):
-    parts, (first, second, lift, press, wide) = refs[:6], refs[6:]
+def sum_kernel(column, *refs):
+    parts, (first, second, lift, press) = refs[:6], refs[6:]
     for t in range(2):
         a, b, c = parts[3 * t : 3 * t + 3]
         total = a[...] + (b[0 : a.shape[0]] + c[0 : a.shape[0]])
@@ -352,9 +361,6 @@
                 lanes = slice(b * 256 + o * 128, b * 256 + (o + 1) * 128)
                 second[pl.ds(b * 64 + 2 * o + t, 16, stride=4), :] = total[64:80, lanes]
         if t == 1:
-            wide[...] = jnp.broadcast_to(head[...], (128, head.shape[1])).T
-            device = (idx[0] * 2 + idx[1]) * 2 + idx[2]
-            column = wide[pl.ds(pl.multiple_of(device * 32, 32), 32), :]
             for b in range(4):
                 at = slice(8 * b, 8 * b + 8)
                 lift[at, :] = column[at] * total[80:88, b * 256 : b * 256 + 128]
@@ -463,14 +469,14 @@
 
     view, second_view, pay = lax.optimization_barrier((view, second_view, pay))
     other = flip(pay, TOWER, 8, 1)
-    w1qh, w1ql = call(
+    w1qh, w1ql, column = call(
         pick_kernel,
-        [bf16(2, 256, 1024)] * 2,
-        [SMEM_SPEC, any_spec],
-        [pltpu.VMEM((4, 64, 16, 128), F32), pltpu.SemaphoreType.DMA((4,))],
+        [bf16(2, 256, 1024)] * 2 + [f32(32, 128)],
+        [SMEM_SPEC, any_spec] + vmem(1),
+        [pltpu.VMEM((4, 64, 16, 128), F32), pltpu.VMEM((local, 128), F32), pltpu.SemaphoreType.DMA((4,))],
         name="pick",
         flops=1e6,
-    )(idx, hbm(view))
+    )(idx, hbm(view), head)
     w2h, w2l = call(natural_kernel, [bf16(2, 1024, 256)] * 2, vmem(1), name="natural", flops=1e6)(second_view)
     other, w1qh, w2h, x2b = lax.optimization_barrier((other, w1qh, w2h, x2b))
     pay = pay + other
@@ -543,11 +549,10 @@
     first, second, lift_out, press_out = call(
         sum_kernel,
         [f32(1024, 128), f32(256, 128), f32(32, rank), f32(32, rank)],
-        [SMEM_SPEC] + vmem(7),
-        [pltpu.VMEM((local, 128), F32)],
+        vmem(7),
         name="sum",
         flops=1e6,
-    )(idx, head, w[0], w1, w3, v[0], v1, v3)
+    )(column, w[0], w1, w3, v[0], v1, v3)
     return (
         jnp.transpose(new_tables, (0, 2, 1))[:, None],
         new_accumulator[:, None],

time: 117 us -> 116 us (level)
  Pallas kernels: 52.6 us -> 50.3 us
    pallas_call x3, Pallas kernels: 9.91 us -> 8.17 us  [grads(): call(lambda *refs: grads_kernel(towers, with_pq, len(extra), *refs), [bf1...]
  transfers between devices with their start and end apart: 28 -> 28, of which waited for: 14 -> 14; matrix products, arithmetic and copies ran while one was open for 1% -> 1% of each run, Pallas kernels for 39% -> 38%
where the time goes in v7:
time: 116 us
  Pallas kernels  50.3 us (43%)
  starting transfers between devices  36.7 us (32%)
  waiting for transfers between devices  26.9 us (23%)
    ppermute x16, starting transfers between devices, shift(): return lax.ppermute(x, axis, [(i, (i + by) % size) for i in range(size)])  23 us
    ppermute x16, waiting for transfers between devices, shift(): return lax.ppermute(x, axis, [(i, (i + by) % size) for i in range(size)])  19.1 us
    ppermute x12, starting transfers between devices, flip(): return lax.ppermute(x, axis, [(i, i ^ bit) for i in range(size)])  13.6 us
    pallas_call x3, Pallas kernels, grads(): call(lambda *refs: grads_kernel(towers, with_pq, len(extra), *refs), [bf1...  8.17 us
    ppermute x12, waiting for transfers between devices, flip(): return lax.ppermute(x, axis, [(i, i ^ bit) for i in range(size)])  7.8 us
    pallas_call x2, Pallas kernels, later_half(): call(lambda *refs: forward_kernel((t,), False, *refs), [f32(1, 1024, 256)...  7.23 us
    pallas_call x1, Pallas kernels, per_device(): call(lambda *refs: forward_kernel((0, 1), True, *refs), [f32(2, 1024, 256...  7.18 us
    pallas_call x2, Pallas kernels, turn(): pl.pallas_call(lambda *refs: turn_kernel(at, *refs), in_specs=[any_spec],...  6.22 us
  transfers between devices with their start and end apart: 28, of which 14 were waited for; matrix products, arithmetic and copies ran while one was open for 1% of the time, Pallas kernels for 38%

profile of v7, /device:TPU:0, one launch (start us, length us, event | category | flops | bytes accessed | tf_op | source)
XLA Modules:
  0.0 115.6 jit_solution(12639127087966203594)
XLA Ops:
  0.7 4.0 %pool_far.1 = (f32[128,256]{1,0:T(8,128)S(1)}, f32[128,256]{1,0:T(8,128)S(1)}, f32[128,256]{1,0:T(8,128)S(1)}, f32[128,256]{1,0:T(8,128)S(1)}, bf16[2,4,512,256]...) custom-call(s32[4]{0:T(128)S(1)} %pad_add_fusion.idx.refs_0_, s32[2,4,2048]{2,1,0:T(4,128)} %bitcast.49, ...), custom_call_target="tpu_custom_call" | custom-call | flops 1000000 | bytes 1048576 | tf_op jit(solution)/shard_map/pool_far/pallas_call | solution.py:390
  4.7 2.1 %collective-permute-start = (f32[128,256]{1,0:T(8,128)S(1)}, f32[128,256]{1,0:T(8,128)S(1)}, u32[]{:S(2)}, u32[]{:S(2)}) collective-permute-start(f32[128,256]{1,0:T(8,128)S(1)} %get-tuple-element.116), channel_id=1, source_target_pairs={{0,4},{4,8},{8,12},{12,0},{1,5},{5,9},{9,13},{13,1},{2,6},{6,10},{... | collective-permute-start | bytes 393224 | tf_op jit(solution)/shard_map/ppermute | solution.py:371
  6.8 3.6 %collective-permute-start.1 = (f32[128,256]{1,0:T(8,128)S(1)}, f32[128,256]{1,0:T(8,128)S(1)}, u32[]{:S(2)}, u32[]{:S(2)}) collective-permute-start(f32[128,256]{1,0:T(8,128)S(1)} %get-tuple-element.117), channel_id=1, source_target_pairs={{0,8},{4,12},{8,0},{12,4},{1,9},{5,13},{9,1},{13,5},{2,10},{6,14},... | collective-permute-start | bytes 393224 | tf_op jit(solution)/shard_map/ppermute | solution.py:371
  10.4 1.0 collective-permute-start.2
  11.4 2.8 %pool_near.1 = (f32[128,256]{1,0:T(8,128)S(1)}, f32[128,256]{1,0:T(8,128)S(1)}, f32[128,256]{1,0:T(8,128)S(1)}, f32[128,256]{1,0:T(8,128)S(1)}, bf16[2,4,512,256]{3,2,1,0:T(8,128)(2,1)S(1)}) custom-call(s32[4]{0:T(128)S(1)} %pad_add_fusion.idx.refs_0_, s32[2,4,2048]{2,1,0:T(4,128)S(1)} %get-tuple-element.119.bag, f32[2,64,512]{2,1,0:T(8,128)S(1)} %get-tuple-element.113.decayed), custom_call_target="tpu_custom_call" | custom-call | flops 1000000 | bytes 1048576 | tf_op jit(solution)/shard_map/pool_near/pallas_call | solution.py:405
  14.2 3.0 %turn_0.1 = (bf16[2,1024,512]{2,1,0:T(8,128)(2,1)S(1)}, bf16[2,1024,512]{2,1,0:T(8,128)(2,1)S(1)}) custom-call(f32[1024,16,128]{2,1,0:T(8,128)} %bitcast.45), custom_call_target="tpu_custom_call" | custom-call | flops 1000000 | bytes 1048576 | tf_op jit(solution)/shard_map/turn_0/pallas_call | solution.py:411
  17.9 3.1 %collective-permute-start.6 = (f32[4,128,256]{2,1,0:T(8,128)S(1)}, f32[4,128,256]{2,1,0:T(8,128)S(1)}, u32[]{:S(2)}, u32[]{:S(2)}) collective-permute-start(f32[4,128,256]{2,1,0:T(8,128)S(1)} %pack.2.refs_1_.refs_2_), channel_id=1, source_target_pairs={{0,2},{2,0},{1,3},{3,1},{4,6},{6,4},{5,7},{7,5},{8,10},{10,8},{9,1... | collective-permute-start | bytes 1572872 | tf_op jit(solution)/shard_map/ppermute | solution.py:375
  21.0 1.0 collective-permute-start.3
  22.0 1.7 %collective-permute-start.4 = (f32[128,256]{1,0:T(8,128)S(1)}, f32[128,256]{1,0:T(8,128)S(1)}, u32[]{:S(2)}, u32[]{:S(2)}) collective-permute-start(f32[128,256]{1,0:T(8,128)S(1)} %get-tuple-element.128), channel_id=1, source_target_pairs={{0,8},{4,12},{8,0},{12,4},{1,9},{5,13},{9,1},{13,5},{2,10},{6,14},... | collective-permute-start | bytes 393224 | tf_op jit(solution)/shard_map/ppermute | solution.py:371
  23.7 1.2 %collective-permute-start.5 = (f32[128,256]{1,0:T(8,128)S(1)}, f32[128,256]{1,0:T(8,128)S(1)}, u32[]{:S(2)}, u32[]{:S(2)}) collective-permute-start(f32[128,256]{1,0:T(8,128)S(1)} %get-tuple-element.129), channel_id=1, source_target_pairs={{0,12},{4,0},{8,4},{12,8},{1,13},{5,1},{9,5},{13,9},{2,14},{6,2},{... | collective-permute-start | bytes 393224 | tf_op jit(solution)/shard_map/ppermute | solution.py:371
  25.0 3.2 %turn_1.1 = (bf16[2,1024,512]{2,1,0:T(8,128)(2,1)S(1)}, bf16[2,1024,512]{2,1,0:T(8,128)(2,1)S(1)}) custom-call(f32[1024,16,128]{2,1,0:T(8,128)} %bitcast.46), custom_call_target="tpu_custom_call" | custom-call | flops 1000000 | bytes 1048576 | tf_op jit(solution)/shard_map/turn_1/pallas_call | solution.py:411
  28.2 1.1 collective-permute-done.3.p1
  30.4 1.9 %collective-permute-done.6.refs_2_ = f32[4,128,256]{2,1,0:T(8,128)S(1)} collective-permute-done((f32[4,128,256]{2,1,0:T(8,128)S(1)}, f32[4,128,256]{2,1,0:T(8,128)S(1)}, u32[]{:S(2)}, u32[]{:S(2)}) %collective-permute-start.6) | collective-permute-done | bytes 524320 | tf_op jit(solution)/shard_map/ppermute | solution.py:375
  32.3 3.0 %collective-permute-start.10 = (f32[4,128,256]{2,1,0:T(8,128)S(1)}, f32[4,128,256]{2,1,0:T(8,128)S(1)}, u32[]{:S(2)}, u32[]{:S(2)}) collective-permute-start(f32[4,128,256]{2,1,0:T(8,128)S(1)} %pack.3.refs_1_), channel_id=1, source_target_pairs={{0,2},{2,0},{1,3},{3,1},{4,6},{6,4},{5,7},{7,5},{8,10},{10,8},{9,1... | collective-permute-start | bytes 1572872 | tf_op jit(solution)/shard_map/ppermute | solution.py:375
  35.3 1.6 %prepare.1 = (bf16[2,256,1024]{2,1,0:T(8,128)(2,1)S(1)}, bf16[2,256,1024]{2,1,0:T(8,128)(2,1)S(1)}, f32[512,128]{1,0:T(8,128)S(1)}, f32[512,128]{1,0:T(8,128)S(1)}, f32[1,512]{1,0:T(1,128)S(1)}) custom-call(s32[4]{0:T(128)S(1)} %pad_add_fusion.idx.refs_0_, f32[1024,4,128]{2,1,0:T(4,128)S(1)} %bitcast.40, f32[4096,128]{1,0:T(8,128)} %lift_hbm, ...), custom_call_target="tpu_custom_call" | custom-call | flops 1000000 | bytes 1048576 | tf_op jit(solution)/shard_map/prepare/pallas_call | solution.py:440
  36.9 7.2 %forward_a.1 = (f32[2,1024,256]{2,1,0:T(8,128)S(1)}, f32[512,256]{1,0:T(8,128)S(1)}, f32[264,128]{1,0:T(8,128)S(1)}) custom-call(s32[4]{0:T(128)S(1)} %pad_add_fusion.idx.refs_0_, f32[4,128,256]{2,1,0:T(8,128)S(1)} %pack.3.refs_1_, f32[4,128,256]{2,1,0:T(8,128)S(1)} %collective-permute-done.6.refs_2_, f32[4,128,256]{2,1,0:T(8,128)S(1)} %collective-permute-done.7.refs_3_, ...), custom_call_target="tpu_custom_call" | custom-call | flops 1000000 | bytes 1048576 | tf_op jit(solution)/shard_map/forward_a/pallas_call | solution.py:451
  44.1 0.7 collective-permute-start.9
  44.8 2.5 %pick.1 = (bf16[2,256,1024]{2,1,0:T(8,128)(2,1)S(1)}, bf16[2,256,1024]{2,1,0:T(8,128)(2,1)S(1)}, f32[32,128]{1,0:T(8,128)S(1)}) custom-call(s32[4]{0:T(128)S(1)} %pad_add_fusion.idx.refs_0_, f32[1024,16,128]{2,1,0:T(8,128)} %bitcast.47, f32[1,512]{1,0:T(1,128)S(1)} %get-tuple-element.143.refs_13_.head.refs_10_), custom_call_target="tpu_custom_call" | custom-call | flops 1000000 | bytes 1048576 | tf_op jit(solution)/shard_map/pick/pallas_call | solution.py:472
  47.8 0.7 collective-permute-done.10.refs_2_
  48.5 2.6 %collective-permute-done.9 = f32[264,128]{1,0:T(8,128)S(1)} collective-permute-done((f32[264,128]{1,0:T(8,128)S(1)}, f32[264,128]{1,0:T(8,128)S(1)}, u32[]{:S(2)}, u32[]{:S(2)}) %collective-permute-start.9) | collective-permute-done | bytes 135200 | tf_op jit(solution)/shard_map/ppermute | solution.py:375
  51.1 1.7 %collective-permute-start.11 = (f32[264,128]{1,0:T(8,128)S(1)}, f32[264,128]{1,0:T(8,128)S(1)}, u32[]{:S(2)}, u32[]{:S(2)}) collective-permute-start(f32[264,128]{1,0:T(8,128)S(1)} %add.16), channel_id=1, source_target_pairs={{0,32},{16,48},{32,0},{48,16},{64,96},{80,112},{96,64},{112,80},{1... | collective-permute-start | bytes 405512 | tf_op jit(solution)/shard_map/ppermute | solution.py:375
  53.0 3.6 %forward_b0.1 = (f32[1,1024,256]{2,1,0:T(8,128)S(1)}, f32[256,256]{1,0:T(8,128)S(1)}) custom-call(s32[4]{0:T(128)S(1)} %pad_add_fusion.idx.refs_0_, f32[4,128,256]{2,1,0:T(8,128)S(1)} %pack.2.refs_1_.refs_2_, f32[4,128,256]{2,1,0:T(8,128)S(1)} %collective-permute-done.10.refs_2_, f32[4,128,256]{2,1,0:T(8,128)S(1)} %collective-permute-done.12.refs_3_, ...), custom_call_target="tpu_custom_call" | custom-call | flops 4000000000 | bytes 1048576 | tf_op jit(solution)/shard_map/forward_b0/pallas_call | solution.py:461
  57.2 3.1 %collective-permute-start.14 = (f32[264,128]{1,0:T(8,128)S(1)}, f32[264,128]{1,0:T(8,128)S(1)}, u32[]{:S(2)}, u32[]{:S(2)}) collective-permute-start(f32[264,128]{1,0:T(8,128)S(1)} %add.17.mine), channel_id=1, source_target_pairs={{0,96},{16,112},{32,64},{48,80},{64,32},{80,48},{96,0},{112,16},{1... | collective-permute-start | bytes 405512 | tf_op jit(solution)/shard_map/ppermute | solution.py:375
  60.3 3.6 %forward_b1.1 = (f32[1,1024,256]{2,1,0:T(8,128)S(1)}, f32[256,256]{1,0:T(8,128)S(1)}) custom-call(s32[4]{0:T(128)S(1)} %pad_add_fusion.idx.refs_0_, f32[4,128,256]{2,1,0:T(8,128)S(1)} %pack.2.refs_1_.refs_2_, f32[4,128,256]{2,1,0:T(8,128)S(1)} %collective-permute-done.10.refs_2_, f32[4,128,256]{2,1,0:T(8,128)S(1)} %collective-permute-done.12.refs_3_, ...), custom_call_target="tpu_custom_call" | custom-call | flops 4000000000 | bytes 1048576 | tf_op jit(solution)/shard_map/forward_b1/pallas_call | solution.py:461
  64.0 1.2 %logit.1 = (f32[264,128]{1,0:T(8,128)S(1)}, f32[1,16]{1,0:T(1,128)}) custom-call(s32[4]{0:T(128)S(1)} %pad_add_fusion.idx.refs_0_, f32[264,128]{1,0:T(8,128)S(1)} %add.17.mine, f32[264,128]{1,0:T(8,128)S(1)} %collective-permute-done.14.other, s32[1,128]{1,0:T(1,128)S(1)} %copy-done.2), custom_call_target="tpu_custom_call" | custom-call | flops 1000000 | bytes 1048576 | tf_op jit(solution)/shard_map/logit/pallas_call | solution.py:493
  65.1 2.0 %collective-permute-start.19 = (f32[264,128]{1,0:T(8,128)S(1)}, f32[264,128]{1,0:T(8,128)S(1)}, u32[]{:S(2)}, u32[]{:S(2)}) collective-permute-start(f32[264,128]{1,0:T(8,128)S(1)} %get-tuple-element.160.refs_1_), channel_id=1, source_target_pairs={{0,2},{2,0},{1,3},{3,1},{4,6},{6,4},{5,7},{7,5},{8,10},{10,8},{9,1... | collective-permute-start | bytes 405512 | tf_op jit(solution)/shard_map/ppermute | solution.py:375
  67.2 3.7 %grads_a.1 = (bf16[2,1024,256]{2,1,0:T(8,128)(2,1)S(1)}, bf16[2,1024,256]{2,1,0:T(8,128)(2,1)S(1)}, f32[2,256,256]{2,1,0:T(8,128)S(1)}, f32[2,64,256]{2,1,0:T(8,...) custom-call(s32[4]{0:T(128)S(1)} %pad_add_fusion.idx.refs_0_, ...), custom_call_target="tpu_custom_call" | custom-call | flops 4000000000 | bytes 1048576 | tf_op jit(solution)/shard_map/grads_a/pallas_call | solution.py:501
  70.9 1.7 %collective-permute-done.19.refs_1_ = f32[264,128]{1,0:T(8,128)S(1)} collective-permute-done((f32[264,128]{1,0:T(8,128)S(1)}, f32[264,128]{1,0:T(8,128)S(1)}, u32[]{:S(2)}, u32[]{:S(2)}) %collective-permute-start.19) | collective-permute-done | bytes 135200 | tf_op jit(solution)/shard_map/ppermute | solution.py:375
  72.6 1.0 collective-permute-start.16
  73.7 2.2 %collective-permute-start.17 = (f32[2,64,256]{2,1,0:T(8,128)S(1)}, f32[2,64,256]{2,1,0:T(8,128)S(1)}, u32[]{:S(2)}, u32[]{:S(2)}) collective-permute-start(f32[2,64,256]{2,1,0:T(8,128)S(1)} %get-tuple-element.168), channel_id=1, source_target_pairs={{0,8},{4,12},{8,0},{12,4},{1,9},{5,13},{9,1},{13,5},{2,10},{6,14},... | collective-permute-start | bytes 393224 | tf_op jit(solution)/shard_map/ppermute | solution.py:371
  76.3 2.2 %grads_b0.1 = (bf16[1,1024,256]{2,1,0:T(8,128)(2,1)S(1)}, bf16[1,1024,256]{2,1,0:T(8,128)(2,1)S(1)}, f32[1,256,256]{2,1,0:T(8,128)S(1)}, f32[1,64,256]{2,1,0:T(8...) custom-call(s32[4]{0:T(128)S(1)} %pad_add_fusion.idx.refs_0_, ...), custom_call_target="tpu_custom_call" | custom-call | flops 4000000000 | bytes 1048576 | tf_op jit(solution)/shard_map/grads_b0/pallas_call | solution.py:501
  78.6 1.8 %weights_0.1 = (f32[80,1024]{1,0:T(8,128)S(1)}, f32[80,1024]{1,0:T(8,128)S(1)}, f32[96,1024]{1,0:T(8,128)S(1)}, f32[96,1024]{1,0:T(8,128)S(1)}) custom-call(s32[4]{0:T(128)S(1)} %pad_add_fusion.idx.refs_0_, f32[4,128,256]{2,1,0:T(8,128)S(1)} %pack.3.refs_1_, f32[4,128,256]{2,1,0:T(8,128)S(1)} %pack.2.refs_1_.refs_2_, ...), custom_call_target="tpu_custom_call" | custom-call | flops 3000000000 | bytes 1048576 | tf_op jit(solution)/shard_map/weights_0/pallas_call | solution.py:516
  80.4 1.6 %collective-permute-start.21 = (f32[96,1024]{1,0:T(8,128)S(1)}, f32[96,1024]{1,0:T(8,128)S(1)}, u32[]{:S(2)}, u32[]{:S(2)}) collective-permute-start(f32[96,1024]{1,0:T(8,128)S(1)} %get-tuple-element.184), channel_id=1, source_target_pairs={{0,4},{4,8},{8,12},{12,0},{1,5},{5,9},{9,13},{13,1},{2,6},{6,10},{... | collective-permute-start | bytes 1179656 | tf_op jit(solution)/shard_map/ppermute | solution.py:371
  82.0 1.7 %collective-permute-start.22 = (f32[96,1024]{1,0:T(8,128)S(1)}, f32[96,1024]{1,0:T(8,128)S(1)}, u32[]{:S(2)}, u32[]{:S(2)}) collective-permute-start(f32[96,1024]{1,0:T(8,128)S(1)} %get-tuple-element.185), channel_id=1, source_target_pairs={{0,12},{4,0},{8,4},{12,8},{1,13},{5,1},{9,5},{13,9},{2,14},{6,2},{... | collective-permute-start | bytes 1179656 | tf_op jit(solution)/shard_map/ppermute | solution.py:371
  83.7 2.2 %grads_b1.1 = (bf16[1,1024,256]{2,1,0:T(8,128)(2,1)S(1)}, bf16[1,1024,256]{2,1,0:T(8,128)(2,1)S(1)}, f32[1,256,256]{2,1,0:T(8,128)S(1)}, f32[1,64,256]{2,1,0:T(8...) custom-call(s32[4]{0:T(128)S(1)} %pad_add_fusion.idx.refs_0_, ...), custom_call_target="tpu_custom_call" | custom-call | flops 4000000000 | bytes 1048576 | tf_op jit(solution)/shard_map/grads_b1/pallas_call | solution.py:501
  86.0 2.0 %weights_1.1 = (f32[88,1024]{1,0:T(8,128)S(1)}, f32[104,1024]{1,0:T(8,128)S(1)}, f32[104,1024]{1,0:T(8,128)S(1)}, f32[88,1024]{1,0:T(8,128)S(1)}, f32[32,1024]{1,0:T(8,128)S(1)}) custom-call(s32[4]{0:T(128)S(1)} %pad_add_fusion.idx.refs_0_, f32[4,128,256]{2,1,0:T(8,128)S(1)} %pack.3.refs_1_, f32[4,128,256]{2,1,0:T(8,128)S(1)} %pack.2.refs_1_.refs_2_, ...), custom_call_target="tpu_custom_call" | custom-call | flops 3000000000 | bytes 1048576 | tf_op jit(solution)/shard_map/weights_1/pallas_call | solution.py:516
  88.0 2.2 %collective-permute-start.23 = (f32[104,1024]{1,0:T(8,128)S(1)}, f32[104,1024]{1,0:T(8,128)S(1)}, u32[]{:S(2)}, u32[]{:S(2)}) collective-permute-start(f32[104,1024]{1,0:T(8,128)S(1)} %get-tuple-element.200), channel_id=1, source_target_pairs={{0,12},{4,0},{8,4},{12,8},{1,13},{5,1},{9,5},{13,9},{2,14},{6,2},{... | collective-permute-start | bytes 1277960 | tf_op jit(solution)/shard_map/ppermute | solution.py:371
  90.2 1.5 %collective-permute-start.25 = (f32[32,1024]{1,0:T(8,128)S(1)}, f32[32,1024]{1,0:T(8,128)S(1)}, u32[]{:S(2)}, u32[]{:S(2)}) collective-permute-start(f32[32,1024]{1,0:T(8,128)S(1)} %get-tuple-element.204), channel_id=1, source_target_pairs={{0,8},{4,12},{8,0},{12,4},{1,9},{5,13},{9,1},{13,5},{2,10},{6,14},... | collective-permute-start | bytes 393224 | tf_op jit(solution)/shard_map/ppermute | solution.py:371
  91.7 0.9 collective-permute-done.21.w_up
  92.7 1.4 %collective-permute-done.22.w_down.refs_2_ = f32[96,1024]{1,0:T(8,128)S(1)} collective-permute-done((f32[96,1024]{1,0:T(8,128)S(1)}, f32[96,1024]{1,0:T(8,128)S(1)}, u32[]{:S(2)}, u32[]{:S(2)}) %collective-permute-start.22) | collective-permute-done | bytes 393248 | tf_op jit(solution)/shard_map/ppermute | solution.py:371
  94.1 1.0 collective-permute-start.26
  95.1 8.8 %collective-permute-done.23.v_down = f32[104,1024]{1,0:T(8,128)S(1)} collective-permute-done((f32[104,1024]{1,0:T(8,128)S(1)}, f32[104,1024]{1,0:T(8,128)S(1)}, u32[]{:S(2)}, u32[]{:S(2)}) %collective-permute-start.23) | collective-permute-done | bytes 426016 | tf_op jit(solution)/shard_map/ppermute | solution.py:371
  103.9 3.0 %collective-permute-done.24.v_up.refs_4_ = f32[104,1024]{1,0:T(8,128)S(1)} collective-permute-done((f32[104,1024]{1,0:T(8,128)S(1)}, f32[104,1024]{1,0:T(8,128)S(1)}, u32[]{:S(2)}, u32[]{:S(2)}) %collective-permute-start.24) | collective-permute-done | bytes 426016 | tf_op jit(solution)/shard_map/ppermute | solution.py:371
  107.0 0.7 collective-permute-start.27
  107.7 2.8 %update.1 = (f32[2,64,512]{2,1,0:T(8,128)}, f32[2,512]{1,0:T(2,128)S(1)}) custom-call(s32[4]{0:T(128)S(1)} %pad_add_fusion.idx.refs_0_, f32[2,64,256]{2,1,0:T(8,128)S(1)} %get-tuple-element.166.ga0, f32[2,64,256]{2,1,0:T(8,128)S(1)} %collective-permute-done.16.refs_11_.ga1, f32[2,64,256]{2,1,0:T(8,128)S(1)} %collective-permute-done.17.refs_12_.ga2, ...), custom_call_target="tpu_custom_call" | custom-call | flops 5000000000 | bytes 1048576 | tf_op jit(solution)/shard_map/update/pallas_call | solution.py:546
  111.1 1.7 %collective-permute-done.26.refs_1_ = f32[80,1024]{1,0:T(8,128)S(1)} collective-permute-done((f32[80,1024]{1,0:T(8,128)S(1)}, f32[80,1024]{1,0:T(8,128)S(1)}, u32[]{:S(2)}, u32[]{:S(2)}) %collective-permute-start.26) | collective-permute-done | bytes 327712 | tf_op jit(solution)/shard_map/ppermute | solution.py:371
  112.7 1.8 %collective-permute-done.27.refs_5_ = f32[88,1024]{1,0:T(8,128)S(1)} collective-permute-done((f32[88,1024]{1,0:T(8,128)S(1)}, f32[88,1024]{1,0:T(8,128)S(1)}, u32[]{:S(2)}, u32[]{:S(2)}) %collective-permute-start.27) | collective-permute-done | bytes 360480 | tf_op jit(solution)/shard_map/ppermute | solution.py:371
  114.5 1.2 %sum.1 = (f32[1024,128]{1,0:T(8,128)}, f32[256,128]{1,0:T(8,128)}, f32[32,128]{1,0:T(8,128)}, f32[32,128]{1,0:T(8,128)}) custom-call(f32[32,128]{1,0:T(8,128)S(1)} %get-tuple-element.209.column, f32[80,1024]{1,0:T(8,128)S(1)} %get-tuple-element.210.refs_0_, f32[80,1024]{1,0:T(8,128)S(1)} %collective-permute-done.26.refs_1_, ...), custom_call_target="tpu_custom_call" | custom-call | flops 1000000 | bytes 1048576 | tf_op jit(solution)/shard_map/sum/pallas_call | solution.py:549
  (43 shorter events, 4.4 us)
Async XLA Ops:
  4.7 12.5 %collective-permute-start = (f32[128,256]{1,0:T(8,128)S(1)}, f32[128,256]{1,0:T(8,128)S(1)}, u32[]{:S(2)}, u32[]{:S(2)}) collective-permute-start(f32[128,256]{1,0:T(8,128)S(1)} %get-tuple-element.116), channel_id=1, source_target_pairs={{0,4},{4,8},{8,12},{12,0},{1,5},{5,9},{9,13},{13,1},{2,6},{6,10},{... | collective-permute-start | bytes 393224 | tf_op jit(solution)/shard_map/ppermute | solution.py:371
  6.8 10.5 %collective-permute-start.1 = (f32[128,256]{1,0:T(8,128)S(1)}, f32[128,256]{1,0:T(8,128)S(1)}, u32[]{:S(2)}, u32[]{:S(2)}) collective-permute-start(f32[128,256]{1,0:T(8,128)S(1)} %get-tuple-element.117), channel_id=1, source_target_pairs={{0,8},{4,12},{8,0},{12,4},{1,9},{5,13},{9,1},{13,5},{2,10},{6,14},... | collective-permute-start | bytes 393224 | tf_op jit(solution)/shard_map/ppermute | solution.py:371
  10.4 6.9 %collective-permute-start.2 = (f32[128,256]{1,0:T(8,128)S(1)}, f32[128,256]{1,0:T(8,128)S(1)}, u32[]{:S(2)}, u32[]{:S(2)}) collective-permute-start(f32[128,256]{1,0:T(8,128)S(1)} %get-tuple-element.118), channel_id=1, source_target_pairs={{0,12},{4,0},{8,4},{12,8},{1,13},{5,1},{9,5},{13,9},{2,14},{6,2},{... | collective-permute-start | bytes 393224 | tf_op jit(solution)/shard_map/ppermute | solution.py:371
  17.9 14.4 %collective-permute-start.6 = (f32[4,128,256]{2,1,0:T(8,128)S(1)}, f32[4,128,256]{2,1,0:T(8,128)S(1)}, u32[]{:S(2)}, u32[]{:S(2)}) collective-permute-start(f32[4,128,256]{2,1,0:T(8,128)S(1)} %pack.2.refs_1_.refs_2_), channel_id=1, source_target_pairs={{0,2},{2,0},{1,3},{3,1},{4,6},{6,4},{5,7},{7,5},{8,10},{10,8},{9,1... | collective-permute-start | bytes 1572872 | tf_op jit(solution)/shard_map/ppermute | solution.py:375
  21.0 8.3 %collective-permute-start.3 = (f32[128,256]{1,0:T(8,128)S(1)}, f32[128,256]{1,0:T(8,128)S(1)}, u32[]{:S(2)}, u32[]{:S(2)}) collective-permute-start(f32[128,256]{1,0:T(8,128)S(1)} %get-tuple-element.127), channel_id=1, source_target_pairs={{0,4},{4,8},{8,12},{12,0},{1,5},{5,9},{9,13},{13,1},{2,6},{6,10},{... | collective-permute-start | bytes 393224 | tf_op jit(solution)/shard_map/ppermute | solution.py:371
  22.0 7.3 %collective-permute-start.4 = (f32[128,256]{1,0:T(8,128)S(1)}, f32[128,256]{1,0:T(8,128)S(1)}, u32[]{:S(2)}, u32[]{:S(2)}) collective-permute-start(f32[128,256]{1,0:T(8,128)S(1)} %get-tuple-element.128), channel_id=1, source_target_pairs={{0,8},{4,12},{8,0},{12,4},{1,9},{5,13},{9,1},{13,5},{2,10},{6,14},... | collective-permute-start | bytes 393224 | tf_op jit(solution)/shard_map/ppermute | solution.py:371
  23.7 11.6 %copy-start.1 = (f32[4096]{0:T(1024)S(1)}, f32[4096]{0:T(1024)}, u32[]{:S(2)}) copy-start(f32[4096]{0:T(1024)} %param.20) | copy-start | bytes 49156
  23.7 6.0 %collective-permute-start.5 = (f32[128,256]{1,0:T(8,128)S(1)}, f32[128,256]{1,0:T(8,128)S(1)}, u32[]{:S(2)}, u32[]{:S(2)}) collective-permute-start(f32[128,256]{1,0:T(8,128)S(1)} %get-tuple-element.129), channel_id=1, source_target_pairs={{0,12},{4,0},{8,4},{12,8},{1,13},{5,1},{9,5},{13,9},{2,14},{6,2},{... | collective-permute-start | bytes 393224 | tf_op jit(solution)/shard_map/ppermute | solution.py:371
  25.0 10.3 %copy-start = (f32[1024,2,256]{2,1,0:T(2,128)S(1)}, f32[1024,2,256]{2,1,0:T(2,128)}, u32[]{:S(2)}) copy-start(f32[1024,2,256]{2,1,0:T(2,128)} %param.17) | copy-start | bytes 6291460
  30.3 6.6 %collective-permute-start.7 = (f32[4,128,256]{2,1,0:T(8,128)S(1)}, f32[4,128,256]{2,1,0:T(8,128)S(1)}, u32[]{:S(2)}, u32[]{:S(2)}) collective-permute-start(f32[4,128,256]{2,1,0:T(8,128)S(1)} %pack.3.refs_1_), channel_id=1, source_target_pairs={{0,1},{1,0},{2,3},{3,2},{4,5},{5,4},{6,7},{7,6},{8,9},{9,8},{10,11... | collective-permute-start | bytes 1572872 | tf_op jit(solution)/shard_map/ppermute | solution.py:375
  32.3 4.6 %collective-permute-start.8 = (f32[4,128,256]{2,1,0:T(8,128)S(1)}, f32[4,128,256]{2,1,0:T(8,128)S(1)}, u32[]{:S(2)}, u32[]{:S(2)}) collective-permute-start(f32[4,128,256]{2,1,0:T(8,128)S(1)} %collective-permute-done.6.refs_2_), channel_id=1, source_target_pairs={{0,1},{1,0},{2,3},{3,2},{4,5},{5,4},{6,7},{7,6},{8,9},{9,8},{10,11... | collective-permute-start | bytes 1572872 | tf_op jit(solution)/shard_map/ppermute | solution.py:375
  32.3 16.2 %collective-permute-start.10 = (f32[4,128,256]{2,1,0:T(8,128)S(1)}, f32[4,128,256]{2,1,0:T(8,128)S(1)}, u32[]{:S(2)}, u32[]{:S(2)}) collective-permute-start(f32[4,128,256]{2,1,0:T(8,128)S(1)} %pack.3.refs_1_), channel_id=1, source_target_pairs={{0,2},{2,0},{1,3},{3,1},{4,6},{6,4},{5,7},{7,5},{8,10},{10,8},{9,1... | collective-permute-start | bytes 1572872 | tf_op jit(solution)/shard_map/ppermute | solution.py:375
  44.1 7.0 %collective-permute-start.9 = (f32[264,128]{1,0:T(8,128)S(1)}, f32[264,128]{1,0:T(8,128)S(1)}, u32[]{:S(2)}, u32[]{:S(2)}) collective-permute-start(f32[264,128]{1,0:T(8,128)S(1)} %get-tuple-element.145), channel_id=1, source_target_pairs={{0,16},{16,0},{32,48},{48,32},{64,80},{80,64},{96,112},{112,96},{1... | collective-permute-start | bytes 405512 | tf_op jit(solution)/shard_map/ppermute | solution.py:375
  44.8 8.0 %collective-permute-start.12 = (f32[4,128,256]{2,1,0:T(8,128)S(1)}, f32[4,128,256]{2,1,0:T(8,128)S(1)}, u32[]{:S(2)}, u32[]{:S(2)}) collective-permute-start(f32[4,128,256]{2,1,0:T(8,128)S(1)} %pack.2.refs_1_.refs_2_), channel_id=1, source_target_pairs={{0,1},{1,0},{2,3},{3,2},{4,5},{5,4},{6,7},{7,6},{8,9},{9,8},{10,11... | collective-permute-start | bytes 1572872 | tf_op jit(solution)/shard_map/ppermute | solution.py:375
  51.1 1.9 %collective-permute-start.13 = (f32[4,128,256]{2,1,0:T(8,128)S(1)}, f32[4,128,256]{2,1,0:T(8,128)S(1)}, u32[]{:S(2)}, u32[]{:S(2)}) collective-permute-start(f32[4,128,256]{2,1,0:T(8,128)S(1)} %collective-permute-done.10.refs_2_), channel_id=1, source_target_pairs={{0,1},{1,0},{2,3},{3,2},{4,5},{5,4},{6,7},{7,6},{8,9},{9,8},{10,11... | collective-permute-start | bytes 1572872 | tf_op jit(solution)/shard_map/ppermute | solution.py:375
  51.1 6.1 %collective-permute-start.11 = (f32[264,128]{1,0:T(8,128)S(1)}, f32[264,128]{1,0:T(8,128)S(1)}, u32[]{:S(2)}, u32[]{:S(2)}) collective-permute-start(f32[264,128]{1,0:T(8,128)S(1)} %add.16), channel_id=1, source_target_pairs={{0,32},{16,48},{32,0},{48,16},{64,96},{80,112},{96,64},{112,80},{1... | collective-permute-start | bytes 405512 | tf_op jit(solution)/shard_map/ppermute | solution.py:375
  57.2 6.7 %copy-start.2 = (s32[1,128]{1,0:T(1,128)S(1)}, s32[1,128]{1,0:T(1,128)}, u32[]{:S(2)}) copy-start(s32[1,128]{1,0:T(1,128)} %labels.1) | copy-start | bytes 1540
  57.2 6.7 %collective-permute-start.14 = (f32[264,128]{1,0:T(8,128)S(1)}, f32[264,128]{1,0:T(8,128)S(1)}, u32[]{:S(2)}, u32[]{:S(2)}) collective-permute-start(f32[264,128]{1,0:T(8,128)S(1)} %add.17.mine), channel_id=1, source_target_pairs={{0,96},{16,112},{32,64},{48,80},{64,32},{80,48},{96,0},{112,16},{1... | collective-permute-start | bytes 405512 | tf_op jit(solution)/shard_map/ppermute | solution.py:375
  65.1 2.0 %collective-permute-start.15 = (f32[264,128]{1,0:T(8,128)S(1)}, f32[264,128]{1,0:T(8,128)S(1)}, u32[]{:S(2)}, u32[]{:S(2)}) collective-permute-start(f32[264,128]{1,0:T(8,128)S(1)} %get-tuple-element.160.refs_1_), channel_id=1, source_target_pairs={{0,1},{1,0},{2,3},{3,2},{4,5},{5,4},{6,7},{7,6},{8,9},{9,8},{10,11... | collective-permute-start | bytes 405512 | tf_op jit(solution)/shard_map/ppermute | solution.py:375
  65.1 7.5 %collective-permute-start.19 = (f32[264,128]{1,0:T(8,128)S(1)}, f32[264,128]{1,0:T(8,128)S(1)}, u32[]{:S(2)}, u32[]{:S(2)}) collective-permute-start(f32[264,128]{1,0:T(8,128)S(1)} %get-tuple-element.160.refs_1_), channel_id=1, source_target_pairs={{0,2},{2,0},{1,3},{3,1},{4,6},{6,4},{5,7},{7,5},{8,10},{10,8},{9,1... | collective-permute-start | bytes 405512 | tf_op jit(solution)/shard_map/ppermute | solution.py:375
  72.6 3.7 %collective-permute-start.20 = (f32[264,128]{1,0:T(8,128)S(1)}, f32[264,128]{1,0:T(8,128)S(1)}, u32[]{:S(2)}, u32[]{:S(2)}) collective-permute-start(f32[264,128]{1,0:T(8,128)S(1)} %collective-permute-done.19.refs_1_), channel_id=1, source_target_pairs={{0,1},{1,0},{2,3},{3,2},{4,5},{5,4},{6,7},{7,6},{8,9},{9,8},{10,11... | collective-permute-start | bytes 405512 | tf_op jit(solution)/shard_map/ppermute | solution.py:375
  72.6 11.1 %collective-permute-start.16 = (f32[2,64,256]{2,1,0:T(8,128)S(1)}, f32[2,64,256]{2,1,0:T(8,128)S(1)}, u32[]{:S(2)}, u32[]{:S(2)}) collective-permute-start(f32[2,64,256]{2,1,0:T(8,128)S(1)} %get-tuple-element.167), channel_id=1, source_target_pairs={{0,4},{4,8},{8,12},{12,0},{1,5},{5,9},{9,13},{13,1},{2,6},{6,10},{... | collective-permute-start | bytes 393224 | tf_op jit(solution)/shard_map/ppermute | solution.py:371
  73.7 10.1 %collective-permute-start.17 = (f32[2,64,256]{2,1,0:T(8,128)S(1)}, f32[2,64,256]{2,1,0:T(8,128)S(1)}, u32[]{:S(2)}, u32[]{:S(2)}) collective-permute-start(f32[2,64,256]{2,1,0:T(8,128)S(1)} %get-tuple-element.168), channel_id=1, source_target_pairs={{0,8},{4,12},{8,0},{12,4},{1,9},{5,13},{9,1},{13,5},{2,10},{6,14},... | collective-permute-start | bytes 393224 | tf_op jit(solution)/shard_map/ppermute | solution.py:371
  75.8 7.9 %collective-permute-start.18 = (f32[2,64,256]{2,1,0:T(8,128)S(1)}, f32[2,64,256]{2,1,0:T(8,128)S(1)}, u32[]{:S(2)}, u32[]{:S(2)}) collective-permute-start(f32[2,64,256]{2,1,0:T(8,128)S(1)} %get-tuple-element.169), channel_id=1, source_target_pairs={{0,12},{4,0},{8,4},{12,8},{1,13},{5,1},{9,5},{13,9},{2,14},{6,2},{... | collective-permute-start | bytes 393224 | tf_op jit(solution)/shard_map/ppermute | solution.py:371
  80.4 12.2 %collective-permute-start.21 = (f32[96,1024]{1,0:T(8,128)S(1)}, f32[96,1024]{1,0:T(8,128)S(1)}, u32[]{:S(2)}, u32[]{:S(2)}) collective-permute-start(f32[96,1024]{1,0:T(8,128)S(1)} %get-tuple-element.184), channel_id=1, source_target_pairs={{0,4},{4,8},{8,12},{12,0},{1,5},{5,9},{9,13},{13,1},{2,6},{6,10},{... | collective-permute-start | bytes 1179656 | tf_op jit(solution)/shard_map/ppermute | solution.py:371
  82.0 12.1 %collective-permute-start.22 = (f32[96,1024]{1,0:T(8,128)S(1)}, f32[96,1024]{1,0:T(8,128)S(1)}, u32[]{:S(2)}, u32[]{:S(2)}) collective-permute-start(f32[96,1024]{1,0:T(8,128)S(1)} %get-tuple-element.185), channel_id=1, source_target_pairs={{0,12},{4,0},{8,4},{12,8},{1,13},{5,1},{9,5},{13,9},{2,14},{6,2},{... | collective-permute-start | bytes 1179656 | tf_op jit(solution)/shard_map/ppermute | solution.py:371
  86.0 4.2 %copy-start.3 = (f32[2,1,512]{2,1,0:T(1,128)S(1)}, f32[2,1,512]{2,1,0:T(1,128)}, u32[]{:S(2)}) copy-start(f32[2,1,512]{2,1,0:T(1,128)} %param.15) | copy-start | bytes 12292
  88.0 15.9 %collective-permute-start.23 = (f32[104,1024]{1,0:T(8,128)S(1)}, f32[104,1024]{1,0:T(8,128)S(1)}, u32[]{:S(2)}, u32[]{:S(2)}) collective-permute-start(f32[104,1024]{1,0:T(8,128)S(1)} %get-tuple-element.200), channel_id=1, source_target_pairs={{0,12},{4,0},{8,4},{12,8},{1,13},{5,1},{9,5},{13,9},{2,14},{6,2},{... | collective-permute-start | bytes 1277960 | tf_op jit(solution)/shard_map/ppermute | solution.py:371
  90.2 16.7 %collective-permute-start.24 = (f32[104,1024]{1,0:T(8,128)S(1)}, f32[104,1024]{1,0:T(8,128)S(1)}, u32[]{:S(2)}, u32[]{:S(2)}) collective-permute-start(f32[104,1024]{1,0:T(8,128)S(1)} %get-tuple-element.201), channel_id=1, source_target_pairs={{0,4},{4,8},{8,12},{12,0},{1,5},{5,9},{9,13},{13,1},{2,6},{6,10},{... | collective-permute-start | bytes 1277960 | tf_op jit(solution)/shard_map/ppermute | solution.py:371
  90.2 17.5 %collective-permute-start.25 = (f32[32,1024]{1,0:T(8,128)S(1)}, f32[32,1024]{1,0:T(8,128)S(1)}, u32[]{:S(2)}, u32[]{:S(2)}) collective-permute-start(f32[32,1024]{1,0:T(8,128)S(1)} %get-tuple-element.204), channel_id=1, source_target_pairs={{0,8},{4,12},{8,0},{12,4},{1,9},{5,13},{9,1},{13,5},{2,10},{6,14},... | collective-permute-start | bytes 393224 | tf_op jit(solution)/shard_map/ppermute | solution.py:371
  94.1 18.6 %collective-permute-start.26 = (f32[80,1024]{1,0:T(8,128)S(1)}, f32[80,1024]{1,0:T(8,128)S(1)}, u32[]{:S(2)}, u32[]{:S(2)}) collective-permute-start(f32[80,1024]{1,0:T(8,128)S(1)} %slice_add_fusion.1), channel_id=1, source_target_pairs={{0,4},{4,8},{8,12},{12,0},{1,5},{5,9},{9,13},{13,1},{2,6},{6,10},{... | collective-permute-start | bytes 983048 | tf_op jit(solution)/shard_map/ppermute | solution.py:371
  107.0 7.5 %collective-permute-start.27 = (f32[88,1024]{1,0:T(8,128)S(1)}, f32[88,1024]{1,0:T(8,128)S(1)}, u32[]{:S(2)}, u32[]{:S(2)}) collective-permute-start(f32[88,1024]{1,0:T(8,128)S(1)} %slice_add_fusion), channel_id=1, source_target_pairs={{0,12},{4,0},{8,4},{12,8},{1,13},{5,1},{9,5},{13,9},{2,14},{6,2},{... | collective-permute-start | bytes 1081352 | tf_op jit(solution)/shard_map/ppermute | solution.py:371

commit v8 on v7

--- a/solution.py
+++ b/solution.py
@@ -468,7 +468,7 @@
         )(at, fq_far, x2b, y1b, y2b, *weights)
 
     view, second_view, pay = lax.optimization_barrier((view, second_view, pay))
-    other = flip(pay, TOWER, 8, 1)
+    other = flip(pay, TOWER, 8, 2)
     w1qh, w1ql, column = call(
         pick_kernel,
         [bf16(2, 256, 1024)] * 2 + [f32(32, 128)],
@@ -481,13 +481,13 @@
     other, w1qh, w2h, x2b = lax.optimization_barrier((other, w1qh, w2h, x2b))
     pay = pay + other
     after, pay = lax.optimization_barrier((idx, pay))
-    other = flip(pay, TOWER, 8, 2)
+    other = flip(pay, TOWER, 8, 6)
     y2b = flip(x2b, "core", 2, 1)
     hid_b0, x0b0 = later_half(after, 0, y2b)
     other, x0b0 = lax.optimization_barrier((other, x0b0))
     pay = pay + other
     after, pay = lax.optimization_barrier((idx, pay))
-    other = flip(pay, TOWER, 8, 6)
+    other = flip(pay, TOWER, 8, 1)
     hid_b1, x0b1 = later_half(after, 1, y2b)
     other, x0b1 = lax.optimization_barrier((other, x0b1))
     pay, logits = call(logit_kernel, [f32(2 * rank + 8, 128), f32(1, 16)], [SMEM_SPEC] + vmem(3), name="logit", flops=1e6)(

time: 116 us -> 114 us (0.983)
  no operation moved by 1% of the time
where the time goes in v8:
time: 114 us
  Pallas kernels  50.3 us (44%)
  starting transfers between devices  35.9 us (31%)
  waiting for transfers between devices  26.4 us (23%)
    ppermute x16, starting transfers between devices, shift(): return lax.ppermute(x, axis, [(i, (i + by) % size) for i in range(size)])  23 us
    ppermute x16, waiting for transfers between devices, shift(): return lax.ppermute(x, axis, [(i, (i + by) % size) for i in range(size)])  19.1 us
    ppermute x12, starting transfers between devices, flip(): return lax.ppermute(x, axis, [(i, i ^ bit) for i in range(size)])  12.9 us
    pallas_call x3, Pallas kernels, grads(): call(lambda *refs: grads_kernel(towers, with_pq, len(extra), *refs), [bf1...  8.17 us
    ppermute x12, waiting for transfers between devices, flip(): return lax.ppermute(x, axis, [(i, i ^ bit) for i in range(size)])  7.28 us
    pallas_call x2, Pallas kernels, later_half(): call(lambda *refs: forward_kernel((t,), False, *refs), [f32(1, 1024, 256)...  7.24 us
    pallas_call x1, Pallas kernels, per_device(): call(lambda *refs: forward_kernel((0, 1), True, *refs), [f32(2, 1024, 256...  7.18 us
    pallas_call x2, Pallas kernels, turn(): pl.pallas_call(lambda *refs: turn_kernel(at, *refs), in_specs=[any_spec],...  6.22 us
  transfers between devices with their start and end apart: 28, of which 14 were waited for; matrix products, arithmetic and copies ran while one was open for 1% of the time, Pallas kernels for 38%

profile of v8, /device:TPU:0, one launch (start us, length us, event | category | flops | bytes accessed | tf_op | source)
XLA Modules:
  0.0 114.3 jit_solution(16118336828059855929)
XLA Ops:
  0.7 4.0 %pool_far.1 = (f32[128,256]{1,0:T(8,128)S(1)}, f32[128,256]{1,0:T(8,128)S(1)}, f32[128,256]{1,0:T(8,128)S(1)}, f32[128,256]{1,0:T(8,128)S(1)}, bf16[2,4,512,256]...) custom-call(s32[4]{0:T(128)S(1)} %pad_add_fusion.idx.refs_0_, s32[2,4,2048]{2,1,0:T(4,128)} %bitcast.49, ...), custom_call_target="tpu_custom_call" | custom-call | flops 1000000 | bytes 1048576 | tf_op jit(solution)/shard_map/pool_far/pallas_call | solution.py:390
  4.7 2.1 %collective-permute-start = (f32[128,256]{1,0:T(8,128)S(1)}, f32[128,256]{1,0:T(8,128)S(1)}, u32[]{:S(2)}, u32[]{:S(2)}) collective-permute-start(f32[128,256]{1,0:T(8,128)S(1)} %get-tuple-element.116), channel_id=1, source_target_pairs={{0,4},{4,8},{8,12},{12,0},{1,5},{5,9},{9,13},{13,1},{2,6},{6,10},{... | collective-permute-start | bytes 393224 | tf_op jit(solution)/shard_map/ppermute | solution.py:371
  6.8 3.6 %collective-permute-start.1 = (f32[128,256]{1,0:T(8,128)S(1)}, f32[128,256]{1,0:T(8,128)S(1)}, u32[]{:S(2)}, u32[]{:S(2)}) collective-permute-start(f32[128,256]{1,0:T(8,128)S(1)} %get-tuple-element.117), channel_id=1, source_target_pairs={{0,8},{4,12},{8,0},{12,4},{1,9},{5,13},{9,1},{13,5},{2,10},{6,14},... | collective-permute-start | bytes 393224 | tf_op jit(solution)/shard_map/ppermute | solution.py:371
  10.4 1.0 collective-permute-start.2
  11.4 2.8 %pool_near.1 = (f32[128,256]{1,0:T(8,128)S(1)}, f32[128,256]{1,0:T(8,128)S(1)}, f32[128,256]{1,0:T(8,128)S(1)}, f32[128,256]{1,0:T(8,128)S(1)}, bf16[2,4,512,256]{3,2,1,0:T(8,128)(2,1)S(1)}) custom-call(s32[4]{0:T(128)S(1)} %pad_add_fusion.idx.refs_0_, s32[2,4,2048]{2,1,0:T(4,128)S(1)} %get-tuple-element.119.bag, f32[2,64,512]{2,1,0:T(8,128)S(1)} %get-tuple-element.113.decayed), custom_call_target="tpu_custom_call" | custom-call | flops 1000000 | bytes 1048576 | tf_op jit(solution)/shard_map/pool_near/pallas_call | solution.py:405
  14.2 3.0 %turn_0.1 = (bf16[2,1024,512]{2,1,0:T(8,128)(2,1)S(1)}, bf16[2,1024,512]{2,1,0:T(8,128)(2,1)S(1)}) custom-call(f32[1024,16,128]{2,1,0:T(8,128)} %bitcast.45), custom_call_target="tpu_custom_call" | custom-call | flops 1000000 | bytes 1048576 | tf_op jit(solution)/shard_map/turn_0/pallas_call | solution.py:411
  17.9 3.1 %collective-permute-start.6 = (f32[4,128,256]{2,1,0:T(8,128)S(1)}, f32[4,128,256]{2,1,0:T(8,128)S(1)}, u32[]{:S(2)}, u32[]{:S(2)}) collective-permute-start(f32[4,128,256]{2,1,0:T(8,128)S(1)} %pack.2.refs_1_.refs_2_), channel_id=1, source_target_pairs={{0,2},{2,0},{1,3},{3,1},{4,6},{6,4},{5,7},{7,5},{8,10},{10,8},{9,1... | collective-permute-start | bytes 1572872 | tf_op jit(solution)/shard_map/ppermute | solution.py:375
  21.0 1.0 collective-permute-start.3
  22.0 1.7 %collective-permute-start.4 = (f32[128,256]{1,0:T(8,128)S(1)}, f32[128,256]{1,0:T(8,128)S(1)}, u32[]{:S(2)}, u32[]{:S(2)}) collective-permute-start(f32[128,256]{1,0:T(8,128)S(1)} %get-tuple-element.128), channel_id=1, source_target_pairs={{0,8},{4,12},{8,0},{12,4},{1,9},{5,13},{9,1},{13,5},{2,10},{6,14},... | collective-permute-start | bytes 393224 | tf_op jit(solution)/shard_map/ppermute | solution.py:371
  23.7 1.2 %collective-permute-start.5 = (f32[128,256]{1,0:T(8,128)S(1)}, f32[128,256]{1,0:T(8,128)S(1)}, u32[]{:S(2)}, u32[]{:S(2)}) collective-permute-start(f32[128,256]{1,0:T(8,128)S(1)} %get-tuple-element.129), channel_id=1, source_target_pairs={{0,12},{4,0},{8,4},{12,8},{1,13},{5,1},{9,5},{13,9},{2,14},{6,2},{... | collective-permute-start | bytes 393224 | tf_op jit(solution)/shard_map/ppermute | solution.py:371
  25.0 3.2 %turn_1.1 = (bf16[2,1024,512]{2,1,0:T(8,128)(2,1)S(1)}, bf16[2,1024,512]{2,1,0:T(8,128)(2,1)S(1)}) custom-call(f32[1024,16,128]{2,1,0:T(8,128)} %bitcast.46), custom_call_target="tpu_custom_call" | custom-call | flops 1000000 | bytes 1048576 | tf_op jit(solution)/shard_map/turn_1/pallas_call | solution.py:411
  28.2 1.1 collective-permute-done.3.p1
  30.4 1.9 %collective-permute-done.6.refs_2_ = f32[4,128,256]{2,1,0:T(8,128)S(1)} collective-permute-done((f32[4,128,256]{2,1,0:T(8,128)S(1)}, f32[4,128,256]{2,1,0:T(8,128)S(1)}, u32[]{:S(2)}, u32[]{:S(2)}) %collective-permute-start.6) | collective-permute-done | bytes 524320 | tf_op jit(solution)/shard_map/ppermute | solution.py:375
  32.3 3.0 %collective-permute-start.10 = (f32[4,128,256]{2,1,0:T(8,128)S(1)}, f32[4,128,256]{2,1,0:T(8,128)S(1)}, u32[]{:S(2)}, u32[]{:S(2)}) collective-permute-start(f32[4,128,256]{2,1,0:T(8,128)S(1)} %pack.3.refs_1_), channel_id=1, source_target_pairs={{0,2},{2,0},{1,3},{3,1},{4,6},{6,4},{5,7},{7,5},{8,10},{10,8},{9,1... | collective-permute-start | bytes 1572872 | tf_op jit(solution)/shard_map/ppermute | solution.py:375
  35.3 1.6 %prepare.1 = (bf16[2,256,1024]{2,1,0:T(8,128)(2,1)S(1)}, bf16[2,256,1024]{2,1,0:T(8,128)(2,1)S(1)}, f32[512,128]{1,0:T(8,128)S(1)}, f32[512,128]{1,0:T(8,128)S(1)}, f32[1,512]{1,0:T(1,128)S(1)}) custom-call(s32[4]{0:T(128)S(1)} %pad_add_fusion.idx.refs_0_, f32[1024,4,128]{2,1,0:T(4,128)S(1)} %bitcast.40, f32[4096,128]{1,0:T(8,128)} %lift_hbm, ...), custom_call_target="tpu_custom_call" | custom-call | flops 1000000 | bytes 1048576 | tf_op jit(solution)/shard_map/prepare/pallas_call | solution.py:440
  36.9 7.2 %forward_a.1 = (f32[2,1024,256]{2,1,0:T(8,128)S(1)}, f32[512,256]{1,0:T(8,128)S(1)}, f32[264,128]{1,0:T(8,128)S(1)}) custom-call(s32[4]{0:T(128)S(1)} %pad_add_fusion.idx.refs_0_, f32[4,128,256]{2,1,0:T(8,128)S(1)} %pack.3.refs_1_, f32[4,128,256]{2,1,0:T(8,128)S(1)} %collective-permute-done.6.refs_2_, f32[4,128,256]{2,1,0:T(8,128)S(1)} %collective-permute-done.7.refs_3_, ...), custom_call_target="tpu_custom_call" | custom-call | flops 1000000 | bytes 1048576 | tf_op jit(solution)/shard_map/forward_a/pallas_call | solution.py:451
  44.1 1.6 %collective-permute-start.9 = (f32[264,128]{1,0:T(8,128)S(1)}, f32[264,128]{1,0:T(8,128)S(1)}, u32[]{:S(2)}, u32[]{:S(2)}) collective-permute-start(f32[264,128]{1,0:T(8,128)S(1)} %get-tuple-element.145), channel_id=1, source_target_pairs={{0,32},{16,48},{32,0},{48,16},{64,96},{80,112},{96,64},{112,80},{1... | collective-permute-start | bytes 405512 | tf_op jit(solution)/shard_map/ppermute | solution.py:375
  45.8 2.5 %pick.1 = (bf16[2,256,1024]{2,1,0:T(8,128)(2,1)S(1)}, bf16[2,256,1024]{2,1,0:T(8,128)(2,1)S(1)}, f32[32,128]{1,0:T(8,128)S(1)}) custom-call(s32[4]{0:T(128)S(1)} %pad_add_fusion.idx.refs_0_, f32[1024,16,128]{2,1,0:T(8,128)} %bitcast.47, f32[1,512]{1,0:T(1,128)S(1)} %get-tuple-element.143.refs_13_.head.refs_10_), custom_call_target="tpu_custom_call" | custom-call | flops 1000000 | bytes 1048576 | tf_op jit(solution)/shard_map/pick/pallas_call | solution.py:472
  48.8 1.1 collective-permute-done.9
  49.9 3.1 %collective-permute-start.11 = (f32[264,128]{1,0:T(8,128)S(1)}, f32[264,128]{1,0:T(8,128)S(1)}, u32[]{:S(2)}, u32[]{:S(2)}) collective-permute-start(f32[264,128]{1,0:T(8,128)S(1)} %add.16), channel_id=1, source_target_pairs={{0,96},{16,112},{32,64},{48,80},{64,32},{80,48},{96,0},{112,16},{1... | collective-permute-start | bytes 405512 | tf_op jit(solution)/shard_map/ppermute | solution.py:375
  53.0 3.6 %forward_b0.1 = (f32[1,1024,256]{2,1,0:T(8,128)S(1)}, f32[256,256]{1,0:T(8,128)S(1)}) custom-call(s32[4]{0:T(128)S(1)} %pad_add_fusion.idx.refs_0_, f32[4,128,256]{2,1,0:T(8,128)S(1)} %pack.2.refs_1_.refs_2_, f32[4,128,256]{2,1,0:T(8,128)S(1)} %collective-permute-done.10.refs_2_, f32[4,128,256]{2,1,0:T(8,128)S(1)} %collective-permute-done.12.refs_3_, ...), custom_call_target="tpu_custom_call" | custom-call | flops 4000000000 | bytes 1048576 | tf_op jit(solution)/shard_map/forward_b0/pallas_call | solution.py:461
  57.3 0.7 collective-permute-start.14
  58.0 3.6 %forward_b1.1 = (f32[1,1024,256]{2,1,0:T(8,128)S(1)}, f32[256,256]{1,0:T(8,128)S(1)}) custom-call(s32[4]{0:T(128)S(1)} %pad_add_fusion.idx.refs_0_, f32[4,128,256]{2,1,0:T(8,128)S(1)} %pack.2.refs_1_.refs_2_, f32[4,128,256]{2,1,0:T(8,128)S(1)} %collective-permute-done.10.refs_2_, f32[4,128,256]{2,1,0:T(8,128)S(1)} %collective-permute-done.12.refs_3_, ...), custom_call_target="tpu_custom_call" | custom-call | flops 4000000000 | bytes 1048576 | tf_op jit(solution)/shard_map/forward_b1/pallas_call | solution.py:461
  61.6 1.1 collective-permute-done.14.other
  62.7 1.2 %logit.1 = (f32[264,128]{1,0:T(8,128)S(1)}, f32[1,16]{1,0:T(1,128)}) custom-call(s32[4]{0:T(128)S(1)} %pad_add_fusion.idx.refs_0_, f32[264,128]{1,0:T(8,128)S(1)} %add.17.mine, f32[264,128]{1,0:T(8,128)S(1)} %collective-permute-done.14.other, s32[1,128]{1,0:T(1,128)S(1)} %copy-done.2), custom_call_target="tpu_custom_call" | custom-call | flops 1000000 | bytes 1048576 | tf_op jit(solution)/shard_map/logit/pallas_call | solution.py:493
  63.8 1.3 %collective-permute-start.19 = (f32[264,128]{1,0:T(8,128)S(1)}, f32[264,128]{1,0:T(8,128)S(1)}, u32[]{:S(2)}, u32[]{:S(2)}) collective-permute-start(f32[264,128]{1,0:T(8,128)S(1)} %get-tuple-element.160.refs_1_), channel_id=1, source_target_pairs={{0,2},{2,0},{1,3},{3,1},{4,6},{6,4},{5,7},{7,5},{8,10},{10,8},{9,1... | collective-permute-start | bytes 405512 | tf_op jit(solution)/shard_map/ppermute | solution.py:375
  65.2 3.7 %grads_a.1 = (bf16[2,1024,256]{2,1,0:T(8,128)(2,1)S(1)}, bf16[2,1024,256]{2,1,0:T(8,128)(2,1)S(1)}, f32[2,256,256]{2,1,0:T(8,128)S(1)}, f32[2,64,256]{2,1,0:T(8,...) custom-call(s32[4]{0:T(128)S(1)} %pad_add_fusion.idx.refs_0_, ...), custom_call_target="tpu_custom_call" | custom-call | flops 4000000000 | bytes 1048576 | tf_op jit(solution)/shard_map/grads_a/pallas_call | solution.py:501
  68.9 2.4 %collective-permute-done.19.refs_1_ = f32[264,128]{1,0:T(8,128)S(1)} collective-permute-done((f32[264,128]{1,0:T(8,128)S(1)}, f32[264,128]{1,0:T(8,128)S(1)}, u32[]{:S(2)}, u32[]{:S(2)}) %collective-permute-start.19) | collective-permute-done | bytes 135200 | tf_op jit(solution)/shard_map/ppermute | solution.py:375
  71.3 1.0 collective-permute-start.16
  72.4 2.2 %collective-permute-start.17 = (f32[2,64,256]{2,1,0:T(8,128)S(1)}, f32[2,64,256]{2,1,0:T(8,128)S(1)}, u32[]{:S(2)}, u32[]{:S(2)}) collective-permute-start(f32[2,64,256]{2,1,0:T(8,128)S(1)} %get-tuple-element.168), channel_id=1, source_target_pairs={{0,8},{4,12},{8,0},{12,4},{1,9},{5,13},{9,1},{13,5},{2,10},{6,14},... | collective-permute-start | bytes 393224 | tf_op jit(solution)/shard_map/ppermute | solution.py:371
  75.0 2.2 %grads_b0.1 = (bf16[1,1024,256]{2,1,0:T(8,128)(2,1)S(1)}, bf16[1,1024,256]{2,1,0:T(8,128)(2,1)S(1)}, f32[1,256,256]{2,1,0:T(8,128)S(1)}, f32[1,64,256]{2,1,0:T(8...) custom-call(s32[4]{0:T(128)S(1)} %pad_add_fusion.idx.refs_0_, ...), custom_call_target="tpu_custom_call" | custom-call | flops 4000000000 | bytes 1048576 | tf_op jit(solution)/shard_map/grads_b0/pallas_call | solution.py:501
  77.3 1.8 %weights_0.1 = (f32[80,1024]{1,0:T(8,128)S(1)}, f32[80,1024]{1,0:T(8,128)S(1)}, f32[96,1024]{1,0:T(8,128)S(1)}, f32[96,1024]{1,0:T(8,128)S(1)}) custom-call(s32[4]{0:T(128)S(1)} %pad_add_fusion.idx.refs_0_, f32[4,128,256]{2,1,0:T(8,128)S(1)} %pack.3.refs_1_, f32[4,128,256]{2,1,0:T(8,128)S(1)} %pack.2.refs_1_.refs_2_, ...), custom_call_target="tpu_custom_call" | custom-call | flops 3000000000 | bytes 1048576 | tf_op jit(solution)/shard_map/weights_0/pallas_call | solution.py:516
  79.1 1.6 %collective-permute-start.21 = (f32[96,1024]{1,0:T(8,128)S(1)}, f32[96,1024]{1,0:T(8,128)S(1)}, u32[]{:S(2)}, u32[]{:S(2)}) collective-permute-start(f32[96,1024]{1,0:T(8,128)S(1)} %get-tuple-element.184), channel_id=1, source_target_pairs={{0,4},{4,8},{8,12},{12,0},{1,5},{5,9},{9,13},{13,1},{2,6},{6,10},{... | collective-permute-start | bytes 1179656 | tf_op jit(solution)/shard_map/ppermute | solution.py:371
  80.7 1.7 %collective-permute-start.22 = (f32[96,1024]{1,0:T(8,128)S(1)}, f32[96,1024]{1,0:T(8,128)S(1)}, u32[]{:S(2)}, u32[]{:S(2)}) collective-permute-start(f32[96,1024]{1,0:T(8,128)S(1)} %get-tuple-element.185), channel_id=1, source_target_pairs={{0,12},{4,0},{8,4},{12,8},{1,13},{5,1},{9,5},{13,9},{2,14},{6,2},{... | collective-permute-start | bytes 1179656 | tf_op jit(solution)/shard_map/ppermute | solution.py:371
  82.4 2.2 %grads_b1.1 = (bf16[1,1024,256]{2,1,0:T(8,128)(2,1)S(1)}, bf16[1,1024,256]{2,1,0:T(8,128)(2,1)S(1)}, f32[1,256,256]{2,1,0:T(8,128)S(1)}, f32[1,64,256]{2,1,0:T(8...) custom-call(s32[4]{0:T(128)S(1)} %pad_add_fusion.idx.refs_0_, ...), custom_call_target="tpu_custom_call" | custom-call | flops 4000000000 | bytes 1048576 | tf_op jit(solution)/shard_map/grads_b1/pallas_call | solution.py:501
  84.7 2.0 %weights_1.1 = (f32[88,1024]{1,0:T(8,128)S(1)}, f32[104,1024]{1,0:T(8,128)S(1)}, f32[104,1024]{1,0:T(8,128)S(1)}, f32[88,1024]{1,0:T(8,128)S(1)}, f32[32,1024]{1,0:T(8,128)S(1)}) custom-call(s32[4]{0:T(128)S(1)} %pad_add_fusion.idx.refs_0_, f32[4,128,256]{2,1,0:T(8,128)S(1)} %pack.3.refs_1_, f32[4,128,256]{2,1,0:T(8,128)S(1)} %pack.2.refs_1_.refs_2_, ...), custom_call_target="tpu_custom_call" | custom-call | flops 3000000000 | bytes 1048576 | tf_op jit(solution)/shard_map/weights_1/pallas_call | solution.py:516
  86.7 2.2 %collective-permute-start.23 = (f32[104,1024]{1,0:T(8,128)S(1)}, f32[104,1024]{1,0:T(8,128)S(1)}, u32[]{:S(2)}, u32[]{:S(2)}) collective-permute-start(f32[104,1024]{1,0:T(8,128)S(1)} %get-tuple-element.200), channel_id=1, source_target_pairs={{0,12},{4,0},{8,4},{12,8},{1,13},{5,1},{9,5},{13,9},{2,14},{6,2},{... | collective-permute-start | bytes 1277960 | tf_op jit(solution)/shard_map/ppermute | solution.py:371
  88.9 1.5 %collective-permute-start.25 = (f32[32,1024]{1,0:T(8,128)S(1)}, f32[32,1024]{1,0:T(8,128)S(1)}, u32[]{:S(2)}, u32[]{:S(2)}) collective-permute-start(f32[32,1024]{1,0:T(8,128)S(1)} %get-tuple-element.204), channel_id=1, source_target_pairs={{0,8},{4,12},{8,0},{12,4},{1,9},{5,13},{9,1},{13,5},{2,10},{6,14},... | collective-permute-start | bytes 393224 | tf_op jit(solution)/shard_map/ppermute | solution.py:371
  90.4 0.9 collective-permute-done.21.w_up
  91.3 1.4 %collective-permute-done.22.w_down.refs_2_ = f32[96,1024]{1,0:T(8,128)S(1)} collective-permute-done((f32[96,1024]{1,0:T(8,128)S(1)}, f32[96,1024]{1,0:T(8,128)S(1)}, u32[]{:S(2)}, u32[]{:S(2)}) %collective-permute-start.22) | collective-permute-done | bytes 393248 | tf_op jit(solution)/shard_map/ppermute | solution.py:371
  92.8 1.0 collective-permute-start.26
  93.8 8.8 %collective-permute-done.23.v_down = f32[104,1024]{1,0:T(8,128)S(1)} collective-permute-done((f32[104,1024]{1,0:T(8,128)S(1)}, f32[104,1024]{1,0:T(8,128)S(1)}, u32[]{:S(2)}, u32[]{:S(2)}) %collective-permute-start.23) | collective-permute-done | bytes 426016 | tf_op jit(solution)/shard_map/ppermute | solution.py:371
  102.6 3.0 %collective-permute-done.24.v_up.refs_4_ = f32[104,1024]{1,0:T(8,128)S(1)} collective-permute-done((f32[104,1024]{1,0:T(8,128)S(1)}, f32[104,1024]{1,0:T(8,128)S(1)}, u32[]{:S(2)}, u32[]{:S(2)}) %collective-permute-start.24) | collective-permute-done | bytes 426016 | tf_op jit(solution)/shard_map/ppermute | solution.py:371
  105.7 0.7 collective-permute-start.27
  106.4 2.8 %update.1 = (f32[2,64,512]{2,1,0:T(8,128)}, f32[2,512]{1,0:T(2,128)S(1)}) custom-call(s32[4]{0:T(128)S(1)} %pad_add_fusion.idx.refs_0_, f32[2,64,256]{2,1,0:T(8,128)S(1)} %get-tuple-element.166.ga0, f32[2,64,256]{2,1,0:T(8,128)S(1)} %collective-permute-done.16.refs_11_.ga1, f32[2,64,256]{2,1,0:T(8,128)S(1)} %collective-permute-done.17.refs_12_.ga2, ...), custom_call_target="tpu_custom_call" | custom-call | flops 5000000000 | bytes 1048576 | tf_op jit(solution)/shard_map/update/pallas_call | solution.py:546
  109.7 1.7 %collective-permute-done.26.refs_1_ = f32[80,1024]{1,0:T(8,128)S(1)} collective-permute-done((f32[80,1024]{1,0:T(8,128)S(1)}, f32[80,1024]{1,0:T(8,128)S(1)}, u32[]{:S(2)}, u32[]{:S(2)}) %collective-permute-start.26) | collective-permute-done | bytes 327712 | tf_op jit(solution)/shard_map/ppermute | solution.py:371
  111.4 1.7 %collective-permute-done.27.refs_5_ = f32[88,1024]{1,0:T(8,128)S(1)} collective-permute-done((f32[88,1024]{1,0:T(8,128)S(1)}, f32[88,1024]{1,0:T(8,128)S(1)}, u32[]{:S(2)}, u32[]{:S(2)}) %collective-permute-start.27) | collective-permute-done | bytes 360480 | tf_op jit(solution)/shard_map/ppermute | solution.py:371
  113.2 1.2 %sum.1 = (f32[1024,128]{1,0:T(8,128)}, f32[256,128]{1,0:T(8,128)}, f32[32,128]{1,0:T(8,128)}, f32[32,128]{1,0:T(8,128)}) custom-call(f32[32,128]{1,0:T(8,128)S(1)} %get-tuple-element.209.column, f32[80,1024]{1,0:T(8,128)S(1)} %get-tuple-element.210.refs_0_, f32[80,1024]{1,0:T(8,128)S(1)} %collective-permute-done.26.refs_1_, ...), custom_call_target="tpu_custom_call" | custom-call | flops 1000000 | bytes 1048576 | tf_op jit(solution)/shard_map/sum/pallas_call | solution.py:549
  (43 shorter events, 4.3 us)
Async XLA Ops:
  4.7 12.5 %collective-permute-start = (f32[128,256]{1,0:T(8,128)S(1)}, f32[128,256]{1,0:T(8,128)S(1)}, u32[]{:S(2)}, u32[]{:S(2)}) collective-permute-start(f32[128,256]{1,0:T(8,128)S(1)} %get-tuple-element.116), channel_id=1, source_target_pairs={{0,4},{4,8},{8,12},{12,0},{1,5},{5,9},{9,13},{13,1},{2,6},{6,10},{... | collective-permute-start | bytes 393224 | tf_op jit(solution)/shard_map/ppermute | solution.py:371
  6.8 10.5 %collective-permute-start.1 = (f32[128,256]{1,0:T(8,128)S(1)}, f32[128,256]{1,0:T(8,128)S(1)}, u32[]{:S(2)}, u32[]{:S(2)}) collective-permute-start(f32[128,256]{1,0:T(8,128)S(1)} %get-tuple-element.117), channel_id=1, source_target_pairs={{0,8},{4,12},{8,0},{12,4},{1,9},{5,13},{9,1},{13,5},{2,10},{6,14},... | collective-permute-start | bytes 393224 | tf_op jit(solution)/shard_map/ppermute | solution.py:371
  10.4 6.9 %collective-permute-start.2 = (f32[128,256]{1,0:T(8,128)S(1)}, f32[128,256]{1,0:T(8,128)S(1)}, u32[]{:S(2)}, u32[]{:S(2)}) collective-permute-start(f32[128,256]{1,0:T(8,128)S(1)} %get-tuple-element.118), channel_id=1, source_target_pairs={{0,12},{4,0},{8,4},{12,8},{1,13},{5,1},{9,5},{13,9},{2,14},{6,2},{... | collective-permute-start | bytes 393224 | tf_op jit(solution)/shard_map/ppermute | solution.py:371
  17.9 14.4 %collective-permute-start.6 = (f32[4,128,256]{2,1,0:T(8,128)S(1)}, f32[4,128,256]{2,1,0:T(8,128)S(1)}, u32[]{:S(2)}, u32[]{:S(2)}) collective-permute-start(f32[4,128,256]{2,1,0:T(8,128)S(1)} %pack.2.refs_1_.refs_2_), channel_id=1, source_target_pairs={{0,2},{2,0},{1,3},{3,1},{4,6},{6,4},{5,7},{7,5},{8,10},{10,8},{9,1... | collective-permute-start | bytes 1572872 | tf_op jit(solution)/shard_map/ppermute | solution.py:375
  21.0 8.3 %collective-permute-start.3 = (f32[128,256]{1,0:T(8,128)S(1)}, f32[128,256]{1,0:T(8,128)S(1)}, u32[]{:S(2)}, u32[]{:S(2)}) collective-permute-start(f32[128,256]{1,0:T(8,128)S(1)} %get-tuple-element.127), channel_id=1, source_target_pairs={{0,4},{4,8},{8,12},{12,0},{1,5},{5,9},{9,13},{13,1},{2,6},{6,10},{... | collective-permute-start | bytes 393224 | tf_op jit(solution)/shard_map/ppermute | solution.py:371
  22.0 7.3 %collective-permute-start.4 = (f32[128,256]{1,0:T(8,128)S(1)}, f32[128,256]{1,0:T(8,128)S(1)}, u32[]{:S(2)}, u32[]{:S(2)}) collective-permute-start(f32[128,256]{1,0:T(8,128)S(1)} %get-tuple-element.128), channel_id=1, source_target_pairs={{0,8},{4,12},{8,0},{12,4},{1,9},{5,13},{9,1},{13,5},{2,10},{6,14},... | collective-permute-start | bytes 393224 | tf_op jit(solution)/shard_map/ppermute | solution.py:371
  23.7 11.6 %copy-start.1 = (f32[4096]{0:T(1024)S(1)}, f32[4096]{0:T(1024)}, u32[]{:S(2)}) copy-start(f32[4096]{0:T(1024)} %param.20) | copy-start | bytes 49156
  23.7 6.0 %collective-permute-start.5 = (f32[128,256]{1,0:T(8,128)S(1)}, f32[128,256]{1,0:T(8,128)S(1)}, u32[]{:S(2)}, u32[]{:S(2)}) collective-permute-start(f32[128,256]{1,0:T(8,128)S(1)} %get-tuple-element.129), channel_id=1, source_target_pairs={{0,12},{4,0},{8,4},{12,8},{1,13},{5,1},{9,5},{13,9},{2,14},{6,2},{... | collective-permute-start | bytes 393224 | tf_op jit(solution)/shard_map/ppermute | solution.py:371
  25.0 10.3 %copy-start = (f32[1024,2,256]{2,1,0:T(2,128)S(1)}, f32[1024,2,256]{2,1,0:T(2,128)}, u32[]{:S(2)}) copy-start(f32[1024,2,256]{2,1,0:T(2,128)} %param.17) | copy-start | bytes 6291460
  30.3 6.6 %collective-permute-start.7 = (f32[4,128,256]{2,1,0:T(8,128)S(1)}, f32[4,128,256]{2,1,0:T(8,128)S(1)}, u32[]{:S(2)}, u32[]{:S(2)}) collective-permute-start(f32[4,128,256]{2,1,0:T(8,128)S(1)} %pack.3.refs_1_), channel_id=1, source_target_pairs={{0,1},{1,0},{2,3},{3,2},{4,5},{5,4},{6,7},{7,6},{8,9},{9,8},{10,11... | collective-permute-start | bytes 1572872 | tf_op jit(solution)/shard_map/ppermute | solution.py:375
  32.3 4.6 %collective-permute-start.8 = (f32[4,128,256]{2,1,0:T(8,128)S(1)}, f32[4,128,256]{2,1,0:T(8,128)S(1)}, u32[]{:S(2)}, u32[]{:S(2)}) collective-permute-start(f32[4,128,256]{2,1,0:T(8,128)S(1)} %collective-permute-done.6.refs_2_), channel_id=1, source_target_pairs={{0,1},{1,0},{2,3},{3,2},{4,5},{5,4},{6,7},{7,6},{8,9},{9,8},{10,11... | collective-permute-start | bytes 1572872 | tf_op jit(solution)/shard_map/ppermute | solution.py:375
  32.3 16.5 %collective-permute-start.10 = (f32[4,128,256]{2,1,0:T(8,128)S(1)}, f32[4,128,256]{2,1,0:T(8,128)S(1)}, u32[]{:S(2)}, u32[]{:S(2)}) collective-permute-start(f32[4,128,256]{2,1,0:T(8,128)S(1)} %pack.3.refs_1_), channel_id=1, source_target_pairs={{0,2},{2,0},{1,3},{3,1},{4,6},{6,4},{5,7},{7,5},{8,10},{10,8},{9,1... | collective-permute-start | bytes 1572872 | tf_op jit(solution)/shard_map/ppermute | solution.py:375
  44.1 5.8 %collective-permute-start.9 = (f32[264,128]{1,0:T(8,128)S(1)}, f32[264,128]{1,0:T(8,128)S(1)}, u32[]{:S(2)}, u32[]{:S(2)}) collective-permute-start(f32[264,128]{1,0:T(8,128)S(1)} %get-tuple-element.145), channel_id=1, source_target_pairs={{0,32},{16,48},{32,0},{48,16},{64,96},{80,112},{96,64},{112,80},{1... | collective-permute-start | bytes 405512 | tf_op jit(solution)/shard_map/ppermute | solution.py:375
  45.8 7.3 %collective-permute-start.12 = (f32[4,128,256]{2,1,0:T(8,128)S(1)}, f32[4,128,256]{2,1,0:T(8,128)S(1)}, u32[]{:S(2)}, u32[]{:S(2)}) collective-permute-start(f32[4,128,256]{2,1,0:T(8,128)S(1)} %pack.2.refs_1_.refs_2_), channel_id=1, source_target_pairs={{0,1},{1,0},{2,3},{3,2},{4,5},{5,4},{6,7},{7,6},{8,9},{9,8},{10,11... | collective-permute-start | bytes 1572872 | tf_op jit(solution)/shard_map/ppermute | solution.py:375
  49.9 3.1 %collective-permute-start.13 = (f32[4,128,256]{2,1,0:T(8,128)S(1)}, f32[4,128,256]{2,1,0:T(8,128)S(1)}, u32[]{:S(2)}, u32[]{:S(2)}) collective-permute-start(f32[4,128,256]{2,1,0:T(8,128)S(1)} %collective-permute-done.10.refs_2_), channel_id=1, source_target_pairs={{0,1},{1,0},{2,3},{3,2},{4,5},{5,4},{6,7},{7,6},{8,9},{9,8},{10,11... | collective-permute-start | bytes 1572872 | tf_op jit(solution)/shard_map/ppermute | solution.py:375
  49.9 7.4 %collective-permute-start.11 = (f32[264,128]{1,0:T(8,128)S(1)}, f32[264,128]{1,0:T(8,128)S(1)}, u32[]{:S(2)}, u32[]{:S(2)}) collective-permute-start(f32[264,128]{1,0:T(8,128)S(1)} %add.16), channel_id=1, source_target_pairs={{0,96},{16,112},{32,64},{48,80},{64,32},{80,48},{96,0},{112,16},{1... | collective-permute-start | bytes 405512 | tf_op jit(solution)/shard_map/ppermute | solution.py:375
  57.3 5.4 %copy-start.2 = (s32[1,128]{1,0:T(1,128)S(1)}, s32[1,128]{1,0:T(1,128)}, u32[]{:S(2)}) copy-start(s32[1,128]{1,0:T(1,128)} %labels.1) | copy-start | bytes 1540
  57.3 5.4 %collective-permute-start.14 = (f32[264,128]{1,0:T(8,128)S(1)}, f32[264,128]{1,0:T(8,128)S(1)}, u32[]{:S(2)}, u32[]{:S(2)}) collective-permute-start(f32[264,128]{1,0:T(8,128)S(1)} %add.17.mine), channel_id=1, source_target_pairs={{0,16},{16,0},{32,48},{48,32},{64,80},{80,64},{96,112},{112,96},{1... | collective-permute-start | bytes 405512 | tf_op jit(solution)/shard_map/ppermute | solution.py:375
  63.8 1.4 %collective-permute-start.15 = (f32[264,128]{1,0:T(8,128)S(1)}, f32[264,128]{1,0:T(8,128)S(1)}, u32[]{:S(2)}, u32[]{:S(2)}) collective-permute-start(f32[264,128]{1,0:T(8,128)S(1)} %get-tuple-element.160.refs_1_), channel_id=1, source_target_pairs={{0,1},{1,0},{2,3},{3,2},{4,5},{5,4},{6,7},{7,6},{8,9},{9,8},{10,11... | collective-permute-start | bytes 405512 | tf_op jit(solution)/shard_map/ppermute | solution.py:375
  63.8 7.5 %collective-permute-start.19 = (f32[264,128]{1,0:T(8,128)S(1)}, f32[264,128]{1,0:T(8,128)S(1)}, u32[]{:S(2)}, u32[]{:S(2)}) collective-permute-start(f32[264,128]{1,0:T(8,128)S(1)} %get-tuple-element.160.refs_1_), channel_id=1, source_target_pairs={{0,2},{2,0},{1,3},{3,1},{4,6},{6,4},{5,7},{7,5},{8,10},{10,8},{9,1... | collective-permute-start | bytes 405512 | tf_op jit(solution)/shard_map/ppermute | solution.py:375
  71.3 3.7 %collective-permute-start.20 = (f32[264,128]{1,0:T(8,128)S(1)}, f32[264,128]{1,0:T(8,128)S(1)}, u32[]{:S(2)}, u32[]{:S(2)}) collective-permute-start(f32[264,128]{1,0:T(8,128)S(1)} %collective-permute-done.19.refs_1_), channel_id=1, source_target_pairs={{0,1},{1,0},{2,3},{3,2},{4,5},{5,4},{6,7},{7,6},{8,9},{9,8},{10,11... | collective-permute-start | bytes 405512 | tf_op jit(solution)/shard_map/ppermute | solution.py:375
  71.3 11.1 %collective-permute-start.16 = (f32[2,64,256]{2,1,0:T(8,128)S(1)}, f32[2,64,256]{2,1,0:T(8,128)S(1)}, u32[]{:S(2)}, u32[]{:S(2)}) collective-permute-start(f32[2,64,256]{2,1,0:T(8,128)S(1)} %get-tuple-element.167), channel_id=1, source_target_pairs={{0,4},{4,8},{8,12},{12,0},{1,5},{5,9},{9,13},{13,1},{2,6},{6,10},{... | collective-permute-start | bytes 393224 | tf_op jit(solution)/shard_map/ppermute | solution.py:371
  72.4 10.1 %collective-permute-start.17 = (f32[2,64,256]{2,1,0:T(8,128)S(1)}, f32[2,64,256]{2,1,0:T(8,128)S(1)}, u32[]{:S(2)}, u32[]{:S(2)}) collective-permute-start(f32[2,64,256]{2,1,0:T(8,128)S(1)} %get-tuple-element.168), channel_id=1, source_target_pairs={{0,8},{4,12},{8,0},{12,4},{1,9},{5,13},{9,1},{13,5},{2,10},{6,14},... | collective-permute-start | bytes 393224 | tf_op jit(solution)/shard_map/ppermute | solution.py:371
  74.5 7.9 %collective-permute-start.18 = (f32[2,64,256]{2,1,0:T(8,128)S(1)}, f32[2,64,256]{2,1,0:T(8,128)S(1)}, u32[]{:S(2)}, u32[]{:S(2)}) collective-permute-start(f32[2,64,256]{2,1,0:T(8,128)S(1)} %get-tuple-element.169), channel_id=1, source_target_pairs={{0,12},{4,0},{8,4},{12,8},{1,13},{5,1},{9,5},{13,9},{2,14},{6,2},{... | collective-permute-start | bytes 393224 | tf_op jit(solution)/shard_map/ppermute | solution.py:371
  79.1 12.2 %collective-permute-start.21 = (f32[96,1024]{1,0:T(8,128)S(1)}, f32[96,1024]{1,0:T(8,128)S(1)}, u32[]{:S(2)}, u32[]{:S(2)}) collective-permute-start(f32[96,1024]{1,0:T(8,128)S(1)} %get-tuple-element.184), channel_id=1, source_target_pairs={{0,4},{4,8},{8,12},{12,0},{1,5},{5,9},{9,13},{13,1},{2,6},{6,10},{... | collective-permute-start | bytes 1179656 | tf_op jit(solution)/shard_map/ppermute | solution.py:371
  80.7 12.1 %collective-permute-start.22 = (f32[96,1024]{1,0:T(8,128)S(1)}, f32[96,1024]{1,0:T(8,128)S(1)}, u32[]{:S(2)}, u32[]{:S(2)}) collective-permute-start(f32[96,1024]{1,0:T(8,128)S(1)} %get-tuple-element.185), channel_id=1, source_target_pairs={{0,12},{4,0},{8,4},{12,8},{1,13},{5,1},{9,5},{13,9},{2,14},{6,2},{... | collective-permute-start | bytes 1179656 | tf_op jit(solution)/shard_map/ppermute | solution.py:371
  84.6 4.3 %copy-start.3 = (f32[2,1,512]{2,1,0:T(1,128)S(1)}, f32[2,1,512]{2,1,0:T(1,128)}, u32[]{:S(2)}) copy-start(f32[2,1,512]{2,1,0:T(1,128)} %param.15) | copy-start | bytes 12292
  86.7 15.9 %collective-permute-start.23 = (f32[104,1024]{1,0:T(8,128)S(1)}, f32[104,1024]{1,0:T(8,128)S(1)}, u32[]{:S(2)}, u32[]{:S(2)}) collective-permute-start(f32[104,1024]{1,0:T(8,128)S(1)} %get-tuple-element.200), channel_id=1, source_target_pairs={{0,12},{4,0},{8,4},{12,8},{1,13},{5,1},{9,5},{13,9},{2,14},{6,2},{... | collective-permute-start | bytes 1277960 | tf_op jit(solution)/shard_map/ppermute | solution.py:371
  88.9 16.7 %collective-permute-start.24 = (f32[104,1024]{1,0:T(8,128)S(1)}, f32[104,1024]{1,0:T(8,128)S(1)}, u32[]{:S(2)}, u32[]{:S(2)}) collective-permute-start(f32[104,1024]{1,0:T(8,128)S(1)} %get-tuple-element.201), channel_id=1, source_target_pairs={{0,4},{4,8},{8,12},{12,0},{1,5},{5,9},{9,13},{13,1},{2,6},{6,10},{... | collective-permute-start | bytes 1277960 | tf_op jit(solution)/shard_map/ppermute | solution.py:371
  88.9 17.5 %collective-permute-start.25 = (f32[32,1024]{1,0:T(8,128)S(1)}, f32[32,1024]{1,0:T(8,128)S(1)}, u32[]{:S(2)}, u32[]{:S(2)}) collective-permute-start(f32[32,1024]{1,0:T(8,128)S(1)} %get-tuple-element.204), channel_id=1, source_target_pairs={{0,8},{4,12},{8,0},{12,4},{1,9},{5,13},{9,1},{13,5},{2,10},{6,14},... | collective-permute-start | bytes 393224 | tf_op jit(solution)/shard_map/ppermute | solution.py:371
  92.8 18.6 %collective-permute-start.26 = (f32[80,1024]{1,0:T(8,128)S(1)}, f32[80,1024]{1,0:T(8,128)S(1)}, u32[]{:S(2)}, u32[]{:S(2)}) collective-permute-start(f32[80,1024]{1,0:T(8,128)S(1)} %slice_add_fusion.1), channel_id=1, source_target_pairs={{0,4},{4,8},{8,12},{12,0},{1,5},{5,9},{9,13},{13,1},{2,6},{6,10},{... | collective-permute-start | bytes 983048 | tf_op jit(solution)/shard_map/ppermute | solution.py:371
  105.7 7.5 %collective-permute-start.27 = (f32[88,1024]{1,0:T(8,128)S(1)}, f32[88,1024]{1,0:T(8,128)S(1)}, u32[]{:S(2)}, u32[]{:S(2)}) collective-permute-start(f32[88,1024]{1,0:T(8,128)S(1)} %slice_add_fusion), channel_id=1, source_target_pairs={{0,12},{4,0},{8,4},{12,8},{1,13},{5,1},{9,5},{13,9},{2,14},{6,2},{... | collective-permute-start | bytes 1081352 | tf_op jit(solution)/shard_map/ppermute | solution.py:371

commit v9 on v8

--- a/solution.py
+++ b/solution.py
@@ -427,14 +427,6 @@
     near = [near[0]] + [shift(near[k], "z", 4, k) for k in (1, 2, 3)]
     view, _ = lax.optimization_barrier((view, fq_far))
     w1hb, w1lb = turn(view, 1)
-    *near, _ = lax.optimization_barrier((*near, w1hb))
-    (fq_near,) = pack(idx, *near)
-    y1 = flip(fq_near, "core", 2, 1)
-    y2 = flip(x2, "core", 2, 1)
-    x2b = flip(fq_near, "xh", 2, 1)
-    y1b = flip(fq_far, "core", 2, 1)
-    y2b = flip(x2b, "core", 2, 1)
-
     _, lift_weight, press_weight = lax.optimization_barrier((w1hb, lift_weight, press_weight))
     second_view = second_weight.reshape(1024, 2, 2, 128).transpose(0, 2, 1, 3).reshape(1024, 4, 128)
     w2th, w2tl, lift, press, head = call(
@@ -445,6 +437,14 @@
         name="prepare",
         flops=1e6,
     )(idx, second_view, hbm(lift_weight), hbm(press_weight), head_weight.reshape(32, 128))
+
+    *near, _, _ = lax.optimization_barrier((*near, w1hb, w2th))
+    (fq_near,) = pack(idx, *near)
+    y1 = flip(fq_near, "core", 2, 1)
+    y2 = flip(x2, "core", 2, 1)
+    x2b = flip(fq_near, "xh", 2, 1)
+    y1b = flip(fq_far, "core", 2, 1)
+    y2b = flip(x2b, "core", 2, 1)
 
     scratch = [pltpu.VMEM((1024, 256), BF16)] * 2
     weights = (w1ha, w1la, w1hb, w1lb, w2th, w2tl, press, lift, head)

time: 114 us -> 113 us (level)
  waiting for transfers between devices: 26.4 us -> 22.5 us
  starting transfers between devices: 35.9 us -> 38.3 us
    ppermute x12, waiting for transfers between devices: 7.28 us -> 4.88 us  [flip(): return lax.ppermute(x, axis, [(i, i ^ bit) for i in range(size)])]
    ppermute x12, starting transfers between devices: 12.9 us -> 15.3 us  [flip(): return lax.ppermute(x, axis, [(i, i ^ bit) for i in range(size)])]
    ppermute x16, waiting for transfers between devices: 19.1 us -> 17.6 us  [shift(): return lax.ppermute(x, axis, [(i, (i + by) % size) for i in range(size)])]
  transfers between devices with their start and end apart: 28 -> 28, of which waited for: 14 -> 12; matrix products, arithmetic and copies ran while one was open for 1% -> 1% of each run, Pallas kernels for 38% -> 38%
where the time goes in v9:
time: 113 us
  Pallas kernels  50.2 us (44%)
  starting transfers between devices  38.3 us (34%)
  waiting for transfers between devices  22.5 us (20%)
    ppermute x16, starting transfers between devices, shift(): return lax.ppermute(x, axis, [(i, (i + by) % size) for i in range(size)])  23 us
    ppermute x16, waiting for transfers between devices, shift(): return lax.ppermute(x, axis, [(i, (i + by) % size) for i in range(size)])  17.6 us
    ppermute x12, starting transfers between devices, flip(): return lax.ppermute(x, axis, [(i, i ^ bit) for i in range(size)])  15.3 us
    pallas_call x3, Pallas kernels, grads(): call(lambda *refs: grads_kernel(towers, with_pq, len(extra), *refs), [bf1...  8.17 us
    pallas_call x2, Pallas kernels, later_half(): call(lambda *refs: forward_kernel((t,), False, *refs), [f32(1, 1024, 256)...  7.24 us
    pallas_call x1, Pallas kernels, per_device(): call(lambda *refs: forward_kernel((0, 1), True, *refs), [f32(2, 1024, 256...  7.18 us
    pallas_call x2, Pallas kernels, turn(): pl.pallas_call(lambda *refs: turn_kernel(at, *refs), in_specs=[any_spec],...  6.07 us
    ppermute x12, waiting for transfers between devices, flip(): return lax.ppermute(x, axis, [(i, i ^ bit) for i in range(size)])  4.88 us
  transfers between devices with their start and end apart: 28, of which 12 were waited for; matrix products, arithmetic and copies ran while one was open for 1% of the time, Pallas kernels for 38%

profile of v9, /device:TPU:0, one launch (start us, length us, event | category | flops | bytes accessed | tf_op | source)
XLA Modules:
  0.0 112.7 jit_solution(16256608511824746793)
XLA Ops:
  0.7 4.0 %pool_far.1 = (f32[128,256]{1,0:T(8,128)S(1)}, f32[128,256]{1,0:T(8,128)S(1)}, f32[128,256]{1,0:T(8,128)S(1)}, f32[128,256]{1,0:T(8,128)S(1)}, bf16[2,4,512,256]...) custom-call(s32[4]{0:T(128)S(1)} %pad_add_fusion.idx.refs_0_, s32[2,4,2048]{2,1,0:T(4,128)} %bitcast.49, ...), custom_call_target="tpu_custom_call" | custom-call | flops 1000000 | bytes 1048576 | tf_op jit(solution)/shard_map/pool_far/pallas_call | solution.py:390
  4.7 2.1 %collective-permute-start = (f32[128,256]{1,0:T(8,128)S(1)}, f32[128,256]{1,0:T(8,128)S(1)}, u32[]{:S(2)}, u32[]{:S(2)}) collective-permute-start(f32[128,256]{1,0:T(8,128)S(1)} %get-tuple-element.116), channel_id=1, source_target_pairs={{0,4},{4,8},{8,12},{12,0},{1,5},{5,9},{9,13},{13,1},{2,6},{6,10},{... | collective-permute-start | bytes 393224 | tf_op jit(solution)/shard_map/ppermute | solution.py:371
  6.8 3.6 %collective-permute-start.1 = (f32[128,256]{1,0:T(8,128)S(1)}, f32[128,256]{1,0:T(8,128)S(1)}, u32[]{:S(2)}, u32[]{:S(2)}) collective-permute-start(f32[128,256]{1,0:T(8,128)S(1)} %get-tuple-element.117), channel_id=1, source_target_pairs={{0,8},{4,12},{8,0},{12,4},{1,9},{5,13},{9,1},{13,5},{2,10},{6,14},... | collective-permute-start | bytes 393224 | tf_op jit(solution)/shard_map/ppermute | solution.py:371
  10.4 1.0 collective-permute-start.2
  11.4 2.8 %pool_near.1 = (f32[128,256]{1,0:T(8,128)S(1)}, f32[128,256]{1,0:T(8,128)S(1)}, f32[128,256]{1,0:T(8,128)S(1)}, f32[128,256]{1,0:T(8,128)S(1)}, bf16[2,4,512,256]{3,2,1,0:T(8,128)(2,1)S(1)}) custom-call(s32[4]{0:T(128)S(1)} %pad_add_fusion.idx.refs_0_, s32[2,4,2048]{2,1,0:T(4,128)S(1)} %get-tuple-element.119.bag, f32[2,64,512]{2,1,0:T(8,128)S(1)} %get-tuple-element.113.decayed), custom_call_target="tpu_custom_call" | custom-call | flops 1000000 | bytes 1048576 | tf_op jit(solution)/shard_map/pool_near/pallas_call | solution.py:405
  14.2 3.0 %turn_0.1 = (bf16[2,1024,512]{2,1,0:T(8,128)(2,1)S(1)}, bf16[2,1024,512]{2,1,0:T(8,128)(2,1)S(1)}) custom-call(f32[1024,16,128]{2,1,0:T(8,128)} %bitcast.45), custom_call_target="tpu_custom_call" | custom-call | flops 1000000 | bytes 1048576 | tf_op jit(solution)/shard_map/turn_0/pallas_call | solution.py:411
  17.9 3.1 %collective-permute-start.6 = (f32[4,128,256]{2,1,0:T(8,128)S(1)}, f32[4,128,256]{2,1,0:T(8,128)S(1)}, u32[]{:S(2)}, u32[]{:S(2)}) collective-permute-start(f32[4,128,256]{2,1,0:T(8,128)S(1)} %pack.2.refs_1_.refs_2_), channel_id=1, source_target_pairs={{0,2},{2,0},{1,3},{3,1},{4,6},{6,4},{5,7},{7,5},{8,10},{10,8},{9,1... | collective-permute-start | bytes 1572872 | tf_op jit(solution)/shard_map/ppermute | solution.py:375
  21.0 1.0 collective-permute-start.3
  22.0 1.7 %collective-permute-start.4 = (f32[128,256]{1,0:T(8,128)S(1)}, f32[128,256]{1,0:T(8,128)S(1)}, u32[]{:S(2)}, u32[]{:S(2)}) collective-permute-start(f32[128,256]{1,0:T(8,128)S(1)} %get-tuple-element.128), channel_id=1, source_target_pairs={{0,8},{4,12},{8,0},{12,4},{1,9},{5,13},{9,1},{13,5},{2,10},{6,14},... | collective-permute-start | bytes 393224 | tf_op jit(solution)/shard_map/ppermute | solution.py:371
  23.7 1.2 %collective-permute-start.5 = (f32[128,256]{1,0:T(8,128)S(1)}, f32[128,256]{1,0:T(8,128)S(1)}, u32[]{:S(2)}, u32[]{:S(2)}) collective-permute-start(f32[128,256]{1,0:T(8,128)S(1)} %get-tuple-element.129), channel_id=1, source_target_pairs={{0,12},{4,0},{8,4},{12,8},{1,13},{5,1},{9,5},{13,9},{2,14},{6,2},{... | collective-permute-start | bytes 393224 | tf_op jit(solution)/shard_map/ppermute | solution.py:371
  25.0 3.0 %turn_1.1 = (bf16[2,1024,512]{2,1,0:T(8,128)(2,1)S(1)}, bf16[2,1024,512]{2,1,0:T(8,128)(2,1)S(1)}) custom-call(f32[1024,16,128]{2,1,0:T(8,128)} %bitcast.46), custom_call_target="tpu_custom_call" | custom-call | flops 1000000 | bytes 1048576 | tf_op jit(solution)/shard_map/turn_1/pallas_call | solution.py:411
  28.0 1.6 %prepare.1 = (bf16[2,256,1024]{2,1,0:T(8,128)(2,1)S(1)}, bf16[2,256,1024]{2,1,0:T(8,128)(2,1)S(1)}, f32[512,128]{1,0:T(8,128)S(1)}, f32[512,128]{1,0:T(8,128)S(1)}, f32[1,512]{1,0:T(1,128)S(1)}) custom-call(s32[4]{0:T(128)S(1)} %pad_add_fusion.idx.refs_0_, f32[1024,4,128]{2,1,0:T(4,128)S(1)} %bitcast.40, f32[4096,128]{1,0:T(8,128)} %lift_hbm, ...), custom_call_target="tpu_custom_call" | custom-call | flops 1000000 | bytes 1048576 | tf_op jit(solution)/shard_map/prepare/pallas_call | solution.py:432
  30.4 1.9 %collective-permute-done.6.refs_2_ = f32[4,128,256]{2,1,0:T(8,128)S(1)} collective-permute-done((f32[4,128,256]{2,1,0:T(8,128)S(1)}, f32[4,128,256]{2,1,0:T(8,128)S(1)}, u32[]{:S(2)}, u32[]{:S(2)}) %collective-permute-start.6) | collective-permute-done | bytes 524320 | tf_op jit(solution)/shard_map/ppermute | solution.py:375
  32.3 3.0 %collective-permute-start.10 = (f32[4,128,256]{2,1,0:T(8,128)S(1)}, f32[4,128,256]{2,1,0:T(8,128)S(1)}, u32[]{:S(2)}, u32[]{:S(2)}) collective-permute-start(f32[4,128,256]{2,1,0:T(8,128)S(1)} %pack.3.refs_1_), channel_id=1, source_target_pairs={{0,2},{2,0},{1,3},{3,1},{4,6},{6,4},{5,7},{7,5},{8,10},{10,8},{9,1... | collective-permute-start | bytes 1572872 | tf_op jit(solution)/shard_map/ppermute | solution.py:375
  35.3 7.2 %forward_a.1 = (f32[2,1024,256]{2,1,0:T(8,128)S(1)}, f32[512,256]{1,0:T(8,128)S(1)}, f32[264,128]{1,0:T(8,128)S(1)}) custom-call(s32[4]{0:T(128)S(1)} %pad_add_fusion.idx.refs_0_, f32[4,128,256]{2,1,0:T(8,128)S(1)} %pack.3.refs_1_, f32[4,128,256]{2,1,0:T(8,128)S(1)} %collective-permute-done.6.refs_2_, f32[4,128,256]{2,1,0:T(8,128)S(1)} %collective-permute-done.7.refs_3_, ...), custom_call_target="tpu_custom_call" | custom-call | flops 1000000 | bytes 1048576 | tf_op jit(solution)/shard_map/forward_a/pallas_call | solution.py:451
  42.5 1.6 %collective-permute-start.9 = (f32[264,128]{1,0:T(8,128)S(1)}, f32[264,128]{1,0:T(8,128)S(1)}, u32[]{:S(2)}, u32[]{:S(2)}) collective-permute-start(f32[264,128]{1,0:T(8,128)S(1)} %get-tuple-element.145), channel_id=1, source_target_pairs={{0,32},{16,48},{32,0},{48,16},{64,96},{80,112},{96,64},{112,80},{1... | collective-permute-start | bytes 405512 | tf_op jit(solution)/shard_map/ppermute | solution.py:375
  44.1 2.5 %pick.1 = (bf16[2,256,1024]{2,1,0:T(8,128)(2,1)S(1)}, bf16[2,256,1024]{2,1,0:T(8,128)(2,1)S(1)}, f32[32,128]{1,0:T(8,128)S(1)}) custom-call(s32[4]{0:T(128)S(1)} %pad_add_fusion.idx.refs_0_, f32[1024,16,128]{2,1,0:T(8,128)} %bitcast.47, f32[1,512]{1,0:T(1,128)S(1)} %get-tuple-element.143.refs_13_.head.refs_10_), custom_call_target="tpu_custom_call" | custom-call | flops 1000000 | bytes 1048576 | tf_op jit(solution)/shard_map/pick/pallas_call | solution.py:472
  47.1 1.0 collective-permute-done.10.refs_2_
  48.3 3.1 %collective-permute-start.11 = (f32[264,128]{1,0:T(8,128)S(1)}, f32[264,128]{1,0:T(8,128)S(1)}, u32[]{:S(2)}, u32[]{:S(2)}) collective-permute-start(f32[264,128]{1,0:T(8,128)S(1)} %add.16), channel_id=1, source_target_pairs={{0,96},{16,112},{32,64},{48,80},{64,32},{80,48},{96,0},{112,16},{1... | collective-permute-start | bytes 405512 | tf_op jit(solution)/shard_map/ppermute | solution.py:375
  51.4 3.6 %forward_b0.1 = (f32[1,1024,256]{2,1,0:T(8,128)S(1)}, f32[256,256]{1,0:T(8,128)S(1)}) custom-call(s32[4]{0:T(128)S(1)} %pad_add_fusion.idx.refs_0_, f32[4,128,256]{2,1,0:T(8,128)S(1)} %pack.2.refs_1_.refs_2_, f32[4,128,256]{2,1,0:T(8,128)S(1)} %collective-permute-done.10.refs_2_, f32[4,128,256]{2,1,0:T(8,128)S(1)} %collective-permute-done.12.refs_3_, ...), custom_call_target="tpu_custom_call" | custom-call | flops 4000000000 | bytes 1048576 | tf_op jit(solution)/shard_map/forward_b0/pallas_call | solution.py:461
  55.0 0.6 collective-permute-done.11
  55.7 1.4 %collective-permute-start.14 = (f32[264,128]{1,0:T(8,128)S(1)}, f32[264,128]{1,0:T(8,128)S(1)}, u32[]{:S(2)}, u32[]{:S(2)}) collective-permute-start(f32[264,128]{1,0:T(8,128)S(1)} %add.17.mine), channel_id=1, source_target_pairs={{0,16},{16,0},{32,48},{48,32},{64,80},{80,64},{96,112},{112,96},{1... | collective-permute-start | bytes 405512 | tf_op jit(solution)/shard_map/ppermute | solution.py:375
  57.1 3.6 %forward_b1.1 = (f32[1,1024,256]{2,1,0:T(8,128)S(1)}, f32[256,256]{1,0:T(8,128)S(1)}) custom-call(s32[4]{0:T(128)S(1)} %pad_add_fusion.idx.refs_0_, f32[4,128,256]{2,1,0:T(8,128)S(1)} %pack.2.refs_1_.refs_2_, f32[4,128,256]{2,1,0:T(8,128)S(1)} %collective-permute-done.10.refs_2_, f32[4,128,256]{2,1,0:T(8,128)S(1)} %collective-permute-done.12.refs_3_, ...), custom_call_target="tpu_custom_call" | custom-call | flops 4000000000 | bytes 1048576 | tf_op jit(solution)/shard_map/forward_b1/pallas_call | solution.py:461
  61.0 1.2 %logit.1 = (f32[264,128]{1,0:T(8,128)S(1)}, f32[1,16]{1,0:T(1,128)}) custom-call(s32[4]{0:T(128)S(1)} %pad_add_fusion.idx.refs_0_, f32[264,128]{1,0:T(8,128)S(1)} %add.17.mine, f32[264,128]{1,0:T(8,128)S(1)} %collective-permute-done.14.other, s32[1,128]{1,0:T(1,128)S(1)} %copy-done.2), custom_call_target="tpu_custom_call" | custom-call | flops 1000000 | bytes 1048576 | tf_op jit(solution)/shard_map/logit/pallas_call | solution.py:493
  62.2 2.9 %collective-permute-start.19 = (f32[264,128]{1,0:T(8,128)S(1)}, f32[264,128]{1,0:T(8,128)S(1)}, u32[]{:S(2)}, u32[]{:S(2)}) collective-permute-start(f32[264,128]{1,0:T(8,128)S(1)} %get-tuple-element.160.refs_1_), channel_id=1, source_target_pairs={{0,2},{2,0},{1,3},{3,1},{4,6},{6,4},{5,7},{7,5},{8,10},{10,8},{9,1... | collective-permute-start | bytes 405512 | tf_op jit(solution)/shard_map/ppermute | solution.py:375
  65.1 3.7 %grads_a.1 = (bf16[2,1024,256]{2,1,0:T(8,128)(2,1)S(1)}, bf16[2,1024,256]{2,1,0:T(8,128)(2,1)S(1)}, f32[2,256,256]{2,1,0:T(8,128)S(1)}, f32[2,64,256]{2,1,0:T(8,...) custom-call(s32[4]{0:T(128)S(1)} %pad_add_fusion.idx.refs_0_, ...), custom_call_target="tpu_custom_call" | custom-call | flops 4000000000 | bytes 1048576 | tf_op jit(solution)/shard_map/grads_a/pallas_call | solution.py:501
  68.8 0.9 collective-permute-done.19.refs_1_
  69.7 1.0 collective-permute-start.16
  70.7 2.2 %collective-permute-start.17 = (f32[2,64,256]{2,1,0:T(8,128)S(1)}, f32[2,64,256]{2,1,0:T(8,128)S(1)}, u32[]{:S(2)}, u32[]{:S(2)}) collective-permute-start(f32[2,64,256]{2,1,0:T(8,128)S(1)} %get-tuple-element.168), channel_id=1, source_target_pairs={{0,8},{4,12},{8,0},{12,4},{1,9},{5,13},{9,1},{13,5},{2,10},{6,14},... | collective-permute-start | bytes 393224 | tf_op jit(solution)/shard_map/ppermute | solution.py:371
  73.4 2.2 %grads_b0.1 = (bf16[1,1024,256]{2,1,0:T(8,128)(2,1)S(1)}, bf16[1,1024,256]{2,1,0:T(8,128)(2,1)S(1)}, f32[1,256,256]{2,1,0:T(8,128)S(1)}, f32[1,64,256]{2,1,0:T(8...) custom-call(s32[4]{0:T(128)S(1)} %pad_add_fusion.idx.refs_0_, ...), custom_call_target="tpu_custom_call" | custom-call | flops 4000000000 | bytes 1048576 | tf_op jit(solution)/shard_map/grads_b0/pallas_call | solution.py:501
  75.7 1.8 %weights_0.1 = (f32[80,1024]{1,0:T(8,128)S(1)}, f32[80,1024]{1,0:T(8,128)S(1)}, f32[96,1024]{1,0:T(8,128)S(1)}, f32[96,1024]{1,0:T(8,128)S(1)}) custom-call(s32[4]{0:T(128)S(1)} %pad_add_fusion.idx.refs_0_, f32[4,128,256]{2,1,0:T(8,128)S(1)} %pack.3.refs_1_, f32[4,128,256]{2,1,0:T(8,128)S(1)} %pack.2.refs_1_.refs_2_, ...), custom_call_target="tpu_custom_call" | custom-call | flops 3000000000 | bytes 1048576 | tf_op jit(solution)/shard_map/weights_0/pallas_call | solution.py:516
  77.5 1.6 %collective-permute-start.21 = (f32[96,1024]{1,0:T(8,128)S(1)}, f32[96,1024]{1,0:T(8,128)S(1)}, u32[]{:S(2)}, u32[]{:S(2)}) collective-permute-start(f32[96,1024]{1,0:T(8,128)S(1)} %get-tuple-element.184), channel_id=1, source_target_pairs={{0,4},{4,8},{8,12},{12,0},{1,5},{5,9},{9,13},{13,1},{2,6},{6,10},{... | collective-permute-start | bytes 1179656 | tf_op jit(solution)/shard_map/ppermute | solution.py:371
  79.1 1.7 %collective-permute-start.22 = (f32[96,1024]{1,0:T(8,128)S(1)}, f32[96,1024]{1,0:T(8,128)S(1)}, u32[]{:S(2)}, u32[]{:S(2)}) collective-permute-start(f32[96,1024]{1,0:T(8,128)S(1)} %get-tuple-element.185), channel_id=1, source_target_pairs={{0,12},{4,0},{8,4},{12,8},{1,13},{5,1},{9,5},{13,9},{2,14},{6,2},{... | collective-permute-start | bytes 1179656 | tf_op jit(solution)/shard_map/ppermute | solution.py:371
  80.8 2.2 %grads_b1.1 = (bf16[1,1024,256]{2,1,0:T(8,128)(2,1)S(1)}, bf16[1,1024,256]{2,1,0:T(8,128)(2,1)S(1)}, f32[1,256,256]{2,1,0:T(8,128)S(1)}, f32[1,64,256]{2,1,0:T(8...) custom-call(s32[4]{0:T(128)S(1)} %pad_add_fusion.idx.refs_0_, ...), custom_call_target="tpu_custom_call" | custom-call | flops 4000000000 | bytes 1048576 | tf_op jit(solution)/shard_map/grads_b1/pallas_call | solution.py:501
  83.0 2.1 %weights_1.1 = (f32[88,1024]{1,0:T(8,128)S(1)}, f32[104,1024]{1,0:T(8,128)S(1)}, f32[104,1024]{1,0:T(8,128)S(1)}, f32[88,1024]{1,0:T(8,128)S(1)}, f32[32,1024]{1,0:T(8,128)S(1)}) custom-call(s32[4]{0:T(128)S(1)} %pad_add_fusion.idx.refs_0_, f32[4,128,256]{2,1,0:T(8,128)S(1)} %pack.3.refs_1_, f32[4,128,256]{2,1,0:T(8,128)S(1)} %pack.2.refs_1_.refs_2_, ...), custom_call_target="tpu_custom_call" | custom-call | flops 3000000000 | bytes 1048576 | tf_op jit(solution)/shard_map/weights_1/pallas_call | solution.py:516
  85.1 2.1 %collective-permute-start.23 = (f32[104,1024]{1,0:T(8,128)S(1)}, f32[104,1024]{1,0:T(8,128)S(1)}, u32[]{:S(2)}, u32[]{:S(2)}) collective-permute-start(f32[104,1024]{1,0:T(8,128)S(1)} %get-tuple-element.200), channel_id=1, source_target_pairs={{0,12},{4,0},{8,4},{12,8},{1,13},{5,1},{9,5},{13,9},{2,14},{6,2},{... | collective-permute-start | bytes 1277960 | tf_op jit(solution)/shard_map/ppermute | solution.py:371
  87.3 1.5 %collective-permute-start.25 = (f32[32,1024]{1,0:T(8,128)S(1)}, f32[32,1024]{1,0:T(8,128)S(1)}, u32[]{:S(2)}, u32[]{:S(2)}) collective-permute-start(f32[32,1024]{1,0:T(8,128)S(1)} %get-tuple-element.204), channel_id=1, source_target_pairs={{0,8},{4,12},{8,0},{12,4},{1,9},{5,13},{9,1},{13,5},{2,10},{6,14},... | collective-permute-start | bytes 393224 | tf_op jit(solution)/shard_map/ppermute | solution.py:371
  88.8 0.9 collective-permute-done.21.w_up
  89.7 1.4 %collective-permute-done.22.w_down.refs_2_ = f32[96,1024]{1,0:T(8,128)S(1)} collective-permute-done((f32[96,1024]{1,0:T(8,128)S(1)}, f32[96,1024]{1,0:T(8,128)S(1)}, u32[]{:S(2)}, u32[]{:S(2)}) %collective-permute-start.22) | collective-permute-done | bytes 393248 | tf_op jit(solution)/shard_map/ppermute | solution.py:371
  91.2 1.0 collective-permute-start.26
  92.1 8.8 %collective-permute-done.23.v_down = f32[104,1024]{1,0:T(8,128)S(1)} collective-permute-done((f32[104,1024]{1,0:T(8,128)S(1)}, f32[104,1024]{1,0:T(8,128)S(1)}, u32[]{:S(2)}, u32[]{:S(2)}) %collective-permute-start.23) | collective-permute-done | bytes 426016 | tf_op jit(solution)/shard_map/ppermute | solution.py:371
  101.0 3.0 %collective-permute-done.24.v_up.refs_4_ = f32[104,1024]{1,0:T(8,128)S(1)} collective-permute-done((f32[104,1024]{1,0:T(8,128)S(1)}, f32[104,1024]{1,0:T(8,128)S(1)}, u32[]{:S(2)}, u32[]{:S(2)}) %collective-permute-start.24) | collective-permute-done | bytes 426016 | tf_op jit(solution)/shard_map/ppermute | solution.py:371
  104.0 0.7 collective-permute-start.27
  104.8 2.8 %update.1 = (f32[2,64,512]{2,1,0:T(8,128)}, f32[2,512]{1,0:T(2,128)S(1)}) custom-call(s32[4]{0:T(128)S(1)} %pad_add_fusion.idx.refs_0_, f32[2,64,256]{2,1,0:T(8,128)S(1)} %get-tuple-element.166.ga0, f32[2,64,256]{2,1,0:T(8,128)S(1)} %collective-permute-done.16.refs_11_.ga1, f32[2,64,256]{2,1,0:T(8,128)S(1)} %collective-permute-done.17.refs_12_.ga2, ...), custom_call_target="tpu_custom_call" | custom-call | flops 5000000000 | bytes 1048576 | tf_op jit(solution)/shard_map/update/pallas_call | solution.py:546
  107.5 0.6 copy.23
  108.1 1.6 %collective-permute-done.26.refs_1_ = f32[80,1024]{1,0:T(8,128)S(1)} collective-permute-done((f32[80,1024]{1,0:T(8,128)S(1)}, f32[80,1024]{1,0:T(8,128)S(1)}, u32[]{:S(2)}, u32[]{:S(2)}) %collective-permute-start.26) | collective-permute-done | bytes 327712 | tf_op jit(solution)/shard_map/ppermute | solution.py:371
  109.8 1.7 %collective-permute-done.27.refs_5_ = f32[88,1024]{1,0:T(8,128)S(1)} collective-permute-done((f32[88,1024]{1,0:T(8,128)S(1)}, f32[88,1024]{1,0:T(8,128)S(1)}, u32[]{:S(2)}, u32[]{:S(2)}) %collective-permute-start.27) | collective-permute-done | bytes 360480 | tf_op jit(solution)/shard_map/ppermute | solution.py:371
  111.5 1.2 %sum.1 = (f32[1024,128]{1,0:T(8,128)}, f32[256,128]{1,0:T(8,128)}, f32[32,128]{1,0:T(8,128)}, f32[32,128]{1,0:T(8,128)}) custom-call(f32[32,128]{1,0:T(8,128)S(1)} %get-tuple-element.209.column, f32[80,1024]{1,0:T(8,128)S(1)} %get-tuple-element.210.refs_0_, f32[80,1024]{1,0:T(8,128)S(1)} %collective-permute-done.26.refs_1_, ...), custom_call_target="tpu_custom_call" | custom-call | flops 1000000 | bytes 1048576 | tf_op jit(solution)/shard_map/sum/pallas_call | solution.py:549
  (43 shorter events, 3.1 us)
Async XLA Ops:
  4.7 12.5 %collective-permute-start = (f32[128,256]{1,0:T(8,128)S(1)}, f32[128,256]{1,0:T(8,128)S(1)}, u32[]{:S(2)}, u32[]{:S(2)}) collective-permute-start(f32[128,256]{1,0:T(8,128)S(1)} %get-tuple-element.116), channel_id=1, source_target_pairs={{0,4},{4,8},{8,12},{12,0},{1,5},{5,9},{9,13},{13,1},{2,6},{6,10},{... | collective-permute-start | bytes 393224 | tf_op jit(solution)/shard_map/ppermute | solution.py:371
  6.8 10.5 %collective-permute-start.1 = (f32[128,256]{1,0:T(8,128)S(1)}, f32[128,256]{1,0:T(8,128)S(1)}, u32[]{:S(2)}, u32[]{:S(2)}) collective-permute-start(f32[128,256]{1,0:T(8,128)S(1)} %get-tuple-element.117), channel_id=1, source_target_pairs={{0,8},{4,12},{8,0},{12,4},{1,9},{5,13},{9,1},{13,5},{2,10},{6,14},... | collective-permute-start | bytes 393224 | tf_op jit(solution)/shard_map/ppermute | solution.py:371
  10.4 6.9 %collective-permute-start.2 = (f32[128,256]{1,0:T(8,128)S(1)}, f32[128,256]{1,0:T(8,128)S(1)}, u32[]{:S(2)}, u32[]{:S(2)}) collective-permute-start(f32[128,256]{1,0:T(8,128)S(1)} %get-tuple-element.118), channel_id=1, source_target_pairs={{0,12},{4,0},{8,4},{12,8},{1,13},{5,1},{9,5},{13,9},{2,14},{6,2},{... | collective-permute-start | bytes 393224 | tf_op jit(solution)/shard_map/ppermute | solution.py:371
  17.9 14.4 %collective-permute-start.6 = (f32[4,128,256]{2,1,0:T(8,128)S(1)}, f32[4,128,256]{2,1,0:T(8,128)S(1)}, u32[]{:S(2)}, u32[]{:S(2)}) collective-permute-start(f32[4,128,256]{2,1,0:T(8,128)S(1)} %pack.2.refs_1_.refs_2_), channel_id=1, source_target_pairs={{0,2},{2,0},{1,3},{3,1},{4,6},{6,4},{5,7},{7,5},{8,10},{10,8},{9,1... | collective-permute-start | bytes 1572872 | tf_op jit(solution)/shard_map/ppermute | solution.py:375
  21.0 8.7 %collective-permute-start.3 = (f32[128,256]{1,0:T(8,128)S(1)}, f32[128,256]{1,0:T(8,128)S(1)}, u32[]{:S(2)}, u32[]{:S(2)}) collective-permute-start(f32[128,256]{1,0:T(8,128)S(1)} %get-tuple-element.127), channel_id=1, source_target_pairs={{0,4},{4,8},{8,12},{12,0},{1,5},{5,9},{9,13},{13,1},{2,6},{6,10},{... | collective-permute-start | bytes 393224 | tf_op jit(solution)/shard_map/ppermute | solution.py:371
  22.0 7.6 %collective-permute-start.4 = (f32[128,256]{1,0:T(8,128)S(1)}, f32[128,256]{1,0:T(8,128)S(1)}, u32[]{:S(2)}, u32[]{:S(2)}) collective-permute-start(f32[128,256]{1,0:T(8,128)S(1)} %get-tuple-element.128), channel_id=1, source_target_pairs={{0,8},{4,12},{8,0},{12,4},{1,9},{5,13},{9,1},{13,5},{2,10},{6,14},... | collective-permute-start | bytes 393224 | tf_op jit(solution)/shard_map/ppermute | solution.py:371
  23.7 4.3 %copy-start = (f32[1024,2,256]{2,1,0:T(2,128)S(1)}, f32[1024,2,256]{2,1,0:T(2,128)}, u32[]{:S(2)}) copy-start(f32[1024,2,256]{2,1,0:T(2,128)} %param.17) | copy-start | bytes 6291460
  23.7 4.3 %copy-start.1 = (f32[4096]{0:T(1024)S(1)}, f32[4096]{0:T(1024)}, u32[]{:S(2)}) copy-start(f32[4096]{0:T(1024)} %param.20) | copy-start | bytes 49156
  23.7 6.0 %collective-permute-start.5 = (f32[128,256]{1,0:T(8,128)S(1)}, f32[128,256]{1,0:T(8,128)S(1)}, u32[]{:S(2)}, u32[]{:S(2)}) collective-permute-start(f32[128,256]{1,0:T(8,128)S(1)} %get-tuple-element.129), channel_id=1, source_target_pairs={{0,12},{4,0},{8,4},{12,8},{1,13},{5,1},{9,5},{13,9},{2,14},{6,2},{... | collective-permute-start | bytes 393224 | tf_op jit(solution)/shard_map/ppermute | solution.py:371
  30.3 5.0 %collective-permute-start.7 = (f32[4,128,256]{2,1,0:T(8,128)S(1)}, f32[4,128,256]{2,1,0:T(8,128)S(1)}, u32[]{:S(2)}, u32[]{:S(2)}) collective-permute-start(f32[4,128,256]{2,1,0:T(8,128)S(1)} %pack.3.refs_1_), channel_id=1, source_target_pairs={{0,1},{1,0},{2,3},{3,2},{4,5},{5,4},{6,7},{7,6},{8,9},{9,8},{10,11... | collective-permute-start | bytes 1572872 | tf_op jit(solution)/shard_map/ppermute | solution.py:375
  32.3 3.0 %collective-permute-start.8 = (f32[4,128,256]{2,1,0:T(8,128)S(1)}, f32[4,128,256]{2,1,0:T(8,128)S(1)}, u32[]{:S(2)}, u32[]{:S(2)}) collective-permute-start(f32[4,128,256]{2,1,0:T(8,128)S(1)} %collective-permute-done.6.refs_2_), channel_id=1, source_target_pairs={{0,1},{1,0},{2,3},{3,2},{4,5},{5,4},{6,7},{7,6},{8,9},{9,8},{10,11... | collective-permute-start | bytes 1572872 | tf_op jit(solution)/shard_map/ppermute | solution.py:375
  32.3 15.8 %collective-permute-start.10 = (f32[4,128,256]{2,1,0:T(8,128)S(1)}, f32[4,128,256]{2,1,0:T(8,128)S(1)}, u32[]{:S(2)}, u32[]{:S(2)}) collective-permute-start(f32[4,128,256]{2,1,0:T(8,128)S(1)} %pack.3.refs_1_), channel_id=1, source_target_pairs={{0,2},{2,0},{1,3},{3,1},{4,6},{6,4},{5,7},{7,5},{8,10},{10,8},{9,1... | collective-permute-start | bytes 1572872 | tf_op jit(solution)/shard_map/ppermute | solution.py:375
  42.5 5.8 %collective-permute-start.9 = (f32[264,128]{1,0:T(8,128)S(1)}, f32[264,128]{1,0:T(8,128)S(1)}, u32[]{:S(2)}, u32[]{:S(2)}) collective-permute-start(f32[264,128]{1,0:T(8,128)S(1)} %get-tuple-element.145), channel_id=1, source_target_pairs={{0,32},{16,48},{32,0},{48,16},{64,96},{80,112},{96,64},{112,80},{1... | collective-permute-start | bytes 405512 | tf_op jit(solution)/shard_map/ppermute | solution.py:375
  44.1 7.3 %collective-permute-start.12 = (f32[4,128,256]{2,1,0:T(8,128)S(1)}, f32[4,128,256]{2,1,0:T(8,128)S(1)}, u32[]{:S(2)}, u32[]{:S(2)}) collective-permute-start(f32[4,128,256]{2,1,0:T(8,128)S(1)} %pack.2.refs_1_.refs_2_), channel_id=1, source_target_pairs={{0,1},{1,0},{2,3},{3,2},{4,5},{5,4},{6,7},{7,6},{8,9},{9,8},{10,11... | collective-permute-start | bytes 1572872 | tf_op jit(solution)/shard_map/ppermute | solution.py:375
  48.3 3.1 %collective-permute-start.13 = (f32[4,128,256]{2,1,0:T(8,128)S(1)}, f32[4,128,256]{2,1,0:T(8,128)S(1)}, u32[]{:S(2)}, u32[]{:S(2)}) collective-permute-start(f32[4,128,256]{2,1,0:T(8,128)S(1)} %collective-permute-done.10.refs_2_), channel_id=1, source_target_pairs={{0,1},{1,0},{2,3},{3,2},{4,5},{5,4},{6,7},{7,6},{8,9},{9,8},{10,11... | collective-permute-start | bytes 1572872 | tf_op jit(solution)/shard_map/ppermute | solution.py:375
  48.3 7.3 %collective-permute-start.11 = (f32[264,128]{1,0:T(8,128)S(1)}, f32[264,128]{1,0:T(8,128)S(1)}, u32[]{:S(2)}, u32[]{:S(2)}) collective-permute-start(f32[264,128]{1,0:T(8,128)S(1)} %add.16), channel_id=1, source_target_pairs={{0,96},{16,112},{32,64},{48,80},{64,32},{80,48},{96,0},{112,16},{1... | collective-permute-start | bytes 405512 | tf_op jit(solution)/shard_map/ppermute | solution.py:375
  55.7 5.4 %copy-start.2 = (s32[1,128]{1,0:T(1,128)S(1)}, s32[1,128]{1,0:T(1,128)}, u32[]{:S(2)}) copy-start(s32[1,128]{1,0:T(1,128)} %labels.1) | copy-start | bytes 1540
  55.7 5.4 %collective-permute-start.14 = (f32[264,128]{1,0:T(8,128)S(1)}, f32[264,128]{1,0:T(8,128)S(1)}, u32[]{:S(2)}, u32[]{:S(2)}) collective-permute-start(f32[264,128]{1,0:T(8,128)S(1)} %add.17.mine), channel_id=1, source_target_pairs={{0,16},{16,0},{32,48},{48,32},{64,80},{80,64},{96,112},{112,96},{1... | collective-permute-start | bytes 405512 | tf_op jit(solution)/shard_map/ppermute | solution.py:375
  62.2 2.9 %collective-permute-start.15 = (f32[264,128]{1,0:T(8,128)S(1)}, f32[264,128]{1,0:T(8,128)S(1)}, u32[]{:S(2)}, u32[]{:S(2)}) collective-permute-start(f32[264,128]{1,0:T(8,128)S(1)} %get-tuple-element.160.refs_1_), channel_id=1, source_target_pairs={{0,1},{1,0},{2,3},{3,2},{4,5},{5,4},{6,7},{7,6},{8,9},{9,8},{10,11... | collective-permute-start | bytes 405512 | tf_op jit(solution)/shard_map/ppermute | solution.py:375
  62.2 7.5 %collective-permute-start.19 = (f32[264,128]{1,0:T(8,128)S(1)}, f32[264,128]{1,0:T(8,128)S(1)}, u32[]{:S(2)}, u32[]{:S(2)}) collective-permute-start(f32[264,128]{1,0:T(8,128)S(1)} %get-tuple-element.160.refs_1_), channel_id=1, source_target_pairs={{0,2},{2,0},{1,3},{3,1},{4,6},{6,4},{5,7},{7,5},{8,10},{10,8},{9,1... | collective-permute-start | bytes 405512 | tf_op jit(solution)/shard_map/ppermute | solution.py:375
  69.7 3.7 %collective-permute-start.20 = (f32[264,128]{1,0:T(8,128)S(1)}, f32[264,128]{1,0:T(8,128)S(1)}, u32[]{:S(2)}, u32[]{:S(2)}) collective-permute-start(f32[264,128]{1,0:T(8,128)S(1)} %collective-permute-done.19.refs_1_), channel_id=1, source_target_pairs={{0,1},{1,0},{2,3},{3,2},{4,5},{5,4},{6,7},{7,6},{8,9},{9,8},{10,11... | collective-permute-start | bytes 405512 | tf_op jit(solution)/shard_map/ppermute | solution.py:375
  69.7 11.1 %collective-permute-start.16 = (f32[2,64,256]{2,1,0:T(8,128)S(1)}, f32[2,64,256]{2,1,0:T(8,128)S(1)}, u32[]{:S(2)}, u32[]{:S(2)}) collective-permute-start(f32[2,64,256]{2,1,0:T(8,128)S(1)} %get-tuple-element.167), channel_id=1, source_target_pairs={{0,4},{4,8},{8,12},{12,0},{1,5},{5,9},{9,13},{13,1},{2,6},{6,10},{... | collective-permute-start | bytes 393224 | tf_op jit(solution)/shard_map/ppermute | solution.py:371
  70.7 10.1 %collective-permute-start.17 = (f32[2,64,256]{2,1,0:T(8,128)S(1)}, f32[2,64,256]{2,1,0:T(8,128)S(1)}, u32[]{:S(2)}, u32[]{:S(2)}) collective-permute-start(f32[2,64,256]{2,1,0:T(8,128)S(1)} %get-tuple-element.168), channel_id=1, source_target_pairs={{0,8},{4,12},{8,0},{12,4},{1,9},{5,13},{9,1},{13,5},{2,10},{6,14},... | collective-permute-start | bytes 393224 | tf_op jit(solution)/shard_map/ppermute | solution.py:371
  72.9 7.9 %collective-permute-start.18 = (f32[2,64,256]{2,1,0:T(8,128)S(1)}, f32[2,64,256]{2,1,0:T(8,128)S(1)}, u32[]{:S(2)}, u32[]{:S(2)}) collective-permute-start(f32[2,64,256]{2,1,0:T(8,128)S(1)} %get-tuple-element.169), channel_id=1, source_target_pairs={{0,12},{4,0},{8,4},{12,8},{1,13},{5,1},{9,5},{13,9},{2,14},{6,2},{... | collective-permute-start | bytes 393224 | tf_op jit(solution)/shard_map/ppermute | solution.py:371
  77.5 12.2 %collective-permute-start.21 = (f32[96,1024]{1,0:T(8,128)S(1)}, f32[96,1024]{1,0:T(8,128)S(1)}, u32[]{:S(2)}, u32[]{:S(2)}) collective-permute-start(f32[96,1024]{1,0:T(8,128)S(1)} %get-tuple-element.184), channel_id=1, source_target_pairs={{0,4},{4,8},{8,12},{12,0},{1,5},{5,9},{9,13},{13,1},{2,6},{6,10},{... | collective-permute-start | bytes 1179656 | tf_op jit(solution)/shard_map/ppermute | solution.py:371
  79.1 12.1 %collective-permute-start.22 = (f32[96,1024]{1,0:T(8,128)S(1)}, f32[96,1024]{1,0:T(8,128)S(1)}, u32[]{:S(2)}, u32[]{:S(2)}) collective-permute-start(f32[96,1024]{1,0:T(8,128)S(1)} %get-tuple-element.185), channel_id=1, source_target_pairs={{0,12},{4,0},{8,4},{12,8},{1,13},{5,1},{9,5},{13,9},{2,14},{6,2},{... | collective-permute-start | bytes 1179656 | tf_op jit(solution)/shard_map/ppermute | solution.py:371
  83.0 4.2 %copy-start.3 = (f32[2,1,512]{2,1,0:T(1,128)S(1)}, f32[2,1,512]{2,1,0:T(1,128)}, u32[]{:S(2)}) copy-start(f32[2,1,512]{2,1,0:T(1,128)} %param.15) | copy-start | bytes 12292
  85.1 15.9 %collective-permute-start.23 = (f32[104,1024]{1,0:T(8,128)S(1)}, f32[104,1024]{1,0:T(8,128)S(1)}, u32[]{:S(2)}, u32[]{:S(2)}) collective-permute-start(f32[104,1024]{1,0:T(8,128)S(1)} %get-tuple-element.200), channel_id=1, source_target_pairs={{0,12},{4,0},{8,4},{12,8},{1,13},{5,1},{9,5},{13,9},{2,14},{6,2},{... | collective-permute-start | bytes 1277960 | tf_op jit(solution)/shard_map/ppermute | solution.py:371
  87.2 16.7 %collective-permute-start.24 = (f32[104,1024]{1,0:T(8,128)S(1)}, f32[104,1024]{1,0:T(8,128)S(1)}, u32[]{:S(2)}, u32[]{:S(2)}) collective-permute-start(f32[104,1024]{1,0:T(8,128)S(1)} %get-tuple-element.201), channel_id=1, source_target_pairs={{0,4},{4,8},{8,12},{12,0},{1,5},{5,9},{9,13},{13,1},{2,6},{6,10},{... | collective-permute-start | bytes 1277960 | tf_op jit(solution)/shard_map/ppermute | solution.py:371
  87.3 17.5 %collective-permute-start.25 = (f32[32,1024]{1,0:T(8,128)S(1)}, f32[32,1024]{1,0:T(8,128)S(1)}, u32[]{:S(2)}, u32[]{:S(2)}) collective-permute-start(f32[32,1024]{1,0:T(8,128)S(1)} %get-tuple-element.204), channel_id=1, source_target_pairs={{0,8},{4,12},{8,0},{12,4},{1,9},{5,13},{9,1},{13,5},{2,10},{6,14},... | collective-permute-start | bytes 393224 | tf_op jit(solution)/shard_map/ppermute | solution.py:371
  91.2 18.6 %collective-permute-start.26 = (f32[80,1024]{1,0:T(8,128)S(1)}, f32[80,1024]{1,0:T(8,128)S(1)}, u32[]{:S(2)}, u32[]{:S(2)}) collective-permute-start(f32[80,1024]{1,0:T(8,128)S(1)} %slice_add_fusion.1), channel_id=1, source_target_pairs={{0,4},{4,8},{8,12},{12,0},{1,5},{5,9},{9,13},{13,1},{2,6},{6,10},{... | collective-permute-start | bytes 983048 | tf_op jit(solution)/shard_map/ppermute | solution.py:371
  104.0 7.5 %collective-permute-start.27 = (f32[88,1024]{1,0:T(8,128)S(1)}, f32[88,1024]{1,0:T(8,128)S(1)}, u32[]{:S(2)}, u32[]{:S(2)}) collective-permute-start(f32[88,1024]{1,0:T(8,128)S(1)} %slice_add_fusion), channel_id=1, source_target_pairs={{0,12},{4,0},{8,4},{12,8},{1,13},{5,1},{9,5},{13,9},{2,14},{6,2},{... | collective-permute-start | bytes 1081352 | tf_op jit(solution)/shard_map/ppermute | solution.py:371
